TPU v7x, 256 devices: a whole 4x4x8 slice. The times are simulated.
256 devices in a mesh: row: 16 (over x, z_hi, core), col: 16 (over z_lo, y).
Axes of the slice: x: 4, y: 4, z: 8 (z_hi: 2, z_lo: 4; z = z_hi * 4 + z_lo), core: 2. Of those that a mesh axis runs over, the one named last changes fastest.
Arguments:
- ancestor_inverse: bfloat16 [24576, 24576], P('row', 'col'), may hold values from -0.0390625 to 0.0390625
- panels: bfloat16 [24576, 3, 512], P(('row', 'col')), may hold values from -1.1953125 to 1.1953125
- diag_inverse: float32 [3, 512, 512], replicated, may hold values from -6 to 6
- tile_mask: int32 [3, 192], replicated, may hold values 0 or 1
Outputs:
- off_diagonal: float32 [24576, 3, 512], P(('row', 'col'))
- diagonal: float32 [3, 512, 512], replicated
All inputs are finite; a program needn't handle non-finite values.
Results may differ from a plain program's by a relative error of at most 0.0003.
Values may be sent and summed in bfloat16 or wider, within the bound.
No kernel may reach another device: no remote copies, remote signals or barrier semaphores. Data moves between devices by JAX's collectives and lax.ppermute only.
A program may use at most 192 MiB of HBM per device.

v0:
```python
import functools

import jax
import jax.numpy as jnp
from jax import lax
from jax.experimental import pallas as pl
from jax.experimental.pallas import tpu as pltpu
from jax.sharding import Mesh
from jax.sharding import PartitionSpec as P

TILE = 128
AXES = ("x", "h", "core", "l", "y")
SIZES = (4, 2, 2, 4, 4)
ROW = ("x", "h", "core")
COL = ("l", "y")
EXTRA = 16
STEPS = 64.0
TOP = 32766.0
LN2 = 0.6931471805599453
VMEM = pl.BlockSpec(memory_space=pltpu.VMEM)
SMEM = pl.BlockSpec(memory_space=pltpu.SMEM)
F32, BF16, I16, I32 = jnp.float32, jnp.bfloat16, jnp.int16, jnp.int32


def coords(device):
    out = []
    for size in SIZES[::-1]:
        out.append(device % size)
        device //= size
    return tuple(out[::-1])


def number(place):
    value = 0
    for size, at in zip(SIZES, place):
        value = value * size + at
    return value


def send(value, move):
    pairs = [(d, number(move(*coords(d)))) for d in range(256)]
    return lax.ppermute(value, AXES, pairs)


def over_x(k):
    return lambda x, h, c, l, y: (x ^ k, h, c, l, y)


def over_y(k):
    return lambda x, h, c, l, y: (x, h, c, l, y ^ k)


def over_l(k):
    return lambda x, h, c, l, y: (x, h, c, l ^ k, y)


def over_h(x, h, c, l, y):
    return (x, 1 - h, c, l, y)


def over_core(x, h, c, l, y):
    return (x, h, 1 - c, l, y)


def spread(x, h, c, l, y):
    return (x ^ l, h, c, l, y)


def turn(i):
    return lambda x, h, c, l, y: (x, (y & 1) ^ i, y >> 1, x ^ l, 2 * h + c)


def params(limit=48):
    return pltpu.CompilerParams(vmem_limit_bytes=limit * 1024 * 1024)


def cost(flops, moved):
    return pl.CostEstimate(flops=flops // 1000, bytes_accessed=moved // 1000, transcendentals=0)


def diagonal_mask(rows, width):
    row = lax.broadcasted_iota(I32, (rows, width), 0)
    lane = lax.broadcasted_iota(I32, (rows, width), 1)
    return row == lane


def encode(value, out_ref, start=0):
    rows, width = value.shape
    largest = jnp.maximum(jnp.max(jnp.abs(value), axis=1, keepdims=True), 1e-30)
    level = jnp.ceil(jnp.log(largest * (1.0 / TOP)) * (STEPS / LN2))
    coded = jnp.round(value * jnp.exp2(level * (-1.0 / STEPS)))
    out_ref[start : start + rows, :] = coded.astype(I32).astype(I16)
    line = jnp.sum(jnp.where(diagonal_mask(rows, width), level, 0.0), axis=0, keepdims=True)
    lines = jnp.broadcast_to(line, (EXTRA, width))
    out_ref[start + rows : start + rows + EXTRA, :] = lines.astype(I32).astype(I16)


def decode(in_ref, start=0, rows=None):
    rows, width = rows or in_ref.shape[0] - EXTRA, in_ref.shape[1]
    coded = in_ref[start : start + rows, :].astype(I32).astype(F32)
    line = in_ref[start + rows : start + rows + EXTRA, :].astype(I32).astype(F32)[:1]
    level = jnp.sum(
        jnp.where(diagonal_mask(rows, width), jnp.broadcast_to(line, (rows, width)), 0.0),
        axis=1,
        keepdims=True,
    )
    return coded * jnp.exp2(level * (1.0 / STEPS))


def product_kernel(at_ref, a_ref, own_ref, other_ref, keep_ref, q1_ref, q2_ref, q3_ref, m_ref):
    step = pl.program_id(0)
    shard = own_ref.shape[2]

    @pl.when(step == 0)
    def _():
        core, h, t = at_ref[1], at_ref[2], at_ref[3]
        for k in range(4):
            for i in range(2):
                base = (k ^ t) * (4 * shard) + (i ^ h) * shard
                first = pl.multiple_of(base + core * (2 * shard), 32)
                second = pl.multiple_of(base + (1 - core) * (2 * shard), 32)
                m_ref[pl.ds(first, shard), :] = own_ref[k, i]
                m_ref[pl.ds(second, shard), :] = other_ref[k, i]

    block = a_ref[...]
    lines = block.reshape(4 * block.shape[2], block.shape[3])
    value = jnp.dot(lines, m_ref[...], preferred_element_type=F32)

    for at, ref in enumerate((q1_ref, q2_ref, q3_ref)):

        @pl.when(step == at)
        def _(ref=ref):
            encode(value, ref)

    @pl.when(step == 3)
    def _():
        keep_ref[...] = value


def product(at, a4, own, other):
    shard, order = a4.shape[2], a4.shape[3]
    width = own.shape[3]
    rows = 4 * shard
    whole = pl.BlockSpec((4, 2, shard, width), lambda g, s: (0, 0, 0, 0))
    coded = pl.BlockSpec((rows + EXTRA, width), lambda g, s: (0, 0))
    return pl.pallas_call(
        product_kernel,
        grid_spec=pltpu.PrefetchScalarGridSpec(
            num_scalar_prefetch=1,
            grid=(4,),
            in_specs=[
                pl.BlockSpec(
                    (4, 1, shard, order), lambda g, s: (0, s[0] ^ ((g + 1) & 3), 0, 0)
                ),
                whole,
                whole,
            ],
            out_specs=[pl.BlockSpec((rows, width), lambda g, s: (0, 0))] + [coded] * 3,
            scratch_shapes=[pltpu.VMEM((order, width), BF16)],
        ),
        out_shape=[jax.ShapeDtypeStruct((rows, width), F32)]
        + [jax.ShapeDtypeStruct((rows + EXTRA, width), I16)] * 3,
        compiler_params=params(),
        cost_estimate=cost(8 * rows * order * width, 2 * order * order),
        name="product",
    )(at, a4, own, other)


def middle_kernel(panels, *refs):
    at_ref, refs = refs[0], refs[1:]
    keeps, refs = refs[:panels], refs[panels:]
    parts, refs = refs[: 3 * panels], refs[3 * panels :]
    own_ref, *coded = refs[:4]
    sum_ref = refs[4]
    shard = own_ref.shape[0] // panels
    l = at_ref[4]

    def part(k):
        return sum_ref[pl.ds(pl.multiple_of((l ^ k) * shard, 32), shard), :]

    for p in range(panels):
        value = keeps[p][...]
        for ref in parts[3 * p : 3 * p + 3]:
            value = value + decode(ref)
        sum_ref[...] = value
        own_ref[p * shard : (p + 1) * shard, :] = part(0)
        for k in (1, 2, 3):
            encode(part(k), coded[k - 1], p * (shard + EXTRA))


def middle(at, keeps, parts):
    rows, width = keeps[0].shape
    panels, shard = len(keeps), rows // 4
    return pl.pallas_call(
        functools.partial(middle_kernel, panels),
        in_specs=[SMEM] + [VMEM] * (4 * panels),
        out_specs=[VMEM] * 4,
        out_shape=[jax.ShapeDtypeStruct((panels * shard, width), F32)]
        + [jax.ShapeDtypeStruct((panels * (shard + EXTRA), width), I16)] * 3,
        scratch_shapes=[pltpu.VMEM((rows, width), F32)],
        compiler_params=params(),
        cost_estimate=cost(8 * rows * width, 16 * rows * width),
        name="middle",
    )(at, *keeps, *sum(parts, []))


def last_kernel(panels, at_ref, own_ref, r1_ref, r2_ref, r3_ref, masked_ref, out_ref, mine_ref, theirs_ref):
    shard = out_ref.shape[1]
    half = mine_ref.shape[0] // panels
    core = at_ref[1]
    for p in range(panels):
        total = own_ref[p * shard : (p + 1) * shard, :]
        for ref in (r1_ref, r2_ref, r3_ref):
            total = total + decode(ref, p * (shard + EXTRA), shard)
        total = -total
        out_ref[p] = total
        high = total.astype(BF16)
        rest = total - high.astype(F32)
        mid = rest.astype(BF16)
        low = (rest - mid.astype(F32)).astype(BF16)
        for which, out in ((core, mine_ref), (1 - core, theirs_ref)):
            left = masked_ref[p, :, pl.ds(pl.multiple_of(which * half, 128), half)]
            dims = (((0,), (0,)), ((), ()))
            terms = [
                lax.dot_general(left, r, dims, preferred_element_type=F32) for r in (low, mid, high)
            ]
            out[p * half : (p + 1) * half, :] = (terms[0] + terms[1]) + terms[2]


def last(at, own, parts, masked):
    panels, shard, width = masked.shape
    return pl.pallas_call(
        functools.partial(last_kernel, panels),
        in_specs=[SMEM] + [VMEM] * 5,
        out_specs=[VMEM] * 3,
        out_shape=[jax.ShapeDtypeStruct((panels, shard, width), F32)]
        + [jax.ShapeDtypeStruct((panels * (width // 2), width), F32)] * 2,
        compiler_params=params(),
        cost_estimate=cost(6 * shard * width * width, 16 * shard * width),
        name="last",
    )(at, own, *parts, masked)


def fold_kernel(*refs):
    out, count = refs[-1], len(refs) // 2
    start = 0
    for p in range(count):
        rows = refs[p].shape[0]
        out[start : start + rows, :] = refs[p][...] + refs[count + p][...]
        start += rows


def fold(mines, theirs):
    width = mines[0].shape[1]
    total = sum(mine.shape[0] for mine in mines)
    return pl.pallas_call(
        fold_kernel,
        in_specs=[VMEM] * (2 * len(mines)),
        out_specs=VMEM,
        out_shape=jax.ShapeDtypeStruct((total, width), F32),
        compiler_params=params(),
        cost_estimate=cost(total * width, 12 * total * width),
        name="fold",
    )(*mines, *theirs)


def finish_kernel(at_ref, mine_ref, theirs_ref, diag_ref, out_ref):
    half = diag_ref.shape[1] // 2
    core = at_ref[1]
    for p in range(diag_ref.shape[0]):
        for which, ref in ((core, mine_ref), (1 - core, theirs_ref)):
            place = pl.ds(pl.multiple_of(which * half, 8), half)
            out_ref[p, place, :] = diag_ref[p, place, :] - ref[p * half : (p + 1) * half, :]


def finish(at, mine, theirs, diag):
    return pl.pallas_call(
        finish_kernel,
        in_specs=[SMEM] + [VMEM] * 3,
        out_specs=VMEM,
        out_shape=jax.ShapeDtypeStruct(diag.shape, F32),
        compiler_params=params(),
        cost_estimate=cost(diag.size, 12 * diag.size),
        name="finish",
    )(at, mine, theirs, diag)


def after(values, *earlier):
    return lax.optimization_barrier((values, earlier))[0]


def body(ancestor_inverse, panels, diag_inverse, tile_mask):
    x, h, core, l, y = (lax.axis_index(axis) for axis in AXES)
    at = jnp.stack([y, core, h, x ^ l, l, x]).astype(I32)
    kept, count, width = panels.shape
    order = ancestor_inverse.shape[1]
    tiles = tile_mask.shape[1]
    start = (((x * 2 + h) * 2 + core) * 16 + l * 4 + y) * kept
    tile = start // TILE
    first = lax.dynamic_slice_in_dim(tile_mask, tile, 1, 1)
    second = lax.dynamic_slice_in_dim(tile_mask, jnp.minimum(tile + 1, tiles - 1), 1, 1)
    in_first = start + jnp.arange(kept) < (tile + 1) * TILE
    own_mask = jnp.where(in_first[None, :], first, second).astype(BF16)
    masked = jnp.swapaxes(panels, 0, 1) * own_mask[:, :, None]

    moved = send(masked, spread)
    turned = [send(moved, turn(i)) for i in range(2)]
    a4 = ancestor_inverse.reshape(4, 4, kept, order)
    def gather(messages):
        found = [send(messages, over_x(k)) for k in (1, 2, 3)]
        return jnp.stack([messages] + found, axis=1)

    messages = jnp.stack([turned[0], turned[1]], axis=1)
    own_a = gather(messages[:1])
    other_a = send(own_a, over_core)
    rest = after(messages[1:], own_a)
    keep, *coded = product(at, a4, own_a[0], other_a[0])
    keeps = [keep]
    parts = [[send(coded[k - 1], over_y(k)) for k in (1, 2, 3)]]
    found = after([send(rest, over_x(k)) for k in (1, 2, 3)], keep)
    own_b = jnp.stack([rest] + found, axis=1)
    other_b = send(own_b, over_core)
    for p in (1, 2):
        own = own_b[p - 1]
        keep, *coded = product(at, a4, own, other_b[p - 1])
        keeps.append(keep)
        parts.append([send(coded[k - 1], over_y(k)) for k in (1, 2, 3)])
    parts[:2] = after(parts[:2], keeps[2], parts[2][0])
    own_01, *coded = middle(at, keeps[:2], parts[:2])
    found = [send(coded[k - 1], over_l(k)) for k in (1, 2, 3)]
    block_01, mine_01, their_01 = last(at, own_01, found, masked[:2])
    swapped_01 = send(their_01, over_core)
    parts[2] = after(parts[2], their_01)
    own_2, *coded = middle(at, keeps[2:], parts[2:])
    found = [send(coded[k - 1], over_l(k)) for k in (1, 2, 3)]
    block_2, mine_2, their_2 = last(at, own_2, found, masked[2:])
    halves = fold([mine_01, mine_2], [swapped_01, send(their_2, over_core)])
    pieces = halves.reshape(16, -1, width)
    total = jnp.sum(lax.all_to_all(pieces, ("x", "y"), 0, 0), axis=0)
    total = total + send(total, over_h)
    total = total + send(total, over_l(1))
    total = total + send(total, over_l(2))
    pieces = jnp.broadcast_to(total[None], (16, *total.shape))
    mine = lax.all_to_all(pieces, ("x", "y"), 0, 0).reshape(halves.shape)
    diagonal = finish(at, mine, send(mine, over_core), diag_inverse)
    off_diagonal = jnp.swapaxes(jnp.concatenate([block_01, block_2]), 0, 1)
    return off_diagonal, diagonal


def solution(mesh):
    finer = Mesh(mesh.devices.reshape(SIZES), AXES)
    placed = (P(ROW, COL), P(AXES, None, None), P(), P())
    return jax.shard_map(
        body, mesh=finer, in_specs=placed, out_specs=(P(AXES, None, None), P()), check_vma=False
    )
```

profile of v0, /device:TPU:1, one launch (start us, length us, event | category | flops | bytes accessed | tf_op | source)
XLA Modules:
  0.0 246.8 jit_solution(1653098033828337317)
XLA Ops:
  3.5 9.4 %collective-permute-start.2 = (bf16[3,96,512]{2,1,0:T(8,128)(2,1)S(1)}, bf16[3,96,512]{2,1,0:T(8,128)(2,1)S(1)}, u32[]{:S(2)}, u32[]{:S(2)}) collective-permute-start(bf16[3,96,512]{2,1,0:T(8,128)(2,1)S(1)} %collective-permute-done), channel_id=1, source_target_pairs={{0,32},{1,0},{2,48},{3,16},{4,36},{5,4},{6,52},{7,20},{8,40},{9,8}... | collective-permute-start | bytes 884744 | tf_op jit(solution)/shard_map/ppermute | solution.py:42
  14.8 4.5 %collective-permute-done.2 = bf16[3,96,512]{2,1,0:T(8,128)(2,1)S(1)} collective-permute-done((bf16[3,96,512]{2,1,0:T(8,128)(2,1)S(1)}, bf16[3,96,512]{2,1,0:T(8,128)(2,1)S(1)}, u32[]{:S(2)}, u32[]{:S(2)}) %collective-permute-start.2) | collective-permute-done | bytes 294944 | tf_op jit(solution)/shard_map/ppermute | solution.py:42
  19.3 4.8 %collective-permute-done.1 = bf16[3,96,512]{2,1,0:T(8,128)(2,1)S(1)} collective-permute-done((bf16[3,96,512]{2,1,0:T(8,128)(2,1)S(1)}, bf16[3,96,512]{2,1,0:T(8,128)(2,1)S(1)}, u32[]{:S(2)}, u32[]{:S(2)}) %collective-permute-start.1) | collective-permute-done | bytes 294944 | tf_op jit(solution)/shard_map/ppermute | solution.py:42
  24.2 18.2 %collective-permute-start.4 = (bf16[1,2,96,512]{3,2,1,0:T(8,128)(2,1)S(1)}, bf16[1,2,96,512]{3,2,1,0:T(8,128)(2,1)S(1)}, u32[]{:S(2)}, u32[]{:S(2)}) collective-permute-start(bf16[1,2,96,512]{3,2,1,0:T(8,128)(2,1)S(1)} %bitcast.47), channel_id=1, source_target_pairs={{0,128},{1,129},{2,130},{3,131},{4,132},{5,133},{6,134},{7,135},{8... | collective-permute-start | bytes 589832 | tf_op jit(solution)/shard_map/ppermute | solution.py:42
  42.4 2.7 %collective-permute-start.3 = (bf16[1,2,96,512]{3,2,1,0:T(8,128)(2,1)S(1)}, bf16[1,2,96,512]{3,2,1,0:T(8,128)(2,1)S(1)}, u32[]{:S(2)}, u32[]{:S(2)}) collective-permute-start(bf16[1,2,96,512]{3,2,1,0:T(8,128)(2,1)S(1)} %bitcast.48), channel_id=1, source_target_pairs={{0,64},{1,65},{2,66},{3,67},{4,68},{5,69},{6,70},{7,71},{8,72},{9,... | collective-permute-start | bytes 589832 | tf_op jit(solution)/shard_map/ppermute | solution.py:42
  45.1 2.5 %collective-permute-done.4 = bf16[1,2,96,512]{3,2,1,0:T(8,128)(2,1)S(1)} collective-permute-done((bf16[1,2,96,512]{3,2,1,0:T(8,128)(2,1)S(1)}, bf16[1,2,96,512]{3,2,1,0:T(8,128)(2,1)S(1)}, u32[]{:S(2)}, u32[]{:S(2)}) %collective-permute-start.4) | collective-permute-done | bytes 196640 | tf_op jit(solution)/shard_map/ppermute | solution.py:42
  47.6 6.5 %collective-permute-done.3 = bf16[1,2,96,512]{3,2,1,0:T(8,128)(2,1)S(1)} collective-permute-done((bf16[1,2,96,512]{3,2,1,0:T(8,128)(2,1)S(1)}, bf16[1,2,96,512]{3,2,1,0:T(8,128)(2,1)S(1)}, u32[]{:S(2)}, u32[]{:S(2)}) %collective-permute-start.3) | collective-permute-done | bytes 196640 | tf_op jit(solution)/shard_map/ppermute | solution.py:42
  54.8 2.7 %collective-permute-start.9 = (bf16[2,2,96,512]{3,2,0,1:T(8,128)(2,1)S(1)}, bf16[2,2,96,512]{3,2,0,1:T(8,128)(2,1)S(1)}, u32[]{:S(2)}, u32[]{:S(2)}) collective-permute-start(bf16[2,2,96,512]{3,2,0,1:T(8,128)(2,1)S(1)} %pad_maximum_fusion.2), channel_id=1, source_target_pairs={{0,192},{1,193},{2,194},{3,195},{4,196},{5,197},{6,198},{7,199},{8... | collective-permute-start | bytes 1179656 | tf_op jit(solution)/shard_map/ppermute | solution.py:42
  58.3 6.2 %product.3 = (f32[384,512]{1,0:T(8,128)S(1)}, s16[400,512]{1,0:T(8,128)(2,1)S(1)}, s16[400,512]{1,0:T(8,128)(2,1)S(1)}, s16[400,512]{1,0:T(8,128)(2,1)S(1)}) custom-call(s32[6]{0:T(128)S(1)} %stack.66.at_ref.refs_0_, bf16[4,4,96,1536]{3,2,1,0:T(8,128)(2,1)} %bitcast.39, bf16[4,2,96,512]{3,2,1,0:T(8,128)(2,1)S(1)} %get-tuple-element.86.own_ref, ...), custom_call_target="tpu_custom_call" | custom-call | flops 2415919 | bytes 4718 | tf_op jit(solution)/shard_map/product/pallas_call | solution.py:146
  64.5 10.6 %collective-permute-done.9 = bf16[2,2,96,512]{3,2,0,1:T(8,128)(2,1)S(1)} collective-permute-done((bf16[2,2,96,512]{3,2,0,1:T(8,128)(2,1)S(1)}, bf16[2,2,96,512]{3,2,0,1:T(8,128)(2,1)S(1)}, u32[]{:S(2)}, u32[]{:S(2)}) %collective-permute-start.9) | collective-permute-done | bytes 393248 | tf_op jit(solution)/shard_map/ppermute | solution.py:42
  79.8 2.5 %collective-permute-start.13 = (s16[400,512]{1,0:T(8,128)(2,1)S(1)}, s16[400,512]{1,0:T(8,128)(2,1)S(1)}, u32[]{:S(2)}, u32[]{:S(2)}) collective-permute-start(s16[400,512]{1,0:T(8,128)(2,1)S(1)} %get-tuple-element.49), channel_id=1, source_target_pairs={{0,3},{1,2},{2,1},{3,0},{4,7},{5,6},{6,5},{7,4},{8,11},{9,10},{10,... | collective-permute-start | bytes 1228808 | tf_op jit(solution)/shard_map/ppermute | solution.py:42
  82.5 6.2 %product.4 = (f32[384,512]{1,0:T(8,128)S(1)}, s16[400,512]{1,0:T(8,128)(2,1)S(1)}, s16[400,512]{1,0:T(8,128)(2,1)S(1)}, s16[400,512]{1,0:T(8,128)(2,1)S(1)}) custom-call(s32[6]{0:T(128)S(1)} %stack.66.at_ref.refs_0_, bf16[4,4,96,1536]{3,2,1,0:T(8,128)(2,1)} %bitcast.40, bf16[4,2,96,512]{3,2,1,0:T(8,128)(2,1)S(1)} %get-tuple-element.84.own_ref, ...), custom_call_target="tpu_custom_call" | custom-call | flops 2415919 | bytes 4718 | tf_op jit(solution)/shard_map/product/pallas_call | solution.py:146
  90.2 6.2 %product.5 = (f32[384,512]{1,0:T(8,128)S(1)}, s16[400,512]{1,0:T(8,128)(2,1)S(1)}, s16[400,512]{1,0:T(8,128)(2,1)S(1)}, s16[400,512]{1,0:T(8,128)(2,1)S(1)}) custom-call(s32[6]{0:T(128)S(1)} %stack.66.at_ref.refs_0_, bf16[4,4,96,1536]{3,2,1,0:T(8,128)(2,1)} %bitcast.41, bf16[4,2,96,512]{3,2,1,0:T(8,128)(2,1)S(1)} %get-tuple-element.85.own_ref, ...), custom_call_target="tpu_custom_call" | custom-call | flops 2415919 | bytes 4718 | tf_op jit(solution)/shard_map/product/pallas_call | solution.py:146
  96.4 2.5 %collective-permute-start.16 = (s16[400,512]{1,0:T(8,128)(2,1)S(1)}, s16[400,512]{1,0:T(8,128)(2,1)S(1)}, u32[]{:S(2)}, u32[]{:S(2)}) collective-permute-start(s16[400,512]{1,0:T(8,128)(2,1)S(1)} %get-tuple-element.52), channel_id=1, source_target_pairs={{0,3},{1,2},{2,1},{3,0},{4,7},{5,6},{6,5},{7,4},{8,11},{9,10},{10,... | collective-permute-start | bytes 1228808 | tf_op jit(solution)/shard_map/ppermute | solution.py:42
  100.3 6.6 %collective-permute-done.14.refs_6_ = s16[400,512]{1,0:T(8,128)(2,1)S(1)} collective-permute-done((s16[400,512]{1,0:T(8,128)(2,1)S(1)}, s16[400,512]{1,0:T(8,128)(2,1)S(1)}, u32[]{:S(2)}, u32[]{:S(2)}) %collective-permute-start.14) | collective-permute-done | bytes 409632 | tf_op jit(solution)/shard_map/ppermute | solution.py:42
  106.8 8.8 %collective-permute-done.15.refs_7_ = s16[400,512]{1,0:T(8,128)(2,1)S(1)} collective-permute-done((s16[400,512]{1,0:T(8,128)(2,1)S(1)}, s16[400,512]{1,0:T(8,128)(2,1)S(1)}, u32[]{:S(2)}, u32[]{:S(2)}) %collective-permute-start.15) | collective-permute-done | bytes 409632 | tf_op jit(solution)/shard_map/ppermute | solution.py:42
  117.9 6.6 %collective-permute-done.17.refs_2_ = s16[400,512]{1,0:T(8,128)(2,1)S(1)} collective-permute-done((s16[400,512]{1,0:T(8,128)(2,1)S(1)}, s16[400,512]{1,0:T(8,128)(2,1)S(1)}, u32[]{:S(2)}, u32[]{:S(2)}) %collective-permute-start.17) | collective-permute-done | bytes 409632 | tf_op jit(solution)/shard_map/ppermute | solution.py:42
  126.4 3.4 %collective-permute-start.20 = (s16[224,512]{1,0:T(8,128)(2,1)S(1)}, s16[224,512]{1,0:T(8,128)(2,1)S(1)}, u32[]{:S(2)}, u32[]{:S(2)}) collective-permute-start(s16[224,512]{1,0:T(8,128)(2,1)S(1)} %get-tuple-element.64), channel_id=1, source_target_pairs={{0,12},{1,13},{2,14},{3,15},{4,8},{5,9},{6,10},{7,11},{8,4},{9,5},... | collective-permute-start | bytes 688136 | tf_op jit(solution)/shard_map/ppermute | solution.py:42
  132.4 3.4 %collective-permute-done.18.r1_ref = s16[224,512]{1,0:T(8,128)(2,1)S(1)} collective-permute-done((s16[224,512]{1,0:T(8,128)(2,1)S(1)}, s16[224,512]{1,0:T(8,128)(2,1)S(1)}, u32[]{:S(2)}, u32[]{:S(2)}) %collective-permute-start.18) | collective-permute-done | bytes 229408 | tf_op jit(solution)/shard_map/ppermute | solution.py:42
  135.8 7.7 %collective-permute-done.19.r2_ref = s16[224,512]{1,0:T(8,128)(2,1)S(1)} collective-permute-done((s16[224,512]{1,0:T(8,128)(2,1)S(1)}, s16[224,512]{1,0:T(8,128)(2,1)S(1)}, u32[]{:S(2)}, u32[]{:S(2)}) %collective-permute-start.19) | collective-permute-done | bytes 229408 | tf_op jit(solution)/shard_map/ppermute | solution.py:42
  145.2 3.1 %collective-permute-start.26 = (f32[512,512]{1,0:T(8,128)S(1)}, f32[512,512]{1,0:T(8,128)S(1)}, u32[]{:S(2)}, u32[]{:S(2)}) collective-permute-start(f32[512,512]{1,0:T(8,128)S(1)} %get-tuple-element.68), channel_id=1, source_target_pairs={{0,16},{1,17},{2,18},{3,19},{4,20},{5,21},{6,22},{7,23},{8,24},{9,... | collective-permute-start | bytes 3145736 | tf_op jit(solution)/shard_map/ppermute | solution.py:42
  148.3 3.2 %collective-permute-done.22.refs_4_ = s16[400,512]{1,0:T(8,128)(2,1)S(1)} collective-permute-done((s16[400,512]{1,0:T(8,128)(2,1)S(1)}, s16[400,512]{1,0:T(8,128)(2,1)S(1)}, u32[]{:S(2)}, u32[]{:S(2)}) %collective-permute-start.22) | collective-permute-done | bytes 409632 | tf_op jit(solution)/shard_map/ppermute | solution.py:42
  153.7 2.9 %collective-permute-start.25 = (s16[112,512]{1,0:T(8,128)(2,1)S(1)}, s16[112,512]{1,0:T(8,128)(2,1)S(1)}, u32[]{:S(2)}, u32[]{:S(2)}) collective-permute-start(s16[112,512]{1,0:T(8,128)(2,1)S(1)} %get-tuple-element.75), channel_id=1, source_target_pairs={{0,12},{1,13},{2,14},{3,15},{4,8},{5,9},{6,10},{7,11},{8,4},{9,5},... | collective-permute-start | bytes 344072 | tf_op jit(solution)/shard_map/ppermute | solution.py:42
  157.2 6.7 %collective-permute-done.24.r2_ref = s16[112,512]{1,0:T(8,128)(2,1)S(1)} collective-permute-done((s16[112,512]{1,0:T(8,128)(2,1)S(1)}, s16[112,512]{1,0:T(8,128)(2,1)S(1)}, u32[]{:S(2)}, u32[]{:S(2)}) %collective-permute-start.24) | collective-permute-done | bytes 114720 | tf_op jit(solution)/shard_map/ppermute | solution.py:42
  168.8 25.6 %all_to_all.10 = f32[16,48,512]{2,1,0:T(8,128)S(1)} all-to-all(f32[16,48,512]{2,1,0:T(8,128)S(1)} %bitcast.37), channel_id=1, replica_groups=mesh['x'=4,'h'=2,'core'=2,'l'=4,'y'=4] {'x','y'}, dimensions={0} | all-to-all | bytes 3145728 | tf_op jit(solution)/shard_map/all_to_all | solution.py:339
  194.5 4.2 %collective-permute-start.28 = (f32[48,512]{1,0:T(8,128)S(1)}, f32[48,512]{1,0:T(8,128)S(1)}, u32[]{:S(2)}, u32[]{:S(2)}) collective-permute-start(f32[48,512]{1,0:T(8,128)S(1)} %reduce_sum.9), channel_id=1, source_target_pairs={{0,32},{1,33},{2,34},{3,35},{4,36},{5,37},{6,38},{7,39},{8,40},{9,... | collective-permute-start | bytes 294920 | tf_op jit(solution)/shard_map/ppermute | solution.py:42
  198.7 3.5 %collective-permute-done.28 = f32[48,512]{1,0:T(8,128)S(1)} collective-permute-done((f32[48,512]{1,0:T(8,128)S(1)}, f32[48,512]{1,0:T(8,128)S(1)}, u32[]{:S(2)}, u32[]{:S(2)}) %collective-permute-start.28) | collective-permute-done | bytes 98336 | tf_op jit(solution)/shard_map/ppermute | solution.py:42
  204.8 2.5 %collective-permute-done.29 = f32[48,512]{1,0:T(8,128)S(1)} collective-permute-done((f32[48,512]{1,0:T(8,128)S(1)}, f32[48,512]{1,0:T(8,128)S(1)}, u32[]{:S(2)}, u32[]{:S(2)}) %collective-permute-start.29) | collective-permute-done | bytes 98336 | tf_op jit(solution)/shard_map/ppermute | solution.py:42
  208.9 3.3 %collective-permute-done.30 = f32[48,512]{1,0:T(8,128)S(1)} collective-permute-done((f32[48,512]{1,0:T(8,128)S(1)}, f32[48,512]{1,0:T(8,128)S(1)}, u32[]{:S(2)}, u32[]{:S(2)}) %collective-permute-start.30) | collective-permute-done | bytes 98336 | tf_op jit(solution)/shard_map/ppermute | solution.py:42
  212.4 22.7 %all_to_all.11 = f32[16,48,512]{2,1,0:T(8,128)S(1)} all-to-all(f32[16,48,512]{2,1,0:T(8,128)S(1)} %broadcast_in_dim.35), channel_id=1, replica_groups=mesh['x'=4,'h'=2,'core'=2,'l'=4,'y'=4] {'x','y'}, dimensions={0} | all-to-all | bytes 3145728 | tf_op jit(solution)/shard_map/all_to_all | solution.py:344
  235.1 4.6 %collective-permute-start.31 = (f32[768,512]{1,0:T(8,128)S(1)}, f32[768,512]{1,0:T(8,128)S(1)}, u32[]{:S(2)}, u32[]{:S(2)}) collective-permute-start(f32[768,512]{1,0:T(8,128)S(1)} %bitcast.35), channel_id=1, source_target_pairs={{0,16},{1,17},{2,18},{3,19},{4,20},{5,21},{6,22},{7,23},{8,24},{9,... | collective-permute-start | bytes 4718600 | tf_op jit(solution)/shard_map/ppermute | solution.py:42
  242.7 4.0 %finish.1 = f32[3,512,512]{2,1,0:T(8,128)} custom-call(s32[6]{0:T(128)S(1)} %stack.66.at_ref.refs_0_, f32[768,512]{1,0:T(8,128)S(1)} %bitcast.36, f32[768,512]{1,0:T(8,128)S(1)} %collective-permute-done.31.theirs_ref, f32[3,512,512]{2,1,0:T(8,128)} %diag_ref.1), custom_call_target="tpu_custom_call" | custom-call | flops 786 | bytes 9437 | tf_op jit(solution)/shard_map/finish/pallas_call | solution.py:277
  (62 shorter events, 37.4 us)
Async XLA Ops:
  2.8 0.7 collective-permute-start
  3.5 15.8 %collective-permute-start.2 = (bf16[3,96,512]{2,1,0:T(8,128)(2,1)S(1)}, bf16[3,96,512]{2,1,0:T(8,128)(2,1)S(1)}, u32[]{:S(2)}, u32[]{:S(2)}) collective-permute-start(bf16[3,96,512]{2,1,0:T(8,128)(2,1)S(1)} %collective-permute-done), channel_id=1, source_target_pairs={{0,32},{1,0},{2,48},{3,16},{4,36},{5,4},{6,52},{7,20},{8,40},{9,8}... | collective-permute-start | bytes 884744 | tf_op jit(solution)/shard_map/ppermute | solution.py:42
  12.9 11.2 %collective-permute-start.1 = (bf16[3,96,512]{2,1,0:T(8,128)(2,1)S(1)}, bf16[3,96,512]{2,1,0:T(8,128)(2,1)S(1)}, u32[]{:S(2)}, u32[]{:S(2)}) collective-permute-start(bf16[3,96,512]{2,1,0:T(8,128)(2,1)S(1)} %collective-permute-done), channel_id=1, source_target_pairs={{0,0},{1,32},{2,16},{3,48},{4,4},{5,36},{6,20},{7,52},{8,8},{9,40}... | collective-permute-start | bytes 884744 | tf_op jit(solution)/shard_map/ppermute | solution.py:42
  24.2 23.4 %collective-permute-start.4 = (bf16[1,2,96,512]{3,2,1,0:T(8,128)(2,1)S(1)}, bf16[1,2,96,512]{3,2,1,0:T(8,128)(2,1)S(1)}, u32[]{:S(2)}, u32[]{:S(2)}) collective-permute-start(bf16[1,2,96,512]{3,2,1,0:T(8,128)(2,1)S(1)} %bitcast.47), channel_id=1, source_target_pairs={{0,128},{1,129},{2,130},{3,131},{4,132},{5,133},{6,134},{7,135},{8... | collective-permute-start | bytes 589832 | tf_op jit(solution)/shard_map/ppermute | solution.py:42
  42.4 11.7 %collective-permute-start.3 = (bf16[1,2,96,512]{3,2,1,0:T(8,128)(2,1)S(1)}, bf16[1,2,96,512]{3,2,1,0:T(8,128)(2,1)S(1)}, u32[]{:S(2)}, u32[]{:S(2)}) collective-permute-start(bf16[1,2,96,512]{3,2,1,0:T(8,128)(2,1)S(1)} %bitcast.48), channel_id=1, source_target_pairs={{0,64},{1,65},{2,66},{3,67},{4,68},{5,69},{6,70},{7,71},{8,72},{9,... | collective-permute-start | bytes 589832 | tf_op jit(solution)/shard_map/ppermute | solution.py:42
  45.1 9.0 %collective-permute-start.5 = (bf16[1,2,96,512]{3,2,0,1:T(8,128)(2,1)S(1)}, bf16[1,2,96,512]{3,2,0,1:T(8,128)(2,1)S(1)}, u32[]{:S(2)}, u32[]{:S(2)}) collective-permute-start(bf16[1,2,96,512]{3,2,0,1:T(8,128)(2,1)S(1)} %pad_maximum_fusion.3), channel_id=1, source_target_pairs={{0,192},{1,193},{2,194},{3,195},{4,196},{5,197},{6,198},{7,199},{8... | collective-permute-start | bytes 589832 | tf_op jit(solution)/shard_map/ppermute | solution.py:42
  54.2 4.0 %collective-permute-start.6 = (bf16[1,4,2,96,512]{4,3,2,1,0:T(8,128)(2,1)S(1)}, bf16[1,4,2,96,512]{4,3,2,1,0:T(8,128)(2,1)S(1)}, u32[]{:S(2)}, u32[]{:S(2)}) collective-permute-start(bf16[1,4,2,96,512]{4,3,2,1,0:T(8,128)(2,1)S(1)} %get-tuple-element.87), channel_id=1, source_target_pairs={{0,16},{1,17},{2,18},{3,19},{4,20},{5,21},{6,22},{7,23},{8,24},{9,... | collective-permute-start | bytes 2359304 | tf_op jit(solution)/shard_map/ppermute | solution.py:42
  54.8 20.3 %collective-permute-start.9 = (bf16[2,2,96,512]{3,2,0,1:T(8,128)(2,1)S(1)}, bf16[2,2,96,512]{3,2,0,1:T(8,128)(2,1)S(1)}, u32[]{:S(2)}, u32[]{:S(2)}) collective-permute-start(bf16[2,2,96,512]{3,2,0,1:T(8,128)(2,1)S(1)} %pad_maximum_fusion.2), channel_id=1, source_target_pairs={{0,192},{1,193},{2,194},{3,195},{4,196},{5,197},{6,198},{7,199},{8... | collective-permute-start | bytes 1179656 | tf_op jit(solution)/shard_map/ppermute | solution.py:42
  57.5 17.6 %collective-permute-start.8 = (bf16[2,2,96,512]{3,2,0,1:T(8,128)(2,1)S(1)}, bf16[2,2,96,512]{3,2,0,1:T(8,128)(2,1)}, u32[]{:S(2)}, u32[]{:S(2)}) collective-permute-start(bf16[2,2,96,512]{3,2,0,1:T(8,128)(2,1)S(1)} %pad_maximum_fusion.2), channel_id=1, source_target_pairs={{0,128},{1,129},{2,130},{3,131},{4,132},{5,133},{6,134},{7,135},{8... | collective-permute-start | bytes 1179656 | tf_op jit(solution)/shard_map/ppermute | solution.py:42
  57.5 18.1 %collective-permute-start.7 = (bf16[2,2,96,512]{3,2,0,1:T(8,128)(2,1)S(1)}, bf16[2,2,96,512]{3,2,0,1:T(8,128)(2,1)}, u32[]{:S(2)}, u32[]{:S(2)}) collective-permute-start(bf16[2,2,96,512]{3,2,0,1:T(8,128)(2,1)S(1)} %pad_maximum_fusion.2), channel_id=1, source_target_pairs={{0,64},{1,65},{2,66},{3,67},{4,68},{5,69},{6,70},{7,71},{8,72},{9,... | collective-permute-start | bytes 1179656 | tf_op jit(solution)/shard_map/ppermute | solution.py:42
  76.9 5.4 %collective-permute-start.10 = (bf16[2,4,2,96,512]{4,3,0,2,1:T(8,128)(2,1)S(1)}, bf16[2,4,2,96,512]{4,3,0,2,1:T(8,128)(2,1)S(1)}, u32[]{:S(2)}, u32[]{:S(2)}) collective-permute-start(bf16[2,4,2,96,512]{4,3,0,2,1:T(8,128)(2,1)S(1)} %pad_maximum_fusion), channel_id=1, source_target_pairs={{0,16},{1,17},{2,18},{3,19},{4,20},{5,21},{6,22},{7,23},{8,24},{9,... | collective-permute-start | bytes 4718600 | tf_op jit(solution)/shard_map/ppermute | solution.py:42
  78.2 18.2 %collective-permute-start.11 = (s16[400,512]{1,0:T(8,128)(2,1)S(1)}, s16[400,512]{1,0:T(8,128)(2,1)S(1)}, u32[]{:S(2)}, u32[]{:S(2)}) collective-permute-start(s16[400,512]{1,0:T(8,128)(2,1)S(1)} %get-tuple-element.47), channel_id=1, source_target_pairs={{0,1},{1,0},{2,3},{3,2},{4,5},{5,4},{6,7},{7,6},{8,9},{9,8},{10,11... | collective-permute-start | bytes 1228808 | tf_op jit(solution)/shard_map/ppermute | solution.py:42
  78.2 20.7 %collective-permute-start.12 = (s16[400,512]{1,0:T(8,128)(2,1)S(1)}, s16[400,512]{1,0:T(8,128)(2,1)S(1)}, u32[]{:S(2)}, u32[]{:S(2)}) collective-permute-start(s16[400,512]{1,0:T(8,128)(2,1)S(1)} %get-tuple-element.48), channel_id=1, source_target_pairs={{0,2},{1,3},{2,0},{3,1},{4,6},{5,7},{6,4},{7,5},{8,10},{9,11},{10,... | collective-permute-start | bytes 1228808 | tf_op jit(solution)/shard_map/ppermute | solution.py:42
  79.8 20.4 %collective-permute-start.13 = (s16[400,512]{1,0:T(8,128)(2,1)S(1)}, s16[400,512]{1,0:T(8,128)(2,1)S(1)}, u32[]{:S(2)}, u32[]{:S(2)}) collective-permute-start(s16[400,512]{1,0:T(8,128)(2,1)S(1)} %get-tuple-element.49), channel_id=1, source_target_pairs={{0,3},{1,2},{2,1},{3,0},{4,7},{5,6},{6,5},{7,4},{8,11},{9,10},{10,... | collective-permute-start | bytes 1228808 | tf_op jit(solution)/shard_map/ppermute | solution.py:42
  88.7 18.2 %collective-permute-start.14 = (s16[400,512]{1,0:T(8,128)(2,1)S(1)}, s16[400,512]{1,0:T(8,128)(2,1)S(1)}, u32[]{:S(2)}, u32[]{:S(2)}) collective-permute-start(s16[400,512]{1,0:T(8,128)(2,1)S(1)} %get-tuple-element.50), channel_id=1, source_target_pairs={{0,1},{1,0},{2,3},{3,2},{4,5},{5,4},{6,7},{7,6},{8,9},{9,8},{10,11... | collective-permute-start | bytes 1228808 | tf_op jit(solution)/shard_map/ppermute | solution.py:42
  88.8 26.9 %collective-permute-start.15 = (s16[400,512]{1,0:T(8,128)(2,1)S(1)}, s16[400,512]{1,0:T(8,128)(2,1)S(1)}, u32[]{:S(2)}, u32[]{:S(2)}) collective-permute-start(s16[400,512]{1,0:T(8,128)(2,1)S(1)} %get-tuple-element.51), channel_id=1, source_target_pairs={{0,2},{1,3},{2,0},{3,1},{4,6},{5,7},{6,4},{7,5},{8,10},{9,11},{10,... | collective-permute-start | bytes 1228808 | tf_op jit(solution)/shard_map/ppermute | solution.py:42
  96.4 21.5 %collective-permute-start.16 = (s16[400,512]{1,0:T(8,128)(2,1)S(1)}, s16[400,512]{1,0:T(8,128)(2,1)S(1)}, u32[]{:S(2)}, u32[]{:S(2)}) collective-permute-start(s16[400,512]{1,0:T(8,128)(2,1)S(1)} %get-tuple-element.52), channel_id=1, source_target_pairs={{0,3},{1,2},{2,1},{3,0},{4,7},{5,6},{6,5},{7,4},{8,11},{9,10},{10,... | collective-permute-start | bytes 1228808 | tf_op jit(solution)/shard_map/ppermute | solution.py:42
  98.9 25.5 %collective-permute-start.17 = (s16[400,512]{1,0:T(8,128)(2,1)S(1)}, s16[400,512]{1,0:T(8,128)(2,1)S(1)}, u32[]{:S(2)}, u32[]{:S(2)}) collective-permute-start(s16[400,512]{1,0:T(8,128)(2,1)S(1)} %get-tuple-element.54), channel_id=1, source_target_pairs={{0,1},{1,0},{2,3},{3,2},{4,5},{5,4},{6,7},{7,6},{8,9},{9,8},{10,11... | collective-permute-start | bytes 1228808 | tf_op jit(solution)/shard_map/ppermute | solution.py:42
  126.2 9.6 %collective-permute-start.18 = (s16[224,512]{1,0:T(8,128)(2,1)S(1)}, s16[224,512]{1,0:T(8,128)(2,1)S(1)}, u32[]{:S(2)}, u32[]{:S(2)}) collective-permute-start(s16[224,512]{1,0:T(8,128)(2,1)S(1)} %get-tuple-element.62), channel_id=1, source_target_pairs={{0,4},{1,5},{2,6},{3,7},{4,0},{5,1},{6,2},{7,3},{8,12},{9,13},{10,... | collective-permute-start | bytes 688136 | tf_op jit(solution)/shard_map/ppermute | solution.py:42
  126.3 17.2 %collective-permute-start.19 = (s16[224,512]{1,0:T(8,128)(2,1)S(1)}, s16[224,512]{1,0:T(8,128)(2,1)S(1)}, u32[]{:S(2)}, u32[]{:S(2)}) collective-permute-start(s16[224,512]{1,0:T(8,128)(2,1)S(1)} %get-tuple-element.63), channel_id=1, source_target_pairs={{0,8},{1,9},{2,10},{3,11},{4,12},{5,13},{6,14},{7,15},{8,0},{9,1},... | collective-permute-start | bytes 688136 | tf_op jit(solution)/shard_map/ppermute | solution.py:42
  126.4 17.1 %collective-permute-start.20 = (s16[224,512]{1,0:T(8,128)(2,1)S(1)}, s16[224,512]{1,0:T(8,128)(2,1)S(1)}, u32[]{:S(2)}, u32[]{:S(2)}) collective-permute-start(s16[224,512]{1,0:T(8,128)(2,1)S(1)} %get-tuple-element.64), channel_id=1, source_target_pairs={{0,12},{1,13},{2,14},{3,15},{4,8},{5,9},{6,10},{7,11},{8,4},{9,5},... | collective-permute-start | bytes 688136 | tf_op jit(solution)/shard_map/ppermute | solution.py:42
  129.9 18.4 %collective-permute-start.21 = (s16[400,512]{1,0:T(8,128)(2,1)S(1)}, s16[400,512]{1,0:T(8,128)(2,1)S(1)}, u32[]{:S(2)}, u32[]{:S(2)}) collective-permute-start(s16[400,512]{1,0:T(8,128)(2,1)S(1)} %get-tuple-element.66), channel_id=1, source_target_pairs={{0,2},{1,3},{2,0},{3,1},{4,6},{5,7},{6,4},{7,5},{8,10},{9,11},{10,... | collective-permute-start | bytes 1228808 | tf_op jit(solution)/shard_map/ppermute | solution.py:42
  130.1 21.4 %collective-permute-start.22 = (s16[400,512]{1,0:T(8,128)(2,1)S(1)}, s16[400,512]{1,0:T(8,128)(2,1)S(1)}, u32[]{:S(2)}, u32[]{:S(2)}) collective-permute-start(s16[400,512]{1,0:T(8,128)(2,1)S(1)} %get-tuple-element.67), channel_id=1, source_target_pairs={{0,3},{1,2},{2,1},{3,0},{4,7},{5,6},{6,5},{7,4},{8,11},{9,10},{10,... | collective-permute-start | bytes 1228808 | tf_op jit(solution)/shard_map/ppermute | solution.py:42
  145.2 23.5 %collective-permute-start.26 = (f32[512,512]{1,0:T(8,128)S(1)}, f32[512,512]{1,0:T(8,128)S(1)}, u32[]{:S(2)}, u32[]{:S(2)}) collective-permute-start(f32[512,512]{1,0:T(8,128)S(1)} %get-tuple-element.68), channel_id=1, source_target_pairs={{0,16},{1,17},{2,18},{3,19},{4,20},{5,21},{6,22},{7,23},{8,24},{9,... | collective-permute-start | bytes 3145736 | tf_op jit(solution)/shard_map/ppermute | solution.py:42
  152.9 4.3 %collective-permute-start.23 = (s16[112,512]{1,0:T(8,128)(2,1)S(1)}, s16[112,512]{1,0:T(8,128)(2,1)S(1)}, u32[]{:S(2)}, u32[]{:S(2)}) collective-permute-start(s16[112,512]{1,0:T(8,128)(2,1)S(1)} %get-tuple-element.73), channel_id=1, source_target_pairs={{0,4},{1,5},{2,6},{3,7},{4,0},{5,1},{6,2},{7,3},{8,12},{9,13},{10,... | collective-permute-start | bytes 344072 | tf_op jit(solution)/shard_map/ppermute | solution.py:42
  153.7 10.3 %collective-permute-start.24 = (s16[112,512]{1,0:T(8,128)(2,1)S(1)}, s16[112,512]{1,0:T(8,128)(2,1)S(1)}, u32[]{:S(2)}, u32[]{:S(2)}) collective-permute-start(s16[112,512]{1,0:T(8,128)(2,1)S(1)} %get-tuple-element.74), channel_id=1, source_target_pairs={{0,8},{1,9},{2,10},{3,11},{4,12},{5,13},{6,14},{7,15},{8,0},{9,1},... | collective-permute-start | bytes 344072 | tf_op jit(solution)/shard_map/ppermute | solution.py:42
  153.7 10.3 %collective-permute-start.25 = (s16[112,512]{1,0:T(8,128)(2,1)S(1)}, s16[112,512]{1,0:T(8,128)(2,1)S(1)}, u32[]{:S(2)}, u32[]{:S(2)}) collective-permute-start(s16[112,512]{1,0:T(8,128)(2,1)S(1)} %get-tuple-element.75), channel_id=1, source_target_pairs={{0,12},{1,13},{2,14},{3,15},{4,8},{5,9},{6,10},{7,11},{8,4},{9,5},... | collective-permute-start | bytes 344072 | tf_op jit(solution)/shard_map/ppermute | solution.py:42
  165.2 3.5 %collective-permute-start.27 = (f32[256,512]{1,0:T(8,128)S(1)}, f32[256,512]{1,0:T(8,128)S(1)}, u32[]{:S(2)}, u32[]{:S(2)}) collective-permute-start(f32[256,512]{1,0:T(8,128)S(1)} %get-tuple-element.79), channel_id=1, source_target_pairs={{0,16},{1,17},{2,18},{3,19},{4,20},{5,21},{6,22},{7,23},{8,24},{9,... | collective-permute-start | bytes 1572872 | tf_op jit(solution)/shard_map/ppermute | solution.py:42
  194.5 7.8 %collective-permute-start.28 = (f32[48,512]{1,0:T(8,128)S(1)}, f32[48,512]{1,0:T(8,128)S(1)}, u32[]{:S(2)}, u32[]{:S(2)}) collective-permute-start(f32[48,512]{1,0:T(8,128)S(1)} %reduce_sum.9), channel_id=1, source_target_pairs={{0,32},{1,33},{2,34},{3,35},{4,36},{5,37},{6,38},{7,39},{8,40},{9,... | collective-permute-start | bytes 294920 | tf_op jit(solution)/shard_map/ppermute | solution.py:42
  202.3 5.0 %collective-permute-start.29 = (f32[48,512]{1,0:T(8,128)S(1)}, f32[48,512]{1,0:T(8,128)S(1)}, u32[]{:S(2)}, u32[]{:S(2)}) collective-permute-start(f32[48,512]{1,0:T(8,128)S(1)} %add.51), channel_id=1, source_target_pairs={{0,4},{1,5},{2,6},{3,7},{4,0},{5,1},{6,2},{7,3},{8,12},{9,13},{10,... | collective-permute-start | bytes 294920 | tf_op jit(solution)/shard_map/ppermute | solution.py:42
  207.3 4.8 %collective-permute-start.30 = (f32[48,512]{1,0:T(8,128)S(1)}, f32[48,512]{1,0:T(8,128)S(1)}, u32[]{:S(2)}, u32[]{:S(2)}) collective-permute-start(f32[48,512]{1,0:T(8,128)S(1)} %add.52), channel_id=1, source_target_pairs={{0,8},{1,9},{2,10},{3,11},{4,12},{5,13},{6,14},{7,15},{8,0},{9,1},... | collective-permute-start | bytes 294920 | tf_op jit(solution)/shard_map/ppermute | solution.py:42
  235.1 7.7 %collective-permute-start.31 = (f32[768,512]{1,0:T(8,128)S(1)}, f32[768,512]{1,0:T(8,128)S(1)}, u32[]{:S(2)}, u32[]{:S(2)}) collective-permute-start(f32[768,512]{1,0:T(8,128)S(1)} %bitcast.35), channel_id=1, source_target_pairs={{0,16},{1,17},{2,18},{3,19},{4,20},{5,21},{6,22},{7,23},{8,24},{9,... | collective-permute-start | bytes 4718600 | tf_op jit(solution)/shard_map/ppermute | solution.py:42
where the time goes:
time: 247 us
  waiting for transfers between devices  89.7 us (36%)
  starting transfers between devices  73.9 us (30%)
  blocking collectives  48.3 us (20%)
  Pallas kernels  28.8 us (12%)
  other arithmetic  3.66 us (1%)
    ppermute x32, waiting for transfers between devices, send(): return lax.ppermute(value, AXES, pairs)  89.7 us
    ppermute x32, starting transfers between devices, send(): return lax.ppermute(value, AXES, pairs)  73.9 us
    all_to_all x1, blocking collectives, body(): total = jnp.sum(lax.all_to_all(pieces, ('x', 'y'), 0, 0), axis=0)  25.6 us
    all_to_all x1, blocking collectives, body(): mine = lax.all_to_all(pieces, ('x', 'y'), 0, 0).reshape(halves.shape)  22.7 us
    pallas_call x3, Pallas kernels, product(): pl.pallas_call(product_kernel, grid_spec=pltpu.PrefetchScalarGridSpec(num...  18.6 us
  transfers between devices with their start and end apart: 32, of which 21 were waited for; matrix products, arithmetic and copies ran while one was open for 1% of the time, Pallas kernels for 9%

commit v1 on v0

v1 whole, which is shorter than its diff:
```python
import functools

import jax
import jax.numpy as jnp
from jax import lax
from jax.experimental import pallas as pl
from jax.experimental.pallas import tpu as pltpu
from jax.sharding import Mesh
from jax.sharding import PartitionSpec as P

TILE = 128
AXES = ("x", "h", "core", "l", "y")
SIZES = (4, 2, 2, 4, 4)
ROW = ("x", "h", "core")
COL = ("l", "y")
EXTRA = 16
STEPS = 64.0
TOP = 32766.0
LN2 = 0.6931471805599453
VMEM = pl.BlockSpec(memory_space=pltpu.VMEM)
SMEM = pl.BlockSpec(memory_space=pltpu.SMEM)
F32, BF16, I16, I32 = jnp.float32, jnp.bfloat16, jnp.int16, jnp.int32


def coords(device):
    out = []
    for size in SIZES[::-1]:
        out.append(device % size)
        device //= size
    return tuple(out[::-1])


def number(place):
    value = 0
    for size, at in zip(SIZES, place):
        value = value * size + at
    return value


def send(value, move):
    pairs = [(d, number(move(*coords(d)))) for d in range(256)]
    return lax.ppermute(value, AXES, pairs)


def over_x(k):
    return lambda x, h, c, l, y: (x ^ k, h, c, l, y)


def over_y(k):
    return lambda x, h, c, l, y: (x, h, c, l, y ^ k)


def over_l(k):
    return lambda x, h, c, l, y: (x, h, c, l ^ k, y)


def over_h(x, h, c, l, y):
    return (x, 1 - h, c, l, y)


def over_core(x, h, c, l, y):
    return (x, h, 1 - c, l, y)


def spread(x, h, c, l, y):
    return (x ^ l, h, c, l, y)


def turn(i):
    return lambda x, h, c, l, y: (x, (y & 1) ^ i, y >> 1, x ^ l, 2 * h + c)


def params(limit=20):
    return pltpu.CompilerParams(vmem_limit_bytes=limit * 1024 * 1024)


def cost(flops, moved):
    return pl.CostEstimate(flops=flops // 1000, bytes_accessed=moved // 1000, transcendentals=0)


def diagonal_mask(rows, width):
    row = lax.broadcasted_iota(I32, (rows, width), 0)
    lane = lax.broadcasted_iota(I32, (rows, width), 1)
    return row == lane


def encode(value, out_ref, start=0):
    rows, width = value.shape
    largest = jnp.maximum(jnp.max(jnp.abs(value), axis=1, keepdims=True), 1e-30)
    level = jnp.ceil(jnp.log(largest * (1.0 / TOP)) * (STEPS / LN2))
    coded = jnp.round(value * jnp.exp2(level * (-1.0 / STEPS)))
    out_ref[start : start + rows, :] = coded.astype(I32).astype(I16)
    line = jnp.sum(jnp.where(diagonal_mask(rows, width), level, 0.0), axis=0, keepdims=True)
    lines = jnp.broadcast_to(line, (EXTRA, width))
    out_ref[start + rows : start + rows + EXTRA, :] = lines.astype(I32).astype(I16)


def decode(in_ref, start=0, rows=None):
    rows, width = rows or in_ref.shape[0] - EXTRA, in_ref.shape[1]
    coded = in_ref[start : start + rows, :].astype(I32).astype(F32)
    line = in_ref[start + rows : start + rows + EXTRA, :].astype(I32).astype(F32)[:1]
    level = jnp.sum(
        jnp.where(diagonal_mask(rows, width), jnp.broadcast_to(line, (rows, width)), 0.0),
        axis=1,
        keepdims=True,
    )
    return coded * jnp.exp2(level * (1.0 / STEPS))


def product_kernel(panels, at_ref, a_ref, own_ref, other_ref, *refs):
    outs, m_ref = refs[: 4 * panels], refs[4 * panels]
    step = pl.program_id(0)
    shard = own_ref.shape[3]

    @pl.when(step == 0)
    def _():
        core, h, t = at_ref[1], at_ref[2], at_ref[3]
        for p in range(panels):
            for k in range(4):
                for i in range(2):
                    base = (k ^ t) * (4 * shard) + (i ^ h) * shard
                    first = pl.multiple_of(base + core * (2 * shard), 32)
                    second = pl.multiple_of(base + (1 - core) * (2 * shard), 32)
                    m_ref[p, pl.ds(first, shard), :] = own_ref[k, i, p]
                    m_ref[p, pl.ds(second, shard), :] = other_ref[k, i, p]

    block = a_ref[...]
    lines = block.reshape(4 * block.shape[2], block.shape[3])
    for p in range(panels):
        value = jnp.dot(lines, m_ref[p], preferred_element_type=F32)
        for at in range(3):

            @pl.when(step == at)
            def _(ref=outs[4 * p + 1 + at], value=value):
                encode(value, ref)

        @pl.when(step == 3)
        def _(ref=outs[4 * p], value=value):
            ref[...] = value


def product(at, a4, own, other, first, panels):
    shard, order = a4.shape[2], a4.shape[3]
    width = own.shape[4]
    rows = 4 * shard
    whole = pl.BlockSpec((4, 2, panels, shard, width), lambda g, s: (0, 0, first // panels, 0, 0))
    kept = pl.BlockSpec((rows, width), lambda g, s: (0, 0))
    coded = pl.BlockSpec((rows + EXTRA, width), lambda g, s: (0, 0))
    one = [jax.ShapeDtypeStruct((rows, width), F32)]
    one += [jax.ShapeDtypeStruct((rows + EXTRA, width), I16)] * 3
    outs = pl.pallas_call(
        functools.partial(product_kernel, panels),
        grid_spec=pltpu.PrefetchScalarGridSpec(
            num_scalar_prefetch=1,
            grid=(4,),
            in_specs=[
                pl.BlockSpec(
                    (4, 1, shard, order), lambda g, s: (0, s[0] ^ ((g + 1) & 3), 0, 0)
                ),
                whole,
                whole,
            ],
            out_specs=([kept] + [coded] * 3) * panels,
            scratch_shapes=[pltpu.VMEM((panels, order, width), BF16)],
        ),
        out_shape=one * panels,
        compiler_params=params(),
        cost_estimate=cost(8 * panels * rows * order * width, 2 * order * order),
        name="product",
    )(at, a4, own, other)
    return [outs[4 * p : 4 * p + 4] for p in range(panels)]


def middle_kernel(panels, base, *refs):
    at_ref, refs = refs[0], refs[1:]
    keeps, refs = refs[:panels], refs[panels:]
    parts, refs = refs[: 3 * panels], refs[3 * panels :]
    masked, refs = refs[:4], refs[4:]
    own_ref, *coded = refs[:4]
    mine_ref, theirs_ref, sum_ref, m_ref = refs[4:]
    shard = own_ref.shape[0] // panels
    half = mine_ref.shape[0] // panels
    core, l = at_ref[1], at_ref[4]

    def place(k):
        return pl.ds(pl.multiple_of((l ^ k) * shard, 32), shard)

    for p in range(panels):
        value = keeps[p][...]
        for ref in parts[3 * p : 3 * p + 3]:
            value = value + decode(ref)
        sum_ref[...] = value
        own_ref[p * shard : (p + 1) * shard, :] = sum_ref[place(0), :]
        for k in (1, 2, 3):
            encode(sum_ref[place(k), :], coded[k - 1], p * (shard + EXTRA))
        for k, ref in enumerate(masked):
            m_ref[place(k), :] = ref[base + p]
        high = value.astype(BF16)
        rest = value - high.astype(F32)
        mid = rest.astype(BF16)
        low = (rest - mid.astype(F32)).astype(BF16)
        for which, out in ((core, mine_ref), (1 - core, theirs_ref)):
            left = m_ref[:, pl.ds(pl.multiple_of(which * half, 128), half)]
            dims = (((0,), (0,)), ((), ()))
            terms = [
                lax.dot_general(left, r, dims, preferred_element_type=F32) for r in (low, mid, high)
            ]
            out[p * half : (p + 1) * half, :] = (terms[0] + terms[1]) + terms[2]


def middle(at, keeps, parts, masked, base):
    rows, width = keeps[0].shape
    panels, shard = len(keeps), rows // 4
    return pl.pallas_call(
        functools.partial(middle_kernel, panels, base),
        in_specs=[SMEM] + [VMEM] * (4 * panels + 4),
        out_specs=[VMEM] * 6,
        out_shape=[jax.ShapeDtypeStruct((panels * shard, width), F32)]
        + [jax.ShapeDtypeStruct((panels * (shard + EXTRA), width), I16)] * 3
        + [jax.ShapeDtypeStruct((panels * (width // 2), width), F32)] * 2,
        scratch_shapes=[pltpu.VMEM((rows, width), F32), pltpu.VMEM((rows, width), BF16)],
        compiler_params=params(),
        cost_estimate=cost(6 * rows * width * width, 16 * rows * width),
        name="middle",
    )(at, *keeps, *sum(parts, []), *masked)


def last_kernel(panels, own_ref, r1_ref, r2_ref, r3_ref, out_ref):
    shard = out_ref.shape[1]
    for p in range(panels):
        total = own_ref[p * shard : (p + 1) * shard, :]
        for ref in (r1_ref, r2_ref, r3_ref):
            total = total + decode(ref, p * (shard + EXTRA), shard)
        out_ref[p] = -total


def last(panels, own, parts):
    rows, width = own.shape
    return pl.pallas_call(
        functools.partial(last_kernel, panels),
        in_specs=[VMEM] * 4,
        out_specs=VMEM,
        out_shape=jax.ShapeDtypeStruct((panels, rows // panels, width), F32),
        compiler_params=params(),
        cost_estimate=cost(8 * rows * width, 16 * rows * width),
        name="last",
    )(own, *parts)


def fold_kernel(*refs):
    out, count = refs[-1], len(refs) // 2
    start = 0
    for p in range(count):
        rows = refs[p].shape[0]
        out[start : start + rows, :] = refs[p][...] + refs[count + p][...]
        start += rows


def fold(mines, theirs):
    width = mines[0].shape[1]
    total = sum(mine.shape[0] for mine in mines)
    return pl.pallas_call(
        fold_kernel,
        in_specs=[VMEM] * (2 * len(mines)),
        out_specs=VMEM,
        out_shape=jax.ShapeDtypeStruct((total, width), F32),
        compiler_params=params(),
        cost_estimate=cost(total * width, 12 * total * width),
        name="fold",
    )(*mines, *theirs)


def finish_kernel(at_ref, mine_ref, theirs_ref, diag_ref, out_ref):
    half = diag_ref.shape[1] // 2
    core = at_ref[1]
    for p in range(diag_ref.shape[0]):
        for which, ref in ((core, mine_ref), (1 - core, theirs_ref)):
            place = pl.ds(pl.multiple_of(which * half, 8), half)
            out_ref[p, place, :] = diag_ref[p, place, :] + ref[p * half : (p + 1) * half, :]


def finish(at, mine, theirs, diag):
    return pl.pallas_call(
        finish_kernel,
        in_specs=[SMEM] + [VMEM] * 3,
        out_specs=VMEM,
        out_shape=jax.ShapeDtypeStruct(diag.shape, F32),
        compiler_params=params(),
        cost_estimate=cost(diag.size, 12 * diag.size),
        name="finish",
    )(at, mine, theirs, diag)


def after(values, *earlier):
    return lax.optimization_barrier((values, earlier))[0]


def body(ancestor_inverse, panels, diag_inverse, tile_mask):
    x, h, core, l, y = (lax.axis_index(axis) for axis in AXES)
    at = jnp.stack([y, core, h, x ^ l, l, x]).astype(I32)
    kept, count, width = panels.shape
    order = ancestor_inverse.shape[1]
    tiles = tile_mask.shape[1]
    start = (((x * 2 + h) * 2 + core) * 16 + l * 4 + y) * kept
    tile = start // TILE
    first = lax.dynamic_slice_in_dim(tile_mask, tile, 1, 1)
    second = lax.dynamic_slice_in_dim(tile_mask, jnp.minimum(tile + 1, tiles - 1), 1, 1)
    in_first = start + jnp.arange(kept) < (tile + 1) * TILE
    own_mask = jnp.where(in_first[None, :], first, second).astype(BF16)
    masked = jnp.swapaxes(panels, 0, 1) * own_mask[:, :, None]

    moved = send(masked, spread)
    turned = [send(moved, turn(i)) for i in range(2)]
    late = after(masked, turned)
    beside = [masked] + [send(late, over_l(k)) for k in (1, 2, 3)]
    a4 = ancestor_inverse.reshape(4, 4, kept, order)
    message = jnp.stack(turned)
    found = [send(message, over_x(k)) for k in (1, 2, 3)]
    own = after(jnp.stack([message] + found), beside)
    other = send(own, over_core)
    keeps, parts = [], []
    for group in ((2,), (0, 1)):
        for keep, *coded in product(at, a4, own, other, group[0], len(group)):
            keeps.append(keep)
            parts.append(coded)
        if len(group) == 1:
            parts[0] = [send(parts[0][k - 1], over_y(k)) for k in (1, 2, 3)]
    pairs = [jnp.stack([parts[1][k], parts[2][k]]) for k in range(3)]
    pairs = after(pairs, parts[0])
    pairs = [send(pairs[k - 1], over_y(k)) for k in (1, 2, 3)]
    own_2, *coded = middle(at, keeps[:1], parts[:1], beside, 2)
    coded_2, (mine_2, their_2) = coded[:3], coded[3:]
    swapped_2 = send(their_2, over_core)
    pairs = after(pairs, mine_2)
    parts = [[pair[p] for pair in pairs] for p in (0, 1)]
    own_01, *coded = middle(at, keeps[1:], parts, beside, 0)
    coded_01, (mine_01, their_01) = coded[:3], coded[3:]
    swapped_01 = send(their_01, over_core)
    halves = fold([mine_01, mine_2], [swapped_01, swapped_2])
    coded = [jnp.concatenate([a, b]) for a, b in zip(coded_01, coded_2)]
    found = [send(coded[k - 1], over_l(k)) for k in (1, 2, 3)]
    pieces = halves.reshape(16, -1, width)
    total = jnp.sum(lax.all_to_all(pieces, ("x", "y"), 0, 0), axis=0)
    found = after(found, total)
    total = total + send(total, over_h)
    total = total + send(total, over_l(1))
    total = total + send(total, over_l(2))
    blocks = last(3, jnp.concatenate([own_01, own_2]), found)
    pieces = jnp.broadcast_to(after(total, blocks)[None], (16, *total.shape))
    mine = lax.all_to_all(pieces, ("x", "y"), 0, 0).reshape(halves.shape)
    diagonal = finish(at, mine, send(mine, over_core), diag_inverse)
    return jnp.swapaxes(blocks, 0, 1), diagonal


def solution(mesh):
    finer = Mesh(mesh.devices.reshape(SIZES), AXES)
    placed = (P(ROW, COL), P(AXES, None, None), P(), P())
    return jax.shard_map(
        body, mesh=finer, in_specs=placed, out_specs=(P(AXES, None, None), P()), check_vma=False
    )
```

time: 247 us -> 242 us (0.980)
  blocking collectives: 48.3 us -> 25.2 us
  waiting for transfers between devices: 89.7 us -> 112 us
  starting transfers between devices: 73.9 us -> 68.3 us
    all_to_all x1 -> x0, blocking collectives: 25.6 us -> none  [body(): total = jnp.sum(lax.all_to_all(pieces, ('x', 'y'), 0, 0), axis=0)]
    all_to_all x0 -> x1, waiting for transfers between devices: none -> 16.4 us  [body(): total = jnp.sum(lax.all_to_all(pieces, ('x', 'y'), 0, 0), axis=0)]
    ppermute x32 -> x25, starting transfers between devices: 73.9 us -> 62.4 us  [send(): return lax.ppermute(value, AXES, pairs)]
    ppermute x32 -> x25, waiting for transfers between devices: 89.7 us -> 95.9 us  [send(): return lax.ppermute(value, AXES, pairs)]
    all_to_all x0 -> x1, starting transfers between devices: none -> 5.93 us  [body(): total = jnp.sum(lax.all_to_all(pieces, ('x', 'y'), 0, 0), axis=0)]
    all_to_all x1, blocking collectives: 22.7 us -> 25.2 us  [body(): mine = lax.all_to_all(pieces, ('x', 'y'), 0, 0).reshape(halves.shape)]
    pallas_call x7 -> x5, Pallas kernels: 24.7 us -> 22.7 us  [the longest x2 16.5 us: product(): pl.pallas_call(functools.partial(product_kernel, panels), grid_spec=pltpu...]
  transfers between devices with their start and end apart: 32 -> 26, of which waited for: 21 -> 15; matrix products, arithmetic and copies ran while one was open for 1% -> 1% of each run, Pallas kernels for 9% -> 6%
where the time goes in v1:
time: 242 us; the launch traced here: 241 us
  waiting for transfers between devices  112 us (46%)
  starting transfers between devices  68.3 us (28%)
  Pallas kernels  26.5 us (11%)
  blocking collectives  25.2 us (10%)
  other arithmetic  4.13 us (2%)
  local copies, waits for them, and re-layouts  3.75 us (2%)
    ppermute x25, waiting for transfers between devices, send(): return lax.ppermute(value, AXES, pairs)  95.9 us
    ppermute x25, starting transfers between devices, send(): return lax.ppermute(value, AXES, pairs)  62.4 us
    all_to_all x1, blocking collectives, body(): mine = lax.all_to_all(pieces, ('x', 'y'), 0, 0).reshape(halves.shape)  25.2 us
    pallas_call x2, Pallas kernels, product(): pl.pallas_call(functools.partial(product_kernel, panels), grid_spec=pltpu...  16.5 us
    all_to_all x1, waiting for transfers between devices, body(): total = jnp.sum(lax.all_to_all(pieces, ('x', 'y'), 0, 0), axis=0)  16.4 us
    all_to_all x1, starting transfers between devices, body(): total = jnp.sum(lax.all_to_all(pieces, ('x', 'y'), 0, 0), axis=0)  5.93 us
    pallas_call x2, Pallas kernels, middle(): pl.pallas_call(functools.partial(middle_kernel, panels, base), in_specs=[...  5.06 us
  transfers between devices with their start and end apart: 26, of which 15 were waited for; matrix products, arithmetic and copies ran while one was open for 1% of the time, Pallas kernels for 6%

profile of v1, /device:TPU:1, one launch (start us, length us, event | category | flops | bytes accessed | tf_op | source)
XLA Modules:
  0.0 241.2 jit_solution(13587597326512079195)
XLA Ops:
  3.5 9.4 %collective-permute-start.2 = (bf16[3,96,512]{2,1,0:T(8,128)(2,1)S(1)}, bf16[3,96,512]{2,1,0:T(8,128)(2,1)S(1)}, u32[]{:S(2)}, u32[]{:S(2)}) collective-permute-start(bf16[3,96,512]{2,1,0:T(8,128)(2,1)S(1)} %collective-permute-done), channel_id=1, source_target_pairs={{0,32},{1,0},{2,48},{3,16},{4,36},{5,4},{6,52},{7,20},{8,40},{9,8}... | collective-permute-start | bytes 884744 | tf_op jit(solution)/shard_map/ppermute | solution.py:42
  14.8 4.5 %collective-permute-done.2 = bf16[3,96,512]{2,1,0:T(8,128)(2,1)S(1)} collective-permute-done((bf16[3,96,512]{2,1,0:T(8,128)(2,1)S(1)}, bf16[3,96,512]{2,1,0:T(8,128)(2,1)S(1)}, u32[]{:S(2)}, u32[]{:S(2)}) %collective-permute-start.2) | collective-permute-done | bytes 294944 | tf_op jit(solution)/shard_map/ppermute | solution.py:42
  19.3 4.8 %collective-permute-done.1 = bf16[3,96,512]{2,1,0:T(8,128)(2,1)S(1)} collective-permute-done((bf16[3,96,512]{2,1,0:T(8,128)(2,1)S(1)}, bf16[3,96,512]{2,1,0:T(8,128)(2,1)S(1)}, u32[]{:S(2)}, u32[]{:S(2)}) %collective-permute-start.1) | collective-permute-done | bytes 294944 | tf_op jit(solution)/shard_map/ppermute | solution.py:42
  24.2 18.2 %collective-permute-start.4 = (bf16[2,3,96,512]{3,2,1,0:T(8,128)(2,1)S(1)}, bf16[2,3,96,512]{3,2,1,0:T(8,128)(2,1)S(1)}, u32[]{:S(2)}, u32[]{:S(2)}) collective-permute-start(bf16[2,3,96,512]{3,2,1,0:T(8,128)(2,1)S(1)} %get-tuple-element.83), channel_id=1, source_target_pairs={{0,128},{1,129},{2,130},{3,131},{4,132},{5,133},{6,134},{7,135},{8... | collective-permute-start | bytes 1769480 | tf_op jit(solution)/shard_map/ppermute | solution.py:42
  42.5 2.7 %collective-permute-start.3 = (bf16[2,3,96,512]{3,2,1,0:T(8,128)(2,1)S(1)}, bf16[2,3,96,512]{3,2,1,0:T(8,128)(2,1)S(1)}, u32[]{:S(2)}, u32[]{:S(2)}) collective-permute-start(bf16[2,3,96,512]{3,2,1,0:T(8,128)(2,1)S(1)} %get-tuple-element.83), channel_id=1, source_target_pairs={{0,64},{1,65},{2,66},{3,67},{4,68},{5,69},{6,70},{7,71},{8,72},{9,... | collective-permute-start | bytes 1769480 | tf_op jit(solution)/shard_map/ppermute | solution.py:42
  45.1 11.0 %collective-permute-done.4 = bf16[2,3,96,512]{3,2,1,0:T(8,128)(2,1)S(1)} collective-permute-done((bf16[2,3,96,512]{3,2,1,0:T(8,128)(2,1)S(1)}, bf16[2,3,96,512]{3,2,1,0:T(8,128)(2,1)S(1)}, u32[]{:S(2)}, u32[]{:S(2)}) %collective-permute-start.4) | collective-permute-done | bytes 589856 | tf_op jit(solution)/shard_map/ppermute | solution.py:42
  56.4 14.9 %collective-permute-done.3 = bf16[2,3,96,512]{3,2,1,0:T(8,128)(2,1)S(1)} collective-permute-done((bf16[2,3,96,512]{3,2,1,0:T(8,128)(2,1)S(1)}, bf16[2,3,96,512]{3,2,1,0:T(8,128)(2,1)S(1)}, u32[]{:S(2)}, u32[]{:S(2)}) %collective-permute-start.3) | collective-permute-done | bytes 589856 | tf_op jit(solution)/shard_map/ppermute | solution.py:42
  72.0 4.4 %collective-permute-done.9.other_ref = bf16[4,2,3,96,512]{4,3,2,1,0:T(8,128)(2,1)} collective-permute-done((bf16[4,2,3,96,512]{4,3,2,1,0:T(8,128)(2,1)S(1)}, bf16[4,2,3,96,512]{4,3,2,1,0:T(8,128)(2,1)}, u32[]{:S(2)}, u32[]{:S(2)}) %collective-permute-start.9) | collective-permute-done | bytes 2359328 | tf_op jit(solution)/shard_map/ppermute | solution.py:42
  76.4 2.3 copy-done
  78.7 6.1 %product.3 = (f32[384,512]{1,0:T(8,128)S(1)}, s16[400,512]{1,0:T(8,128)(2,1)S(1)}, s16[400,512]{1,0:T(8,128)(2,1)S(1)}, s16[400,512]{1,0:T(8,128)(2,1)S(1)}) custom-call(s32[6]{0:T(128)S(1)} %stack.78.at_ref.refs_0_, bf16[4,4,96,1536]{3,2,1,0:T(8,128)(2,1)S(1)} %bitcast.37, bf16[4,2,3,96,512]{4,3,2,1,0:T(8,128)(2,1)S(1)} %pad_maximum_fusion.own_ref, ...), custom_call_target="tpu_custom_call" | custom-call | flops 2415919 | bytes 4718 | tf_op jit(solution)/shard_map/product/pallas_call | solution.py:151
  86.8 2.0 collective-permute-start.12
  88.8 10.4 %product.2 = (f32[384,512]{1,0:T(8,128)S(1)}, s16[400,512]{1,0:T(8,128)(2,1)S(1)}, s16[400,512]{1,0:T(8,128)(2,1)S(1)}, s16[400,512]{1,0:T(8,128)(2,1)S(1)}, f32...) custom-call(s32[6]{0:T(128)S(1)} %stack.78.at_ref.refs_0_, ...), custom_call_target="tpu_custom_call" | custom-call | flops 4831838 | bytes 4718 | tf_op jit(solution)/shard_map/product/pallas_call | solution.py:151
  99.4 5.6 %collective-permute-done.11.refs_3_ = s16[400,512]{1,0:T(8,128)(2,1)S(1)} collective-permute-done((s16[400,512]{1,0:T(8,128)(2,1)S(1)}, s16[400,512]{1,0:T(8,128)(2,1)S(1)}, u32[]{:S(2)}, u32[]{:S(2)}) %collective-permute-start.11) | collective-permute-done | bytes 409632 | tf_op jit(solution)/shard_map/ppermute | solution.py:42
  105.0 2.1 collective-permute-done.12.refs_4_
  107.1 3.1 %collective-permute-start.14 = (s16[2,400,512]{2,1,0:T(8,128)(2,1)S(1)}, s16[2,400,512]{2,1,0:T(8,128)(2,1)S(1)}, u32[]{:S(2)}, u32[]{:S(2)}) collective-permute-start(s16[2,400,512]{2,1,0:T(8,128)(2,1)S(1)} %get-tuple-element.52), channel_id=1, source_target_pairs={{0,2},{1,3},{2,0},{3,1},{4,6},{5,7},{6,4},{7,5},{8,10},{9,11},{10,... | collective-permute-start | bytes 2457608 | tf_op jit(solution)/shard_map/ppermute | solution.py:42
  113.0 12.4 %collective-permute-done.13 = s16[2,400,512]{2,1,0:T(8,128)(2,1)S(1)} collective-permute-done((s16[2,400,512]{2,1,0:T(8,128)(2,1)S(1)}, s16[2,400,512]{2,1,0:T(8,128)(2,1)S(1)}, u32[]{:S(2)}, u32[]{:S(2)}) %collective-permute-start.13) | collective-permute-done | bytes 819232 | tf_op jit(solution)/shard_map/ppermute | solution.py:42
  125.4 19.1 %collective-permute-done.14 = s16[2,400,512]{2,1,0:T(8,128)(2,1)S(1)} collective-permute-done((s16[2,400,512]{2,1,0:T(8,128)(2,1)S(1)}, s16[2,400,512]{2,1,0:T(8,128)(2,1)S(1)}, u32[]{:S(2)}, u32[]{:S(2)}) %collective-permute-start.14) | collective-permute-done | bytes 819232 | tf_op jit(solution)/shard_map/ppermute | solution.py:42
  144.6 3.1 %middle.3 = (f32[192,512]{1,0:T(8,128)S(1)}, s16[224,512]{1,0:T(8,128)(2,1)S(1)}, s16[224,512]{1,0:T(8,128)(2,1)S(1)}, s16[224,512]{1,0:T(8,128)(2,1)S(1)}, f32[...) custom-call(s32[6]{0:T(128)S(1)} %stack.78.at_ref.refs_0_, f32[384,512]{1,0:T(8,128)S(1)} %get-tuple-element.40.refs_1_, ...), custom_call_target="tpu_custom_call" | custom-call | flops 603979 | bytes 3145 | tf_op jit(solution)/shard_map/middle/pallas_call | solution.py:214
  147.7 5.3 %collective-permute-start.19 = (f32[512,512]{1,0:T(8,128)S(1)}, f32[512,512]{1,0:T(8,128)S(1)}, u32[]{:S(2)}, u32[]{:S(2)}) collective-permute-start(f32[512,512]{1,0:T(8,128)S(1)} %get-tuple-element.68), channel_id=1, source_target_pairs={{0,16},{1,17},{2,18},{3,19},{4,20},{5,21},{6,22},{7,23},{8,24},{9,... | collective-permute-start | bytes 3145736 | tf_op jit(solution)/shard_map/ppermute | solution.py:42
  153.1 2.9 %collective-permute-done.20.refs_3_ = f32[256,512]{1,0:T(8,128)S(1)} collective-permute-done((f32[256,512]{1,0:T(8,128)S(1)}, f32[256,512]{1,0:T(8,128)S(1)}, u32[]{:S(2)}, u32[]{:S(2)}) %collective-permute-start.20) | collective-permute-done | bytes 524320 | tf_op jit(solution)/shard_map/ppermute | solution.py:42
  157.3 5.9 %all-to-all-start = ((f32[16,48,512]{2,1,0:T(8,128)}), f32[16,48,512]{2,1,0:T(8,128)S(1)}, u32[]{:S(2)}, u32[]{:S(2)}) async-start(f32[16,48,512]{2,1,0:T(8,128)} %bitcast.26), calls=%async_computation | async-start | bytes 3145728 | tf_op jit(solution)/shard_map/all_to_all | solution.py:343
  166.8 2.3 collective-permute-start.16
  169.1 16.4 %all-to-all-done = f32[16,48,512]{2,1,0:T(8,128)S(1)} async-done(((f32[16,48,512]{2,1,0:T(8,128)}), f32[16,48,512]{2,1,0:T(8,128)S(1)}, u32[]{:S(2)}, u32[]{:S(2)}) %all-to-all-start) | async-done | bytes 1572896 | tf_op jit(solution)/shard_map/all_to_all | solution.py:343
  185.6 3.9 %collective-permute-start.21 = (f32[48,512]{1,0:T(8,128)S(1)}, f32[48,512]{1,0:T(8,128)S(1)}, u32[]{:S(2)}, u32[]{:S(2)}) collective-permute-start(f32[48,512]{1,0:T(8,128)S(1)} %reduce_sum.9), channel_id=1, source_target_pairs={{0,32},{1,33},{2,34},{3,35},{4,36},{5,37},{6,38},{7,39},{8,40},{9,... | collective-permute-start | bytes 294920 | tf_op jit(solution)/shard_map/ppermute | solution.py:42
  189.5 4.4 %collective-permute-done.21 = f32[48,512]{1,0:T(8,128)S(1)} collective-permute-done((f32[48,512]{1,0:T(8,128)S(1)}, f32[48,512]{1,0:T(8,128)S(1)}, u32[]{:S(2)}, u32[]{:S(2)}) %collective-permute-start.21) | collective-permute-done | bytes 98336 | tf_op jit(solution)/shard_map/ppermute | solution.py:42
  193.9 2.4 %collective-permute-start.22 = (f32[48,512]{1,0:T(8,128)S(1)}, f32[48,512]{1,0:T(8,128)S(1)}, u32[]{:S(2)}, u32[]{:S(2)}) collective-permute-start(f32[48,512]{1,0:T(8,128)S(1)} %add.51), channel_id=1, source_target_pairs={{0,4},{1,5},{2,6},{3,7},{4,0},{5,1},{6,2},{7,3},{8,12},{9,13},{10,... | collective-permute-start | bytes 294920 | tf_op jit(solution)/shard_map/ppermute | solution.py:42
  196.3 4.1 %collective-permute-done.22 = f32[48,512]{1,0:T(8,128)S(1)} collective-permute-done((f32[48,512]{1,0:T(8,128)S(1)}, f32[48,512]{1,0:T(8,128)S(1)}, u32[]{:S(2)}, u32[]{:S(2)}) %collective-permute-start.22) | collective-permute-done | bytes 98336 | tf_op jit(solution)/shard_map/ppermute | solution.py:42
  202.8 2.6 %collective-permute-done.23 = f32[48,512]{1,0:T(8,128)S(1)} collective-permute-done((f32[48,512]{1,0:T(8,128)S(1)}, f32[48,512]{1,0:T(8,128)S(1)}, u32[]{:S(2)}, u32[]{:S(2)}) %collective-permute-start.23) | collective-permute-done | bytes 98336 | tf_op jit(solution)/shard_map/ppermute | solution.py:42
  205.6 25.2 %all_to_all.10 = f32[16,48,512]{2,1,0:T(8,128)S(1)} all-to-all(f32[16,48,512]{2,1,0:T(8,128)S(1)} %broadcast_in_dim.35), channel_id=1, replica_groups=mesh['x'=4,'h'=2,'core'=2,'l'=4,'y'=4] {'x','y'}, dimensions={0} | all-to-all | bytes 3145728 | tf_op jit(solution)/shard_map/all_to_all | solution.py:350
  230.8 4.8 %collective-permute-start.24 = (f32[768,512]{1,0:T(8,128)S(1)}, f32[768,512]{1,0:T(8,128)S(1)}, u32[]{:S(2)}, u32[]{:S(2)}) collective-permute-start(f32[768,512]{1,0:T(8,128)S(1)} %bitcast.39), channel_id=1, source_target_pairs={{0,16},{1,17},{2,18},{3,19},{4,20},{5,21},{6,22},{7,23},{8,24},{9,... | collective-permute-start | bytes 4718600 | tf_op jit(solution)/shard_map/ppermute | solution.py:42
  235.7 3.0 %collective-permute-done.24.theirs_ref = f32[768,512]{1,0:T(8,128)S(1)} collective-permute-done((f32[768,512]{1,0:T(8,128)S(1)}, f32[768,512]{1,0:T(8,128)S(1)}, u32[]{:S(2)}, u32[]{:S(2)}) %collective-permute-start.24) | collective-permute-done | bytes 1572896 | tf_op jit(solution)/shard_map/ppermute | solution.py:42
  238.7 2.5 %finish.1 = f32[3,512,512]{2,1,0:T(8,128)} custom-call(s32[6]{0:T(128)S(1)} %stack.78.at_ref.refs_0_, f32[768,512]{1,0:T(8,128)S(1)} %bitcast.40, f32[768,512]{1,0:T(8,128)S(1)} %collective-permute-done.24.theirs_ref, f32[3,512,512]{2,1,0:T(8,128)S(1)} %copy-done.1), custom_call_target="tpu_custom_call" | custom-call | flops 786 | bytes 9437 | tf_op jit(solution)/shard_map/finish/pallas_call | solution.py:283
  (53 shorter events, 18.3 us)
Async XLA Ops:
  2.8 0.7 collective-permute-start
  3.5 15.8 %collective-permute-start.2 = (bf16[3,96,512]{2,1,0:T(8,128)(2,1)S(1)}, bf16[3,96,512]{2,1,0:T(8,128)(2,1)S(1)}, u32[]{:S(2)}, u32[]{:S(2)}) collective-permute-start(bf16[3,96,512]{2,1,0:T(8,128)(2,1)S(1)} %collective-permute-done), channel_id=1, source_target_pairs={{0,32},{1,0},{2,48},{3,16},{4,36},{5,4},{6,52},{7,20},{8,40},{9,8}... | collective-permute-start | bytes 884744 | tf_op jit(solution)/shard_map/ppermute | solution.py:42
  12.9 11.2 %collective-permute-start.1 = (bf16[3,96,512]{2,1,0:T(8,128)(2,1)S(1)}, bf16[3,96,512]{2,1,0:T(8,128)(2,1)S(1)}, u32[]{:S(2)}, u32[]{:S(2)}) collective-permute-start(bf16[3,96,512]{2,1,0:T(8,128)(2,1)S(1)} %collective-permute-done), channel_id=1, source_target_pairs={{0,0},{1,32},{2,16},{3,48},{4,4},{5,36},{6,20},{7,52},{8,8},{9,40}... | collective-permute-start | bytes 884744 | tf_op jit(solution)/shard_map/ppermute | solution.py:42
  24.2 32.0 %collective-permute-start.4 = (bf16[2,3,96,512]{3,2,1,0:T(8,128)(2,1)S(1)}, bf16[2,3,96,512]{3,2,1,0:T(8,128)(2,1)S(1)}, u32[]{:S(2)}, u32[]{:S(2)}) collective-permute-start(bf16[2,3,96,512]{3,2,1,0:T(8,128)(2,1)S(1)} %get-tuple-element.83), channel_id=1, source_target_pairs={{0,128},{1,129},{2,130},{3,131},{4,132},{5,133},{6,134},{7,135},{8... | collective-permute-start | bytes 1769480 | tf_op jit(solution)/shard_map/ppermute | solution.py:42
  42.5 28.8 %collective-permute-start.3 = (bf16[2,3,96,512]{3,2,1,0:T(8,128)(2,1)S(1)}, bf16[2,3,96,512]{3,2,1,0:T(8,128)(2,1)S(1)}, u32[]{:S(2)}, u32[]{:S(2)}) collective-permute-start(bf16[2,3,96,512]{3,2,1,0:T(8,128)(2,1)S(1)} %get-tuple-element.83), channel_id=1, source_target_pairs={{0,64},{1,65},{2,66},{3,67},{4,68},{5,69},{6,70},{7,71},{8,72},{9,... | collective-permute-start | bytes 1769480 | tf_op jit(solution)/shard_map/ppermute | solution.py:42
  45.1 26.2 %collective-permute-start.5 = (bf16[2,3,96,512]{3,2,1,0:T(8,128)(2,1)S(1)}, bf16[2,3,96,512]{3,2,1,0:T(8,128)(2,1)S(1)}, u32[]{:S(2)}, u32[]{:S(2)}) collective-permute-start(bf16[2,3,96,512]{3,2,1,0:T(8,128)(2,1)S(1)} %get-tuple-element.83), channel_id=1, source_target_pairs={{0,192},{1,193},{2,194},{3,195},{4,196},{5,197},{6,198},{7,199},{8... | collective-permute-start | bytes 1769480 | tf_op jit(solution)/shard_map/ppermute | solution.py:42
  45.1 26.5 %collective-permute-start.8 = (bf16[3,96,512]{2,1,0:T(8,128)(2,1)S(1)}, bf16[3,96,512]{2,1,0:T(8,128)(2,1)S(1)}, u32[]{:S(2)}, u32[]{:S(2)}) collective-permute-start(bf16[3,96,512]{2,1,0:T(8,128)(2,1)S(1)} %bitcast_multiply_fusion.refs_5_.refs_9_), channel_id=1, source_target_pairs={{0,12},{1,13},{2,14},{3,15},{4,8},{5,9},{6,10},{7,11},{8,4},{9,5},... | collective-permute-start | bytes 884744 | tf_op jit(solution)/shard_map/ppermute | solution.py:42
  45.1 26.5 %collective-permute-start.7 = (bf16[3,96,512]{2,1,0:T(8,128)(2,1)S(1)}, bf16[3,96,512]{2,1,0:T(8,128)(2,1)S(1)}, u32[]{:S(2)}, u32[]{:S(2)}) collective-permute-start(bf16[3,96,512]{2,1,0:T(8,128)(2,1)S(1)} %bitcast_multiply_fusion.refs_5_.refs_9_), channel_id=1, source_target_pairs={{0,8},{1,9},{2,10},{3,11},{4,12},{5,13},{6,14},{7,15},{8,0},{9,1},... | collective-permute-start | bytes 884744 | tf_op jit(solution)/shard_map/ppermute | solution.py:42
  56.2 15.5 %collective-permute-start.6 = (bf16[3,96,512]{2,1,0:T(8,128)(2,1)S(1)}, bf16[3,96,512]{2,1,0:T(8,128)(2,1)S(1)}, u32[]{:S(2)}, u32[]{:S(2)}) collective-permute-start(bf16[3,96,512]{2,1,0:T(8,128)(2,1)S(1)} %bitcast_multiply_fusion.refs_5_.refs_9_), channel_id=1, source_target_pairs={{0,4},{1,5},{2,6},{3,7},{4,0},{5,1},{6,2},{7,3},{8,12},{9,13},{10,... | collective-permute-start | bytes 884744 | tf_op jit(solution)/shard_map/ppermute | solution.py:42
  71.6 4.8 %collective-permute-start.9 = (bf16[4,2,3,96,512]{4,3,2,1,0:T(8,128)(2,1)S(1)}, bf16[4,2,3,96,512]{4,3,2,1,0:T(8,128)(2,1)}, u32[]{:S(2)}, u32[]{:S(2)}) collective-permute-start(bf16[4,2,3,96,512]{4,3,2,1,0:T(8,128)(2,1)S(1)} %pad_maximum_fusion.own_ref), channel_id=1, source_target_pairs={{0,16},{1,17},{2,18},{3,19},{4,20},{5,21},{6,22},{7,23},{8,24},{9,... | collective-permute-start | bytes 7077896 | tf_op jit(solution)/shard_map/ppermute | solution.py:42
  76.4 2.3 copy-start
  84.8 14.6 %collective-permute-start.10 = (s16[400,512]{1,0:T(8,128)(2,1)S(1)}, s16[400,512]{1,0:T(8,128)(2,1)S(1)}, u32[]{:S(2)}, u32[]{:S(2)}) collective-permute-start(s16[400,512]{1,0:T(8,128)(2,1)S(1)} %get-tuple-element.48), channel_id=1, source_target_pairs={{0,1},{1,0},{2,3},{3,2},{4,5},{5,4},{6,7},{7,6},{8,9},{9,8},{10,11... | collective-permute-start | bytes 1228808 | tf_op jit(solution)/shard_map/ppermute | solution.py:42
  84.9 20.1 %collective-permute-start.11 = (s16[400,512]{1,0:T(8,128)(2,1)S(1)}, s16[400,512]{1,0:T(8,128)(2,1)S(1)}, u32[]{:S(2)}, u32[]{:S(2)}) collective-permute-start(s16[400,512]{1,0:T(8,128)(2,1)S(1)} %get-tuple-element.49), channel_id=1, source_target_pairs={{0,2},{1,3},{2,0},{3,1},{4,6},{5,7},{6,4},{7,5},{8,10},{9,11},{10,... | collective-permute-start | bytes 1228808 | tf_op jit(solution)/shard_map/ppermute | solution.py:42
  86.8 20.4 %collective-permute-start.12 = (s16[400,512]{1,0:T(8,128)(2,1)S(1)}, s16[400,512]{1,0:T(8,128)(2,1)S(1)}, u32[]{:S(2)}, u32[]{:S(2)}) collective-permute-start(s16[400,512]{1,0:T(8,128)(2,1)S(1)} %get-tuple-element.50), channel_id=1, source_target_pairs={{0,3},{1,2},{2,1},{3,0},{4,7},{5,6},{6,5},{7,4},{8,11},{9,10},{10,... | collective-permute-start | bytes 1228808 | tf_op jit(solution)/shard_map/ppermute | solution.py:42
  107.1 18.2 %collective-permute-start.13 = (s16[2,400,512]{2,1,0:T(8,128)(2,1)S(1)}, s16[2,400,512]{2,1,0:T(8,128)(2,1)S(1)}, u32[]{:S(2)}, u32[]{:S(2)}) collective-permute-start(s16[2,400,512]{2,1,0:T(8,128)(2,1)S(1)} %get-tuple-element.51), channel_id=1, source_target_pairs={{0,1},{1,0},{2,3},{3,2},{4,5},{5,4},{6,7},{7,6},{8,9},{9,8},{10,11... | collective-permute-start | bytes 2457608 | tf_op jit(solution)/shard_map/ppermute | solution.py:42
  107.1 37.3 %collective-permute-start.14 = (s16[2,400,512]{2,1,0:T(8,128)(2,1)S(1)}, s16[2,400,512]{2,1,0:T(8,128)(2,1)S(1)}, u32[]{:S(2)}, u32[]{:S(2)}) collective-permute-start(s16[2,400,512]{2,1,0:T(8,128)(2,1)S(1)} %get-tuple-element.52), channel_id=1, source_target_pairs={{0,2},{1,3},{2,0},{3,1},{4,6},{5,7},{6,4},{7,5},{8,10},{9,11},{10,... | collective-permute-start | bytes 2457608 | tf_op jit(solution)/shard_map/ppermute | solution.py:42
  110.2 34.2 %collective-permute-start.15 = (s16[2,400,512]{2,1,0:T(8,128)(2,1)S(1)}, s16[2,400,512]{2,1,0:T(8,128)(2,1)S(1)}, u32[]{:S(2)}, u32[]{:S(2)}) collective-permute-start(s16[2,400,512]{2,1,0:T(8,128)(2,1)S(1)} %pad_add_fusion.2), channel_id=1, source_target_pairs={{0,3},{1,2},{2,1},{3,0},{4,7},{5,6},{6,5},{7,4},{8,11},{9,10},{10,... | collective-permute-start | bytes 2457608 | tf_op jit(solution)/shard_map/ppermute | solution.py:42
  147.7 8.3 %collective-permute-start.19 = (f32[512,512]{1,0:T(8,128)S(1)}, f32[512,512]{1,0:T(8,128)S(1)}, u32[]{:S(2)}, u32[]{:S(2)}) collective-permute-start(f32[512,512]{1,0:T(8,128)S(1)} %get-tuple-element.68), channel_id=1, source_target_pairs={{0,16},{1,17},{2,18},{3,19},{4,20},{5,21},{6,22},{7,23},{8,24},{9,... | collective-permute-start | bytes 3145736 | tf_op jit(solution)/shard_map/ppermute | solution.py:42
  153.0 3.0 %collective-permute-start.20 = (f32[256,512]{1,0:T(8,128)S(1)}, f32[256,512]{1,0:T(8,128)S(1)}, u32[]{:S(2)}, u32[]{:S(2)}) collective-permute-start(f32[256,512]{1,0:T(8,128)S(1)} %get-tuple-element.69), channel_id=1, source_target_pairs={{0,16},{1,17},{2,18},{3,19},{4,20},{5,21},{6,22},{7,23},{8,24},{9,... | collective-permute-start | bytes 1572872 | tf_op jit(solution)/shard_map/ppermute | solution.py:42
  157.3 28.1 %all-to-all-start = ((f32[16,48,512]{2,1,0:T(8,128)}), f32[16,48,512]{2,1,0:T(8,128)S(1)}, u32[]{:S(2)}, u32[]{:S(2)}) async-start(f32[16,48,512]{2,1,0:T(8,128)} %bitcast.26), calls=%async_computation | async-start | bytes 3145728 | tf_op jit(solution)/shard_map/all_to_all | solution.py:343
  164.0 37.6 %collective-permute-start.18 = (s16[336,512]{1,0:T(8,128)(2,1)}, s16[336,512]{1,0:T(8,128)(2,1)S(1)}, u32[]{:S(2)}, u32[]{:S(2)}) collective-permute-start(s16[336,512]{1,0:T(8,128)(2,1)} %pad_add_fusion.5), channel_id=1, source_target_pairs={{0,12},{1,13},{2,14},{3,15},{4,8},{5,9},{6,10},{7,11},{8,4},{9,5},... | collective-permute-start | bytes 1032200 | tf_op jit(solution)/shard_map/ppermute | solution.py:42
  166.0 35.6 %collective-permute-start.17 = (s16[336,512]{1,0:T(8,128)(2,1)}, s16[336,512]{1,0:T(8,128)(2,1)S(1)}, u32[]{:S(2)}, u32[]{:S(2)}) collective-permute-start(s16[336,512]{1,0:T(8,128)(2,1)} %pad_add_fusion.4), channel_id=1, source_target_pairs={{0,8},{1,9},{2,10},{3,11},{4,12},{5,13},{6,14},{7,15},{8,0},{9,1},... | collective-permute-start | bytes 1032200 | tf_op jit(solution)/shard_map/ppermute | solution.py:42
  166.8 34.8 %collective-permute-start.16 = (s16[336,512]{1,0:T(8,128)(2,1)}, s16[336,512]{1,0:T(8,128)(2,1)S(1)}, u32[]{:S(2)}, u32[]{:S(2)}) collective-permute-start(s16[336,512]{1,0:T(8,128)(2,1)} %pad_add_fusion.3), channel_id=1, source_target_pairs={{0,4},{1,5},{2,6},{3,7},{4,0},{5,1},{6,2},{7,3},{8,12},{9,13},{10,... | collective-permute-start | bytes 1032200 | tf_op jit(solution)/shard_map/ppermute | solution.py:42
  185.6 8.3 %collective-permute-start.21 = (f32[48,512]{1,0:T(8,128)S(1)}, f32[48,512]{1,0:T(8,128)S(1)}, u32[]{:S(2)}, u32[]{:S(2)}) collective-permute-start(f32[48,512]{1,0:T(8,128)S(1)} %reduce_sum.9), channel_id=1, source_target_pairs={{0,32},{1,33},{2,34},{3,35},{4,36},{5,37},{6,38},{7,39},{8,40},{9,... | collective-permute-start | bytes 294920 | tf_op jit(solution)/shard_map/ppermute | solution.py:42
  193.9 6.5 %collective-permute-start.22 = (f32[48,512]{1,0:T(8,128)S(1)}, f32[48,512]{1,0:T(8,128)S(1)}, u32[]{:S(2)}, u32[]{:S(2)}) collective-permute-start(f32[48,512]{1,0:T(8,128)S(1)} %add.51), channel_id=1, source_target_pairs={{0,4},{1,5},{2,6},{3,7},{4,0},{5,1},{6,2},{7,3},{8,12},{9,13},{10,... | collective-permute-start | bytes 294920 | tf_op jit(solution)/shard_map/ppermute | solution.py:42
  200.4 5.0 %collective-permute-start.23 = (f32[48,512]{1,0:T(8,128)S(1)}, f32[48,512]{1,0:T(8,128)S(1)}, u32[]{:S(2)}, u32[]{:S(2)}) collective-permute-start(f32[48,512]{1,0:T(8,128)S(1)} %add.52), channel_id=1, source_target_pairs={{0,8},{1,9},{2,10},{3,11},{4,12},{5,13},{6,14},{7,15},{8,0},{9,1},... | collective-permute-start | bytes 294920 | tf_op jit(solution)/shard_map/ppermute | solution.py:42
  205.4 33.3 %copy-start.1 = (f32[3,512,512]{2,1,0:T(8,128)S(1)}, f32[3,512,512]{2,1,0:T(8,128)}, u32[]{:S(2)}) copy-start(f32[3,512,512]{2,1,0:T(8,128)} %diag_ref.1) | copy-start | bytes 9437188
  230.8 7.9 %collective-permute-start.24 = (f32[768,512]{1,0:T(8,128)S(1)}, f32[768,512]{1,0:T(8,128)S(1)}, u32[]{:S(2)}, u32[]{:S(2)}) collective-permute-start(f32[768,512]{1,0:T(8,128)S(1)} %bitcast.39), channel_id=1, source_target_pairs={{0,16},{1,17},{2,18},{3,19},{4,20},{5,21},{6,22},{7,23},{8,24},{9,... | collective-permute-start | bytes 4718600 | tf_op jit(solution)/shard_map/ppermute | solution.py:42

commit v2 on v1

--- a/solution.py
+++ b/solution.py
@@ -139,11 +139,11 @@
             ref[...] = value
 
 
-def product(at, a4, own, other, first, panels):
+def product(at, a4, own, other):
     shard, order = a4.shape[2], a4.shape[3]
-    width = own.shape[4]
+    panels, width = own.shape[2], own.shape[4]
     rows = 4 * shard
-    whole = pl.BlockSpec((4, 2, panels, shard, width), lambda g, s: (0, 0, first // panels, 0, 0))
+    whole = pl.BlockSpec((4, 2, panels, shard, width), lambda g, s: (0, 0, 0, 0, 0))
     kept = pl.BlockSpec((rows, width), lambda g, s: (0, 0))
     coded = pl.BlockSpec((rows + EXTRA, width), lambda g, s: (0, 0))
     one = [jax.ShapeDtypeStruct((rows, width), F32)]
@@ -164,7 +164,7 @@
             scratch_shapes=[pltpu.VMEM((panels, order, width), BF16)],
         ),
         out_shape=one * panels,
-        compiler_params=params(),
+        compiler_params=params(44),
         cost_estimate=cost(8 * panels * rows * order * width, 2 * order * order),
         name="product",
     )(at, a4, own, other)
@@ -309,25 +309,26 @@
     own_mask = jnp.where(in_first[None, :], first, second).astype(BF16)
     masked = jnp.swapaxes(panels, 0, 1) * own_mask[:, :, None]
 
-    moved = send(masked, spread)
-    turned = [send(moved, turn(i)) for i in range(2)]
-    late = after(masked, turned)
+    def gather(message):
+        return [message] + [send(message, over_x(k)) for k in (1, 2, 3)]
+
+    a4 = ancestor_inverse.reshape(4, 4, kept, order)
+    moved_a, moved_b = send(masked[2:], spread), send(masked[:2], spread)
+    turned_a = [send(moved_a, turn(i)) for i in range(2)]
+    turned_b = [send(moved_b, turn(i)) for i in range(2)]
+    own_a = gather(after(jnp.stack(turned_a), moved_b))
+    own_a = after(jnp.stack(own_a), turned_b)
+    own_b = gather(after(jnp.stack(turned_b), own_a))
+    ((keep_a, *coded),) = product(at, a4, own_a, send(own_a, over_core))
+    parts_a = [send(coded[k - 1], over_y(k)) for k in (1, 2, 3)]
+    own_b = after(jnp.stack(own_b), parts_a[0], parts_a[2])
+    outs = product(at, a4, own_b, send(own_b, over_core))
+    late = after(masked, own_b)
     beside = [masked] + [send(late, over_l(k)) for k in (1, 2, 3)]
-    a4 = ancestor_inverse.reshape(4, 4, kept, order)
-    message = jnp.stack(turned)
-    found = [send(message, over_x(k)) for k in (1, 2, 3)]
-    own = after(jnp.stack([message] + found), beside)
-    other = send(own, over_core)
-    keeps, parts = [], []
-    for group in ((2,), (0, 1)):
-        for keep, *coded in product(at, a4, own, other, group[0], len(group)):
-            keeps.append(keep)
-            parts.append(coded)
-        if len(group) == 1:
-            parts[0] = [send(parts[0][k - 1], over_y(k)) for k in (1, 2, 3)]
-    pairs = [jnp.stack([parts[1][k], parts[2][k]]) for k in range(3)]
-    pairs = after(pairs, parts[0])
+    pairs = [jnp.stack([outs[0][k], outs[1][k]]) for k in (1, 2, 3)]
+    pairs = after(pairs, parts_a)
     pairs = [send(pairs[k - 1], over_y(k)) for k in (1, 2, 3)]
+    keeps, parts = [keep_a, outs[0][0], outs[1][0]], [parts_a]
     own_2, *coded = middle(at, keeps[:1], parts[:1], beside, 2)
     coded_2, (mine_2, their_2) = coded[:3], coded[3:]
     swapped_2 = send(their_2, over_core)

time: 242 us -> 231 us (0.955)
  waiting for transfers between devices: 112 us -> 84 us
  starting transfers between devices: 68.3 us -> 86.3 us
    ppermute x25 -> x32, waiting for transfers between devices: 95.9 us -> 67.7 us  [send(): return lax.ppermute(value, AXES, pairs)]
    ppermute x25 -> x32, starting transfers between devices: 62.4 us -> 82.2 us  [send(): return lax.ppermute(value, AXES, pairs)]
  transfers between devices with their start and end apart: 26 -> 33, of which waited for: 15 -> 17; matrix products, arithmetic and copies ran while one was open for 1% -> 1% of each run, Pallas kernels for 6% -> 8%
where the time goes in v2:
time: 231 us
  starting transfers between devices  86.3 us (37%)
  waiting for transfers between devices  84 us (36%)
  blocking collectives  26.9 us (12%)
  Pallas kernels  24.9 us (11%)
  other arithmetic  4.14 us (2%)
  local copies, waits for them, and re-layouts  3.77 us (2%)
    ppermute x32, starting transfers between devices, send(): return lax.ppermute(value, AXES, pairs)  82.2 us
    ppermute x32, waiting for transfers between devices, send(): return lax.ppermute(value, AXES, pairs)  67.7 us
    all_to_all x1, blocking collectives, body(): mine = lax.all_to_all(pieces, ('x', 'y'), 0, 0).reshape(halves.shape)  26.9 us
    all_to_all x1, waiting for transfers between devices, body(): total = jnp.sum(lax.all_to_all(pieces, ('x', 'y'), 0, 0), axis=0)  16.4 us
    pallas_call x2, Pallas kernels, product(): pl.pallas_call(functools.partial(product_kernel, panels), grid_spec=pltpu...  14.9 us
    pallas_call x2, Pallas kernels, middle(): pl.pallas_call(functools.partial(middle_kernel, panels, base), in_specs=[...  5.07 us
  transfers between devices with their start and end apart: 33, of which 17 were waited for; matrix products, arithmetic and copies ran while one was open for 1% of the time, Pallas kernels for 8%

profile of v2, /device:TPU:1, one launch (start us, length us, event | category | flops | bytes accessed | tf_op | source)
XLA Modules:
  0.0 231.0 jit_solution(12573323620815351231)
XLA Ops:
  3.5 4.6 %collective-permute-start.4 = (bf16[1,96,512]{2,1,0:T(8,128)(2,1)S(1)}, bf16[1,96,512]{2,1,0:T(8,128)(2,1)S(1)}, u32[]{:S(2)}, u32[]{:S(2)}) collective-permute-start(bf16[1,96,512]{2,1,0:T(8,128)(2,1)S(1)} %collective-permute-done.3), channel_id=1, source_target_pairs={{0,0},{1,32},{2,16},{3,48},{4,4},{5,36},{6,20},{7,52},{8,8},{9,40}... | collective-permute-start | bytes 294920 | tf_op jit(solution)/shard_map/ppermute | solution.py:42
  8.1 8.3 %collective-permute-start.5 = (bf16[1,96,512]{2,1,0:T(8,128)(2,1)S(1)}, bf16[1,96,512]{2,1,0:T(8,128)(2,1)S(1)}, u32[]{:S(2)}, u32[]{:S(2)}) collective-permute-start(bf16[1,96,512]{2,1,0:T(8,128)(2,1)S(1)} %collective-permute-done.3), channel_id=1, source_target_pairs={{0,32},{1,0},{2,48},{3,16},{4,36},{5,4},{6,52},{7,20},{8,40},{9,8}... | collective-permute-start | bytes 294920 | tf_op jit(solution)/shard_map/ppermute | solution.py:42
  18.4 5.3 %collective-permute-start.6 = (bf16[2,1,96,512]{3,2,0,1:T(8,128)(2,1)S(1)}, bf16[2,1,96,512]{3,2,0,1:T(8,128)(2,1)S(1)}, u32[]{:S(2)}, u32[]{:S(2)}) collective-permute-start(bf16[2,1,96,512]{3,2,0,1:T(8,128)(2,1)S(1)} %bitcast.58), channel_id=1, source_target_pairs={{0,64},{1,65},{2,66},{3,67},{4,68},{5,69},{6,70},{7,71},{8,72},{9,... | collective-permute-start | bytes 589832 | tf_op jit(solution)/shard_map/ppermute | solution.py:42
  23.7 8.9 %collective-permute-start.7 = (bf16[2,1,96,512]{3,2,0,1:T(8,128)(2,1)S(1)}, bf16[2,1,96,512]{3,2,0,1:T(8,128)(2,1)S(1)}, u32[]{:S(2)}, u32[]{:S(2)}) collective-permute-start(bf16[2,1,96,512]{3,2,0,1:T(8,128)(2,1)S(1)} %bitcast.59), channel_id=1, source_target_pairs={{0,128},{1,129},{2,130},{3,131},{4,132},{5,133},{6,134},{7,135},{8... | collective-permute-start | bytes 589832 | tf_op jit(solution)/shard_map/ppermute | solution.py:42
  32.6 2.9 %collective-permute-start.1 = (bf16[2,96,512]{2,1,0:T(8,128)(2,1)S(1)}, bf16[2,96,512]{2,1,0:T(8,128)(2,1)S(1)}, u32[]{:S(2)}, u32[]{:S(2)}) collective-permute-start(bf16[2,96,512]{2,1,0:T(8,128)(2,1)S(1)} %collective-permute-done), channel_id=1, source_target_pairs={{0,0},{1,32},{2,16},{3,48},{4,4},{5,36},{6,20},{7,52},{8,8},{9,40}... | collective-permute-start | bytes 589832 | tf_op jit(solution)/shard_map/ppermute | solution.py:42
  35.6 4.2 %collective-permute-start.2 = (bf16[2,96,512]{2,1,0:T(8,128)(2,1)S(1)}, bf16[2,96,512]{2,1,0:T(8,128)(2,1)S(1)}, u32[]{:S(2)}, u32[]{:S(2)}) collective-permute-start(bf16[2,96,512]{2,1,0:T(8,128)(2,1)S(1)} %collective-permute-done), channel_id=1, source_target_pairs={{0,32},{1,0},{2,48},{3,16},{4,36},{5,4},{6,52},{7,20},{8,40},{9,8}... | collective-permute-start | bytes 589832 | tf_op jit(solution)/shard_map/ppermute | solution.py:42
  40.5 2.8 %collective-permute-done.8 = bf16[2,1,96,512]{3,2,1,0:T(8,128)(2,1)S(1)} collective-permute-done((bf16[2,1,96,512]{3,2,1,0:T(8,128)(2,1)S(1)}, bf16[2,1,96,512]{3,2,1,0:T(8,128)(2,1)S(1)}, u32[]{:S(2)}, u32[]{:S(2)}) %collective-permute-start.8) | collective-permute-done | bytes 196640 | tf_op jit(solution)/shard_map/ppermute | solution.py:42
  45.2 6.1 %collective-permute-start.9 = (bf16[2,2,96,512]{3,2,1,0:T(8,128)(2,1)S(1)}, bf16[2,2,96,512]{3,2,1,0:T(8,128)(2,1)S(1)}, u32[]{:S(2)}, u32[]{:S(2)}) collective-permute-start(bf16[2,2,96,512]{3,2,1,0:T(8,128)(2,1)S(1)} %pad_maximum_fusion.3), channel_id=1, source_target_pairs={{0,64},{1,65},{2,66},{3,67},{4,68},{5,69},{6,70},{7,71},{8,72},{9,... | collective-permute-start | bytes 1179656 | tf_op jit(solution)/shard_map/ppermute | solution.py:42
  51.3 6.9 %collective-permute-start.10 = (bf16[2,2,96,512]{3,2,1,0:T(8,128)(2,1)S(1)}, bf16[2,2,96,512]{3,2,1,0:T(8,128)(2,1)S(1)}, u32[]{:S(2)}, u32[]{:S(2)}) collective-permute-start(bf16[2,2,96,512]{3,2,1,0:T(8,128)(2,1)S(1)} %pad_maximum_fusion.3), channel_id=1, source_target_pairs={{0,128},{1,129},{2,130},{3,131},{4,132},{5,133},{6,134},{7,135},{8... | collective-permute-start | bytes 1179656 | tf_op jit(solution)/shard_map/ppermute | solution.py:42
  58.3 2.3 %copy-done = bf16[1536,1536]{1,0:T(8,128)(2,1)S(1)} copy-done((bf16[1536,1536]{1,0:T(8,128)(2,1)S(1)}, bf16[1536,1536]{1,0:T(8,128)(2,1)}, u32[]{:S(2)}) %copy-start) | copy-done | bytes 4718616
  60.7 5.0 %product.2 = (f32[384,512]{1,0:T(8,128)S(1)}, s16[400,512]{1,0:T(8,128)(2,1)S(1)}, s16[400,512]{1,0:T(8,128)(2,1)S(1)}, s16[400,512]{1,0:T(8,128)(2,1)S(1)}) custom-call(s32[6]{0:T(128)S(1)} %stack.102.at_ref.refs_0_, bf16[4,4,96,1536]{3,2,1,0:T(8,128)(2,1)S(1)} %bitcast.46, bf16[4,2,1,96,512]{4,3,2,1,0:T(8,128)(2,1)S(1)} %bitcast.49, ...), custom_call_target="tpu_custom_call" | custom-call | flops 2415919 | bytes 4718 | tf_op jit(solution)/shard_map/product/pallas_call | solution.py:151
  65.8 2.5 %collective-permute-start.14 = (s16[400,512]{1,0:T(8,128)(2,1)S(1)}, s16[400,512]{1,0:T(8,128)(2,1)S(1)}, u32[]{:S(2)}, u32[]{:S(2)}) collective-permute-start(s16[400,512]{1,0:T(8,128)(2,1)S(1)} %get-tuple-element.45), channel_id=1, source_target_pairs={{0,3},{1,2},{2,1},{3,0},{4,7},{5,6},{6,5},{7,4},{8,11},{9,10},{10,... | collective-permute-start | bytes 1228808 | tf_op jit(solution)/shard_map/ppermute | solution.py:42
  68.2 7.8 %collective-permute-done.10 = bf16[2,2,96,512]{3,2,1,0:T(8,128)(2,1)S(1)} collective-permute-done((bf16[2,2,96,512]{3,2,1,0:T(8,128)(2,1)S(1)}, bf16[2,2,96,512]{3,2,1,0:T(8,128)(2,1)S(1)}, u32[]{:S(2)}, u32[]{:S(2)}) %collective-permute-start.10) | collective-permute-done | bytes 393248 | tf_op jit(solution)/shard_map/ppermute | solution.py:42
  82.8 9.9 %product.3 = (f32[384,512]{1,0:T(8,128)S(1)}, s16[400,512]{1,0:T(8,128)(2,1)S(1)}, s16[400,512]{1,0:T(8,128)(2,1)S(1)}, s16[400,512]{1,0:T(8,128)(2,1)S(1)}, f32...) custom-call(s32[6]{0:T(128)S(1)} %stack.102.at_ref.refs_0_, ...), custom_call_target="tpu_custom_call" | custom-call | flops 4831838 | bytes 4718 | tf_op jit(solution)/shard_map/product/pallas_call | solution.py:151
  93.0 2.8 %collective-permute-start.18 = (s16[2,400,512]{2,1,0:T(8,128)(2,1)S(1)}, s16[2,400,512]{2,1,0:T(8,128)(2,1)S(1)}, u32[]{:S(2)}, u32[]{:S(2)}) collective-permute-start(s16[2,400,512]{2,1,0:T(8,128)(2,1)S(1)} %get-tuple-element.57), channel_id=1, source_target_pairs={{0,2},{1,3},{2,0},{3,1},{4,6},{5,7},{6,4},{7,5},{8,10},{9,11},{10,... | collective-permute-start | bytes 2457608 | tf_op jit(solution)/shard_map/ppermute | solution.py:42
  97.3 2.2 collective-permute-start.21
  99.5 11.1 %collective-permute-done.20.refs_6_.refs_10_ = bf16[3,96,512]{2,1,0:T(8,128)(2,1)S(1)} collective-permute-done((bf16[3,96,512]{2,1,0:T(8,128)(2,1)S(1)}, bf16[3,96,512]{2,1,0:T(8,128)(2,1)S(1)}, u32[]{:S(2)}, u32[]{:S(2)}) %collective-permute-start.20) | collective-permute-done | bytes 294944 | tf_op jit(solution)/shard_map/ppermute | solution.py:42
  111.2 7.9 %collective-permute-done.22.refs_8_.refs_12_ = bf16[3,96,512]{2,1,0:T(8,128)(2,1)S(1)} collective-permute-done((bf16[3,96,512]{2,1,0:T(8,128)(2,1)S(1)}, bf16[3,96,512]{2,1,0:T(8,128)(2,1)S(1)}, u32[]{:S(2)}, u32[]{:S(2)}) %collective-permute-start.22) | collective-permute-done | bytes 294944 | tf_op jit(solution)/shard_map/ppermute | solution.py:42
  121.1 10.3 %collective-permute-done.18 = s16[2,400,512]{2,1,0:T(8,128)(2,1)S(1)} collective-permute-done((s16[2,400,512]{2,1,0:T(8,128)(2,1)S(1)}, s16[2,400,512]{2,1,0:T(8,128)(2,1)S(1)}, u32[]{:S(2)}, u32[]{:S(2)}) %collective-permute-start.18) | collective-permute-done | bytes 819232 | tf_op jit(solution)/shard_map/ppermute | solution.py:42
  133.5 3.1 %middle.3 = (f32[192,512]{1,0:T(8,128)S(1)}, s16[224,512]{1,0:T(8,128)(2,1)S(1)}, s16[224,512]{1,0:T(8,128)(2,1)S(1)}, s16[224,512]{1,0:T(8,128)(2,1)S(1)}, f32[...) custom-call(s32[6]{0:T(128)S(1)} %stack.102.at_ref.refs_0_, f32[384,512]{1,0:T(8,128)S(1)} %get-tuple-element.47.refs_1_, ...), custom_call_target="tpu_custom_call" | custom-call | flops 603979 | bytes 3145 | tf_op jit(solution)/shard_map/middle/pallas_call | solution.py:214
  138.7 2.9 %collective-permute-done.27.refs_3_ = f32[256,512]{1,0:T(8,128)S(1)} collective-permute-done((f32[256,512]{1,0:T(8,128)S(1)}, f32[256,512]{1,0:T(8,128)S(1)}, u32[]{:S(2)}, u32[]{:S(2)}) %collective-permute-start.27) | collective-permute-done | bytes 524320 | tf_op jit(solution)/shard_map/ppermute | solution.py:42
  142.9 4.1 %all-to-all-start = ((f32[16,48,512]{2,1,0:T(8,128)}), f32[16,48,512]{2,1,0:T(8,128)S(1)}, u32[]{:S(2)}, u32[]{:S(2)}) async-start(f32[16,48,512]{2,1,0:T(8,128)} %bitcast.35), calls=%async_computation | async-start | bytes 3145728 | tf_op jit(solution)/shard_map/all_to_all | solution.py:344
  147.8 3.1 %collective-permute-start.25 = (s16[336,512]{1,0:T(8,128)(2,1)}, s16[336,512]{1,0:T(8,128)(2,1)S(1)}, u32[]{:S(2)}, u32[]{:S(2)}) collective-permute-start(s16[336,512]{1,0:T(8,128)(2,1)} %pad_add_fusion.5), channel_id=1, source_target_pairs={{0,12},{1,13},{2,14},{3,15},{4,8},{5,9},{6,10},{7,11},{8,4},{9,5},... | collective-permute-start | bytes 1032200 | tf_op jit(solution)/shard_map/ppermute | solution.py:42
  152.8 16.4 %all-to-all-done = f32[16,48,512]{2,1,0:T(8,128)S(1)} async-done(((f32[16,48,512]{2,1,0:T(8,128)}), f32[16,48,512]{2,1,0:T(8,128)S(1)}, u32[]{:S(2)}, u32[]{:S(2)}) %all-to-all-start) | async-done | bytes 1572896 | tf_op jit(solution)/shard_map/all_to_all | solution.py:344
  169.3 2.4 %collective-permute-start.28 = (f32[48,512]{1,0:T(8,128)S(1)}, f32[48,512]{1,0:T(8,128)S(1)}, u32[]{:S(2)}, u32[]{:S(2)}) collective-permute-start(f32[48,512]{1,0:T(8,128)S(1)} %reduce_sum.9), channel_id=1, source_target_pairs={{0,32},{1,33},{2,34},{3,35},{4,36},{5,37},{6,38},{7,39},{8,40},{9,... | collective-permute-start | bytes 294920 | tf_op jit(solution)/shard_map/ppermute | solution.py:42
  171.7 5.5 %collective-permute-done.28 = f32[48,512]{1,0:T(8,128)S(1)} collective-permute-done((f32[48,512]{1,0:T(8,128)S(1)}, f32[48,512]{1,0:T(8,128)S(1)}, u32[]{:S(2)}, u32[]{:S(2)}) %collective-permute-start.28) | collective-permute-done | bytes 98336 | tf_op jit(solution)/shard_map/ppermute | solution.py:42
  177.2 10.7 %collective-permute-start.29 = (f32[48,512]{1,0:T(8,128)S(1)}, f32[48,512]{1,0:T(8,128)S(1)}, u32[]{:S(2)}, u32[]{:S(2)}) collective-permute-start(f32[48,512]{1,0:T(8,128)S(1)} %add.51), channel_id=1, source_target_pairs={{0,4},{1,5},{2,6},{3,7},{4,0},{5,1},{6,2},{7,3},{8,12},{9,13},{10,... | collective-permute-start | bytes 294920 | tf_op jit(solution)/shard_map/ppermute | solution.py:42
  187.9 2.7 %collective-permute-done.29 = f32[48,512]{1,0:T(8,128)S(1)} collective-permute-done((f32[48,512]{1,0:T(8,128)S(1)}, f32[48,512]{1,0:T(8,128)S(1)}, u32[]{:S(2)}, u32[]{:S(2)}) %collective-permute-start.29) | collective-permute-done | bytes 98336 | tf_op jit(solution)/shard_map/ppermute | solution.py:42
  192.1 4.3 %collective-permute-done.30 = f32[48,512]{1,0:T(8,128)S(1)} collective-permute-done((f32[48,512]{1,0:T(8,128)S(1)}, f32[48,512]{1,0:T(8,128)S(1)}, u32[]{:S(2)}, u32[]{:S(2)}) %collective-permute-start.30) | collective-permute-done | bytes 98336 | tf_op jit(solution)/shard_map/ppermute | solution.py:42
  196.6 26.9 %all_to_all.10 = f32[16,48,512]{2,1,0:T(8,128)S(1)} all-to-all(f32[16,48,512]{2,1,0:T(8,128)S(1)} %broadcast_in_dim.35), channel_id=1, replica_groups=mesh['x'=4,'h'=2,'core'=2,'l'=4,'y'=4] {'x','y'}, dimensions={0} | all-to-all | bytes 3145728 | tf_op jit(solution)/shard_map/all_to_all | solution.py:351
  225.5 3.0 %collective-permute-done.31.theirs_ref = f32[768,512]{1,0:T(8,128)S(1)} collective-permute-done((f32[768,512]{1,0:T(8,128)S(1)}, f32[768,512]{1,0:T(8,128)S(1)}, u32[]{:S(2)}, u32[]{:S(2)}) %collective-permute-start.31) | collective-permute-done | bytes 1572896 | tf_op jit(solution)/shard_map/ppermute | solution.py:42
  228.5 2.5 %finish.1 = f32[3,512,512]{2,1,0:T(8,128)} custom-call(s32[6]{0:T(128)S(1)} %stack.102.at_ref.refs_0_, f32[768,512]{1,0:T(8,128)S(1)} %bitcast.48, f32[768,512]{1,0:T(8,128)S(1)} %collective-permute-done.31.theirs_ref, f32[3,512,512]{2,1,0:T(8,128)S(1)} %copy-done.1), custom_call_target="tpu_custom_call" | custom-call | flops 786 | bytes 9437 | tf_op jit(solution)/shard_map/finish/pallas_call | solution.py:283
  (71 shorter events, 30.7 us)
Async XLA Ops:
  3.5 13.6 %collective-permute-start.4 = (bf16[1,96,512]{2,1,0:T(8,128)(2,1)S(1)}, bf16[1,96,512]{2,1,0:T(8,128)(2,1)S(1)}, u32[]{:S(2)}, u32[]{:S(2)}) collective-permute-start(bf16[1,96,512]{2,1,0:T(8,128)(2,1)S(1)} %collective-permute-done.3), channel_id=1, source_target_pairs={{0,0},{1,32},{2,16},{3,48},{4,4},{5,36},{6,20},{7,52},{8,8},{9,40}... | collective-permute-start | bytes 294920 | tf_op jit(solution)/shard_map/ppermute | solution.py:42
  8.1 10.3 %collective-permute-start.5 = (bf16[1,96,512]{2,1,0:T(8,128)(2,1)S(1)}, bf16[1,96,512]{2,1,0:T(8,128)(2,1)S(1)}, u32[]{:S(2)}, u32[]{:S(2)}) collective-permute-start(bf16[1,96,512]{2,1,0:T(8,128)(2,1)S(1)} %collective-permute-done.3), channel_id=1, source_target_pairs={{0,32},{1,0},{2,48},{3,16},{4,36},{5,4},{6,52},{7,20},{8,40},{9,8}... | collective-permute-start | bytes 294920 | tf_op jit(solution)/shard_map/ppermute | solution.py:42
  16.4 2.0 collective-permute-start
  18.4 21.4 %collective-permute-start.6 = (bf16[2,1,96,512]{3,2,0,1:T(8,128)(2,1)S(1)}, bf16[2,1,96,512]{3,2,0,1:T(8,128)(2,1)S(1)}, u32[]{:S(2)}, u32[]{:S(2)}) collective-permute-start(bf16[2,1,96,512]{3,2,0,1:T(8,128)(2,1)S(1)} %bitcast.58), channel_id=1, source_target_pairs={{0,64},{1,65},{2,66},{3,67},{4,68},{5,69},{6,70},{7,71},{8,72},{9,... | collective-permute-start | bytes 589832 | tf_op jit(solution)/shard_map/ppermute | solution.py:42
  23.7 16.8 %collective-permute-start.7 = (bf16[2,1,96,512]{3,2,0,1:T(8,128)(2,1)S(1)}, bf16[2,1,96,512]{3,2,0,1:T(8,128)(2,1)S(1)}, u32[]{:S(2)}, u32[]{:S(2)}) collective-permute-start(bf16[2,1,96,512]{3,2,0,1:T(8,128)(2,1)S(1)} %bitcast.59), channel_id=1, source_target_pairs={{0,128},{1,129},{2,130},{3,131},{4,132},{5,133},{6,134},{7,135},{8... | collective-permute-start | bytes 589832 | tf_op jit(solution)/shard_map/ppermute | solution.py:42
  32.6 10.7 %collective-permute-start.8 = (bf16[2,1,96,512]{3,2,1,0:T(8,128)(2,1)S(1)}, bf16[2,1,96,512]{3,2,1,0:T(8,128)(2,1)S(1)}, u32[]{:S(2)}, u32[]{:S(2)}) collective-permute-start(bf16[2,1,96,512]{3,2,1,0:T(8,128)(2,1)S(1)} %pad_maximum_fusion.4), channel_id=1, source_target_pairs={{0,192},{1,193},{2,194},{3,195},{4,196},{5,197},{6,198},{7,199},{8... | collective-permute-start | bytes 589832 | tf_op jit(solution)/shard_map/ppermute | solution.py:42
  32.6 10.8 %collective-permute-start.1 = (bf16[2,96,512]{2,1,0:T(8,128)(2,1)S(1)}, bf16[2,96,512]{2,1,0:T(8,128)(2,1)S(1)}, u32[]{:S(2)}, u32[]{:S(2)}) collective-permute-start(bf16[2,96,512]{2,1,0:T(8,128)(2,1)S(1)} %collective-permute-done), channel_id=1, source_target_pairs={{0,0},{1,32},{2,16},{3,48},{4,4},{5,36},{6,20},{7,52},{8,8},{9,40}... | collective-permute-start | bytes 589832 | tf_op jit(solution)/shard_map/ppermute | solution.py:42
  35.6 9.6 %collective-permute-start.2 = (bf16[2,96,512]{2,1,0:T(8,128)(2,1)S(1)}, bf16[2,96,512]{2,1,0:T(8,128)(2,1)S(1)}, u32[]{:S(2)}, u32[]{:S(2)}) collective-permute-start(bf16[2,96,512]{2,1,0:T(8,128)(2,1)S(1)} %collective-permute-done), channel_id=1, source_target_pairs={{0,32},{1,0},{2,48},{3,16},{4,36},{5,4},{6,52},{7,20},{8,40},{9,8}... | collective-permute-start | bytes 589832 | tf_op jit(solution)/shard_map/ppermute | solution.py:42
  45.2 13.2 %collective-permute-start.12 = (bf16[4,2,1,96,512]{4,3,1,2,0:T(8,128)(2,1)S(1)}, bf16[4,2,1,96,512]{4,3,1,2,0:T(8,128)(2,1)S(1)}, u32[]{:S(2)}, u32[]{:S(2)}) collective-permute-start(bf16[4,2,1,96,512]{4,3,1,2,0:T(8,128)(2,1)S(1)} %pad_maximum_fusion.1), channel_id=1, source_target_pairs={{0,16},{1,17},{2,18},{3,19},{4,20},{5,21},{6,22},{7,23},{8,24},{9,... | collective-permute-start | bytes 2359304 | tf_op jit(solution)/shard_map/ppermute | solution.py:42
  45.2 23.0 %collective-permute-start.9 = (bf16[2,2,96,512]{3,2,1,0:T(8,128)(2,1)S(1)}, bf16[2,2,96,512]{3,2,1,0:T(8,128)(2,1)S(1)}, u32[]{:S(2)}, u32[]{:S(2)}) collective-permute-start(bf16[2,2,96,512]{3,2,1,0:T(8,128)(2,1)S(1)} %pad_maximum_fusion.3), channel_id=1, source_target_pairs={{0,64},{1,65},{2,66},{3,67},{4,68},{5,69},{6,70},{7,71},{8,72},{9,... | collective-permute-start | bytes 1179656 | tf_op jit(solution)/shard_map/ppermute | solution.py:42
  51.3 24.7 %collective-permute-start.10 = (bf16[2,2,96,512]{3,2,1,0:T(8,128)(2,1)S(1)}, bf16[2,2,96,512]{3,2,1,0:T(8,128)(2,1)S(1)}, u32[]{:S(2)}, u32[]{:S(2)}) collective-permute-start(bf16[2,2,96,512]{3,2,1,0:T(8,128)(2,1)S(1)} %pad_maximum_fusion.3), channel_id=1, source_target_pairs={{0,128},{1,129},{2,130},{3,131},{4,132},{5,133},{6,134},{7,135},{8... | collective-permute-start | bytes 1179656 | tf_op jit(solution)/shard_map/ppermute | solution.py:42
  58.2 19.7 %collective-permute-start.11 = (bf16[2,2,96,512]{3,2,1,0:T(8,128)(2,1)S(1)}, bf16[2,2,96,512]{3,2,1,0:T(8,128)(2,1)S(1)}, u32[]{:S(2)}, u32[]{:S(2)}) collective-permute-start(bf16[2,2,96,512]{3,2,1,0:T(8,128)(2,1)S(1)} %pad_maximum_fusion.3), channel_id=1, source_target_pairs={{0,192},{1,193},{2,194},{3,195},{4,196},{5,197},{6,198},{7,199},{8... | collective-permute-start | bytes 1179656 | tf_op jit(solution)/shard_map/ppermute | solution.py:42
  65.7 12.5 %collective-permute-start.13 = (s16[400,512]{1,0:T(8,128)(2,1)S(1)}, s16[400,512]{1,0:T(8,128)(2,1)S(1)}, u32[]{:S(2)}, u32[]{:S(2)}) collective-permute-start(s16[400,512]{1,0:T(8,128)(2,1)S(1)} %get-tuple-element.44), channel_id=1, source_target_pairs={{0,1},{1,0},{2,3},{3,2},{4,5},{5,4},{6,7},{7,6},{8,9},{9,8},{10,11... | collective-permute-start | bytes 1228808 | tf_op jit(solution)/shard_map/ppermute | solution.py:42
  65.8 12.5 %collective-permute-start.14 = (s16[400,512]{1,0:T(8,128)(2,1)S(1)}, s16[400,512]{1,0:T(8,128)(2,1)S(1)}, u32[]{:S(2)}, u32[]{:S(2)}) collective-permute-start(s16[400,512]{1,0:T(8,128)(2,1)S(1)} %get-tuple-element.45), channel_id=1, source_target_pairs={{0,3},{1,2},{2,1},{3,0},{4,7},{5,6},{6,5},{7,4},{8,11},{9,10},{10,... | collective-permute-start | bytes 1228808 | tf_op jit(solution)/shard_map/ppermute | solution.py:42
  78.2 4.5 %collective-permute-start.15 = (bf16[4,2,2,96,512]{4,3,2,1,0:T(8,128)(2,1)S(1)}, bf16[4,2,2,96,512]{4,3,2,1,0:T(8,128)(2,1)S(1)}, u32[]{:S(2)}, u32[]{:S(2)}) collective-permute-start(bf16[4,2,2,96,512]{4,3,2,1,0:T(8,128)(2,1)S(1)} %pad_maximum_fusion.own_ref), channel_id=1, source_target_pairs={{0,16},{1,17},{2,18},{3,19},{4,20},{5,21},{6,22},{7,23},{8,24},{9,... | collective-permute-start | bytes 4718600 | tf_op jit(solution)/shard_map/ppermute | solution.py:42
  79.7 13.2 %collective-permute-start.16 = (s16[400,512]{1,0:T(8,128)(2,1)S(1)}, s16[400,512]{1,0:T(8,128)(2,1)S(1)}, u32[]{:S(2)}, u32[]{:S(2)}) collective-permute-start(s16[400,512]{1,0:T(8,128)(2,1)S(1)} %get-tuple-element.55), channel_id=1, source_target_pairs={{0,2},{1,3},{2,0},{3,1},{4,6},{5,7},{6,4},{7,5},{8,10},{9,11},{10,... | collective-permute-start | bytes 1228808 | tf_op jit(solution)/shard_map/ppermute | solution.py:42
  92.9 28.2 %collective-permute-start.17 = (s16[2,400,512]{2,1,0:T(8,128)(2,1)S(1)}, s16[2,400,512]{2,1,0:T(8,128)(2,1)S(1)}, u32[]{:S(2)}, u32[]{:S(2)}) collective-permute-start(s16[2,400,512]{2,1,0:T(8,128)(2,1)S(1)} %get-tuple-element.56), channel_id=1, source_target_pairs={{0,1},{1,0},{2,3},{3,2},{4,5},{5,4},{6,7},{7,6},{8,9},{9,8},{10,11... | collective-permute-start | bytes 2457608 | tf_op jit(solution)/shard_map/ppermute | solution.py:42
  93.0 38.4 %collective-permute-start.18 = (s16[2,400,512]{2,1,0:T(8,128)(2,1)S(1)}, s16[2,400,512]{2,1,0:T(8,128)(2,1)S(1)}, u32[]{:S(2)}, u32[]{:S(2)}) collective-permute-start(s16[2,400,512]{2,1,0:T(8,128)(2,1)S(1)} %get-tuple-element.57), channel_id=1, source_target_pairs={{0,2},{1,3},{2,0},{3,1},{4,6},{5,7},{6,4},{7,5},{8,10},{9,11},{10,... | collective-permute-start | bytes 2457608 | tf_op jit(solution)/shard_map/ppermute | solution.py:42
  95.8 37.6 %collective-permute-start.19 = (s16[2,400,512]{2,1,0:T(8,128)(2,1)S(1)}, s16[2,400,512]{2,1,0:T(8,128)(2,1)S(1)}, u32[]{:S(2)}, u32[]{:S(2)}) collective-permute-start(s16[2,400,512]{2,1,0:T(8,128)(2,1)S(1)} %pad_add_fusion.2), channel_id=1, source_target_pairs={{0,3},{1,2},{2,1},{3,0},{4,7},{5,6},{6,5},{7,4},{8,11},{9,10},{10,... | collective-permute-start | bytes 2457608 | tf_op jit(solution)/shard_map/ppermute | solution.py:42
  96.8 13.8 %collective-permute-start.20 = (bf16[3,96,512]{2,1,0:T(8,128)(2,1)S(1)}, bf16[3,96,512]{2,1,0:T(8,128)(2,1)S(1)}, u32[]{:S(2)}, u32[]{:S(2)}) collective-permute-start(bf16[3,96,512]{2,1,0:T(8,128)(2,1)S(1)} %bitcast_multiply_fusion.refs_5_.refs_9_), channel_id=1, source_target_pairs={{0,4},{1,5},{2,6},{3,7},{4,0},{5,1},{6,2},{7,3},{8,12},{9,13},{10,... | collective-permute-start | bytes 884744 | tf_op jit(solution)/shard_map/ppermute | solution.py:42
  97.3 13.9 %collective-permute-start.21 = (bf16[3,96,512]{2,1,0:T(8,128)(2,1)S(1)}, bf16[3,96,512]{2,1,0:T(8,128)(2,1)S(1)}, u32[]{:S(2)}, u32[]{:S(2)}) collective-permute-start(bf16[3,96,512]{2,1,0:T(8,128)(2,1)S(1)} %bitcast_multiply_fusion.refs_5_.refs_9_), channel_id=1, source_target_pairs={{0,8},{1,9},{2,10},{3,11},{4,12},{5,13},{6,14},{7,15},{8,0},{9,1},... | collective-permute-start | bytes 884744 | tf_op jit(solution)/shard_map/ppermute | solution.py:42
  110.6 8.4 %collective-permute-start.22 = (bf16[3,96,512]{2,1,0:T(8,128)(2,1)S(1)}, bf16[3,96,512]{2,1,0:T(8,128)(2,1)S(1)}, u32[]{:S(2)}, u32[]{:S(2)}) collective-permute-start(bf16[3,96,512]{2,1,0:T(8,128)(2,1)S(1)} %bitcast_multiply_fusion.refs_5_.refs_9_), channel_id=1, source_target_pairs={{0,12},{1,13},{2,14},{3,15},{4,8},{5,9},{6,10},{7,11},{8,4},{9,5},... | collective-permute-start | bytes 884744 | tf_op jit(solution)/shard_map/ppermute | solution.py:42
  136.6 5.0 %collective-permute-start.26 = (f32[512,512]{1,0:T(8,128)S(1)}, f32[512,512]{1,0:T(8,128)S(1)}, u32[]{:S(2)}, u32[]{:S(2)}) collective-permute-start(f32[512,512]{1,0:T(8,128)S(1)} %get-tuple-element.74), channel_id=1, source_target_pairs={{0,16},{1,17},{2,18},{3,19},{4,20},{5,21},{6,22},{7,23},{8,24},{9,... | collective-permute-start | bytes 3145736 | tf_op jit(solution)/shard_map/ppermute | solution.py:42
  138.6 3.0 %collective-permute-start.27 = (f32[256,512]{1,0:T(8,128)S(1)}, f32[256,512]{1,0:T(8,128)S(1)}, u32[]{:S(2)}, u32[]{:S(2)}) collective-permute-start(f32[256,512]{1,0:T(8,128)S(1)} %get-tuple-element.75), channel_id=1, source_target_pairs={{0,16},{1,17},{2,18},{3,19},{4,20},{5,21},{6,22},{7,23},{8,24},{9,... | collective-permute-start | bytes 1572872 | tf_op jit(solution)/shard_map/ppermute | solution.py:42
  142.9 26.3 %all-to-all-start = ((f32[16,48,512]{2,1,0:T(8,128)}), f32[16,48,512]{2,1,0:T(8,128)S(1)}, u32[]{:S(2)}, u32[]{:S(2)}) async-start(f32[16,48,512]{2,1,0:T(8,128)} %bitcast.35), calls=%async_computation | async-start | bytes 3145728 | tf_op jit(solution)/shard_map/all_to_all | solution.py:344
  147.8 43.1 %collective-permute-start.25 = (s16[336,512]{1,0:T(8,128)(2,1)}, s16[336,512]{1,0:T(8,128)(2,1)S(1)}, u32[]{:S(2)}, u32[]{:S(2)}) collective-permute-start(s16[336,512]{1,0:T(8,128)(2,1)} %pad_add_fusion.5), channel_id=1, source_target_pairs={{0,12},{1,13},{2,14},{3,15},{4,8},{5,9},{6,10},{7,11},{8,4},{9,5},... | collective-permute-start | bytes 1032200 | tf_op jit(solution)/shard_map/ppermute | solution.py:42
  151.6 39.3 %collective-permute-start.24 = (s16[336,512]{1,0:T(8,128)(2,1)}, s16[336,512]{1,0:T(8,128)(2,1)S(1)}, u32[]{:S(2)}, u32[]{:S(2)}) collective-permute-start(s16[336,512]{1,0:T(8,128)(2,1)} %pad_add_fusion.4), channel_id=1, source_target_pairs={{0,8},{1,9},{2,10},{3,11},{4,12},{5,13},{6,14},{7,15},{8,0},{9,1},... | collective-permute-start | bytes 1032200 | tf_op jit(solution)/shard_map/ppermute | solution.py:42
  152.3 38.5 %collective-permute-start.23 = (s16[336,512]{1,0:T(8,128)(2,1)}, s16[336,512]{1,0:T(8,128)(2,1)S(1)}, u32[]{:S(2)}, u32[]{:S(2)}) collective-permute-start(s16[336,512]{1,0:T(8,128)(2,1)} %pad_add_fusion.3), channel_id=1, source_target_pairs={{0,4},{1,5},{2,6},{3,7},{4,0},{5,1},{6,2},{7,3},{8,12},{9,13},{10,... | collective-permute-start | bytes 1032200 | tf_op jit(solution)/shard_map/ppermute | solution.py:42
  169.3 7.9 %collective-permute-start.28 = (f32[48,512]{1,0:T(8,128)S(1)}, f32[48,512]{1,0:T(8,128)S(1)}, u32[]{:S(2)}, u32[]{:S(2)}) collective-permute-start(f32[48,512]{1,0:T(8,128)S(1)} %reduce_sum.9), channel_id=1, source_target_pairs={{0,32},{1,33},{2,34},{3,35},{4,36},{5,37},{6,38},{7,39},{8,40},{9,... | collective-permute-start | bytes 294920 | tf_op jit(solution)/shard_map/ppermute | solution.py:42
  177.2 13.4 %collective-permute-start.29 = (f32[48,512]{1,0:T(8,128)S(1)}, f32[48,512]{1,0:T(8,128)S(1)}, u32[]{:S(2)}, u32[]{:S(2)}) collective-permute-start(f32[48,512]{1,0:T(8,128)S(1)} %add.51), channel_id=1, source_target_pairs={{0,4},{1,5},{2,6},{3,7},{4,0},{5,1},{6,2},{7,3},{8,12},{9,13},{10,... | collective-permute-start | bytes 294920 | tf_op jit(solution)/shard_map/ppermute | solution.py:42
  190.6 5.8 %collective-permute-start.30 = (f32[48,512]{1,0:T(8,128)S(1)}, f32[48,512]{1,0:T(8,128)S(1)}, u32[]{:S(2)}, u32[]{:S(2)}) collective-permute-start(f32[48,512]{1,0:T(8,128)S(1)} %add.52), channel_id=1, source_target_pairs={{0,8},{1,9},{2,10},{3,11},{4,12},{5,13},{6,14},{7,15},{8,0},{9,1},... | collective-permute-start | bytes 294920 | tf_op jit(solution)/shard_map/ppermute | solution.py:42
  223.5 5.0 %collective-permute-start.31 = (f32[768,512]{1,0:T(8,128)S(1)}, f32[768,512]{1,0:T(8,128)S(1)}, u32[]{:S(2)}, u32[]{:S(2)}) collective-permute-start(f32[768,512]{1,0:T(8,128)S(1)} %bitcast.47), channel_id=1, source_target_pairs={{0,16},{1,17},{2,18},{3,19},{4,20},{5,21},{6,22},{7,23},{8,24},{9,... | collective-permute-start | bytes 4718600 | tf_op jit(solution)/shard_map/ppermute | solution.py:42
  (3 other events, 34.9 us)

commit v3 on v2

v3 whole, which is shorter than its diff:
```python
import functools

import jax
import jax.numpy as jnp
from jax import lax
from jax.experimental import pallas as pl
from jax.experimental.pallas import tpu as pltpu
from jax.sharding import Mesh
from jax.sharding import PartitionSpec as P

TILE = 128
AXES = ("x", "h", "core", "l", "y")
SIZES = (4, 2, 2, 4, 4)
ROW = ("x", "h", "core")
COL = ("l", "y")
EXTRA = 16
STEPS = 64.0
TOP = 32766.0
LN2 = 0.6931471805599453
VMEM = pl.BlockSpec(memory_space=pltpu.VMEM)
SMEM = pl.BlockSpec(memory_space=pltpu.SMEM)
F32, BF16, I16, I32 = jnp.float32, jnp.bfloat16, jnp.int16, jnp.int32


def coords(device):
    out = []
    for size in SIZES[::-1]:
        out.append(device % size)
        device //= size
    return tuple(out[::-1])


def number(place):
    value = 0
    for size, at in zip(SIZES, place):
        value = value * size + at
    return value


def send(value, move):
    pairs = [(d, number(move(*coords(d)))) for d in range(256)]
    return lax.ppermute(value, AXES, pairs)


def over_x(k):
    return lambda x, h, c, l, y: (x ^ k, h, c, l, y)


def over_y(k):
    return lambda x, h, c, l, y: (x, h, c, l, y ^ k)


def over_l(k):
    return lambda x, h, c, l, y: (x, h, c, l ^ k, y)


def over_h(x, h, c, l, y):
    return (x, 1 - h, c, l, y)


def over_core(x, h, c, l, y):
    return (x, h, 1 - c, l, y)


def spread(x, h, c, l, y):
    return (x ^ l, h, c, l, y)


def turn(i):
    return lambda x, h, c, l, y: (x, (y & 1) ^ i, y >> 1, x ^ l, 2 * h + c)


def params(limit=16):
    return pltpu.CompilerParams(vmem_limit_bytes=limit * 1024 * 1024)


def cost(flops, moved):
    return pl.CostEstimate(flops=flops // 1000, bytes_accessed=moved // 1000, transcendentals=0)


def diagonal_mask(rows, width):
    row = lax.broadcasted_iota(I32, (rows, width), 0)
    lane = lax.broadcasted_iota(I32, (rows, width), 1)
    return row == lane


def encode(value, out_ref, start=0):
    rows, width = value.shape
    largest = jnp.maximum(jnp.max(jnp.abs(value), axis=1, keepdims=True), 1e-30)
    level = jnp.ceil(jnp.log(largest * (1.0 / TOP)) * (STEPS / LN2))
    coded = jnp.round(value * jnp.exp2(level * (-1.0 / STEPS)))
    out_ref[start : start + rows, :] = coded.astype(I32).astype(I16)
    line = jnp.sum(jnp.where(diagonal_mask(rows, width), level, 0.0), axis=0, keepdims=True)
    lines = jnp.broadcast_to(line, (EXTRA, width))
    out_ref[start + rows : start + rows + EXTRA, :] = lines.astype(I32).astype(I16)


def decode(in_ref, start=0, rows=None):
    rows, width = rows or in_ref.shape[0] - EXTRA, in_ref.shape[1]
    coded = in_ref[start : start + rows, :].astype(I32).astype(F32)
    line = in_ref[start + rows : start + rows + EXTRA, :].astype(I32).astype(F32)[:1]
    level = jnp.sum(
        jnp.where(diagonal_mask(rows, width), jnp.broadcast_to(line, (rows, width)), 0.0),
        axis=1,
        keepdims=True,
    )
    return coded * jnp.exp2(level * (1.0 / STEPS))


def product_kernel(at_ref, a_ref, own_ref, other_ref, keep_ref, q_ref, m_ref):
    step = pl.program_id(0)
    shard = own_ref.shape[3]

    @pl.when(step == 0)
    def _():
        core, h, t = at_ref[1], at_ref[2], at_ref[3]
        for k in range(4):
            for i in range(2):
                base = (k ^ t) * (4 * shard) + (i ^ h) * shard
                first = pl.multiple_of(base + core * (2 * shard), 32)
                second = pl.multiple_of(base + (1 - core) * (2 * shard), 32)
                m_ref[pl.ds(first, shard), :] = own_ref[k, i, 0]
                m_ref[pl.ds(second, shard), :] = other_ref[k, i, 0]

    block = a_ref[...]
    lines = block.reshape(4 * block.shape[2], block.shape[3])
    value = jnp.dot(lines, m_ref[...], preferred_element_type=F32)
    encode(value, q_ref.at[at_ref[0] ^ ((step + 1) & 3)])

    @pl.when(step == 3)
    def _():
        keep_ref[...] = value


def product(at, a4, own, other, first=0):
    shard, order = a4.shape[2], a4.shape[3]
    width = own.shape[4]
    rows = 4 * shard
    whole = pl.BlockSpec((4, 2, 1, shard, width), lambda g, s: (0, 0, first, 0, 0))
    return pl.pallas_call(
        product_kernel,
        grid_spec=pltpu.PrefetchScalarGridSpec(
            num_scalar_prefetch=1,
            grid=(4,),
            in_specs=[
                pl.BlockSpec(
                    (4, 1, shard, order), lambda g, s: (0, s[0] ^ ((g + 1) & 3), 0, 0)
                ),
                whole,
                whole,
            ],
            out_specs=[
                pl.BlockSpec((rows, width), lambda g, s: (0, 0)),
                pl.BlockSpec((4, rows + EXTRA, width), lambda g, s: (0, 0, 0)),
            ],
            scratch_shapes=[pltpu.VMEM((order, width), BF16)],
        ),
        out_shape=[
            jax.ShapeDtypeStruct((rows, width), F32),
            jax.ShapeDtypeStruct((4, rows + EXTRA, width), I16),
        ],
        compiler_params=params(20),
        cost_estimate=cost(8 * rows * order * width, 2 * order * order),
        name="product",
    )(at, a4, own, other)


def middle_kernel(panels, which, *refs):
    at_ref, refs = refs[0], refs[1:]
    keeps, parts, refs = refs[:panels], refs[panels : 2 * panels], refs[2 * panels :]
    masked, refs = refs[:4], refs[4:]
    own_ref, *coded = refs[:4]
    mine_ref, theirs_ref, sum_ref, m_ref = refs[4:]
    shard = own_ref.shape[0] // panels
    half = mine_ref.shape[0] // panels
    y, core, l = at_ref[0], at_ref[1], at_ref[4]
    for p in range(panels):
        value = keeps[p][...]
        for k in (1, 2, 3):
            value = value + decode(parts[p].at[y ^ k])
        sum_ref[...] = value
        for k in range(4):
            place = pl.ds(pl.multiple_of((l ^ k) * shard, 32), shard)
            part = sum_ref[place, :]
            if k:
                encode(part, coded[k - 1], p * (shard + EXTRA))
            else:
                own_ref[p * shard : (p + 1) * shard, :] = part
            m_ref[place, :] = masked[k][which[p]]
        high = value.astype(BF16)
        rest = value - high.astype(F32)
        mid = rest.astype(BF16)
        low = (rest - mid.astype(F32)).astype(BF16)
        for side, out in ((core, mine_ref), (1 - core, theirs_ref)):
            left = m_ref[:, pl.ds(pl.multiple_of(side * half, 128), half)]
            dims = (((0,), (0,)), ((), ()))
            terms = [
                lax.dot_general(left, r, dims, preferred_element_type=F32) for r in (low, mid, high)
            ]
            out[p * half : (p + 1) * half, :] = (terms[0] + terms[1]) + terms[2]


def middle(at, keeps, parts, masked, which):
    rows, width = keeps[0].shape
    panels, shard = len(keeps), rows // 4
    return pl.pallas_call(
        functools.partial(middle_kernel, panels, which),
        in_specs=[SMEM] + [VMEM] * (2 * panels + 4),
        out_specs=[VMEM] * 6,
        out_shape=[jax.ShapeDtypeStruct((panels * shard, width), F32)]
        + [jax.ShapeDtypeStruct((panels * (shard + EXTRA), width), I16)] * 3
        + [jax.ShapeDtypeStruct((panels * (width // 2), width), F32)] * 2,
        scratch_shapes=[pltpu.VMEM((rows, width), F32), pltpu.VMEM((rows, width), BF16)],
        compiler_params=params(),
        cost_estimate=cost(6 * rows * width * width, 16 * rows * width),
        name="middle",
    )(at, *keeps, *parts, *masked)


def last_kernel(groups, *refs):
    out_ref = refs[-1]
    shard = out_ref.shape[1]
    for g, which in enumerate(groups):
        own_ref, *parts = refs[4 * g : 4 * g + 4]
        for p, panel in enumerate(which):
            total = own_ref[p * shard : (p + 1) * shard, :]
            for ref in parts:
                total = total + decode(ref, p * (shard + EXTRA), shard)
            out_ref[panel] = -total


def last(groups, shape):
    ins = [ref for own, parts, _ in groups for ref in (own, *parts)]
    return pl.pallas_call(
        functools.partial(last_kernel, [which for _, _, which in groups]),
        in_specs=[VMEM] * len(ins),
        out_specs=VMEM,
        out_shape=jax.ShapeDtypeStruct(shape, F32),
        compiler_params=params(),
        cost_estimate=cost(8 * shape[1] * shape[2], 16 * shape[1] * shape[2]),
        name="last",
    )(*ins)


def fold_kernel(*refs):
    out, count = refs[-1], len(refs) // 2
    start = 0
    for p in range(count):
        rows = refs[p].shape[0]
        out[start : start + rows, :] = refs[p][...] + refs[count + p][...]
        start += rows


def fold(mines, theirs):
    width = mines[0].shape[1]
    total = sum(mine.shape[0] for mine in mines)
    return pl.pallas_call(
        fold_kernel,
        in_specs=[VMEM] * (2 * len(mines)),
        out_specs=VMEM,
        out_shape=jax.ShapeDtypeStruct((total, width), F32),
        compiler_params=params(),
        cost_estimate=cost(total * width, 12 * total * width),
        name="fold",
    )(*mines, *theirs)


def finish_kernel(at_ref, mine_ref, theirs_ref, diag_ref, out_ref):
    half = diag_ref.shape[1] // 2
    core = at_ref[1]
    for at, p in enumerate((0, 2, 1)):
        for side, ref in ((core, mine_ref), (1 - core, theirs_ref)):
            place = pl.ds(pl.multiple_of(side * half, 8), half)
            out_ref[p, place, :] = diag_ref[p, place, :] + ref[at * half : (at + 1) * half, :]


def finish(at, mine, theirs, diag):
    return pl.pallas_call(
        finish_kernel,
        in_specs=[SMEM] + [VMEM] * 3,
        out_specs=VMEM,
        out_shape=jax.ShapeDtypeStruct(diag.shape, F32),
        compiler_params=params(),
        cost_estimate=cost(diag.size, 12 * diag.size),
        name="finish",
    )(at, mine, theirs, diag)


def after(values, *earlier):
    return lax.optimization_barrier((values, earlier))[0]


def body(ancestor_inverse, panels, diag_inverse, tile_mask):
    x, h, core, l, y = (lax.axis_index(axis) for axis in AXES)
    at = jnp.stack([y, core, h, x ^ l, l, x]).astype(I32)
    kept, count, width = panels.shape
    order = ancestor_inverse.shape[1]
    tiles = tile_mask.shape[1]
    start = (((x * 2 + h) * 2 + core) * 16 + l * 4 + y) * kept
    tile = start // TILE
    first = lax.dynamic_slice_in_dim(tile_mask, tile, 1, 1)
    second = lax.dynamic_slice_in_dim(tile_mask, jnp.minimum(tile + 1, tiles - 1), 1, 1)
    in_first = start + jnp.arange(kept) < (tile + 1) * TILE
    own_mask = jnp.where(in_first[None, :], first, second).astype(BF16)
    masked = jnp.swapaxes(panels, 0, 1) * own_mask[:, :, None]

    def gather(message):
        return [message] + [send(message, over_x(k)) for k in (1, 2, 3)]

    def exchange(value, axis):
        return lax.all_to_all(value, axis, 0, 0)

    a4 = ancestor_inverse.reshape(4, 4, kept, order)
    moved_a, moved_b = send(masked[2:], spread), send(masked[:2], spread)
    turned_a = [send(moved_a, turn(i)) for i in range(2)]
    turned_b = [send(moved_b, turn(i)) for i in range(2)]
    own_a = gather(after(jnp.stack(turned_a), moved_b))
    own_a = after(jnp.stack(own_a), turned_b)
    own_b = gather(after(jnp.stack(turned_b), own_a))
    late = after(masked, own_a)
    beside = [masked] + [send(late, over_l(k)) for k in (1, 2, 3)]
    keep_a, coded = product(at, a4, own_a, send(own_a, over_core))
    part_a = exchange(coded, "y")
    own_b = jnp.stack(after(own_b, keep_a, beside[2]))
    other_b = send(own_b, over_core)
    keep_b, coded = product(after(at, beside[1], beside[3]), a4, own_b, other_b, 0)
    part_b = exchange(coded, "y")
    keep_c, coded = product(at, a4, own_b, other_b, 1)
    part_c = exchange(coded, "y")
    own_ab, *coded = middle(at, [keep_b, keep_a], [part_b, part_a], beside, (0, 2))
    coded_ab, (mine_ab, their_ab) = coded[:3], coded[3:]
    swapped_ab = send(their_ab, over_core)
    found_ab = [send(coded_ab[k - 1], over_l(k)) for k in (1, 2, 3)]
    part_c = after(part_c, found_ab)
    own_c, *coded = middle(at, [keep_c], [part_c], beside, (1,))
    coded_c, (mine_c, their_c) = coded[:3], coded[3:]
    halves = fold([mine_ab, mine_c], [swapped_ab, send(their_c, over_core)])
    found_c = [send(coded_c[k - 1], over_l(k)) for k in (1, 2, 3)]
    total = jnp.sum(exchange(halves.reshape(16, -1, width), ("x", "y")), axis=0)
    found_c = after(found_c, total)
    total = total + send(total, over_h)
    total = total + send(total, over_l(1))
    total = total + send(total, over_l(2))
    blocks = last([(own_ab, found_ab, (0, 2)), (own_c, found_c, (1,))], masked.shape)
    pieces = jnp.broadcast_to(after(total, blocks)[None], (16, *total.shape))
    mine = exchange(pieces, ("x", "y")).reshape(halves.shape)
    diagonal = finish(at, mine, send(mine, over_core), diag_inverse)
    return jnp.swapaxes(blocks, 0, 1), diagonal


def solution(mesh):
    finer = Mesh(mesh.devices.reshape(SIZES), AXES)
    placed = (P(ROW, COL), P(AXES, None, None), P(), P())
    return jax.shard_map(
        body, mesh=finer, in_specs=placed, out_specs=(P(AXES, None, None), P()), check_vma=False
    )
```

time: 231 us -> 276 us (1.19)
  local copies, waits for them, and re-layouts: 3.77 us -> 30.4 us
  blocking collectives: 26.9 us -> 51.9 us
  starting transfers between devices: 86.3 us -> 78 us
    unnamed x4 -> x88, local copies, waits for them, and re-layouts: 2.35 us -> 29.1 us
    all_to_all x1 -> x2, blocking collectives: 26.9 us -> 51.9 us  [exchange(): return lax.all_to_all(value, axis, 0, 0)]
    ppermute x32 -> x29, starting transfers between devices: 82.2 us -> 66.3 us  [send(): return lax.ppermute(value, AXES, pairs)]
    all_to_all x1 -> x3, starting transfers between devices: 4.06 us -> 11.8 us  [exchange(): return lax.all_to_all(value, axis, 0, 0)]
    all_to_all x1 -> x3, waiting for transfers between devices: 16.4 us -> 12.3 us  [exchange(): return lax.all_to_all(value, axis, 0, 0)]
    pallas_call x5 -> x6, Pallas kernels: 21.1 us -> 24.7 us  [the longest x3 16.6 us: product(): pl.pallas_call(product_kernel, grid_spec=pltpu.PrefetchScalarGridSpec(num...]
    ppermute x32 -> x29, waiting for transfers between devices: 67.7 us -> 70.8 us  [send(): return lax.ppermute(value, AXES, pairs)]
  transfers between devices with their start and end apart: 33 -> 32, of which waited for: 17 -> 20; matrix products, arithmetic and copies ran while one was open for 1% -> 0% of each run, Pallas kernels for 8% -> 9%
where the time goes in v3:
time: 276 us; the launch traced here: 275 us
  waiting for transfers between devices  83.1 us (30%)
  starting transfers between devices  78 us (28%)
  blocking collectives  51.9 us (19%)
  local copies, waits for them, and re-layouts  30.4 us (11%)
  Pallas kernels  27.4 us (10%)
  other arithmetic  3.02 us (1%)
    ppermute x29, waiting for transfers between devices, send(): return lax.ppermute(value, AXES, pairs)  70.8 us
    ppermute x29, starting transfers between devices, send(): return lax.ppermute(value, AXES, pairs)  66.3 us
    all_to_all x2, blocking collectives, exchange(): return lax.all_to_all(value, axis, 0, 0)  51.9 us
    unnamed x88, local copies, waits for them, and re-layouts  29.1 us
    pallas_call x3, Pallas kernels, product(): pl.pallas_call(product_kernel, grid_spec=pltpu.PrefetchScalarGridSpec(num...  16.6 us
    all_to_all x3, waiting for transfers between devices, exchange(): return lax.all_to_all(value, axis, 0, 0)  12.3 us
    all_to_all x3, starting transfers between devices, exchange(): return lax.all_to_all(value, axis, 0, 0)  11.8 us
    pallas_call x2, Pallas kernels, middle(): pl.pallas_call(functools.partial(middle_kernel, panels, which), in_specs=...  6.9 us
  transfers between devices with their start and end apart: 32, of which 20 were waited for; matrix products, arithmetic and copies ran while one was open for 0% of the time, Pallas kernels for 9%

profile of v3, /device:TPU:1, one launch (start us, length us, event | category | flops | bytes accessed | tf_op | source)
XLA Modules:
  0.0 274.9 jit_solution(14375971428933260657)
XLA Ops:
  3.5 9.4 %collective-permute-start.2 = (bf16[1,96,512]{2,1,0:T(8,128)(2,1)S(1)}, bf16[1,96,512]{2,1,0:T(8,128)(2,1)S(1)}, u32[]{:S(2)}, u32[]{:S(2)}) collective-permute-start(bf16[1,96,512]{2,1,0:T(8,128)(2,1)S(1)} %collective-permute-done), channel_id=1, source_target_pairs={{0,32},{1,0},{2,48},{3,16},{4,36},{5,4},{6,52},{7,20},{8,40},{9,8}... | collective-permute-start | bytes 294920 | tf_op jit(solution)/shard_map/ppermute | solution.py:42
  15.6 4.8 %collective-permute-done.1 = bf16[1,96,512]{2,1,0:T(8,128)(2,1)S(1)} collective-permute-done((bf16[1,96,512]{2,1,0:T(8,128)(2,1)S(1)}, bf16[1,96,512]{2,1,0:T(8,128)(2,1)S(1)}, u32[]{:S(2)}, u32[]{:S(2)}) %collective-permute-start.1) | collective-permute-done | bytes 98336 | tf_op jit(solution)/shard_map/ppermute | solution.py:42
  20.4 11.0 %collective-permute-start.5 = (bf16[2,1,96,512]{3,2,0,1:T(8,128)(2,1)S(1)}, bf16[2,1,96,512]{3,2,0,1:T(8,128)(2,1)S(1)}, u32[]{:S(2)}, u32[]{:S(2)}) collective-permute-start(bf16[2,1,96,512]{3,2,0,1:T(8,128)(2,1)S(1)} %bitcast.36), channel_id=1, source_target_pairs={{0,128},{1,129},{2,130},{3,131},{4,132},{5,133},{6,134},{7,135},{8... | collective-permute-start | bytes 589832 | tf_op jit(solution)/shard_map/ppermute | solution.py:42
  36.7 2.8 %collective-permute-done.4 = bf16[2,1,96,512]{3,2,0,1:T(8,128)(2,1)S(1)} collective-permute-done((bf16[2,1,96,512]{3,2,0,1:T(8,128)(2,1)S(1)}, bf16[2,1,96,512]{3,2,0,1:T(8,128)(2,1)S(1)}, u32[]{:S(2)}, u32[]{:S(2)}) %collective-permute-start.4) | collective-permute-done | bytes 196640 | tf_op jit(solution)/shard_map/ppermute | solution.py:42
  39.8 6.8 %collective-permute-done.7 = bf16[2,96,512]{2,1,0:T(8,128)(2,1)S(1)} collective-permute-done((bf16[2,96,512]{2,1,0:T(8,128)(2,1)S(1)}, bf16[2,96,512]{2,1,0:T(8,128)(2,1)S(1)}, u32[]{:S(2)}, u32[]{:S(2)}) %collective-permute-start.7) | collective-permute-done | bytes 196640 | tf_op jit(solution)/shard_map/ppermute | solution.py:42
  46.7 9.6 %collective-permute-start.13 = (bf16[2,2,96,512]{3,2,1,0:T(8,128)(2,1)S(1)}, bf16[2,2,96,512]{3,2,1,0:T(8,128)(2,1)S(1)}, u32[]{:S(2)}, u32[]{:S(2)}) collective-permute-start(bf16[2,2,96,512]{3,2,1,0:T(8,128)(2,1)S(1)} %pad_maximum_fusion.2), channel_id=1, source_target_pairs={{0,192},{1,193},{2,194},{3,195},{4,196},{5,197},{6,198},{7,199},{8... | collective-permute-start | bytes 1179656 | tf_op jit(solution)/shard_map/ppermute | solution.py:42
  57.1 2.3 copy-done
  59.4 4.8 %product.3 = (f32[384,512]{1,0:T(8,128)S(1)}, s16[4,400,512]{2,1,0:T(8,128)(2,1)S(1)}) custom-call(s32[6]{0:T(128)S(1)} %stack.75.at_ref.refs_0_, bf16[4,4,96,1536]{3,2,1,0:T(8,128)(2,1)S(1)} %bitcast.27, bf16[4,2,1,96,512]{4,3,2,1,0:T(8,128)(2,1)S(1)} %bitcast.33, bf16[4,2,1,96,512]{4,3,2,1,0:T(8,128)(2,1)S(1)} %bitcast.34), custom_call_target="tpu_custom_call" | custom-call | flops 2415919 | bytes 4718 | tf_op jit(solution)/shard_map/product/pallas_call | solution.py:140
  64.2 6.3 %collective-permute-done.15.refs_7_.refs_5_ = bf16[3,96,512]{2,1,0:T(8,128)(2,1)S(1)} collective-permute-done((bf16[3,96,512]{2,1,0:T(8,128)(2,1)S(1)}, bf16[3,96,512]{2,1,0:T(8,128)(2,1)S(1)}, u32[]{:S(2)}, u32[]{:S(2)}) %collective-permute-start.15) | collective-permute-done | bytes 294944 | tf_op jit(solution)/shard_map/ppermute | solution.py:42
  70.6 3.2 %collective-permute-done.13 = bf16[2,2,96,512]{3,2,1,0:T(8,128)(2,1)S(1)} collective-permute-done((bf16[2,2,96,512]{3,2,1,0:T(8,128)(2,1)S(1)}, bf16[2,2,96,512]{3,2,1,0:T(8,128)(2,1)S(1)}, u32[]{:S(2)}, u32[]{:S(2)}) %collective-permute-start.13) | collective-permute-done | bytes 393248 | tf_op jit(solution)/shard_map/ppermute | solution.py:42
  77.3 3.6 %all-to-all-start.1 = ((s16[4,400,512]{2,1,0:T(8,128)(2,1)}), s16[4,400,512]{2,1,0:T(8,128)(2,1)S(1)}, u32[]{:S(2)}, u32[]{:S(2)}) async-start(s16[4,400,512]{2,1,0:T(8,128)(2,1)} %copy-done.7), calls=%async_computation.1 | async-start | bytes 3276800 | tf_op jit(solution)/shard_map/all_to_all | solution.py:311
  81.0 3.5 %collective-permute-start.10 = (bf16[3,96,512]{2,1,0:T(8,128)(2,1)S(1)}, bf16[3,96,512]{2,1,0:T(8,128)(2,1)S(1)}, u32[]{:S(2)}, u32[]{:S(2)}) collective-permute-start(bf16[3,96,512]{2,1,0:T(8,128)(2,1)S(1)} %bitcast_multiply_fusion.refs_5_.refs_3_), channel_id=1, source_target_pairs={{0,12},{1,13},{2,14},{3,15},{4,8},{5,9},{6,10},{7,11},{8,4},{9,5},... | collective-permute-start | bytes 884744 | tf_op jit(solution)/shard_map/ppermute | solution.py:42
  85.4 6.3 %collective-permute-done.10.refs_8_.refs_6_ = bf16[3,96,512]{2,1,0:T(8,128)(2,1)S(1)} collective-permute-done((bf16[3,96,512]{2,1,0:T(8,128)(2,1)S(1)}, bf16[3,96,512]{2,1,0:T(8,128)(2,1)S(1)}, u32[]{:S(2)}, u32[]{:S(2)}) %collective-permute-start.10) | collective-permute-done | bytes 294944 | tf_op jit(solution)/shard_map/ppermute | solution.py:42
  92.4 6.0 %collective-permute-done.9.refs_6_.refs_4_ = bf16[3,96,512]{2,1,0:T(8,128)(2,1)S(1)} collective-permute-done((bf16[3,96,512]{2,1,0:T(8,128)(2,1)S(1)}, bf16[3,96,512]{2,1,0:T(8,128)(2,1)S(1)}, u32[]{:S(2)}, u32[]{:S(2)}) %collective-permute-start.9) | collective-permute-done | bytes 294944 | tf_op jit(solution)/shard_map/ppermute | solution.py:42
  101.4 5.9 %product.4 = (f32[384,512]{1,0:T(8,128)S(1)}, s16[4,400,512]{2,1,0:T(8,128)(2,1)S(1)}) custom-call(s32[6]{0:T(128)S(1)} %stack.75.at_ref.refs_0_, bf16[4,4,96,1536]{3,2,1,0:T(8,128)(2,1)S(1)} %bitcast.28, bf16[4,2,2,96,512]{4,3,2,1,0:T(8,128)(2,1)S(1)} %pad_maximum_fusion.own_ref, bf16[4,2,2,96,512]{4,3,2,1,0:T(8,128)(2,1)} %collective-permute-done.16.other_ref), custom_call_target="tpu_custom_call" | custom-call | flops 2415919 | bytes 4718 | tf_op jit(solution)/shard_map/product/pallas_call | solution.py:140
  109.4 4.4 %all-to-all-start = ((s16[4,400,512]{2,1,0:T(8,128)(2,1)}), s16[4,400,512]{2,1,0:T(8,128)(2,1)}, u32[]{:S(2)}, u32[]{:S(2)}) async-start(s16[4,400,512]{2,1,0:T(8,128)(2,1)} %copy-done.9), calls=%async_computation | async-start | bytes 3276800 | tf_op jit(solution)/shard_map/all_to_all | solution.py:311
  116.1 5.9 %product.5 = (f32[384,512]{1,0:T(8,128)S(1)}, s16[4,400,512]{2,1,0:T(8,128)(2,1)S(1)}) custom-call(s32[6]{0:T(128)S(1)} %stack.75.at_ref.refs_0_, bf16[4,4,96,1536]{3,2,1,0:T(8,128)(2,1)S(1)} %bitcast.29, bf16[4,2,2,96,512]{4,3,2,1,0:T(8,128)(2,1)S(1)} %pad_maximum_fusion.own_ref, bf16[4,2,2,96,512]{4,3,2,1,0:T(8,128)(2,1)} %collective-permute-done.16.other_ref), custom_call_target="tpu_custom_call" | custom-call | flops 2415919 | bytes 4718 | tf_op jit(solution)/shard_map/product/pallas_call | solution.py:140
  124.1 10.6 %all-to-all-done.refs_3_ = s16[4,400,512]{2,1,0:T(8,128)(2,1)} async-done(((s16[4,400,512]{2,1,0:T(8,128)(2,1)}), s16[4,400,512]{2,1,0:T(8,128)(2,1)}, u32[]{:S(2)}, u32[]{:S(2)}) %all-to-all-start) | async-done | bytes 1638432 | tf_op jit(solution)/shard_map/all_to_all | solution.py:311
  134.7 3.7 %all-to-all-start.2 = ((s16[4,400,512]{2,1,0:T(8,128)(2,1)}), s16[4,400,512]{2,1,0:T(8,128)(2,1)S(1)}, u32[]{:S(2)}, u32[]{:S(2)}) async-start(s16[4,400,512]{2,1,0:T(8,128)(2,1)} %copy-done.8), calls=%async_computation.2 | async-start | bytes 3276800 | tf_op jit(solution)/shard_map/all_to_all | solution.py:311
  144.6 4.9 %middle.2 = (f32[192,512]{1,0:T(8,128)S(1)}, s16[224,512]{1,0:T(8,128)(2,1)}, s16[224,512]{1,0:T(8,128)(2,1)}, s16[224,512]{1,0:T(8,128)(2,1)}, f32[512,512]{1,0:T(8,128)S(1)}, /*index=5*/f32[512,512]{1,0:T(8,128)}) custom-call(s32[6]{0:T(128)S(1)} %stack.75.at_ref.refs_0_, f32[384,512]{1,0:T(8,128)S(1)} %copy-done.24, f32[384,512]{1,0:T(8,128)S(1)} %copy-done.22, ...), custom_call_target="tpu_custom_call" | custom-call | flops 603979 | bytes 3145 | tf_op jit(solution)/shard_map/middle/pallas_call | solution.py:206
  158.2 6.8 %collective-permute-done.17.refs_1_ = s16[224,512]{1,0:T(8,128)(2,1)S(1)} collective-permute-done((s16[224,512]{1,0:T(8,128)(2,1)}, s16[224,512]{1,0:T(8,128)(2,1)S(1)}, u32[]{:S(2)}, u32[]{:S(2)}) %collective-permute-start.17) | collective-permute-done | bytes 229408 | tf_op jit(solution)/shard_map/ppermute | solution.py:42
  165.7 6.6 %collective-permute-done.19.refs_3_ = s16[224,512]{1,0:T(8,128)(2,1)S(1)} collective-permute-done((s16[224,512]{1,0:T(8,128)(2,1)}, s16[224,512]{1,0:T(8,128)(2,1)S(1)}, u32[]{:S(2)}, u32[]{:S(2)}) %collective-permute-start.19) | collective-permute-done | bytes 229408 | tf_op jit(solution)/shard_map/ppermute | solution.py:42
  185.5 27.3 %all_to_all.25 = f32[16,48,512]{2,1,0:T(8,128)S(1)} all-to-all(f32[16,48,512]{2,1,0:T(8,128)S(1)} %bitcast.32), channel_id=1, replica_groups=mesh['x'=4,'h'=2,'core'=2,'l'=4,'y'=4] {'x','y'}, dimensions={0} | all-to-all | bytes 3145728 | tf_op jit(solution)/shard_map/all_to_all | solution.py:311
  212.9 2.4 collective-permute-start.25
  215.3 5.1 %collective-permute-done.25 = f32[48,512]{1,0:T(8,128)S(1)} collective-permute-done((f32[48,512]{1,0:T(8,128)S(1)}, f32[48,512]{1,0:T(8,128)S(1)}, u32[]{:S(2)}, u32[]{:S(2)}) %collective-permute-start.25) | collective-permute-done | bytes 98336 | tf_op jit(solution)/shard_map/ppermute | solution.py:42
  220.4 4.9 %collective-permute-start.26 = (f32[48,512]{1,0:T(8,128)S(1)}, f32[48,512]{1,0:T(8,128)S(1)}, u32[]{:S(2)}, u32[]{:S(2)}) collective-permute-start(f32[48,512]{1,0:T(8,128)S(1)} %add.51), channel_id=1, source_target_pairs={{0,4},{1,5},{2,6},{3,7},{4,0},{5,1},{6,2},{7,3},{8,12},{9,13},{10,... | collective-permute-start | bytes 294920 | tf_op jit(solution)/shard_map/ppermute | solution.py:42
  230.8 3.5 %collective-permute-done.22.refs_7_ = s16[112,512]{1,0:T(8,128)(2,1)S(1)} collective-permute-done((s16[112,512]{1,0:T(8,128)(2,1)S(1)}, s16[112,512]{1,0:T(8,128)(2,1)S(1)}, u32[]{:S(2)}, u32[]{:S(2)}) %collective-permute-start.22) | collective-permute-done | bytes 114720 | tf_op jit(solution)/shard_map/ppermute | solution.py:42
  235.5 5.5 %collective-permute-done.27 = f32[48,512]{1,0:T(8,128)S(1)} collective-permute-done((f32[48,512]{1,0:T(8,128)S(1)}, f32[48,512]{1,0:T(8,128)S(1)}, u32[]{:S(2)}, u32[]{:S(2)}) %collective-permute-start.27) | collective-permute-done | bytes 98336 | tf_op jit(solution)/shard_map/ppermute | solution.py:42
  241.2 24.6 %all_to_all.26 = f32[16,48,512]{2,1,0:T(8,128)S(1)} all-to-all(f32[16,48,512]{2,1,0:T(8,128)S(1)} %broadcast_in_dim.35), channel_id=1, replica_groups=mesh['x'=4,'h'=2,'core'=2,'l'=4,'y'=4] {'x','y'}, dimensions={0} | all-to-all | bytes 3145728 | tf_op jit(solution)/shard_map/all_to_all | solution.py:311
  265.8 3.5 %collective-permute-start.28 = (f32[768,512]{1,0:T(8,128)S(1)}, f32[768,512]{1,0:T(8,128)S(1)}, u32[]{:S(2)}, u32[]{:S(2)}) collective-permute-start(f32[768,512]{1,0:T(8,128)S(1)} %bitcast.30), channel_id=1, source_target_pairs={{0,16},{1,17},{2,18},{3,19},{4,20},{5,21},{6,22},{7,23},{8,24},{9,... | collective-permute-start | bytes 4718600 | tf_op jit(solution)/shard_map/ppermute | solution.py:42
  269.3 3.0 %collective-permute-done.28.theirs_ref = f32[768,512]{1,0:T(8,128)S(1)} collective-permute-done((f32[768,512]{1,0:T(8,128)S(1)}, f32[768,512]{1,0:T(8,128)S(1)}, u32[]{:S(2)}, u32[]{:S(2)}) %collective-permute-start.28) | collective-permute-done | bytes 1572896 | tf_op jit(solution)/shard_map/ppermute | solution.py:42
  272.4 2.6 finish.1
  (146 shorter events, 62.0 us)
Async XLA Ops:
  2.9 0.7 collective-permute-start
  3.5 12.0 %collective-permute-start.2 = (bf16[1,96,512]{2,1,0:T(8,128)(2,1)S(1)}, bf16[1,96,512]{2,1,0:T(8,128)(2,1)S(1)}, u32[]{:S(2)}, u32[]{:S(2)}) collective-permute-start(bf16[1,96,512]{2,1,0:T(8,128)(2,1)S(1)} %collective-permute-done), channel_id=1, source_target_pairs={{0,32},{1,0},{2,48},{3,16},{4,36},{5,4},{6,52},{7,20},{8,40},{9,8}... | collective-permute-start | bytes 294920 | tf_op jit(solution)/shard_map/ppermute | solution.py:42
  12.9 7.4 %collective-permute-start.1 = (bf16[1,96,512]{2,1,0:T(8,128)(2,1)S(1)}, bf16[1,96,512]{2,1,0:T(8,128)(2,1)S(1)}, u32[]{:S(2)}, u32[]{:S(2)}) collective-permute-start(bf16[1,96,512]{2,1,0:T(8,128)(2,1)S(1)} %collective-permute-done), channel_id=1, source_target_pairs={{0,0},{1,32},{2,16},{3,48},{4,4},{5,36},{6,20},{7,52},{8,8},{9,40}... | collective-permute-start | bytes 294920 | tf_op jit(solution)/shard_map/ppermute | solution.py:42
  14.9 5.5 %collective-permute-start.3 = (bf16[2,96,512]{2,1,0:T(8,128)(2,1)S(1)}, bf16[2,96,512]{2,1,0:T(8,128)(2,1)S(1)}, u32[]{:S(2)}, u32[]{:S(2)}) collective-permute-start(bf16[2,96,512]{2,1,0:T(8,128)(2,1)S(1)} %slice.9), channel_id=1, source_target_pairs={{0,0},{1,1},{2,2},{3,3},{4,68},{5,69},{6,70},{7,71},{8,136},{9,137... | collective-permute-start | bytes 589832 | tf_op jit(solution)/shard_map/ppermute | solution.py:42
  20.4 16.3 %collective-permute-start.5 = (bf16[2,1,96,512]{3,2,0,1:T(8,128)(2,1)S(1)}, bf16[2,1,96,512]{3,2,0,1:T(8,128)(2,1)S(1)}, u32[]{:S(2)}, u32[]{:S(2)}) collective-permute-start(bf16[2,1,96,512]{3,2,0,1:T(8,128)(2,1)S(1)} %bitcast.36), channel_id=1, source_target_pairs={{0,128},{1,129},{2,130},{3,131},{4,132},{5,133},{6,134},{7,135},{8... | collective-permute-start | bytes 589832 | tf_op jit(solution)/shard_map/ppermute | solution.py:42
  31.4 8.1 %collective-permute-start.4 = (bf16[2,1,96,512]{3,2,0,1:T(8,128)(2,1)S(1)}, bf16[2,1,96,512]{3,2,0,1:T(8,128)(2,1)S(1)}, u32[]{:S(2)}, u32[]{:S(2)}) collective-permute-start(bf16[2,1,96,512]{3,2,0,1:T(8,128)(2,1)S(1)} %bitcast.37), channel_id=1, source_target_pairs={{0,64},{1,65},{2,66},{3,67},{4,68},{5,69},{6,70},{7,71},{8,72},{9,... | collective-permute-start | bytes 589832 | tf_op jit(solution)/shard_map/ppermute | solution.py:42
  32.4 7.3 %collective-permute-start.6 = (bf16[2,1,96,512]{3,2,1,0:T(8,128)(2,1)S(1)}, bf16[2,1,96,512]{3,2,1,0:T(8,128)(2,1)S(1)}, u32[]{:S(2)}, u32[]{:S(2)}) collective-permute-start(bf16[2,1,96,512]{3,2,1,0:T(8,128)(2,1)S(1)} %pad_maximum_fusion.3), channel_id=1, source_target_pairs={{0,192},{1,193},{2,194},{3,195},{4,196},{5,197},{6,198},{7,199},{8... | collective-permute-start | bytes 589832 | tf_op jit(solution)/shard_map/ppermute | solution.py:42
  32.4 7.4 %collective-permute-start.8 = (bf16[2,96,512]{2,1,0:T(8,128)(2,1)S(1)}, bf16[2,96,512]{2,1,0:T(8,128)(2,1)S(1)}, u32[]{:S(2)}, u32[]{:S(2)}) collective-permute-start(bf16[2,96,512]{2,1,0:T(8,128)(2,1)S(1)} %collective-permute-done.3), channel_id=1, source_target_pairs={{0,32},{1,0},{2,48},{3,16},{4,36},{5,4},{6,52},{7,20},{8,40},{9,8}... | collective-permute-start | bytes 589832 | tf_op jit(solution)/shard_map/ppermute | solution.py:42
  34.2 12.4 %collective-permute-start.7 = (bf16[2,96,512]{2,1,0:T(8,128)(2,1)S(1)}, bf16[2,96,512]{2,1,0:T(8,128)(2,1)S(1)}, u32[]{:S(2)}, u32[]{:S(2)}) collective-permute-start(bf16[2,96,512]{2,1,0:T(8,128)(2,1)S(1)} %collective-permute-done.3), channel_id=1, source_target_pairs={{0,0},{1,32},{2,16},{3,48},{4,4},{5,36},{6,20},{7,52},{8,8},{9,40}... | collective-permute-start | bytes 589832 | tf_op jit(solution)/shard_map/ppermute | solution.py:42
  46.6 10.4 %collective-permute-start.14 = (bf16[4,2,1,96,512]{4,3,1,2,0:T(8,128)(2,1)S(1)}, bf16[4,2,1,96,512]{4,3,1,2,0:T(8,128)(2,1)S(1)}, u32[]{:S(2)}, u32[]{:S(2)}) collective-permute-start(bf16[4,2,1,96,512]{4,3,1,2,0:T(8,128)(2,1)S(1)} %pad_maximum_fusion.1), channel_id=1, source_target_pairs={{0,16},{1,17},{2,18},{3,19},{4,20},{5,21},{6,22},{7,23},{8,24},{9,... | collective-permute-start | bytes 2359304 | tf_op jit(solution)/shard_map/ppermute | solution.py:42
  46.7 27.1 %collective-permute-start.13 = (bf16[2,2,96,512]{3,2,1,0:T(8,128)(2,1)S(1)}, bf16[2,2,96,512]{3,2,1,0:T(8,128)(2,1)S(1)}, u32[]{:S(2)}, u32[]{:S(2)}) collective-permute-start(bf16[2,2,96,512]{3,2,1,0:T(8,128)(2,1)S(1)} %pad_maximum_fusion.2), channel_id=1, source_target_pairs={{0,192},{1,193},{2,194},{3,195},{4,196},{5,197},{6,198},{7,199},{8... | collective-permute-start | bytes 1179656 | tf_op jit(solution)/shard_map/ppermute | solution.py:42
  56.3 17.5 %collective-permute-start.12 = (bf16[2,2,96,512]{3,2,1,0:T(8,128)(2,1)S(1)}, bf16[2,2,96,512]{3,2,1,0:T(8,128)(2,1)S(1)}, u32[]{:S(2)}, u32[]{:S(2)}) collective-permute-start(bf16[2,2,96,512]{3,2,1,0:T(8,128)(2,1)S(1)} %pad_maximum_fusion.2), channel_id=1, source_target_pairs={{0,128},{1,129},{2,130},{3,131},{4,132},{5,133},{6,134},{7,135},{8... | collective-permute-start | bytes 1179656 | tf_op jit(solution)/shard_map/ppermute | solution.py:42
  56.3 18.0 %collective-permute-start.11 = (bf16[2,2,96,512]{3,2,1,0:T(8,128)(2,1)S(1)}, bf16[2,2,96,512]{3,2,1,0:T(8,128)(2,1)}, u32[]{:S(2)}, u32[]{:S(2)}) collective-permute-start(bf16[2,2,96,512]{3,2,1,0:T(8,128)(2,1)S(1)} %pad_maximum_fusion.2), channel_id=1, source_target_pairs={{0,64},{1,65},{2,66},{3,67},{4,68},{5,69},{6,70},{7,71},{8,72},{9,... | collective-permute-start | bytes 1179656 | tf_op jit(solution)/shard_map/ppermute | solution.py:42
  57.0 13.6 %collective-permute-start.15 = (bf16[3,96,512]{2,1,0:T(8,128)(2,1)S(1)}, bf16[3,96,512]{2,1,0:T(8,128)(2,1)S(1)}, u32[]{:S(2)}, u32[]{:S(2)}) collective-permute-start(bf16[3,96,512]{2,1,0:T(8,128)(2,1)S(1)} %bitcast_multiply_fusion.refs_5_.refs_3_), channel_id=1, source_target_pairs={{0,8},{1,9},{2,10},{3,11},{4,12},{5,13},{6,14},{7,15},{8,0},{9,1},... | collective-permute-start | bytes 884744 | tf_op jit(solution)/shard_map/ppermute | solution.py:42
  76.2 22.9 %collective-permute-start.16 = (bf16[4,2,2,96,512]{4,3,2,1,0:T(8,128)(2,1)S(1)}, bf16[4,2,2,96,512]{4,3,2,1,0:T(8,128)(2,1)}, u32[]{:S(2)}, u32[]{:S(2)}) collective-permute-start(bf16[4,2,2,96,512]{4,3,2,1,0:T(8,128)(2,1)S(1)} %pad_maximum_fusion.own_ref), channel_id=1, source_target_pairs={{0,16},{1,17},{2,18},{3,19},{4,20},{5,21},{6,22},{7,23},{8,24},{9,... | collective-permute-start | bytes 4718600 | tf_op jit(solution)/shard_map/ppermute | solution.py:42
  77.3 32.1 %all-to-all-start.1 = ((s16[4,400,512]{2,1,0:T(8,128)(2,1)}), s16[4,400,512]{2,1,0:T(8,128)(2,1)S(1)}, u32[]{:S(2)}, u32[]{:S(2)}) async-start(s16[4,400,512]{2,1,0:T(8,128)(2,1)} %copy-done.7), calls=%async_computation.1 | async-start | bytes 3276800 | tf_op jit(solution)/shard_map/all_to_all | solution.py:311
  81.0 10.7 %collective-permute-start.10 = (bf16[3,96,512]{2,1,0:T(8,128)(2,1)S(1)}, bf16[3,96,512]{2,1,0:T(8,128)(2,1)S(1)}, u32[]{:S(2)}, u32[]{:S(2)}) collective-permute-start(bf16[3,96,512]{2,1,0:T(8,128)(2,1)S(1)} %bitcast_multiply_fusion.refs_5_.refs_3_), channel_id=1, source_target_pairs={{0,12},{1,13},{2,14},{3,15},{4,8},{5,9},{6,10},{7,11},{8,4},{9,5},... | collective-permute-start | bytes 884744 | tf_op jit(solution)/shard_map/ppermute | solution.py:42
  84.5 13.9 %collective-permute-start.9 = (bf16[3,96,512]{2,1,0:T(8,128)(2,1)S(1)}, bf16[3,96,512]{2,1,0:T(8,128)(2,1)S(1)}, u32[]{:S(2)}, u32[]{:S(2)}) collective-permute-start(bf16[3,96,512]{2,1,0:T(8,128)(2,1)S(1)} %bitcast_multiply_fusion.refs_5_.refs_3_), channel_id=1, source_target_pairs={{0,4},{1,5},{2,6},{3,7},{4,0},{5,1},{6,2},{7,3},{8,12},{9,13},{10,... | collective-permute-start | bytes 884744 | tf_op jit(solution)/shard_map/ppermute | solution.py:42
  109.4 25.3 %all-to-all-start = ((s16[4,400,512]{2,1,0:T(8,128)(2,1)}), s16[4,400,512]{2,1,0:T(8,128)(2,1)}, u32[]{:S(2)}, u32[]{:S(2)}) async-start(s16[4,400,512]{2,1,0:T(8,128)(2,1)} %copy-done.9), calls=%async_computation | async-start | bytes 3276800 | tf_op jit(solution)/shard_map/all_to_all | solution.py:311
  134.7 23.5 %all-to-all-start.2 = ((s16[4,400,512]{2,1,0:T(8,128)(2,1)}), s16[4,400,512]{2,1,0:T(8,128)(2,1)S(1)}, u32[]{:S(2)}, u32[]{:S(2)}) async-start(s16[4,400,512]{2,1,0:T(8,128)(2,1)} %copy-done.8), calls=%async_computation.2 | async-start | bytes 3276800 | tf_op jit(solution)/shard_map/all_to_all | solution.py:311
  151.3 34.0 %collective-permute-start.23 = (f32[512,512]{1,0:T(8,128)}, f32[512,512]{1,0:T(8,128)S(1)}, u32[]{:S(2)}, u32[]{:S(2)}) collective-permute-start(f32[512,512]{1,0:T(8,128)} %get-tuple-element.60), channel_id=1, source_target_pairs={{0,16},{1,17},{2,18},{3,19},{4,20},{5,21},{6,22},{7,23},{8,24},{9,... | collective-permute-start | bytes 3145736 | tf_op jit(solution)/shard_map/ppermute | solution.py:42
  152.8 12.2 %collective-permute-start.17 = (s16[224,512]{1,0:T(8,128)(2,1)}, s16[224,512]{1,0:T(8,128)(2,1)S(1)}, u32[]{:S(2)}, u32[]{:S(2)}) collective-permute-start(s16[224,512]{1,0:T(8,128)(2,1)} %get-tuple-element.48), channel_id=1, source_target_pairs={{0,4},{1,5},{2,6},{3,7},{4,0},{5,1},{6,2},{7,3},{8,12},{9,13},{10,... | collective-permute-start | bytes 688136 | tf_op jit(solution)/shard_map/ppermute | solution.py:42
  153.7 11.2 %collective-permute-start.18 = (s16[224,512]{1,0:T(8,128)(2,1)}, s16[224,512]{1,0:T(8,128)(2,1)S(1)}, u32[]{:S(2)}, u32[]{:S(2)}) collective-permute-start(s16[224,512]{1,0:T(8,128)(2,1)} %get-tuple-element.49), channel_id=1, source_target_pairs={{0,8},{1,9},{2,10},{3,11},{4,12},{5,13},{6,14},{7,15},{8,0},{9,1},... | collective-permute-start | bytes 688136 | tf_op jit(solution)/shard_map/ppermute | solution.py:42
  155.3 17.0 %collective-permute-start.19 = (s16[224,512]{1,0:T(8,128)(2,1)}, s16[224,512]{1,0:T(8,128)(2,1)S(1)}, u32[]{:S(2)}, u32[]{:S(2)}) collective-permute-start(s16[224,512]{1,0:T(8,128)(2,1)} %get-tuple-element.50), channel_id=1, source_target_pairs={{0,12},{1,13},{2,14},{3,15},{4,8},{5,9},{6,10},{7,11},{8,4},{9,5},... | collective-permute-start | bytes 688136 | tf_op jit(solution)/shard_map/ppermute | solution.py:42
  181.9 3.4 %collective-permute-start.24 = (f32[256,512]{1,0:T(8,128)S(1)}, f32[256,512]{1,0:T(8,128)S(1)}, u32[]{:S(2)}, u32[]{:S(2)}) collective-permute-start(f32[256,512]{1,0:T(8,128)S(1)} %get-tuple-element.61), channel_id=1, source_target_pairs={{0,16},{1,17},{2,18},{3,19},{4,20},{5,21},{6,22},{7,23},{8,24},{9,... | collective-permute-start | bytes 1572872 | tf_op jit(solution)/shard_map/ppermute | solution.py:42
  212.9 7.5 %collective-permute-start.25 = (f32[48,512]{1,0:T(8,128)S(1)}, f32[48,512]{1,0:T(8,128)S(1)}, u32[]{:S(2)}, u32[]{:S(2)}) collective-permute-start(f32[48,512]{1,0:T(8,128)S(1)} %reduce_sum.9), channel_id=1, source_target_pairs={{0,32},{1,33},{2,34},{3,35},{4,36},{5,37},{6,38},{7,39},{8,40},{9,... | collective-permute-start | bytes 294920 | tf_op jit(solution)/shard_map/ppermute | solution.py:42
  220.4 8.5 %collective-permute-start.26 = (f32[48,512]{1,0:T(8,128)S(1)}, f32[48,512]{1,0:T(8,128)S(1)}, u32[]{:S(2)}, u32[]{:S(2)}) collective-permute-start(f32[48,512]{1,0:T(8,128)S(1)} %add.51), channel_id=1, source_target_pairs={{0,4},{1,5},{2,6},{3,7},{4,0},{5,1},{6,2},{7,3},{8,12},{9,13},{10,... | collective-permute-start | bytes 294920 | tf_op jit(solution)/shard_map/ppermute | solution.py:42
  225.3 5.5 %collective-permute-start.20 = (s16[112,512]{1,0:T(8,128)(2,1)S(1)}, s16[112,512]{1,0:T(8,128)(2,1)S(1)}, u32[]{:S(2)}, u32[]{:S(2)}) collective-permute-start(s16[112,512]{1,0:T(8,128)(2,1)S(1)} %copy-done.40), channel_id=1, source_target_pairs={{0,4},{1,5},{2,6},{3,7},{4,0},{5,1},{6,2},{7,3},{8,12},{9,13},{10,... | collective-permute-start | bytes 344072 | tf_op jit(solution)/shard_map/ppermute | solution.py:42
  225.4 5.4 %collective-permute-start.21 = (s16[112,512]{1,0:T(8,128)(2,1)S(1)}, s16[112,512]{1,0:T(8,128)(2,1)S(1)}, u32[]{:S(2)}, u32[]{:S(2)}) collective-permute-start(s16[112,512]{1,0:T(8,128)(2,1)S(1)} %copy-done.38), channel_id=1, source_target_pairs={{0,8},{1,9},{2,10},{3,11},{4,12},{5,13},{6,14},{7,15},{8,0},{9,1},... | collective-permute-start | bytes 344072 | tf_op jit(solution)/shard_map/ppermute | solution.py:42
  227.4 6.9 %collective-permute-start.22 = (s16[112,512]{1,0:T(8,128)(2,1)S(1)}, s16[112,512]{1,0:T(8,128)(2,1)S(1)}, u32[]{:S(2)}, u32[]{:S(2)}) collective-permute-start(s16[112,512]{1,0:T(8,128)(2,1)S(1)} %copy-done.36), channel_id=1, source_target_pairs={{0,12},{1,13},{2,14},{3,15},{4,8},{5,9},{6,10},{7,11},{8,4},{9,5},... | collective-permute-start | bytes 344072 | tf_op jit(solution)/shard_map/ppermute | solution.py:42
  228.9 12.1 %collective-permute-start.27 = (f32[48,512]{1,0:T(8,128)S(1)}, f32[48,512]{1,0:T(8,128)S(1)}, u32[]{:S(2)}, u32[]{:S(2)}) collective-permute-start(f32[48,512]{1,0:T(8,128)S(1)} %add.52), channel_id=1, source_target_pairs={{0,8},{1,9},{2,10},{3,11},{4,12},{5,13},{6,14},{7,15},{8,0},{9,1},... | collective-permute-start | bytes 294920 | tf_op jit(solution)/shard_map/ppermute | solution.py:42
  265.8 6.6 %collective-permute-start.28 = (f32[768,512]{1,0:T(8,128)S(1)}, f32[768,512]{1,0:T(8,128)S(1)}, u32[]{:S(2)}, u32[]{:S(2)}) collective-permute-start(f32[768,512]{1,0:T(8,128)S(1)} %bitcast.30), channel_id=1, source_target_pairs={{0,16},{1,17},{2,18},{3,19},{4,20},{5,21},{6,22},{7,23},{8,24},{9,... | collective-permute-start | bytes 4718600 | tf_op jit(solution)/shard_map/ppermute | solution.py:42
  (44 other events, 328.6 us)

commit v4 on v2

--- a/solution.py
+++ b/solution.py
@@ -14,6 +14,7 @@
 ROW = ("x", "h", "core")
 COL = ("l", "y")
 EXTRA = 16
+LANES = 128
 STEPS = 64.0
 TOP = 32766.0
 LN2 = 0.6931471805599453
@@ -247,12 +248,29 @@
     )(own, *parts)
 
 
+def encode_lanes(value, out_ref, start=0):
+    rows, width = value.shape
+    largest = jnp.maximum(jnp.max(jnp.abs(value), axis=1, keepdims=True), 1e-30)
+    level = jnp.ceil(jnp.log(largest * (1.0 / TOP)) * (STEPS / LN2))
+    coded = jnp.round(value * jnp.exp2(level * (-1.0 / STEPS)))
+    out_ref[start : start + rows, :width] = coded.astype(I32).astype(I16)
+    lanes = jnp.broadcast_to(level, (rows, LANES))
+    out_ref[start : start + rows, width:] = lanes.astype(I32).astype(I16)
+
+
+def decode_lanes(block):
+    width = block.shape[1] - LANES
+    coded = block[:, :width].astype(I32).astype(F32)
+    level = block[:, width:].astype(I32).astype(F32)[:, :1]
+    return coded * jnp.exp2(level * (1.0 / STEPS))
+
+
 def fold_kernel(*refs):
     out, count = refs[-1], len(refs) // 2
     start = 0
     for p in range(count):
         rows = refs[p].shape[0]
-        out[start : start + rows, :] = refs[p][...] + refs[count + p][...]
+        encode_lanes(refs[p][...] + refs[count + p][...], out, start)
         start += rows
 
 
@@ -263,11 +281,51 @@
         fold_kernel,
         in_specs=[VMEM] * (2 * len(mines)),
         out_specs=VMEM,
-        out_shape=jax.ShapeDtypeStruct((total, width), F32),
+        out_shape=jax.ShapeDtypeStruct((total, width + LANES), I16),
         compiler_params=params(),
         cost_estimate=cost(total * width, 12 * total * width),
         name="fold",
     )(*mines, *theirs)
+
+
+def gathered_kernel(in_ref, out_ref):
+    total = decode_lanes(in_ref[0])
+    for k in range(1, in_ref.shape[0]):
+        total = total + decode_lanes(in_ref[k])
+    out_ref[...] = total
+
+
+def gathered(pieces):
+    count, rows, lanes = pieces.shape
+    return pl.pallas_call(
+        gathered_kernel,
+        in_specs=[VMEM],
+        out_specs=VMEM,
+        out_shape=jax.ShapeDtypeStruct((rows, lanes - LANES), F32),
+        compiler_params=params(),
+        cost_estimate=cost(count * rows * lanes, 2 * count * rows * lanes),
+        name="gathered",
+    )(pieces)
+
+
+def copies_kernel(own_ref, r1_ref, r2_ref, r3_ref, out_ref):
+    total = (own_ref[...] + r1_ref[...]) + (r2_ref[...] + r3_ref[...])
+    encode_lanes(total, out_ref.at[0])
+    for k in range(1, out_ref.shape[0]):
+        out_ref[k] = out_ref[0]
+
+
+def copies(own, found):
+    rows, width = own.shape
+    return pl.pallas_call(
+        copies_kernel,
+        in_specs=[VMEM] * 4,
+        out_specs=VMEM,
+        out_shape=jax.ShapeDtypeStruct((16, rows, width + LANES), I16),
+        compiler_params=params(),
+        cost_estimate=cost(rows * width, 32 * rows * width),
+        name="copies",
+    )(own, *found)
 
 
 def finish_kernel(at_ref, mine_ref, theirs_ref, diag_ref, out_ref):
@@ -276,7 +334,8 @@
     for p in range(diag_ref.shape[0]):
         for which, ref in ((core, mine_ref), (1 - core, theirs_ref)):
             place = pl.ds(pl.multiple_of(which * half, 8), half)
-            out_ref[p, place, :] = diag_ref[p, place, :] + ref[p * half : (p + 1) * half, :]
+            part = decode_lanes(ref[p * half : (p + 1) * half, :])
+            out_ref[p, place, :] = diag_ref[p, place, :] + part
 
 
 def finish(at, mine, theirs, diag):
@@ -340,14 +399,13 @@
     halves = fold([mine_01, mine_2], [swapped_01, swapped_2])
     coded = [jnp.concatenate([a, b]) for a, b in zip(coded_01, coded_2)]
     found = [send(coded[k - 1], over_l(k)) for k in (1, 2, 3)]
-    pieces = halves.reshape(16, -1, width)
-    total = jnp.sum(lax.all_to_all(pieces, ("x", "y"), 0, 0), axis=0)
+    pieces = halves.reshape(16, -1, width + LANES)
+    total = gathered(lax.all_to_all(pieces, ("x", "y"), 0, 0))
     found = after(found, total)
     total = total + send(total, over_h)
-    total = total + send(total, over_l(1))
-    total = total + send(total, over_l(2))
+    beyond = [send(total, over_l(k)) for k in (1, 2, 3)]
     blocks = last(3, jnp.concatenate([own_01, own_2]), found)
-    pieces = jnp.broadcast_to(after(total, blocks)[None], (16, *total.shape))
+    pieces = copies(total, after(beyond, blocks))
     mine = lax.all_to_all(pieces, ("x", "y"), 0, 0).reshape(halves.shape)
     diagonal = finish(at, mine, send(mine, over_core), diag_inverse)
     return jnp.swapaxes(blocks, 0, 1), diagonal

time: 231 us -> 222 us (0.961)
  starting transfers between devices: 86.3 us -> 77.7 us
  blocking collectives: 26.9 us -> 21.7 us
  waiting for transfers between devices: 84 us -> 87.9 us
    ppermute x32 -> x33, waiting for transfers between devices: 67.7 us -> 78.2 us  [send(): return lax.ppermute(value, AXES, pairs)]
    ppermute x32 -> x33, starting transfers between devices: 82.2 us -> 73.7 us  [send(): return lax.ppermute(value, AXES, pairs)]
    all_to_all x1, waiting for transfers between devices: 16.4 us -> 9.71 us  [body(): total = gathered(lax.all_to_all(pieces, ('x', 'y'), 0, 0))]
    all_to_all x1, blocking collectives: 26.9 us -> 21.7 us  [body(): mine = lax.all_to_all(pieces, ('x', 'y'), 0, 0).reshape(halves.shape)]
  transfers between devices with their start and end apart: 33 -> 34, of which waited for: 17 -> 17; matrix products, arithmetic and copies ran while one was open for 1% -> 1% of each run, Pallas kernels for 8% -> 8%
where the time goes in v4:
time: 222 us; the launch traced here: 221 us
  waiting for transfers between devices  87.9 us (40%)
  starting transfers between devices  77.7 us (35%)
  Pallas kernels  25.7 us (12%)
  blocking collectives  21.7 us (10%)
  other arithmetic  3.64 us (2%)
  local copies, waits for them, and re-layouts  3.59 us (2%)
    ppermute x33, waiting for transfers between devices, send(): return lax.ppermute(value, AXES, pairs)  78.2 us
    ppermute x33, starting transfers between devices, send(): return lax.ppermute(value, AXES, pairs)  73.7 us
    all_to_all x1, blocking collectives, body(): mine = lax.all_to_all(pieces, ('x', 'y'), 0, 0).reshape(halves.shape)  21.7 us
    pallas_call x2, Pallas kernels, product(): pl.pallas_call(functools.partial(product_kernel, panels), grid_spec=pltpu...  14.9 us
    all_to_all x1, waiting for transfers between devices, body(): total = gathered(lax.all_to_all(pieces, ('x', 'y'), 0, 0))  9.71 us
    pallas_call x2, Pallas kernels, middle(): pl.pallas_call(functools.partial(middle_kernel, panels, base), in_specs=[...  5.07 us
  transfers between devices with their start and end apart: 34, of which 17 were waited for; matrix products, arithmetic and copies ran while one was open for 1% of the time, Pallas kernels for 8%

profile of v4, /device:TPU:1, one launch (start us, length us, event | category | flops | bytes accessed | tf_op | source)
XLA Modules:
  0.0 221.3 jit_solution(1752180448903030619)
XLA Ops:
  3.5 4.6 %collective-permute-start.4 = (bf16[1,96,512]{2,1,0:T(8,128)(2,1)S(1)}, bf16[1,96,512]{2,1,0:T(8,128)(2,1)S(1)}, u32[]{:S(2)}, u32[]{:S(2)}) collective-permute-start(bf16[1,96,512]{2,1,0:T(8,128)(2,1)S(1)} %collective-permute-done.3), channel_id=1, source_target_pairs={{0,0},{1,32},{2,16},{3,48},{4,4},{5,36},{6,20},{7,52},{8,8},{9,40}... | collective-permute-start | bytes 294920 | tf_op jit(solution)/shard_map/ppermute | solution.py:43
  8.1 8.3 %collective-permute-start.5 = (bf16[1,96,512]{2,1,0:T(8,128)(2,1)S(1)}, bf16[1,96,512]{2,1,0:T(8,128)(2,1)S(1)}, u32[]{:S(2)}, u32[]{:S(2)}) collective-permute-start(bf16[1,96,512]{2,1,0:T(8,128)(2,1)S(1)} %collective-permute-done.3), channel_id=1, source_target_pairs={{0,32},{1,0},{2,48},{3,16},{4,36},{5,4},{6,52},{7,20},{8,40},{9,8}... | collective-permute-start | bytes 294920 | tf_op jit(solution)/shard_map/ppermute | solution.py:43
  18.4 5.3 %collective-permute-start.6 = (bf16[2,1,96,512]{3,2,0,1:T(8,128)(2,1)S(1)}, bf16[2,1,96,512]{3,2,0,1:T(8,128)(2,1)S(1)}, u32[]{:S(2)}, u32[]{:S(2)}) collective-permute-start(bf16[2,1,96,512]{3,2,0,1:T(8,128)(2,1)S(1)} %bitcast.58), channel_id=1, source_target_pairs={{0,64},{1,65},{2,66},{3,67},{4,68},{5,69},{6,70},{7,71},{8,72},{9,... | collective-permute-start | bytes 589832 | tf_op jit(solution)/shard_map/ppermute | solution.py:43
  23.7 8.9 %collective-permute-start.7 = (bf16[2,1,96,512]{3,2,0,1:T(8,128)(2,1)S(1)}, bf16[2,1,96,512]{3,2,0,1:T(8,128)(2,1)S(1)}, u32[]{:S(2)}, u32[]{:S(2)}) collective-permute-start(bf16[2,1,96,512]{3,2,0,1:T(8,128)(2,1)S(1)} %bitcast.59), channel_id=1, source_target_pairs={{0,128},{1,129},{2,130},{3,131},{4,132},{5,133},{6,134},{7,135},{8... | collective-permute-start | bytes 589832 | tf_op jit(solution)/shard_map/ppermute | solution.py:43
  32.6 2.9 %collective-permute-start.1 = (bf16[2,96,512]{2,1,0:T(8,128)(2,1)S(1)}, bf16[2,96,512]{2,1,0:T(8,128)(2,1)S(1)}, u32[]{:S(2)}, u32[]{:S(2)}) collective-permute-start(bf16[2,96,512]{2,1,0:T(8,128)(2,1)S(1)} %collective-permute-done), channel_id=1, source_target_pairs={{0,0},{1,32},{2,16},{3,48},{4,4},{5,36},{6,20},{7,52},{8,8},{9,40}... | collective-permute-start | bytes 589832 | tf_op jit(solution)/shard_map/ppermute | solution.py:43
  35.6 4.2 %collective-permute-start.2 = (bf16[2,96,512]{2,1,0:T(8,128)(2,1)S(1)}, bf16[2,96,512]{2,1,0:T(8,128)(2,1)S(1)}, u32[]{:S(2)}, u32[]{:S(2)}) collective-permute-start(bf16[2,96,512]{2,1,0:T(8,128)(2,1)S(1)} %collective-permute-done), channel_id=1, source_target_pairs={{0,32},{1,0},{2,48},{3,16},{4,36},{5,4},{6,52},{7,20},{8,40},{9,8}... | collective-permute-start | bytes 589832 | tf_op jit(solution)/shard_map/ppermute | solution.py:43
  40.5 2.8 %collective-permute-done.8 = bf16[2,1,96,512]{3,2,1,0:T(8,128)(2,1)S(1)} collective-permute-done((bf16[2,1,96,512]{3,2,1,0:T(8,128)(2,1)S(1)}, bf16[2,1,96,512]{3,2,1,0:T(8,128)(2,1)S(1)}, u32[]{:S(2)}, u32[]{:S(2)}) %collective-permute-start.8) | collective-permute-done | bytes 196640 | tf_op jit(solution)/shard_map/ppermute | solution.py:43
  45.2 6.1 %collective-permute-start.9 = (bf16[2,2,96,512]{3,2,1,0:T(8,128)(2,1)S(1)}, bf16[2,2,96,512]{3,2,1,0:T(8,128)(2,1)S(1)}, u32[]{:S(2)}, u32[]{:S(2)}) collective-permute-start(bf16[2,2,96,512]{3,2,1,0:T(8,128)(2,1)S(1)} %pad_maximum_fusion.3), channel_id=1, source_target_pairs={{0,64},{1,65},{2,66},{3,67},{4,68},{5,69},{6,70},{7,71},{8,72},{9,... | collective-permute-start | bytes 1179656 | tf_op jit(solution)/shard_map/ppermute | solution.py:43
  51.3 6.9 %collective-permute-start.10 = (bf16[2,2,96,512]{3,2,1,0:T(8,128)(2,1)S(1)}, bf16[2,2,96,512]{3,2,1,0:T(8,128)(2,1)}, u32[]{:S(2)}, u32[]{:S(2)}) collective-permute-start(bf16[2,2,96,512]{3,2,1,0:T(8,128)(2,1)S(1)} %pad_maximum_fusion.3), channel_id=1, source_target_pairs={{0,128},{1,129},{2,130},{3,131},{4,132},{5,133},{6,134},{7,135},{8... | collective-permute-start | bytes 1179656 | tf_op jit(solution)/shard_map/ppermute | solution.py:43
  58.3 2.3 %copy-done = bf16[1536,1536]{1,0:T(8,128)(2,1)S(1)} copy-done((bf16[1536,1536]{1,0:T(8,128)(2,1)S(1)}, bf16[1536,1536]{1,0:T(8,128)(2,1)}, u32[]{:S(2)}) %copy-start) | copy-done | bytes 4718616
  60.7 5.0 %product.2 = (f32[384,512]{1,0:T(8,128)S(1)}, s16[400,512]{1,0:T(8,128)(2,1)S(1)}, s16[400,512]{1,0:T(8,128)(2,1)S(1)}, s16[400,512]{1,0:T(8,128)(2,1)S(1)}) custom-call(s32[6]{0:T(128)S(1)} %stack.102.at_ref.refs_0_, bf16[4,4,96,1536]{3,2,1,0:T(8,128)(2,1)S(1)} %bitcast.46, bf16[4,2,1,96,512]{4,3,2,1,0:T(8,128)(2,1)S(1)} %bitcast.49, ...), custom_call_target="tpu_custom_call" | custom-call | flops 2415919 | bytes 4718 | tf_op jit(solution)/shard_map/product/pallas_call | solution.py:152
  65.8 2.5 %collective-permute-start.14 = (s16[400,512]{1,0:T(8,128)(2,1)S(1)}, s16[400,512]{1,0:T(8,128)(2,1)S(1)}, u32[]{:S(2)}, u32[]{:S(2)}) collective-permute-start(s16[400,512]{1,0:T(8,128)(2,1)S(1)} %get-tuple-element.47), channel_id=1, source_target_pairs={{0,3},{1,2},{2,1},{3,0},{4,7},{5,6},{6,5},{7,4},{8,11},{9,10},{10,... | collective-permute-start | bytes 1228808 | tf_op jit(solution)/shard_map/ppermute | solution.py:43
  68.2 7.9 %collective-permute-done.10 = bf16[2,2,96,512]{3,2,1,0:T(8,128)(2,1)} collective-permute-done((bf16[2,2,96,512]{3,2,1,0:T(8,128)(2,1)S(1)}, bf16[2,2,96,512]{3,2,1,0:T(8,128)(2,1)}, u32[]{:S(2)}, u32[]{:S(2)}) %collective-permute-start.10) | collective-permute-done | bytes 393248 | tf_op jit(solution)/shard_map/ppermute | solution.py:43
  76.1 2.0 collective-permute-done.11
  81.2 2.8 %collective-permute-done.15.other_ref = bf16[4,2,2,96,512]{4,3,2,1,0:T(8,128)(2,1)S(1)} collective-permute-done((bf16[4,2,2,96,512]{4,3,2,1,0:T(8,128)(2,1)S(1)}, bf16[4,2,2,96,512]{4,3,2,1,0:T(8,128)(2,1)S(1)}, u32[]{:S(2)}, u32[]{:S(2)}) %collective-permute-start.15) | collective-permute-done | bytes 1572896 | tf_op jit(solution)/shard_map/ppermute | solution.py:43
  84.0 9.9 %product.3 = (f32[384,512]{1,0:T(8,128)S(1)}, s16[400,512]{1,0:T(8,128)(2,1)S(1)}, s16[400,512]{1,0:T(8,128)(2,1)S(1)}, s16[400,512]{1,0:T(8,128)(2,1)S(1)}, f32...) custom-call(s32[6]{0:T(128)S(1)} %stack.102.at_ref.refs_0_, ...), custom_call_target="tpu_custom_call" | custom-call | flops 4831838 | bytes 4718 | tf_op jit(solution)/shard_map/product/pallas_call | solution.py:152
  95.8 2.3 %collective-permute-start.19 = (s16[2,400,512]{2,1,0:T(8,128)(2,1)S(1)}, s16[2,400,512]{2,1,0:T(8,128)(2,1)S(1)}, u32[]{:S(2)}, u32[]{:S(2)}) collective-permute-start(s16[2,400,512]{2,1,0:T(8,128)(2,1)S(1)} %pad_add_fusion.2), channel_id=1, source_target_pairs={{0,3},{1,2},{2,1},{3,0},{4,7},{5,6},{6,5},{7,4},{8,11},{9,10},{10,... | collective-permute-start | bytes 2457608 | tf_op jit(solution)/shard_map/ppermute | solution.py:43
  99.5 11.4 %collective-permute-done.20.refs_6_.refs_10_ = bf16[3,96,512]{2,1,0:T(8,128)(2,1)S(1)} collective-permute-done((bf16[3,96,512]{2,1,0:T(8,128)(2,1)S(1)}, bf16[3,96,512]{2,1,0:T(8,128)(2,1)S(1)}, u32[]{:S(2)}, u32[]{:S(2)}) %collective-permute-start.20) | collective-permute-done | bytes 294944 | tf_op jit(solution)/shard_map/ppermute | solution.py:43
  112.4 6.9 %collective-permute-done.22.refs_8_.refs_12_ = bf16[3,96,512]{2,1,0:T(8,128)(2,1)S(1)} collective-permute-done((bf16[3,96,512]{2,1,0:T(8,128)(2,1)S(1)}, bf16[3,96,512]{2,1,0:T(8,128)(2,1)S(1)}, u32[]{:S(2)}, u32[]{:S(2)}) %collective-permute-start.22) | collective-permute-done | bytes 294944 | tf_op jit(solution)/shard_map/ppermute | solution.py:43
  121.3 10.0 %collective-permute-done.18 = s16[2,400,512]{2,1,0:T(8,128)(2,1)S(1)} collective-permute-done((s16[2,400,512]{2,1,0:T(8,128)(2,1)S(1)}, s16[2,400,512]{2,1,0:T(8,128)(2,1)S(1)}, u32[]{:S(2)}, u32[]{:S(2)}) %collective-permute-start.18) | collective-permute-done | bytes 819232 | tf_op jit(solution)/shard_map/ppermute | solution.py:43
  133.5 3.1 %middle.3 = (f32[192,512]{1,0:T(8,128)S(1)}, s16[224,512]{1,0:T(8,128)(2,1)S(1)}, s16[224,512]{1,0:T(8,128)(2,1)S(1)}, s16[224,512]{1,0:T(8,128)(2,1)S(1)}, f32[...) custom-call(s32[6]{0:T(128)S(1)} %stack.102.at_ref.refs_0_, f32[384,512]{1,0:T(8,128)S(1)} %get-tuple-element.49.refs_1_, ...), custom_call_target="tpu_custom_call" | custom-call | flops 603979 | bytes 3145 | tf_op jit(solution)/shard_map/middle/pallas_call | solution.py:215
  138.7 2.9 %collective-permute-done.27.refs_3_ = f32[256,512]{1,0:T(8,128)S(1)} collective-permute-done((f32[256,512]{1,0:T(8,128)S(1)}, f32[256,512]{1,0:T(8,128)S(1)}, u32[]{:S(2)}, u32[]{:S(2)}) %collective-permute-start.27) | collective-permute-done | bytes 524320 | tf_op jit(solution)/shard_map/ppermute | solution.py:43
  143.0 4.1 %all-to-all-start = ((s16[16,48,640]{2,1,0:T(8,128)(2,1)}), s16[16,48,640]{2,1,0:T(8,128)(2,1)S(1)}, u32[]{:S(2)}, u32[]{:S(2)}) async-start(s16[16,48,640]{2,1,0:T(8,128)(2,1)} %bitcast.35), calls=%async_computation | async-start | bytes 1966080 | tf_op jit(solution)/shard_map/all_to_all | solution.py:403
  147.9 3.0 %collective-permute-start.25 = (s16[336,512]{1,0:T(8,128)(2,1)}, s16[336,512]{1,0:T(8,128)(2,1)S(1)}, u32[]{:S(2)}, u32[]{:S(2)}) collective-permute-start(s16[336,512]{1,0:T(8,128)(2,1)} %pad_add_fusion.5), channel_id=1, source_target_pairs={{0,12},{1,13},{2,14},{3,15},{4,8},{5,9},{6,10},{7,11},{8,4},{9,5},... | collective-permute-start | bytes 1032200 | tf_op jit(solution)/shard_map/ppermute | solution.py:43
  151.9 9.7 %all-to-all-done.in_ref = s16[16,48,640]{2,1,0:T(8,128)(2,1)S(1)} async-done(((s16[16,48,640]{2,1,0:T(8,128)(2,1)}), s16[16,48,640]{2,1,0:T(8,128)(2,1)S(1)}, u32[]{:S(2)}, u32[]{:S(2)}) %all-to-all-start) | async-done | bytes 983072 | tf_op jit(solution)/shard_map/all_to_all | solution.py:403
  161.8 2.4 %collective-permute-start.28 = (f32[48,512]{1,0:T(8,128)S(1)}, f32[48,512]{1,0:T(8,128)S(1)}, u32[]{:S(2)}, u32[]{:S(2)}) collective-permute-start(f32[48,512]{1,0:T(8,128)S(1)} %gathered.1), channel_id=1, source_target_pairs={{0,32},{1,33},{2,34},{3,35},{4,36},{5,37},{6,38},{7,39},{8,40},{9,... | collective-permute-start | bytes 294920 | tf_op jit(solution)/shard_map/ppermute | solution.py:43
  164.2 16.2 %collective-permute-done.28 = f32[48,512]{1,0:T(8,128)S(1)} collective-permute-done((f32[48,512]{1,0:T(8,128)S(1)}, f32[48,512]{1,0:T(8,128)S(1)}, u32[]{:S(2)}, u32[]{:S(2)}) %collective-permute-start.28) | collective-permute-done | bytes 98336 | tf_op jit(solution)/shard_map/ppermute | solution.py:43
  181.4 2.7 %collective-permute-start.31 = (f32[48,512]{1,0:T(8,128)S(1)}, f32[48,512]{1,0:T(8,128)S(1)}, u32[]{:S(2)}, u32[]{:S(2)}) collective-permute-start(f32[48,512]{1,0:T(8,128)S(1)} %add.45.own_ref), channel_id=1, source_target_pairs={{0,12},{1,13},{2,14},{3,15},{4,8},{5,9},{6,10},{7,11},{8,4},{9,5},... | collective-permute-start | bytes 294920 | tf_op jit(solution)/shard_map/ppermute | solution.py:43
  184.2 6.3 %collective-permute-done.24.r2_ref = s16[336,512]{1,0:T(8,128)(2,1)S(1)} collective-permute-done((s16[336,512]{1,0:T(8,128)(2,1)S(1)}, s16[336,512]{1,0:T(8,128)(2,1)S(1)}, u32[]{:S(2)}, u32[]{:S(2)}) %collective-permute-start.24) | collective-permute-done | bytes 344096 | tf_op jit(solution)/shard_map/ppermute | solution.py:43
  192.8 21.7 %all_to_all.10 = s16[16,48,640]{2,1,0:T(8,128)(2,1)S(1)} all-to-all(s16[16,48,640]{2,1,0:T(8,128)(2,1)S(1)} %copies.1), channel_id=1, replica_groups=mesh['x'=4,'h'=2,'core'=2,'l'=4,'y'=4] {'x','y'}, dimensions={0} | all-to-all | bytes 1966080 | tf_op jit(solution)/shard_map/all_to_all | solution.py:409
  216.3 2.2 collective-permute-done.32.theirs_ref
  218.5 2.7 %finish.1 = f32[3,512,512]{2,1,0:T(8,128)} custom-call(s32[6]{0:T(128)S(1)} %stack.102.at_ref.refs_0_, s16[768,640]{1,0:T(8,128)(2,1)S(1)} %bitcast.48, s16[768,640]{1,0:T(8,128)(2,1)S(1)} %collective-permute-done.32.theirs_ref, f32[3,512,512]{2,1,0:T(8,128)S(1)} %copy-done.1), custom_call_target="tpu_custom_call" | custom-call | flops 786 | bytes 9437 | tf_op jit(solution)/shard_map/finish/pallas_call | solution.py:342
  (71 shorter events, 30.0 us)
Async XLA Ops:
  3.5 13.6 %collective-permute-start.4 = (bf16[1,96,512]{2,1,0:T(8,128)(2,1)S(1)}, bf16[1,96,512]{2,1,0:T(8,128)(2,1)S(1)}, u32[]{:S(2)}, u32[]{:S(2)}) collective-permute-start(bf16[1,96,512]{2,1,0:T(8,128)(2,1)S(1)} %collective-permute-done.3), channel_id=1, source_target_pairs={{0,0},{1,32},{2,16},{3,48},{4,4},{5,36},{6,20},{7,52},{8,8},{9,40}... | collective-permute-start | bytes 294920 | tf_op jit(solution)/shard_map/ppermute | solution.py:43
  8.1 10.3 %collective-permute-start.5 = (bf16[1,96,512]{2,1,0:T(8,128)(2,1)S(1)}, bf16[1,96,512]{2,1,0:T(8,128)(2,1)S(1)}, u32[]{:S(2)}, u32[]{:S(2)}) collective-permute-start(bf16[1,96,512]{2,1,0:T(8,128)(2,1)S(1)} %collective-permute-done.3), channel_id=1, source_target_pairs={{0,32},{1,0},{2,48},{3,16},{4,36},{5,4},{6,52},{7,20},{8,40},{9,8}... | collective-permute-start | bytes 294920 | tf_op jit(solution)/shard_map/ppermute | solution.py:43
  18.4 21.4 %collective-permute-start.6 = (bf16[2,1,96,512]{3,2,0,1:T(8,128)(2,1)S(1)}, bf16[2,1,96,512]{3,2,0,1:T(8,128)(2,1)S(1)}, u32[]{:S(2)}, u32[]{:S(2)}) collective-permute-start(bf16[2,1,96,512]{3,2,0,1:T(8,128)(2,1)S(1)} %bitcast.58), channel_id=1, source_target_pairs={{0,64},{1,65},{2,66},{3,67},{4,68},{5,69},{6,70},{7,71},{8,72},{9,... | collective-permute-start | bytes 589832 | tf_op jit(solution)/shard_map/ppermute | solution.py:43
  23.7 16.8 %collective-permute-start.7 = (bf16[2,1,96,512]{3,2,0,1:T(8,128)(2,1)S(1)}, bf16[2,1,96,512]{3,2,0,1:T(8,128)(2,1)S(1)}, u32[]{:S(2)}, u32[]{:S(2)}) collective-permute-start(bf16[2,1,96,512]{3,2,0,1:T(8,128)(2,1)S(1)} %bitcast.59), channel_id=1, source_target_pairs={{0,128},{1,129},{2,130},{3,131},{4,132},{5,133},{6,134},{7,135},{8... | collective-permute-start | bytes 589832 | tf_op jit(solution)/shard_map/ppermute | solution.py:43
  32.6 10.7 %collective-permute-start.8 = (bf16[2,1,96,512]{3,2,1,0:T(8,128)(2,1)S(1)}, bf16[2,1,96,512]{3,2,1,0:T(8,128)(2,1)S(1)}, u32[]{:S(2)}, u32[]{:S(2)}) collective-permute-start(bf16[2,1,96,512]{3,2,1,0:T(8,128)(2,1)S(1)} %pad_maximum_fusion.4), channel_id=1, source_target_pairs={{0,192},{1,193},{2,194},{3,195},{4,196},{5,197},{6,198},{7,199},{8... | collective-permute-start | bytes 589832 | tf_op jit(solution)/shard_map/ppermute | solution.py:43
  32.6 10.8 %collective-permute-start.1 = (bf16[2,96,512]{2,1,0:T(8,128)(2,1)S(1)}, bf16[2,96,512]{2,1,0:T(8,128)(2,1)S(1)}, u32[]{:S(2)}, u32[]{:S(2)}) collective-permute-start(bf16[2,96,512]{2,1,0:T(8,128)(2,1)S(1)} %collective-permute-done), channel_id=1, source_target_pairs={{0,0},{1,32},{2,16},{3,48},{4,4},{5,36},{6,20},{7,52},{8,8},{9,40}... | collective-permute-start | bytes 589832 | tf_op jit(solution)/shard_map/ppermute | solution.py:43
  35.6 9.6 %collective-permute-start.2 = (bf16[2,96,512]{2,1,0:T(8,128)(2,1)S(1)}, bf16[2,96,512]{2,1,0:T(8,128)(2,1)S(1)}, u32[]{:S(2)}, u32[]{:S(2)}) collective-permute-start(bf16[2,96,512]{2,1,0:T(8,128)(2,1)S(1)} %collective-permute-done), channel_id=1, source_target_pairs={{0,32},{1,0},{2,48},{3,16},{4,36},{5,4},{6,52},{7,20},{8,40},{9,8}... | collective-permute-start | bytes 589832 | tf_op jit(solution)/shard_map/ppermute | solution.py:43
  45.2 13.2 %collective-permute-start.12 = (bf16[4,2,1,96,512]{4,3,1,2,0:T(8,128)(2,1)S(1)}, bf16[4,2,1,96,512]{4,3,1,2,0:T(8,128)(2,1)S(1)}, u32[]{:S(2)}, u32[]{:S(2)}) collective-permute-start(bf16[4,2,1,96,512]{4,3,1,2,0:T(8,128)(2,1)S(1)} %pad_maximum_fusion.1), channel_id=1, source_target_pairs={{0,16},{1,17},{2,18},{3,19},{4,20},{5,21},{6,22},{7,23},{8,24},{9,... | collective-permute-start | bytes 2359304 | tf_op jit(solution)/shard_map/ppermute | solution.py:43
  45.2 23.0 %collective-permute-start.9 = (bf16[2,2,96,512]{3,2,1,0:T(8,128)(2,1)S(1)}, bf16[2,2,96,512]{3,2,1,0:T(8,128)(2,1)S(1)}, u32[]{:S(2)}, u32[]{:S(2)}) collective-permute-start(bf16[2,2,96,512]{3,2,1,0:T(8,128)(2,1)S(1)} %pad_maximum_fusion.3), channel_id=1, source_target_pairs={{0,64},{1,65},{2,66},{3,67},{4,68},{5,69},{6,70},{7,71},{8,72},{9,... | collective-permute-start | bytes 1179656 | tf_op jit(solution)/shard_map/ppermute | solution.py:43
  51.3 24.8 %collective-permute-start.10 = (bf16[2,2,96,512]{3,2,1,0:T(8,128)(2,1)S(1)}, bf16[2,2,96,512]{3,2,1,0:T(8,128)(2,1)}, u32[]{:S(2)}, u32[]{:S(2)}) collective-permute-start(bf16[2,2,96,512]{3,2,1,0:T(8,128)(2,1)S(1)} %pad_maximum_fusion.3), channel_id=1, source_target_pairs={{0,128},{1,129},{2,130},{3,131},{4,132},{5,133},{6,134},{7,135},{8... | collective-permute-start | bytes 1179656 | tf_op jit(solution)/shard_map/ppermute | solution.py:43
  58.2 19.9 %collective-permute-start.11 = (bf16[2,2,96,512]{3,2,1,0:T(8,128)(2,1)S(1)}, bf16[2,2,96,512]{3,2,1,0:T(8,128)(2,1)}, u32[]{:S(2)}, u32[]{:S(2)}) collective-permute-start(bf16[2,2,96,512]{3,2,1,0:T(8,128)(2,1)S(1)} %pad_maximum_fusion.3), channel_id=1, source_target_pairs={{0,192},{1,193},{2,194},{3,195},{4,196},{5,197},{6,198},{7,199},{8... | collective-permute-start | bytes 1179656 | tf_op jit(solution)/shard_map/ppermute | solution.py:43
  65.7 13.8 %collective-permute-start.13 = (s16[400,512]{1,0:T(8,128)(2,1)S(1)}, s16[400,512]{1,0:T(8,128)(2,1)S(1)}, u32[]{:S(2)}, u32[]{:S(2)}) collective-permute-start(s16[400,512]{1,0:T(8,128)(2,1)S(1)} %get-tuple-element.46), channel_id=1, source_target_pairs={{0,1},{1,0},{2,3},{3,2},{4,5},{5,4},{6,7},{7,6},{8,9},{9,8},{10,11... | collective-permute-start | bytes 1228808 | tf_op jit(solution)/shard_map/ppermute | solution.py:43
  65.8 13.7 %collective-permute-start.14 = (s16[400,512]{1,0:T(8,128)(2,1)S(1)}, s16[400,512]{1,0:T(8,128)(2,1)S(1)}, u32[]{:S(2)}, u32[]{:S(2)}) collective-permute-start(s16[400,512]{1,0:T(8,128)(2,1)S(1)} %get-tuple-element.47), channel_id=1, source_target_pairs={{0,3},{1,2},{2,1},{3,0},{4,7},{5,6},{6,5},{7,4},{8,11},{9,10},{10,... | collective-permute-start | bytes 1228808 | tf_op jit(solution)/shard_map/ppermute | solution.py:43
  79.4 4.5 %collective-permute-start.15 = (bf16[4,2,2,96,512]{4,3,2,1,0:T(8,128)(2,1)S(1)}, bf16[4,2,2,96,512]{4,3,2,1,0:T(8,128)(2,1)S(1)}, u32[]{:S(2)}, u32[]{:S(2)}) collective-permute-start(bf16[4,2,2,96,512]{4,3,2,1,0:T(8,128)(2,1)S(1)} %pad_maximum_fusion.own_ref), channel_id=1, source_target_pairs={{0,16},{1,17},{2,18},{3,19},{4,20},{5,21},{6,22},{7,23},{8,24},{9,... | collective-permute-start | bytes 4718600 | tf_op jit(solution)/shard_map/ppermute | solution.py:43
  80.9 13.2 %collective-permute-start.16 = (s16[400,512]{1,0:T(8,128)(2,1)S(1)}, s16[400,512]{1,0:T(8,128)(2,1)S(1)}, u32[]{:S(2)}, u32[]{:S(2)}) collective-permute-start(s16[400,512]{1,0:T(8,128)(2,1)S(1)} %get-tuple-element.57), channel_id=1, source_target_pairs={{0,2},{1,3},{2,0},{3,1},{4,6},{5,7},{6,4},{7,5},{8,10},{9,11},{10,... | collective-permute-start | bytes 1228808 | tf_op jit(solution)/shard_map/ppermute | solution.py:43
  94.1 27.2 %collective-permute-start.17 = (s16[2,400,512]{2,1,0:T(8,128)(2,1)S(1)}, s16[2,400,512]{2,1,0:T(8,128)(2,1)S(1)}, u32[]{:S(2)}, u32[]{:S(2)}) collective-permute-start(s16[2,400,512]{2,1,0:T(8,128)(2,1)S(1)} %get-tuple-element.58), channel_id=1, source_target_pairs={{0,1},{1,0},{2,3},{3,2},{4,5},{5,4},{6,7},{7,6},{8,9},{9,8},{10,11... | collective-permute-start | bytes 2457608 | tf_op jit(solution)/shard_map/ppermute | solution.py:43
  94.2 37.1 %collective-permute-start.18 = (s16[2,400,512]{2,1,0:T(8,128)(2,1)S(1)}, s16[2,400,512]{2,1,0:T(8,128)(2,1)S(1)}, u32[]{:S(2)}, u32[]{:S(2)}) collective-permute-start(s16[2,400,512]{2,1,0:T(8,128)(2,1)S(1)} %get-tuple-element.59), channel_id=1, source_target_pairs={{0,2},{1,3},{2,0},{3,1},{4,6},{5,7},{6,4},{7,5},{8,10},{9,11},{10,... | collective-permute-start | bytes 2457608 | tf_op jit(solution)/shard_map/ppermute | solution.py:43
  95.8 37.6 %collective-permute-start.19 = (s16[2,400,512]{2,1,0:T(8,128)(2,1)S(1)}, s16[2,400,512]{2,1,0:T(8,128)(2,1)S(1)}, u32[]{:S(2)}, u32[]{:S(2)}) collective-permute-start(s16[2,400,512]{2,1,0:T(8,128)(2,1)S(1)} %pad_add_fusion.2), channel_id=1, source_target_pairs={{0,3},{1,2},{2,1},{3,0},{4,7},{5,6},{6,5},{7,4},{8,11},{9,10},{10,... | collective-permute-start | bytes 2457608 | tf_op jit(solution)/shard_map/ppermute | solution.py:43
  98.1 12.9 %collective-permute-start.20 = (bf16[3,96,512]{2,1,0:T(8,128)(2,1)S(1)}, bf16[3,96,512]{2,1,0:T(8,128)(2,1)S(1)}, u32[]{:S(2)}, u32[]{:S(2)}) collective-permute-start(bf16[3,96,512]{2,1,0:T(8,128)(2,1)S(1)} %bitcast_multiply_fusion.refs_5_.refs_9_), channel_id=1, source_target_pairs={{0,4},{1,5},{2,6},{3,7},{4,0},{5,1},{6,2},{7,3},{8,12},{9,13},{10,... | collective-permute-start | bytes 884744 | tf_op jit(solution)/shard_map/ppermute | solution.py:43
  98.6 13.9 %collective-permute-start.21 = (bf16[3,96,512]{2,1,0:T(8,128)(2,1)S(1)}, bf16[3,96,512]{2,1,0:T(8,128)(2,1)S(1)}, u32[]{:S(2)}, u32[]{:S(2)}) collective-permute-start(bf16[3,96,512]{2,1,0:T(8,128)(2,1)S(1)} %bitcast_multiply_fusion.refs_5_.refs_9_), channel_id=1, source_target_pairs={{0,8},{1,9},{2,10},{3,11},{4,12},{5,13},{6,14},{7,15},{8,0},{9,1},... | collective-permute-start | bytes 884744 | tf_op jit(solution)/shard_map/ppermute | solution.py:43
  110.9 8.4 %collective-permute-start.22 = (bf16[3,96,512]{2,1,0:T(8,128)(2,1)S(1)}, bf16[3,96,512]{2,1,0:T(8,128)(2,1)S(1)}, u32[]{:S(2)}, u32[]{:S(2)}) collective-permute-start(bf16[3,96,512]{2,1,0:T(8,128)(2,1)S(1)} %bitcast_multiply_fusion.refs_5_.refs_9_), channel_id=1, source_target_pairs={{0,12},{1,13},{2,14},{3,15},{4,8},{5,9},{6,10},{7,11},{8,4},{9,5},... | collective-permute-start | bytes 884744 | tf_op jit(solution)/shard_map/ppermute | solution.py:43
  136.6 5.0 %collective-permute-start.26 = (f32[512,512]{1,0:T(8,128)S(1)}, f32[512,512]{1,0:T(8,128)S(1)}, u32[]{:S(2)}, u32[]{:S(2)}) collective-permute-start(f32[512,512]{1,0:T(8,128)S(1)} %get-tuple-element.76), channel_id=1, source_target_pairs={{0,16},{1,17},{2,18},{3,19},{4,20},{5,21},{6,22},{7,23},{8,24},{9,... | collective-permute-start | bytes 3145736 | tf_op jit(solution)/shard_map/ppermute | solution.py:43
  138.6 3.0 %collective-permute-start.27 = (f32[256,512]{1,0:T(8,128)S(1)}, f32[256,512]{1,0:T(8,128)S(1)}, u32[]{:S(2)}, u32[]{:S(2)}) collective-permute-start(f32[256,512]{1,0:T(8,128)S(1)} %get-tuple-element.77), channel_id=1, source_target_pairs={{0,16},{1,17},{2,18},{3,19},{4,20},{5,21},{6,22},{7,23},{8,24},{9,... | collective-permute-start | bytes 1572872 | tf_op jit(solution)/shard_map/ppermute | solution.py:43
  143.0 18.5 %all-to-all-start = ((s16[16,48,640]{2,1,0:T(8,128)(2,1)}), s16[16,48,640]{2,1,0:T(8,128)(2,1)S(1)}, u32[]{:S(2)}, u32[]{:S(2)}) async-start(s16[16,48,640]{2,1,0:T(8,128)(2,1)} %bitcast.35), calls=%async_computation | async-start | bytes 1966080 | tf_op jit(solution)/shard_map/all_to_all | solution.py:403
  147.9 33.6 %collective-permute-start.25 = (s16[336,512]{1,0:T(8,128)(2,1)}, s16[336,512]{1,0:T(8,128)(2,1)S(1)}, u32[]{:S(2)}, u32[]{:S(2)}) collective-permute-start(s16[336,512]{1,0:T(8,128)(2,1)} %pad_add_fusion.5), channel_id=1, source_target_pairs={{0,12},{1,13},{2,14},{3,15},{4,8},{5,9},{6,10},{7,11},{8,4},{9,5},... | collective-permute-start | bytes 1032200 | tf_op jit(solution)/shard_map/ppermute | solution.py:43
  150.9 39.6 %collective-permute-start.24 = (s16[336,512]{1,0:T(8,128)(2,1)S(1)}, s16[336,512]{1,0:T(8,128)(2,1)S(1)}, u32[]{:S(2)}, u32[]{:S(2)}) collective-permute-start(s16[336,512]{1,0:T(8,128)(2,1)S(1)} %pad_add_fusion.4), channel_id=1, source_target_pairs={{0,8},{1,9},{2,10},{3,11},{4,12},{5,13},{6,14},{7,15},{8,0},{9,1},... | collective-permute-start | bytes 1032200 | tf_op jit(solution)/shard_map/ppermute | solution.py:43
  151.8 38.7 %collective-permute-start.23 = (s16[336,512]{1,0:T(8,128)(2,1)S(1)}, s16[336,512]{1,0:T(8,128)(2,1)S(1)}, u32[]{:S(2)}, u32[]{:S(2)}) collective-permute-start(s16[336,512]{1,0:T(8,128)(2,1)S(1)} %pad_add_fusion.3), channel_id=1, source_target_pairs={{0,4},{1,5},{2,6},{3,7},{4,0},{5,1},{6,2},{7,3},{8,12},{9,13},{10,... | collective-permute-start | bytes 1032200 | tf_op jit(solution)/shard_map/ppermute | solution.py:43
  161.8 18.6 %collective-permute-start.28 = (f32[48,512]{1,0:T(8,128)S(1)}, f32[48,512]{1,0:T(8,128)S(1)}, u32[]{:S(2)}, u32[]{:S(2)}) collective-permute-start(f32[48,512]{1,0:T(8,128)S(1)} %gathered.1), channel_id=1, source_target_pairs={{0,32},{1,33},{2,34},{3,35},{4,36},{5,37},{6,38},{7,39},{8,40},{9,... | collective-permute-start | bytes 294920 | tf_op jit(solution)/shard_map/ppermute | solution.py:43
  180.5 11.2 %collective-permute-start.29 = (f32[48,512]{1,0:T(8,128)S(1)}, f32[48,512]{1,0:T(8,128)S(1)}, u32[]{:S(2)}, u32[]{:S(2)}) collective-permute-start(f32[48,512]{1,0:T(8,128)S(1)} %add.45.own_ref), channel_id=1, source_target_pairs={{0,4},{1,5},{2,6},{3,7},{4,0},{5,1},{6,2},{7,3},{8,12},{9,13},{10,... | collective-permute-start | bytes 294920 | tf_op jit(solution)/shard_map/ppermute | solution.py:43
  180.6 12.0 %collective-permute-start.30 = (f32[48,512]{1,0:T(8,128)S(1)}, f32[48,512]{1,0:T(8,128)S(1)}, u32[]{:S(2)}, u32[]{:S(2)}) collective-permute-start(f32[48,512]{1,0:T(8,128)S(1)} %add.45.own_ref), channel_id=1, source_target_pairs={{0,8},{1,9},{2,10},{3,11},{4,12},{5,13},{6,14},{7,15},{8,0},{9,1},... | collective-permute-start | bytes 294920 | tf_op jit(solution)/shard_map/ppermute | solution.py:43
  181.4 11.2 %collective-permute-start.31 = (f32[48,512]{1,0:T(8,128)S(1)}, f32[48,512]{1,0:T(8,128)S(1)}, u32[]{:S(2)}, u32[]{:S(2)}) collective-permute-start(f32[48,512]{1,0:T(8,128)S(1)} %add.45.own_ref), channel_id=1, source_target_pairs={{0,12},{1,13},{2,14},{3,15},{4,8},{5,9},{6,10},{7,11},{8,4},{9,5},... | collective-permute-start | bytes 294920 | tf_op jit(solution)/shard_map/ppermute | solution.py:43
  214.5 4.1 %collective-permute-start.32 = (s16[768,640]{1,0:T(8,128)(2,1)S(1)}, s16[768,640]{1,0:T(8,128)(2,1)S(1)}, u32[]{:S(2)}, u32[]{:S(2)}) collective-permute-start(s16[768,640]{1,0:T(8,128)(2,1)S(1)} %bitcast.47), channel_id=1, source_target_pairs={{0,16},{1,17},{2,18},{3,19},{4,20},{5,21},{6,22},{7,23},{8,24},{9,... | collective-permute-start | bytes 2949128 | tf_op jit(solution)/shard_map/ppermute | solution.py:43
  (4 other events, 31.9 us)

commit v5 on v4

--- a/solution.py
+++ b/solution.py
@@ -140,11 +140,11 @@
             ref[...] = value
 
 
-def product(at, a4, own, other):
+def product(at, a4, own, other, first=0):
     shard, order = a4.shape[2], a4.shape[3]
-    panels, width = own.shape[2], own.shape[4]
+    panels, width = 1, own.shape[4]
     rows = 4 * shard
-    whole = pl.BlockSpec((4, 2, panels, shard, width), lambda g, s: (0, 0, 0, 0, 0))
+    whole = pl.BlockSpec((4, 2, panels, shard, width), lambda g, s: (0, 0, first, 0, 0))
     kept = pl.BlockSpec((rows, width), lambda g, s: (0, 0))
     coded = pl.BlockSpec((rows + EXTRA, width), lambda g, s: (0, 0))
     one = [jax.ShapeDtypeStruct((rows, width), F32)]
@@ -226,26 +226,29 @@
     )(at, *keeps, *sum(parts, []), *masked)
 
 
-def last_kernel(panels, own_ref, r1_ref, r2_ref, r3_ref, out_ref):
+def last_kernel(groups, *refs):
+    out_ref = refs[-1]
     shard = out_ref.shape[1]
-    for p in range(panels):
-        total = own_ref[p * shard : (p + 1) * shard, :]
-        for ref in (r1_ref, r2_ref, r3_ref):
-            total = total + decode(ref, p * (shard + EXTRA), shard)
-        out_ref[p] = -total
-
-
-def last(panels, own, parts):
-    rows, width = own.shape
-    return pl.pallas_call(
-        functools.partial(last_kernel, panels),
-        in_specs=[VMEM] * 4,
+    for g, which in enumerate(groups):
+        own_ref, *parts = refs[4 * g : 4 * g + 4]
+        for p, panel in enumerate(which):
+            total = own_ref[p * shard : (p + 1) * shard, :]
+            for ref in parts:
+                total = total + decode(ref, p * (shard + EXTRA), shard)
+            out_ref[panel] = -total
+
+
+def last(groups, shape):
+    ins = [ref for own, parts, _ in groups for ref in (own, *parts)]
+    return pl.pallas_call(
+        functools.partial(last_kernel, [which for _, _, which in groups]),
+        in_specs=[VMEM] * len(ins),
         out_specs=VMEM,
-        out_shape=jax.ShapeDtypeStruct((panels, rows // panels, width), F32),
-        compiler_params=params(),
-        cost_estimate=cost(8 * rows * width, 16 * rows * width),
+        out_shape=jax.ShapeDtypeStruct(shape, F32),
+        compiler_params=params(),
+        cost_estimate=cost(8 * shape[1] * shape[2], 16 * shape[1] * shape[2]),
         name="last",
-    )(own, *parts)
+    )(*ins)
 
 
 def encode_lanes(value, out_ref, start=0):
@@ -381,32 +384,32 @@
     ((keep_a, *coded),) = product(at, a4, own_a, send(own_a, over_core))
     parts_a = [send(coded[k - 1], over_y(k)) for k in (1, 2, 3)]
     own_b = after(jnp.stack(own_b), parts_a[0], parts_a[2])
-    outs = product(at, a4, own_b, send(own_b, over_core))
-    late = after(masked, own_b)
+    other_b = send(own_b, over_core)
+    ((keep_b, *coded),) = product(at, a4, own_b, other_b)
+    parts_b = [send(q, over_y(k)) for k, q in zip((1, 2, 3), after(coded, parts_a[0], parts_a[2]))]
+    ((keep_c, *coded),) = product(at, a4, own_b, other_b, 1)
+    parts_c = [send(q, over_y(k)) for k, q in zip((1, 2, 3), coded)]
+    late = after(masked, keep_c)
     beside = [masked] + [send(late, over_l(k)) for k in (1, 2, 3)]
-    pairs = [jnp.stack([outs[0][k], outs[1][k]]) for k in (1, 2, 3)]
-    pairs = after(pairs, parts_a)
-    pairs = [send(pairs[k - 1], over_y(k)) for k in (1, 2, 3)]
-    keeps, parts = [keep_a, outs[0][0], outs[1][0]], [parts_a]
-    own_2, *coded = middle(at, keeps[:1], parts[:1], beside, 2)
+    parts_b = after(parts_b, keep_c)
+    own_2, *coded = middle(at, [keep_a], [after(parts_a, parts_b)], beside, 2)
     coded_2, (mine_2, their_2) = coded[:3], coded[3:]
     swapped_2 = send(their_2, over_core)
-    pairs = after(pairs, mine_2)
-    parts = [[pair[p] for pair in pairs] for p in (0, 1)]
-    own_01, *coded = middle(at, keeps[1:], parts, beside, 0)
+    found_2 = [send(coded_2[k - 1], over_l(k)) for k in (1, 2, 3)]
+    parts_c = after(parts_c, mine_2)
+    own_01, *coded = middle(at, [keep_b, keep_c], [parts_b, parts_c], beside, 0)
     coded_01, (mine_01, their_01) = coded[:3], coded[3:]
     swapped_01 = send(their_01, over_core)
-    halves = fold([mine_01, mine_2], [swapped_01, swapped_2])
-    coded = [jnp.concatenate([a, b]) for a, b in zip(coded_01, coded_2)]
-    found = [send(coded[k - 1], over_l(k)) for k in (1, 2, 3)]
+    halves = fold([mine_01, after(mine_2, found_2)], [swapped_01, swapped_2])
+    found_01 = [send(coded_01[k - 1], over_l(k)) for k in (1, 2, 3)]
     pieces = halves.reshape(16, -1, width + LANES)
     total = gathered(lax.all_to_all(pieces, ("x", "y"), 0, 0))
-    found = after(found, total)
+    found_01 = after(found_01, total)
     total = total + send(total, over_h)
     beyond = [send(total, over_l(k)) for k in (1, 2, 3)]
-    blocks = last(3, jnp.concatenate([own_01, own_2]), found)
-    pieces = copies(total, after(beyond, blocks))
+    pieces = copies(total, after(beyond, found_01))
     mine = lax.all_to_all(pieces, ("x", "y"), 0, 0).reshape(halves.shape)
+    blocks = last([(own_01, found_01, (0, 1)), (own_2, found_2, (2,))], masked.shape)
     diagonal = finish(at, mine, send(mine, over_core), diag_inverse)
     return jnp.swapaxes(blocks, 0, 1), diagonal
 

time: 222 us -> 220 us (level)
  starting transfers between devices: 77.7 us -> 91 us
  waiting for transfers between devices: 87.9 us -> 77.2 us
  blocking collectives: 21.7 us -> 18.5 us
    ppermute x33 -> x39, starting transfers between devices: 73.7 us -> 87.1 us  [send(): return lax.ppermute(value, AXES, pairs)]
    ppermute x33 -> x39, waiting for transfers between devices: 78.2 us -> 68.4 us  [send(): return lax.ppermute(value, AXES, pairs)]
    all_to_all x1, blocking collectives: 21.7 us -> 18.5 us  [body(): mine = lax.all_to_all(pieces, ('x', 'y'), 0, 0).reshape(halves.shape)]
    pallas_call x2 -> x3, Pallas kernels: 14.9 us -> 15.1 us  [product(): pl.pallas_call(functools.partial(product_kernel, panels), grid_spec=pltpu...]
  transfers between devices with their start and end apart: 34 -> 40, of which waited for: 17 -> 17; matrix products, arithmetic and copies ran while one was open for 1% -> 1% of each run, Pallas kernels for 8% -> 8%
where the time goes in v5:
time: 220 us
  starting transfers between devices  91 us (41%)
  waiting for transfers between devices  77.2 us (35%)
  Pallas kernels  25.9 us (12%)
  blocking collectives  18.5 us (8%)
  local copies, waits for them, and re-layouts  3.43 us (2%)
  other arithmetic  2.64 us (1%)
    ppermute x39, starting transfers between devices, send(): return lax.ppermute(value, AXES, pairs)  87.1 us
    ppermute x39, waiting for transfers between devices, send(): return lax.ppermute(value, AXES, pairs)  68.4 us
    all_to_all x1, blocking collectives, body(): mine = lax.all_to_all(pieces, ('x', 'y'), 0, 0).reshape(halves.shape)  18.5 us
    pallas_call x3, Pallas kernels, product(): pl.pallas_call(functools.partial(product_kernel, panels), grid_spec=pltpu...  15.1 us
    all_to_all x1, waiting for transfers between devices, body(): total = gathered(lax.all_to_all(pieces, ('x', 'y'), 0, 0))  8.78 us
    pallas_call x2, Pallas kernels, middle(): pl.pallas_call(functools.partial(middle_kernel, panels, base), in_specs=[...  5.07 us
  transfers between devices with their start and end apart: 40, of which 17 were waited for; matrix products, arithmetic and copies ran while one was open for 1% of the time, Pallas kernels for 8%

profile of v5, /device:TPU:1, one launch (start us, length us, event | category | flops | bytes accessed | tf_op | source)
XLA Modules:
  0.0 219.6 jit_solution(701133061125430600)
XLA Ops:
  3.5 9.4 %collective-permute-start.5 = (bf16[1,96,512]{2,1,0:T(8,128)(2,1)S(1)}, bf16[1,96,512]{2,1,0:T(8,128)(2,1)S(1)}, u32[]{:S(2)}, u32[]{:S(2)}) collective-permute-start(bf16[1,96,512]{2,1,0:T(8,128)(2,1)S(1)} %collective-permute-done.3), channel_id=1, source_target_pairs={{0,32},{1,0},{2,48},{3,16},{4,36},{5,4},{6,52},{7,20},{8,40},{9,8}... | collective-permute-start | bytes 294920 | tf_op jit(solution)/shard_map/ppermute | solution.py:43
  15.6 4.8 %collective-permute-done.4 = bf16[1,96,512]{2,1,0:T(8,128)(2,1)S(1)} collective-permute-done((bf16[1,96,512]{2,1,0:T(8,128)(2,1)S(1)}, bf16[1,96,512]{2,1,0:T(8,128)(2,1)S(1)}, u32[]{:S(2)}, u32[]{:S(2)}) %collective-permute-start.4) | collective-permute-done | bytes 98336 | tf_op jit(solution)/shard_map/ppermute | solution.py:43
  20.4 11.0 %collective-permute-start.7 = (bf16[2,1,96,512]{3,2,0,1:T(8,128)(2,1)S(1)}, bf16[2,1,96,512]{3,2,0,1:T(8,128)(2,1)S(1)}, u32[]{:S(2)}, u32[]{:S(2)}) collective-permute-start(bf16[2,1,96,512]{3,2,0,1:T(8,128)(2,1)S(1)} %bitcast.35), channel_id=1, source_target_pairs={{0,128},{1,129},{2,130},{3,131},{4,132},{5,133},{6,134},{7,135},{8... | collective-permute-start | bytes 589832 | tf_op jit(solution)/shard_map/ppermute | solution.py:43
  36.7 2.8 %collective-permute-done.6 = bf16[2,1,96,512]{3,2,0,1:T(8,128)(2,1)S(1)} collective-permute-done((bf16[2,1,96,512]{3,2,0,1:T(8,128)(2,1)S(1)}, bf16[2,1,96,512]{3,2,0,1:T(8,128)(2,1)S(1)}, u32[]{:S(2)}, u32[]{:S(2)}) %collective-permute-start.6) | collective-permute-done | bytes 196640 | tf_op jit(solution)/shard_map/ppermute | solution.py:43
  39.8 6.8 %collective-permute-done.1 = bf16[2,96,512]{2,1,0:T(8,128)(2,1)S(1)} collective-permute-done((bf16[2,96,512]{2,1,0:T(8,128)(2,1)S(1)}, bf16[2,96,512]{2,1,0:T(8,128)(2,1)S(1)}, u32[]{:S(2)}, u32[]{:S(2)}) %collective-permute-start.1) | collective-permute-done | bytes 196640 | tf_op jit(solution)/shard_map/ppermute | solution.py:43
  46.6 9.6 %collective-permute-start.11 = (bf16[2,2,96,512]{3,2,1,0:T(8,128)(2,1)S(1)}, bf16[2,2,96,512]{3,2,1,0:T(8,128)(2,1)S(1)}, u32[]{:S(2)}, u32[]{:S(2)}) collective-permute-start(bf16[2,2,96,512]{3,2,1,0:T(8,128)(2,1)S(1)} %pad_maximum_fusion.2), channel_id=1, source_target_pairs={{0,192},{1,193},{2,194},{3,195},{4,196},{5,197},{6,198},{7,199},{8... | collective-permute-start | bytes 1179656 | tf_op jit(solution)/shard_map/ppermute | solution.py:43
  57.0 2.3 %copy-done = bf16[1536,1536]{1,0:T(8,128)(2,1)S(1)} copy-done((bf16[1536,1536]{1,0:T(8,128)(2,1)S(1)}, bf16[1536,1536]{1,0:T(8,128)(2,1)}, u32[]{:S(2)}) %copy-start) | copy-done | bytes 4718616
  59.4 5.0 %product.3 = (f32[384,512]{1,0:T(8,128)S(1)}, s16[400,512]{1,0:T(8,128)(2,1)S(1)}, s16[400,512]{1,0:T(8,128)(2,1)S(1)}, s16[400,512]{1,0:T(8,128)(2,1)S(1)}) custom-call(s32[6]{0:T(128)S(1)} %stack.75.at_ref.refs_0_, bf16[4,4,96,1536]{3,2,1,0:T(8,128)(2,1)S(1)} %bitcast.27, bf16[4,2,1,96,512]{4,3,2,1,0:T(8,128)(2,1)S(1)} %bitcast.32, ...), custom_call_target="tpu_custom_call" | custom-call | flops 2415919 | bytes 4718 | tf_op jit(solution)/shard_map/product/pallas_call | solution.py:152
  66.5 7.2 %collective-permute-done.11 = bf16[2,2,96,512]{3,2,1,0:T(8,128)(2,1)S(1)} collective-permute-done((bf16[2,2,96,512]{3,2,1,0:T(8,128)(2,1)S(1)}, bf16[2,2,96,512]{3,2,1,0:T(8,128)(2,1)S(1)}, u32[]{:S(2)}, u32[]{:S(2)}) %collective-permute-start.11) | collective-permute-done | bytes 393248 | tf_op jit(solution)/shard_map/ppermute | solution.py:43
  75.6 2.3 %collective-permute-start.15 = (bf16[4,2,2,96,512]{4,3,2,1,0:T(8,128)(2,1)S(1)}, bf16[4,2,2,96,512]{4,3,2,1,0:T(8,128)(2,1)S(1)}, u32[]{:S(2)}, u32[]{:S(2)}) collective-permute-start(bf16[4,2,2,96,512]{4,3,2,1,0:T(8,128)(2,1)S(1)} %pad_maximum_fusion.own_ref), channel_id=1, source_target_pairs={{0,16},{1,17},{2,18},{3,19},{4,20},{5,21},{6,22},{7,23},{8,24},{9,... | collective-permute-start | bytes 4718600 | tf_op jit(solution)/shard_map/ppermute | solution.py:43
  78.8 2.1 collective-permute-done.15.other_ref
  80.9 5.1 %product.4 = (f32[384,512]{1,0:T(8,128)S(1)}, s16[400,512]{1,0:T(8,128)(2,1)S(1)}, s16[400,512]{1,0:T(8,128)(2,1)S(1)}, s16[400,512]{1,0:T(8,128)(2,1)S(1)}) custom-call(s32[6]{0:T(128)S(1)} %stack.75.at_ref.refs_0_, bf16[4,4,96,1536]{3,2,1,0:T(8,128)(2,1)S(1)} %bitcast.28, bf16[4,2,2,96,512]{4,3,2,1,0:T(8,128)(2,1)S(1)} %pad_maximum_fusion.own_ref, ...), custom_call_target="tpu_custom_call" | custom-call | flops 2415919 | bytes 4718 | tf_op jit(solution)/shard_map/product/pallas_call | solution.py:152
  86.1 2.9 %collective-permute-start.17 = (s16[400,512]{1,0:T(8,128)(2,1)S(1)}, s16[400,512]{1,0:T(8,128)(2,1)S(1)}, u32[]{:S(2)}, u32[]{:S(2)}) collective-permute-start(s16[400,512]{1,0:T(8,128)(2,1)S(1)} %get-tuple-element.62), channel_id=1, source_target_pairs={{0,2},{1,3},{2,0},{3,1},{4,6},{5,7},{6,4},{7,5},{8,10},{9,11},{10,... | collective-permute-start | bytes 1228808 | tf_op jit(solution)/shard_map/ppermute | solution.py:43
  89.9 5.1 %product.5 = (f32[384,512]{1,0:T(8,128)S(1)}, s16[400,512]{1,0:T(8,128)(2,1)S(1)}, s16[400,512]{1,0:T(8,128)(2,1)S(1)}, s16[400,512]{1,0:T(8,128)(2,1)S(1)}) custom-call(s32[6]{0:T(128)S(1)} %stack.75.at_ref.refs_0_, bf16[4,4,96,1536]{3,2,1,0:T(8,128)(2,1)S(1)} %bitcast.29, bf16[4,2,2,96,512]{4,3,2,1,0:T(8,128)(2,1)S(1)} %pad_maximum_fusion.own_ref, ...), custom_call_target="tpu_custom_call" | custom-call | flops 2415919 | bytes 4718 | tf_op jit(solution)/shard_map/product/pallas_call | solution.py:152
  95.0 3.2 %collective-permute-start.25 = (bf16[3,96,512]{2,1,0:T(8,128)(2,1)S(1)}, bf16[3,96,512]{2,1,0:T(8,128)(2,1)S(1)}, u32[]{:S(2)}, u32[]{:S(2)}) collective-permute-start(bf16[3,96,512]{2,1,0:T(8,128)(2,1)S(1)} %bitcast_multiply_fusion.refs_5_.refs_9_), channel_id=1, source_target_pairs={{0,12},{1,13},{2,14},{3,15},{4,8},{5,9},{6,10},{7,11},{8,4},{9,5},... | collective-permute-start | bytes 884744 | tf_op jit(solution)/shard_map/ppermute | solution.py:43
  98.2 6.0 %collective-permute-done.25.refs_8_.refs_12_ = bf16[3,96,512]{2,1,0:T(8,128)(2,1)S(1)} collective-permute-done((bf16[3,96,512]{2,1,0:T(8,128)(2,1)S(1)}, bf16[3,96,512]{2,1,0:T(8,128)(2,1)S(1)}, u32[]{:S(2)}, u32[]{:S(2)}) %collective-permute-start.25) | collective-permute-done | bytes 294944 | tf_op jit(solution)/shard_map/ppermute | solution.py:43
  108.1 8.3 %collective-permute-start.24 = (bf16[3,96,512]{2,1,0:T(8,128)(2,1)S(1)}, bf16[3,96,512]{2,1,0:T(8,128)(2,1)S(1)}, u32[]{:S(2)}, u32[]{:S(2)}) collective-permute-start(bf16[3,96,512]{2,1,0:T(8,128)(2,1)S(1)} %bitcast_multiply_fusion.refs_5_.refs_9_), channel_id=1, source_target_pairs={{0,8},{1,9},{2,10},{3,11},{4,12},{5,13},{6,14},{7,15},{8,0},{9,1},... | collective-permute-start | bytes 884744 | tf_op jit(solution)/shard_map/ppermute | solution.py:43
  116.4 13.2 %collective-permute-done.24.refs_7_.refs_11_ = bf16[3,96,512]{2,1,0:T(8,128)(2,1)S(1)} collective-permute-done((bf16[3,96,512]{2,1,0:T(8,128)(2,1)S(1)}, bf16[3,96,512]{2,1,0:T(8,128)(2,1)S(1)}, u32[]{:S(2)}, u32[]{:S(2)}) %collective-permute-start.24) | collective-permute-done | bytes 294944 | tf_op jit(solution)/shard_map/ppermute | solution.py:43
  131.6 3.1 %middle.3 = (f32[192,512]{1,0:T(8,128)S(1)}, s16[224,512]{1,0:T(8,128)(2,1)S(1)}, s16[224,512]{1,0:T(8,128)(2,1)S(1)}, s16[224,512]{1,0:T(8,128)(2,1)S(1)}, f32[...) custom-call(s32[6]{0:T(128)S(1)} %stack.75.at_ref.refs_0_, f32[384,512]{1,0:T(8,128)S(1)} %get-tuple-element.56.refs_1_, ...), custom_call_target="tpu_custom_call" | custom-call | flops 603979 | bytes 3145 | tf_op jit(solution)/shard_map/middle/pallas_call | solution.py:215
  137.9 2.5 %collective-permute-start.30 = (s16[112,512]{1,0:T(8,128)(2,1)S(1)}, s16[112,512]{1,0:T(8,128)(2,1)S(1)}, u32[]{:S(2)}, u32[]{:S(2)}) collective-permute-start(s16[112,512]{1,0:T(8,128)(2,1)S(1)} %get-tuple-element.86), channel_id=1, source_target_pairs={{0,8},{1,9},{2,10},{3,11},{4,12},{5,13},{6,14},{7,15},{8,0},{9,1},... | collective-permute-start | bytes 344072 | tf_op jit(solution)/shard_map/ppermute | solution.py:43
  143.1 6.2 %collective-permute-done.31.refs_7_ = s16[112,512]{1,0:T(8,128)(2,1)S(1)} collective-permute-done((s16[112,512]{1,0:T(8,128)(2,1)S(1)}, s16[112,512]{1,0:T(8,128)(2,1)S(1)}, u32[]{:S(2)}, u32[]{:S(2)}) %collective-permute-start.31) | collective-permute-done | bytes 114720 | tf_op jit(solution)/shard_map/ppermute | solution.py:43
  150.8 3.9 %all-to-all-start = ((s16[16,48,640]{2,1,0:T(8,128)(2,1)}), s16[16,48,640]{2,1,0:T(8,128)(2,1)S(1)}, u32[]{:S(2)}, u32[]{:S(2)}) async-start(s16[16,48,640]{2,1,0:T(8,128)(2,1)} %bitcast.23), calls=%async_computation | async-start | bytes 1966080 | tf_op jit(solution)/shard_map/all_to_all | solution.py:406
  154.6 2.5 %collective-permute-start.26 = (s16[224,512]{1,0:T(8,128)(2,1)S(1)}, s16[224,512]{1,0:T(8,128)(2,1)S(1)}, u32[]{:S(2)}, u32[]{:S(2)}) collective-permute-start(s16[224,512]{1,0:T(8,128)(2,1)S(1)} %get-tuple-element.81), channel_id=1, source_target_pairs={{0,4},{1,5},{2,6},{3,7},{4,0},{5,1},{6,2},{7,3},{8,12},{9,13},{10,... | collective-permute-start | bytes 688136 | tf_op jit(solution)/shard_map/ppermute | solution.py:43
  157.2 2.0 collective-permute-start.27
  160.3 8.8 %all-to-all-done.in_ref = s16[16,48,640]{2,1,0:T(8,128)(2,1)S(1)} async-done(((s16[16,48,640]{2,1,0:T(8,128)(2,1)}), s16[16,48,640]{2,1,0:T(8,128)(2,1)S(1)}, u32[]{:S(2)}, u32[]{:S(2)}) %all-to-all-start) | async-done | bytes 983072 | tf_op jit(solution)/shard_map/all_to_all | solution.py:406
  170.6 6.2 %collective-permute-done.34 = f32[48,512]{1,0:T(8,128)S(1)} collective-permute-done((f32[48,512]{1,0:T(8,128)S(1)}, f32[48,512]{1,0:T(8,128)S(1)}, u32[]{:S(2)}, u32[]{:S(2)}) %collective-permute-start.34) | collective-permute-done | bytes 98336 | tf_op jit(solution)/shard_map/ppermute | solution.py:43
  176.9 3.1 %collective-permute-start.37 = (f32[48,512]{1,0:T(8,128)S(1)}, f32[48,512]{1,0:T(8,128)S(1)}, u32[]{:S(2)}, u32[]{:S(2)}) collective-permute-start(f32[48,512]{1,0:T(8,128)S(1)} %add.45.own_ref), channel_id=1, source_target_pairs={{0,12},{1,13},{2,14},{3,15},{4,8},{5,9},{6,10},{7,11},{8,4},{9,5},... | collective-permute-start | bytes 294920 | tf_op jit(solution)/shard_map/ppermute | solution.py:43
  180.0 3.0 %collective-permute-start.36 = (f32[48,512]{1,0:T(8,128)S(1)}, f32[48,512]{1,0:T(8,128)S(1)}, u32[]{:S(2)}, u32[]{:S(2)}) collective-permute-start(f32[48,512]{1,0:T(8,128)S(1)} %add.45.own_ref), channel_id=1, source_target_pairs={{0,8},{1,9},{2,10},{3,11},{4,12},{5,13},{6,14},{7,15},{8,0},{9,1},... | collective-permute-start | bytes 294920 | tf_op jit(solution)/shard_map/ppermute | solution.py:43
  183.2 8.1 %collective-permute-done.36.r2_ref = f32[48,512]{1,0:T(8,128)S(1)} collective-permute-done((f32[48,512]{1,0:T(8,128)S(1)}, f32[48,512]{1,0:T(8,128)S(1)}, u32[]{:S(2)}, u32[]{:S(2)}) %collective-permute-start.36) | collective-permute-done | bytes 98336 | tf_op jit(solution)/shard_map/ppermute | solution.py:43
  191.5 18.5 %all_to_all.10 = s16[16,48,640]{2,1,0:T(8,128)(2,1)S(1)} all-to-all(s16[16,48,640]{2,1,0:T(8,128)(2,1)S(1)} %copies.1), channel_id=1, replica_groups=mesh['x'=4,'h'=2,'core'=2,'l'=4,'y'=4] {'x','y'}, dimensions={0} | all-to-all | bytes 1966080 | tf_op jit(solution)/shard_map/all_to_all | solution.py:411
  210.0 4.6 %collective-permute-start.38 = (s16[768,640]{1,0:T(8,128)(2,1)S(1)}, s16[768,640]{1,0:T(8,128)(2,1)S(1)}, u32[]{:S(2)}, u32[]{:S(2)}) collective-permute-start(s16[768,640]{1,0:T(8,128)(2,1)S(1)} %bitcast.30), channel_id=1, source_target_pairs={{0,16},{1,17},{2,18},{3,19},{4,20},{5,21},{6,22},{7,23},{8,24},{9,... | collective-permute-start | bytes 2949128 | tf_op jit(solution)/shard_map/ppermute | solution.py:43
  216.8 2.7 %finish.1 = f32[3,512,512]{2,1,0:T(8,128)} custom-call(s32[6]{0:T(128)S(1)} %stack.75.at_ref.refs_0_, s16[768,640]{1,0:T(8,128)(2,1)S(1)} %bitcast.31, s16[768,640]{1,0:T(8,128)(2,1)S(1)} %collective-permute-done.38.theirs_ref, f32[3,512,512]{2,1,0:T(8,128)S(1)} %copy-done.1), custom_call_target="tpu_custom_call" | custom-call | flops 786 | bytes 9437 | tf_op jit(solution)/shard_map/finish/pallas_call | solution.py:345
  (75 shorter events, 36.2 us)
Async XLA Ops:
  3.5 12.0 %collective-permute-start.5 = (bf16[1,96,512]{2,1,0:T(8,128)(2,1)S(1)}, bf16[1,96,512]{2,1,0:T(8,128)(2,1)S(1)}, u32[]{:S(2)}, u32[]{:S(2)}) collective-permute-start(bf16[1,96,512]{2,1,0:T(8,128)(2,1)S(1)} %collective-permute-done.3), channel_id=1, source_target_pairs={{0,32},{1,0},{2,48},{3,16},{4,36},{5,4},{6,52},{7,20},{8,40},{9,8}... | collective-permute-start | bytes 294920 | tf_op jit(solution)/shard_map/ppermute | solution.py:43
  12.9 7.4 %collective-permute-start.4 = (bf16[1,96,512]{2,1,0:T(8,128)(2,1)S(1)}, bf16[1,96,512]{2,1,0:T(8,128)(2,1)S(1)}, u32[]{:S(2)}, u32[]{:S(2)}) collective-permute-start(bf16[1,96,512]{2,1,0:T(8,128)(2,1)S(1)} %collective-permute-done.3), channel_id=1, source_target_pairs={{0,0},{1,32},{2,16},{3,48},{4,4},{5,36},{6,20},{7,52},{8,8},{9,40}... | collective-permute-start | bytes 294920 | tf_op jit(solution)/shard_map/ppermute | solution.py:43
  20.4 16.3 %collective-permute-start.7 = (bf16[2,1,96,512]{3,2,0,1:T(8,128)(2,1)S(1)}, bf16[2,1,96,512]{3,2,0,1:T(8,128)(2,1)S(1)}, u32[]{:S(2)}, u32[]{:S(2)}) collective-permute-start(bf16[2,1,96,512]{3,2,0,1:T(8,128)(2,1)S(1)} %bitcast.35), channel_id=1, source_target_pairs={{0,128},{1,129},{2,130},{3,131},{4,132},{5,133},{6,134},{7,135},{8... | collective-permute-start | bytes 589832 | tf_op jit(solution)/shard_map/ppermute | solution.py:43
  31.4 8.1 %collective-permute-start.6 = (bf16[2,1,96,512]{3,2,0,1:T(8,128)(2,1)S(1)}, bf16[2,1,96,512]{3,2,0,1:T(8,128)(2,1)S(1)}, u32[]{:S(2)}, u32[]{:S(2)}) collective-permute-start(bf16[2,1,96,512]{3,2,0,1:T(8,128)(2,1)S(1)} %bitcast.36), channel_id=1, source_target_pairs={{0,64},{1,65},{2,66},{3,67},{4,68},{5,69},{6,70},{7,71},{8,72},{9,... | collective-permute-start | bytes 589832 | tf_op jit(solution)/shard_map/ppermute | solution.py:43
  32.4 7.4 %collective-permute-start.2 = (bf16[2,96,512]{2,1,0:T(8,128)(2,1)S(1)}, bf16[2,96,512]{2,1,0:T(8,128)(2,1)S(1)}, u32[]{:S(2)}, u32[]{:S(2)}) collective-permute-start(bf16[2,96,512]{2,1,0:T(8,128)(2,1)S(1)} %collective-permute-done), channel_id=1, source_target_pairs={{0,32},{1,0},{2,48},{3,16},{4,36},{5,4},{6,52},{7,20},{8,40},{9,8}... | collective-permute-start | bytes 589832 | tf_op jit(solution)/shard_map/ppermute | solution.py:43
  34.2 12.4 %collective-permute-start.1 = (bf16[2,96,512]{2,1,0:T(8,128)(2,1)S(1)}, bf16[2,96,512]{2,1,0:T(8,128)(2,1)S(1)}, u32[]{:S(2)}, u32[]{:S(2)}) collective-permute-start(bf16[2,96,512]{2,1,0:T(8,128)(2,1)S(1)} %collective-permute-done), channel_id=1, source_target_pairs={{0,0},{1,32},{2,16},{3,48},{4,4},{5,36},{6,20},{7,52},{8,8},{9,40}... | collective-permute-start | bytes 589832 | tf_op jit(solution)/shard_map/ppermute | solution.py:43
  46.6 10.4 %collective-permute-start.12 = (bf16[4,2,1,96,512]{4,3,1,2,0:T(8,128)(2,1)S(1)}, bf16[4,2,1,96,512]{4,3,1,2,0:T(8,128)(2,1)S(1)}, u32[]{:S(2)}, u32[]{:S(2)}) collective-permute-start(bf16[4,2,1,96,512]{4,3,1,2,0:T(8,128)(2,1)S(1)} %pad_maximum_fusion.1), channel_id=1, source_target_pairs={{0,16},{1,17},{2,18},{3,19},{4,20},{5,21},{6,22},{7,23},{8,24},{9,... | collective-permute-start | bytes 2359304 | tf_op jit(solution)/shard_map/ppermute | solution.py:43
  46.6 27.1 %collective-permute-start.11 = (bf16[2,2,96,512]{3,2,1,0:T(8,128)(2,1)S(1)}, bf16[2,2,96,512]{3,2,1,0:T(8,128)(2,1)S(1)}, u32[]{:S(2)}, u32[]{:S(2)}) collective-permute-start(bf16[2,2,96,512]{3,2,1,0:T(8,128)(2,1)S(1)} %pad_maximum_fusion.2), channel_id=1, source_target_pairs={{0,192},{1,193},{2,194},{3,195},{4,196},{5,197},{6,198},{7,199},{8... | collective-permute-start | bytes 1179656 | tf_op jit(solution)/shard_map/ppermute | solution.py:43
  56.3 17.5 %collective-permute-start.10 = (bf16[2,2,96,512]{3,2,1,0:T(8,128)(2,1)S(1)}, bf16[2,2,96,512]{3,2,1,0:T(8,128)(2,1)}, u32[]{:S(2)}, u32[]{:S(2)}) collective-permute-start(bf16[2,2,96,512]{3,2,1,0:T(8,128)(2,1)S(1)} %pad_maximum_fusion.2), channel_id=1, source_target_pairs={{0,128},{1,129},{2,130},{3,131},{4,132},{5,133},{6,134},{7,135},{8... | collective-permute-start | bytes 1179656 | tf_op jit(solution)/shard_map/ppermute | solution.py:43
  56.3 18.0 %collective-permute-start.9 = (bf16[2,2,96,512]{3,2,1,0:T(8,128)(2,1)S(1)}, bf16[2,2,96,512]{3,2,1,0:T(8,128)(2,1)}, u32[]{:S(2)}, u32[]{:S(2)}) collective-permute-start(bf16[2,2,96,512]{3,2,1,0:T(8,128)(2,1)S(1)} %pad_maximum_fusion.2), channel_id=1, source_target_pairs={{0,64},{1,65},{2,66},{3,67},{4,68},{5,69},{6,70},{7,71},{8,72},{9,... | collective-permute-start | bytes 1179656 | tf_op jit(solution)/shard_map/ppermute | solution.py:43
  64.4 11.2 %collective-permute-start.13 = (s16[400,512]{1,0:T(8,128)(2,1)S(1)}, s16[400,512]{1,0:T(8,128)(2,1)S(1)}, u32[]{:S(2)}, u32[]{:S(2)}) collective-permute-start(s16[400,512]{1,0:T(8,128)(2,1)S(1)} %get-tuple-element.53), channel_id=1, source_target_pairs={{0,1},{1,0},{2,3},{3,2},{4,5},{5,4},{6,7},{7,6},{8,9},{9,8},{10,11... | collective-permute-start | bytes 1228808 | tf_op jit(solution)/shard_map/ppermute | solution.py:43
  64.8 10.8 %collective-permute-start.14 = (s16[400,512]{1,0:T(8,128)(2,1)S(1)}, s16[400,512]{1,0:T(8,128)(2,1)S(1)}, u32[]{:S(2)}, u32[]{:S(2)}) collective-permute-start(s16[400,512]{1,0:T(8,128)(2,1)S(1)} %get-tuple-element.54), channel_id=1, source_target_pairs={{0,3},{1,2},{2,1},{3,0},{4,7},{5,6},{6,5},{7,4},{8,11},{9,10},{10,... | collective-permute-start | bytes 1228808 | tf_op jit(solution)/shard_map/ppermute | solution.py:43
  77.9 20.3 %collective-permute-start.22 = (s16[400,512]{1,0:T(8,128)(2,1)S(1)}, s16[400,512]{1,0:T(8,128)(2,1)S(1)}, u32[]{:S(2)}, u32[]{:S(2)}) collective-permute-start(s16[400,512]{1,0:T(8,128)(2,1)S(1)} %get-tuple-element.71), channel_id=1, source_target_pairs={{0,2},{1,3},{2,0},{3,1},{4,6},{5,7},{6,4},{7,5},{8,10},{9,11},{10,... | collective-permute-start | bytes 1228808 | tf_op jit(solution)/shard_map/ppermute | solution.py:43
  86.0 20.2 %collective-permute-start.16 = (s16[400,512]{1,0:T(8,128)(2,1)S(1)}, s16[400,512]{1,0:T(8,128)(2,1)S(1)}, u32[]{:S(2)}, u32[]{:S(2)}) collective-permute-start(s16[400,512]{1,0:T(8,128)(2,1)S(1)} %get-tuple-element.61), channel_id=1, source_target_pairs={{0,1},{1,0},{2,3},{3,2},{4,5},{5,4},{6,7},{7,6},{8,9},{9,8},{10,11... | collective-permute-start | bytes 1228808 | tf_op jit(solution)/shard_map/ppermute | solution.py:43
  86.1 22.0 %collective-permute-start.17 = (s16[400,512]{1,0:T(8,128)(2,1)S(1)}, s16[400,512]{1,0:T(8,128)(2,1)S(1)}, u32[]{:S(2)}, u32[]{:S(2)}) collective-permute-start(s16[400,512]{1,0:T(8,128)(2,1)S(1)} %get-tuple-element.62), channel_id=1, source_target_pairs={{0,2},{1,3},{2,0},{3,1},{4,6},{5,7},{6,4},{7,5},{8,10},{9,11},{10,... | collective-permute-start | bytes 1228808 | tf_op jit(solution)/shard_map/ppermute | solution.py:43
  89.0 27.4 %collective-permute-start.18 = (s16[400,512]{1,0:T(8,128)(2,1)S(1)}, s16[400,512]{1,0:T(8,128)(2,1)S(1)}, u32[]{:S(2)}, u32[]{:S(2)}) collective-permute-start(s16[400,512]{1,0:T(8,128)(2,1)S(1)} %get-tuple-element.63), channel_id=1, source_target_pairs={{0,3},{1,2},{2,1},{3,0},{4,7},{5,6},{6,5},{7,4},{8,11},{9,10},{10,... | collective-permute-start | bytes 1228808 | tf_op jit(solution)/shard_map/ppermute | solution.py:43
  95.0 9.2 %collective-permute-start.25 = (bf16[3,96,512]{2,1,0:T(8,128)(2,1)S(1)}, bf16[3,96,512]{2,1,0:T(8,128)(2,1)S(1)}, u32[]{:S(2)}, u32[]{:S(2)}) collective-permute-start(bf16[3,96,512]{2,1,0:T(8,128)(2,1)S(1)} %bitcast_multiply_fusion.refs_5_.refs_9_), channel_id=1, source_target_pairs={{0,12},{1,13},{2,14},{3,15},{4,8},{5,9},{6,10},{7,11},{8,4},{9,5},... | collective-permute-start | bytes 884744 | tf_op jit(solution)/shard_map/ppermute | solution.py:43
  98.2 33.4 %collective-permute-start.19 = (s16[400,512]{1,0:T(8,128)(2,1)S(1)}, s16[400,512]{1,0:T(8,128)(2,1)S(1)}, u32[]{:S(2)}, u32[]{:S(2)}) collective-permute-start(s16[400,512]{1,0:T(8,128)(2,1)S(1)} %get-tuple-element.67), channel_id=1, source_target_pairs={{0,1},{1,0},{2,3},{3,2},{4,5},{5,4},{6,7},{7,6},{8,9},{9,8},{10,11... | collective-permute-start | bytes 1228808 | tf_op jit(solution)/shard_map/ppermute | solution.py:43
  104.2 27.3 %collective-permute-start.20 = (s16[400,512]{1,0:T(8,128)(2,1)S(1)}, s16[400,512]{1,0:T(8,128)(2,1)S(1)}, u32[]{:S(2)}, u32[]{:S(2)}) collective-permute-start(s16[400,512]{1,0:T(8,128)(2,1)S(1)} %get-tuple-element.68), channel_id=1, source_target_pairs={{0,2},{1,3},{2,0},{3,1},{4,6},{5,7},{6,4},{7,5},{8,10},{9,11},{10,... | collective-permute-start | bytes 1228808 | tf_op jit(solution)/shard_map/ppermute | solution.py:43
  106.1 25.4 %collective-permute-start.21 = (s16[400,512]{1,0:T(8,128)(2,1)S(1)}, s16[400,512]{1,0:T(8,128)(2,1)S(1)}, u32[]{:S(2)}, u32[]{:S(2)}) collective-permute-start(s16[400,512]{1,0:T(8,128)(2,1)S(1)} %get-tuple-element.69), channel_id=1, source_target_pairs={{0,3},{1,2},{2,1},{3,0},{4,7},{5,6},{6,5},{7,4},{8,11},{9,10},{10,... | collective-permute-start | bytes 1228808 | tf_op jit(solution)/shard_map/ppermute | solution.py:43
  108.1 21.5 %collective-permute-start.24 = (bf16[3,96,512]{2,1,0:T(8,128)(2,1)S(1)}, bf16[3,96,512]{2,1,0:T(8,128)(2,1)S(1)}, u32[]{:S(2)}, u32[]{:S(2)}) collective-permute-start(bf16[3,96,512]{2,1,0:T(8,128)(2,1)S(1)} %bitcast_multiply_fusion.refs_5_.refs_9_), channel_id=1, source_target_pairs={{0,8},{1,9},{2,10},{3,11},{4,12},{5,13},{6,14},{7,15},{8,0},{9,1},... | collective-permute-start | bytes 884744 | tf_op jit(solution)/shard_map/ppermute | solution.py:43
  116.4 13.2 %collective-permute-start.23 = (bf16[3,96,512]{2,1,0:T(8,128)(2,1)S(1)}, bf16[3,96,512]{2,1,0:T(8,128)(2,1)S(1)}, u32[]{:S(2)}, u32[]{:S(2)}) collective-permute-start(bf16[3,96,512]{2,1,0:T(8,128)(2,1)S(1)} %bitcast_multiply_fusion.refs_5_.refs_9_), channel_id=1, source_target_pairs={{0,4},{1,5},{2,6},{3,7},{4,0},{5,1},{6,2},{7,3},{8,12},{9,13},{10,... | collective-permute-start | bytes 884744 | tf_op jit(solution)/shard_map/ppermute | solution.py:43
  134.7 14.7 %collective-permute-start.32 = (f32[512,512]{1,0:T(8,128)S(1)}, f32[512,512]{1,0:T(8,128)S(1)}, u32[]{:S(2)}, u32[]{:S(2)}) collective-permute-start(f32[512,512]{1,0:T(8,128)S(1)} %get-tuple-element.89), channel_id=1, source_target_pairs={{0,16},{1,17},{2,18},{3,19},{4,20},{5,21},{6,22},{7,23},{8,24},{9,... | collective-permute-start | bytes 3145736 | tf_op jit(solution)/shard_map/ppermute | solution.py:43
  136.6 12.7 %collective-permute-start.33 = (f32[256,512]{1,0:T(8,128)S(1)}, f32[256,512]{1,0:T(8,128)S(1)}, u32[]{:S(2)}, u32[]{:S(2)}) collective-permute-start(f32[256,512]{1,0:T(8,128)S(1)} %get-tuple-element.90), channel_id=1, source_target_pairs={{0,16},{1,17},{2,18},{3,19},{4,20},{5,21},{6,22},{7,23},{8,24},{9,... | collective-permute-start | bytes 1572872 | tf_op jit(solution)/shard_map/ppermute | solution.py:43
  140.4 9.0 %collective-permute-start.31 = (s16[112,512]{1,0:T(8,128)(2,1)S(1)}, s16[112,512]{1,0:T(8,128)(2,1)S(1)}, u32[]{:S(2)}, u32[]{:S(2)}) collective-permute-start(s16[112,512]{1,0:T(8,128)(2,1)S(1)} %get-tuple-element.87), channel_id=1, source_target_pairs={{0,12},{1,13},{2,14},{3,15},{4,8},{5,9},{6,10},{7,11},{8,4},{9,5},... | collective-permute-start | bytes 344072 | tf_op jit(solution)/shard_map/ppermute | solution.py:43
  150.8 18.3 %all-to-all-start = ((s16[16,48,640]{2,1,0:T(8,128)(2,1)}), s16[16,48,640]{2,1,0:T(8,128)(2,1)S(1)}, u32[]{:S(2)}, u32[]{:S(2)}) async-start(s16[16,48,640]{2,1,0:T(8,128)(2,1)} %bitcast.23), calls=%async_computation | async-start | bytes 1966080 | tf_op jit(solution)/shard_map/all_to_all | solution.py:406
  154.6 28.4 %collective-permute-start.26 = (s16[224,512]{1,0:T(8,128)(2,1)S(1)}, s16[224,512]{1,0:T(8,128)(2,1)S(1)}, u32[]{:S(2)}, u32[]{:S(2)}) collective-permute-start(s16[224,512]{1,0:T(8,128)(2,1)S(1)} %get-tuple-element.81), channel_id=1, source_target_pairs={{0,4},{1,5},{2,6},{3,7},{4,0},{5,1},{6,2},{7,3},{8,12},{9,13},{10,... | collective-permute-start | bytes 688136 | tf_op jit(solution)/shard_map/ppermute | solution.py:43
  157.2 26.1 %collective-permute-start.27 = (s16[224,512]{1,0:T(8,128)(2,1)S(1)}, s16[224,512]{1,0:T(8,128)(2,1)S(1)}, u32[]{:S(2)}, u32[]{:S(2)}) collective-permute-start(s16[224,512]{1,0:T(8,128)(2,1)S(1)} %get-tuple-element.82), channel_id=1, source_target_pairs={{0,8},{1,9},{2,10},{3,11},{4,12},{5,13},{6,14},{7,15},{8,0},{9,1},... | collective-permute-start | bytes 688136 | tf_op jit(solution)/shard_map/ppermute | solution.py:43
  159.2 24.1 %collective-permute-start.28 = (s16[224,512]{1,0:T(8,128)(2,1)S(1)}, s16[224,512]{1,0:T(8,128)(2,1)S(1)}, u32[]{:S(2)}, u32[]{:S(2)}) collective-permute-start(s16[224,512]{1,0:T(8,128)(2,1)S(1)} %get-tuple-element.83), channel_id=1, source_target_pairs={{0,12},{1,13},{2,14},{3,15},{4,8},{5,9},{6,10},{7,11},{8,4},{9,5},... | collective-permute-start | bytes 688136 | tf_op jit(solution)/shard_map/ppermute | solution.py:43
  169.3 7.6 %collective-permute-start.34 = (f32[48,512]{1,0:T(8,128)S(1)}, f32[48,512]{1,0:T(8,128)S(1)}, u32[]{:S(2)}, u32[]{:S(2)}) collective-permute-start(f32[48,512]{1,0:T(8,128)S(1)} %gathered.1), channel_id=1, source_target_pairs={{0,32},{1,33},{2,34},{3,35},{4,36},{5,37},{6,38},{7,39},{8,40},{9,... | collective-permute-start | bytes 294920 | tf_op jit(solution)/shard_map/ppermute | solution.py:43
  180.0 11.3 %collective-permute-start.36 = (f32[48,512]{1,0:T(8,128)S(1)}, f32[48,512]{1,0:T(8,128)S(1)}, u32[]{:S(2)}, u32[]{:S(2)}) collective-permute-start(f32[48,512]{1,0:T(8,128)S(1)} %add.45.own_ref), channel_id=1, source_target_pairs={{0,8},{1,9},{2,10},{3,11},{4,12},{5,13},{6,14},{7,15},{8,0},{9,1},... | collective-permute-start | bytes 294920 | tf_op jit(solution)/shard_map/ppermute | solution.py:43
  183.0 8.3 %collective-permute-start.35 = (f32[48,512]{1,0:T(8,128)S(1)}, f32[48,512]{1,0:T(8,128)S(1)}, u32[]{:S(2)}, u32[]{:S(2)}) collective-permute-start(f32[48,512]{1,0:T(8,128)S(1)} %add.45.own_ref), channel_id=1, source_target_pairs={{0,4},{1,5},{2,6},{3,7},{4,0},{5,1},{6,2},{7,3},{8,12},{9,13},{10,... | collective-permute-start | bytes 294920 | tf_op jit(solution)/shard_map/ppermute | solution.py:43
  (10 other events, 69.6 us)

commit v6 on v5

--- a/solution.py
+++ b/solution.py
@@ -383,14 +383,15 @@
     own_b = gather(after(jnp.stack(turned_b), own_a))
     ((keep_a, *coded),) = product(at, a4, own_a, send(own_a, over_core))
     parts_a = [send(coded[k - 1], over_y(k)) for k in (1, 2, 3)]
+    far = send(after(masked, own_a), over_l(2))
     own_b = after(jnp.stack(own_b), parts_a[0], parts_a[2])
     other_b = send(own_b, over_core)
     ((keep_b, *coded),) = product(at, a4, own_b, other_b)
     parts_b = [send(q, over_y(k)) for k, q in zip((1, 2, 3), after(coded, parts_a[0], parts_a[2]))]
-    ((keep_c, *coded),) = product(at, a4, own_b, other_b, 1)
+    ((keep_c, *coded),) = product(after(at, far), a4, own_b, other_b, 1)
     parts_c = [send(q, over_y(k)) for k, q in zip((1, 2, 3), coded)]
     late = after(masked, keep_c)
-    beside = [masked] + [send(late, over_l(k)) for k in (1, 2, 3)]
+    beside = [masked, send(late, over_l(1)), far, send(late, over_l(3))]
     parts_b = after(parts_b, keep_c)
     own_2, *coded = middle(at, [keep_a], [after(parts_a, parts_b)], beside, 2)
     coded_2, (mine_2, their_2) = coded[:3], coded[3:]
@@ -400,7 +401,7 @@
     own_01, *coded = middle(at, [keep_b, keep_c], [parts_b, parts_c], beside, 0)
     coded_01, (mine_01, their_01) = coded[:3], coded[3:]
     swapped_01 = send(their_01, over_core)
-    halves = fold([mine_01, after(mine_2, found_2)], [swapped_01, swapped_2])
+    halves = fold([mine_01, mine_2], [swapped_01, swapped_2])
     found_01 = [send(coded_01[k - 1], over_l(k)) for k in (1, 2, 3)]
     pieces = halves.reshape(16, -1, width + LANES)
     total = gathered(lax.all_to_all(pieces, ("x", "y"), 0, 0))
@@ -408,7 +409,7 @@
     total = total + send(total, over_h)
     beyond = [send(total, over_l(k)) for k in (1, 2, 3)]
     pieces = copies(total, after(beyond, found_01))
-    mine = lax.all_to_all(pieces, ("x", "y"), 0, 0).reshape(halves.shape)
+    mine = after(lax.all_to_all(pieces, ("x", "y"), 0, 0), found_2).reshape(halves.shape)
     blocks = last([(own_01, found_01, (0, 1)), (own_2, found_2, (2,))], masked.shape)
     diagonal = finish(at, mine, send(mine, over_core), diag_inverse)
     return jnp.swapaxes(blocks, 0, 1), diagonal

time: 220 us -> 213 us (0.968)
  blocking collectives: 18.5 us -> 0 us
  waiting for transfers between devices: 77.2 us -> 91.9 us
  starting transfers between devices: 91 us -> 84.4 us
    all_to_all x1 -> x0, blocking collectives: 18.5 us -> none  [body(): mine = lax.all_to_all(pieces, ('x', 'y'), 0, 0).reshape(halves.shape)]
    ppermute x39, starting transfers between devices: 87.1 us -> 74.7 us  [send(): return lax.ppermute(value, AXES, pairs)]
    ppermute x39, waiting for transfers between devices: 68.4 us -> 74.8 us  [send(): return lax.ppermute(value, AXES, pairs)]
    all_to_all x0 -> x1, starting transfers between devices: none -> 6.09 us  [body(): lax.all_to_all(pieces, ('x', 'y'), 0, 0)]
    all_to_all x0 -> x1, waiting for transfers between devices: none -> 5.04 us  [body(): lax.all_to_all(pieces, ('x', 'y'), 0, 0)]
    all_to_all x1, waiting for transfers between devices: 8.78 us -> 12 us  [body(): total = gathered(lax.all_to_all(pieces, ('x', 'y'), 0, 0))]
  transfers between devices with their start and end apart: 40 -> 41, of which waited for: 17 -> 22; matrix products, arithmetic and copies ran while one was open for 1% -> 1% of each run, Pallas kernels for 8% -> 9%
where the time goes in v6:
time: 213 us; the launch traced here: 212 us
  waiting for transfers between devices  91.9 us (43%)
  starting transfers between devices  84.4 us (40%)
  Pallas kernels  26.9 us (13%)
  local copies, waits for them, and re-layouts  5.31 us (2%)
  other arithmetic  2.64 us (1%)
    ppermute x39, waiting for transfers between devices, send(): return lax.ppermute(value, AXES, pairs)  74.8 us
    ppermute x39, starting transfers between devices, send(): return lax.ppermute(value, AXES, pairs)  74.7 us
    pallas_call x3, Pallas kernels, product(): pl.pallas_call(functools.partial(product_kernel, panels), grid_spec=pltpu...  15.1 us
    all_to_all x1, waiting for transfers between devices, body(): total = gathered(lax.all_to_all(pieces, ('x', 'y'), 0, 0))  12 us
    all_to_all x1, starting transfers between devices, body(): lax.all_to_all(pieces, ('x', 'y'), 0, 0)  6.09 us
    pallas_call x2, Pallas kernels, middle(): pl.pallas_call(functools.partial(middle_kernel, panels, base), in_specs=[...  5.06 us
    all_to_all x1, waiting for transfers between devices, body(): lax.all_to_all(pieces, ('x', 'y'), 0, 0)  5.04 us
  transfers between devices with their start and end apart: 41, of which 22 were waited for; matrix products, arithmetic and copies ran while one was open for 1% of the time, Pallas kernels for 9%

profile of v6, /device:TPU:1, one launch (start us, length us, event | category | flops | bytes accessed | tf_op | source)
XLA Modules:
  0.0 212.1 jit_solution(14818363626520507904)
XLA Ops:
  3.5 9.4 %collective-permute-start.5 = (bf16[1,96,512]{2,1,0:T(8,128)(2,1)S(1)}, bf16[1,96,512]{2,1,0:T(8,128)(2,1)S(1)}, u32[]{:S(2)}, u32[]{:S(2)}) collective-permute-start(bf16[1,96,512]{2,1,0:T(8,128)(2,1)S(1)} %collective-permute-done.3), channel_id=1, source_target_pairs={{0,32},{1,0},{2,48},{3,16},{4,36},{5,4},{6,52},{7,20},{8,40},{9,8}... | collective-permute-start | bytes 294920 | tf_op jit(solution)/shard_map/ppermute | solution.py:43
  15.6 4.8 %collective-permute-done.4 = bf16[1,96,512]{2,1,0:T(8,128)(2,1)S(1)} collective-permute-done((bf16[1,96,512]{2,1,0:T(8,128)(2,1)S(1)}, bf16[1,96,512]{2,1,0:T(8,128)(2,1)S(1)}, u32[]{:S(2)}, u32[]{:S(2)}) %collective-permute-start.4) | collective-permute-done | bytes 98336 | tf_op jit(solution)/shard_map/ppermute | solution.py:43
  20.4 11.0 %collective-permute-start.7 = (bf16[2,1,96,512]{3,2,0,1:T(8,128)(2,1)S(1)}, bf16[2,1,96,512]{3,2,0,1:T(8,128)(2,1)S(1)}, u32[]{:S(2)}, u32[]{:S(2)}) collective-permute-start(bf16[2,1,96,512]{3,2,0,1:T(8,128)(2,1)S(1)} %bitcast.35), channel_id=1, source_target_pairs={{0,128},{1,129},{2,130},{3,131},{4,132},{5,133},{6,134},{7,135},{8... | collective-permute-start | bytes 589832 | tf_op jit(solution)/shard_map/ppermute | solution.py:43
  36.7 2.8 %collective-permute-done.6 = bf16[2,1,96,512]{3,2,0,1:T(8,128)(2,1)S(1)} collective-permute-done((bf16[2,1,96,512]{3,2,0,1:T(8,128)(2,1)S(1)}, bf16[2,1,96,512]{3,2,0,1:T(8,128)(2,1)S(1)}, u32[]{:S(2)}, u32[]{:S(2)}) %collective-permute-start.6) | collective-permute-done | bytes 196640 | tf_op jit(solution)/shard_map/ppermute | solution.py:43
  39.8 6.8 %collective-permute-done.1 = bf16[2,96,512]{2,1,0:T(8,128)(2,1)S(1)} collective-permute-done((bf16[2,96,512]{2,1,0:T(8,128)(2,1)S(1)}, bf16[2,96,512]{2,1,0:T(8,128)(2,1)S(1)}, u32[]{:S(2)}, u32[]{:S(2)}) %collective-permute-start.1) | collective-permute-done | bytes 196640 | tf_op jit(solution)/shard_map/ppermute | solution.py:43
  46.6 9.6 %collective-permute-start.11 = (bf16[2,2,96,512]{3,2,1,0:T(8,128)(2,1)S(1)}, bf16[2,2,96,512]{3,2,1,0:T(8,128)(2,1)S(1)}, u32[]{:S(2)}, u32[]{:S(2)}) collective-permute-start(bf16[2,2,96,512]{3,2,1,0:T(8,128)(2,1)S(1)} %pad_maximum_fusion.2), channel_id=1, source_target_pairs={{0,192},{1,193},{2,194},{3,195},{4,196},{5,197},{6,198},{7,199},{8... | collective-permute-start | bytes 1179656 | tf_op jit(solution)/shard_map/ppermute | solution.py:43
  57.0 2.3 %copy-done = bf16[1536,1536]{1,0:T(8,128)(2,1)S(1)} copy-done((bf16[1536,1536]{1,0:T(8,128)(2,1)S(1)}, bf16[1536,1536]{1,0:T(8,128)(2,1)}, u32[]{:S(2)}) %copy-start) | copy-done | bytes 4718616
  59.4 5.0 %product.3 = (f32[384,512]{1,0:T(8,128)S(1)}, s16[400,512]{1,0:T(8,128)(2,1)S(1)}, s16[400,512]{1,0:T(8,128)(2,1)S(1)}, s16[400,512]{1,0:T(8,128)(2,1)S(1)}) custom-call(s32[6]{0:T(128)S(1)} %stack.75.at_ref.refs_0_, bf16[4,4,96,1536]{3,2,1,0:T(8,128)(2,1)S(1)} %bitcast.27, bf16[4,2,1,96,512]{4,3,2,1,0:T(8,128)(2,1)S(1)} %bitcast.32, ...), custom_call_target="tpu_custom_call" | custom-call | flops 2415919 | bytes 4718 | tf_op jit(solution)/shard_map/product/pallas_call | solution.py:152
  66.5 7.2 %collective-permute-done.11 = bf16[2,2,96,512]{3,2,1,0:T(8,128)(2,1)S(1)} collective-permute-done((bf16[2,2,96,512]{3,2,1,0:T(8,128)(2,1)S(1)}, bf16[2,2,96,512]{3,2,1,0:T(8,128)(2,1)S(1)}, u32[]{:S(2)}, u32[]{:S(2)}) %collective-permute-start.11) | collective-permute-done | bytes 393248 | tf_op jit(solution)/shard_map/ppermute | solution.py:43
  75.6 2.3 %collective-permute-start.15 = (bf16[4,2,2,96,512]{4,3,2,1,0:T(8,128)(2,1)S(1)}, bf16[4,2,2,96,512]{4,3,2,1,0:T(8,128)(2,1)S(1)}, u32[]{:S(2)}, u32[]{:S(2)}) collective-permute-start(bf16[4,2,2,96,512]{4,3,2,1,0:T(8,128)(2,1)S(1)} %pad_maximum_fusion.own_ref), channel_id=1, source_target_pairs={{0,16},{1,17},{2,18},{3,19},{4,20},{5,21},{6,22},{7,23},{8,24},{9,... | collective-permute-start | bytes 4718600 | tf_op jit(solution)/shard_map/ppermute | solution.py:43
  78.8 2.1 collective-permute-done.15.other_ref
  80.9 5.1 %product.4 = (f32[384,512]{1,0:T(8,128)S(1)}, s16[400,512]{1,0:T(8,128)(2,1)S(1)}, s16[400,512]{1,0:T(8,128)(2,1)S(1)}, s16[400,512]{1,0:T(8,128)(2,1)S(1)}) custom-call(s32[6]{0:T(128)S(1)} %stack.75.at_ref.refs_0_, bf16[4,4,96,1536]{3,2,1,0:T(8,128)(2,1)S(1)} %bitcast.28, bf16[4,2,2,96,512]{4,3,2,1,0:T(8,128)(2,1)S(1)} %pad_maximum_fusion.own_ref, ...), custom_call_target="tpu_custom_call" | custom-call | flops 2415919 | bytes 4718 | tf_op jit(solution)/shard_map/product/pallas_call | solution.py:152
  86.1 4.0 %collective-permute-start.16 = (bf16[3,96,512]{2,1,0:T(8,128)(2,1)S(1)}, bf16[3,96,512]{2,1,0:T(8,128)(2,1)S(1)}, u32[]{:S(2)}, u32[]{:S(2)}) collective-permute-start(bf16[3,96,512]{2,1,0:T(8,128)(2,1)S(1)} %bitcast_multiply_fusion.refs_5_.refs_9_), channel_id=1, source_target_pairs={{0,8},{1,9},{2,10},{3,11},{4,12},{5,13},{6,14},{7,15},{8,0},{9,1},... | collective-permute-start | bytes 884744 | tf_op jit(solution)/shard_map/ppermute | solution.py:43
  90.1 3.6 %collective-permute-start.18 = (s16[400,512]{1,0:T(8,128)(2,1)S(1)}, s16[400,512]{1,0:T(8,128)(2,1)S(1)}, u32[]{:S(2)}, u32[]{:S(2)}) collective-permute-start(s16[400,512]{1,0:T(8,128)(2,1)S(1)} %get-tuple-element.66), channel_id=1, source_target_pairs={{0,2},{1,3},{2,0},{3,1},{4,6},{5,7},{6,4},{7,5},{8,10},{9,11},{10,... | collective-permute-start | bytes 1228808 | tf_op jit(solution)/shard_map/ppermute | solution.py:43
  93.6 9.6 %collective-permute-done.16.refs_7_.refs_11_ = bf16[3,96,512]{2,1,0:T(8,128)(2,1)S(1)} collective-permute-done((bf16[3,96,512]{2,1,0:T(8,128)(2,1)S(1)}, bf16[3,96,512]{2,1,0:T(8,128)(2,1)S(1)}, u32[]{:S(2)}, u32[]{:S(2)}) %collective-permute-start.16) | collective-permute-done | bytes 294944 | tf_op jit(solution)/shard_map/ppermute | solution.py:43
  103.3 5.1 %product.5 = (f32[384,512]{1,0:T(8,128)S(1)}, s16[400,512]{1,0:T(8,128)(2,1)S(1)}, s16[400,512]{1,0:T(8,128)(2,1)S(1)}, s16[400,512]{1,0:T(8,128)(2,1)S(1)}) custom-call(s32[6]{0:T(128)S(1)} %stack.75.at_ref.refs_0_, bf16[4,4,96,1536]{3,2,1,0:T(8,128)(2,1)S(1)} %bitcast.29, bf16[4,2,2,96,512]{4,3,2,1,0:T(8,128)(2,1)S(1)} %pad_maximum_fusion.own_ref, ...), custom_call_target="tpu_custom_call" | custom-call | flops 2415919 | bytes 4718 | tf_op jit(solution)/shard_map/product/pallas_call | solution.py:152
  109.6 2.7 %collective-permute-start.21 = (s16[400,512]{1,0:T(8,128)(2,1)S(1)}, s16[400,512]{1,0:T(8,128)(2,1)S(1)}, u32[]{:S(2)}, u32[]{:S(2)}) collective-permute-start(s16[400,512]{1,0:T(8,128)(2,1)S(1)} %get-tuple-element.72), channel_id=1, source_target_pairs={{0,2},{1,3},{2,0},{3,1},{4,6},{5,7},{6,4},{7,5},{8,10},{9,11},{10,... | collective-permute-start | bytes 1228808 | tf_op jit(solution)/shard_map/ppermute | solution.py:43
  114.0 7.6 %collective-permute-done.25.refs_8_.refs_12_ = bf16[3,96,512]{2,1,0:T(8,128)(2,1)S(1)} collective-permute-done((bf16[3,96,512]{2,1,0:T(8,128)(2,1)S(1)}, bf16[3,96,512]{2,1,0:T(8,128)(2,1)S(1)}, u32[]{:S(2)}, u32[]{:S(2)}) %collective-permute-start.25) | collective-permute-done | bytes 294944 | tf_op jit(solution)/shard_map/ppermute | solution.py:43
  121.6 7.4 %collective-permute-done.24.refs_6_.refs_10_ = bf16[3,96,512]{2,1,0:T(8,128)(2,1)S(1)} collective-permute-done((bf16[3,96,512]{2,1,0:T(8,128)(2,1)S(1)}, bf16[3,96,512]{2,1,0:T(8,128)(2,1)S(1)}, u32[]{:S(2)}, u32[]{:S(2)}) %collective-permute-start.24) | collective-permute-done | bytes 294944 | tf_op jit(solution)/shard_map/ppermute | solution.py:43
  129.0 2.0 middle.2
  132.2 3.1 %middle.3 = (f32[192,512]{1,0:T(8,128)S(1)}, s16[224,512]{1,0:T(8,128)(2,1)S(1)}, s16[224,512]{1,0:T(8,128)(2,1)S(1)}, s16[224,512]{1,0:T(8,128)(2,1)S(1)}, f32[...) custom-call(s32[6]{0:T(128)S(1)} %stack.75.at_ref.refs_0_, f32[384,512]{1,0:T(8,128)S(1)} %get-tuple-element.58.refs_1_, ...), custom_call_target="tpu_custom_call" | custom-call | flops 603979 | bytes 3145 | tf_op jit(solution)/shard_map/middle/pallas_call | solution.py:215
  135.3 2.0 collective-permute-start.29
  137.5 2.9 %collective-permute-done.30.refs_3_ = f32[256,512]{1,0:T(8,128)S(1)} collective-permute-done((f32[256,512]{1,0:T(8,128)S(1)}, f32[256,512]{1,0:T(8,128)S(1)}, u32[]{:S(2)}, u32[]{:S(2)}) %collective-permute-start.30) | collective-permute-done | bytes 524320 | tf_op jit(solution)/shard_map/ppermute | solution.py:43
  141.8 3.6 %all-to-all-start = ((s16[16,48,640]{2,1,0:T(8,128)(2,1)}), s16[16,48,640]{2,1,0:T(8,128)(2,1)S(1)}, u32[]{:S(2)}, u32[]{:S(2)}) async-start(s16[16,48,640]{2,1,0:T(8,128)(2,1)} %bitcast.23), calls=%async_computation | async-start | bytes 1966080 | tf_op jit(solution)/shard_map/all_to_all | solution.py:407
  149.1 12.0 %all-to-all-done.in_ref = s16[16,48,640]{2,1,0:T(8,128)(2,1)S(1)} async-done(((s16[16,48,640]{2,1,0:T(8,128)(2,1)}), s16[16,48,640]{2,1,0:T(8,128)(2,1)S(1)}, u32[]{:S(2)}, u32[]{:S(2)}) %all-to-all-start) | async-done | bytes 983072 | tf_op jit(solution)/shard_map/all_to_all | solution.py:407
  162.5 6.8 %collective-permute-done.34 = f32[48,512]{1,0:T(8,128)S(1)} collective-permute-done((f32[48,512]{1,0:T(8,128)S(1)}, f32[48,512]{1,0:T(8,128)S(1)}, u32[]{:S(2)}, u32[]{:S(2)}) %collective-permute-start.34) | collective-permute-done | bytes 98336 | tf_op jit(solution)/shard_map/ppermute | solution.py:43
  174.9 5.7 %collective-permute-done.36.r2_ref = f32[48,512]{1,0:T(8,128)S(1)} collective-permute-done((f32[48,512]{1,0:T(8,128)S(1)}, f32[48,512]{1,0:T(8,128)S(1)}, u32[]{:S(2)}, u32[]{:S(2)}) %collective-permute-start.36) | collective-permute-done | bytes 98336 | tf_op jit(solution)/shard_map/ppermute | solution.py:43
  181.8 6.1 %all-to-all-start.1 = ((s16[16,48,640]{2,1,0:T(8,128)(2,1)}), s16[16,48,640]{2,1,0:T(8,128)(2,1)S(1)}, u32[]{:S(2)}, u32[]{:S(2)}) async-start(s16[16,48,640]{2,1,0:T(8,128)(2,1)} %copies.1), calls=%async_computation.1 | async-start | bytes 1966080 | tf_op jit(solution)/shard_map/all_to_all | solution.py:412
  193.2 3.8 %collective-permute-done.33.refs_7_ = s16[112,512]{1,0:T(8,128)(2,1)S(1)} collective-permute-done((s16[112,512]{1,0:T(8,128)(2,1)S(1)}, s16[112,512]{1,0:T(8,128)(2,1)S(1)}, u32[]{:S(2)}, u32[]{:S(2)}) %collective-permute-start.33) | collective-permute-done | bytes 114720 | tf_op jit(solution)/shard_map/ppermute | solution.py:43
  197.0 5.0 %all-to-all-done.1 = s16[16,48,640]{2,1,0:T(8,128)(2,1)S(1)} async-done(((s16[16,48,640]{2,1,0:T(8,128)(2,1)}), s16[16,48,640]{2,1,0:T(8,128)(2,1)S(1)}, u32[]{:S(2)}, u32[]{:S(2)}) %all-to-all-start.1) | async-done | bytes 983072 | tf_op jit(solution)/shard_map/all_to_all | solution.py:412
  202.0 3.2 %collective-permute-start.38 = (s16[768,640]{1,0:T(8,128)(2,1)S(1)}, s16[768,640]{1,0:T(8,128)(2,1)S(1)}, u32[]{:S(2)}, u32[]{:S(2)}) collective-permute-start(s16[768,640]{1,0:T(8,128)(2,1)S(1)} %bitcast.30), channel_id=1, source_target_pairs={{0,16},{1,17},{2,18},{3,19},{4,20},{5,21},{6,22},{7,23},{8,24},{9,... | collective-permute-start | bytes 2949128 | tf_op jit(solution)/shard_map/ppermute | solution.py:43
  209.3 2.7 %finish.1 = f32[3,512,512]{2,1,0:T(8,128)} custom-call(s32[6]{0:T(128)S(1)} %stack.75.at_ref.refs_0_, s16[768,640]{1,0:T(8,128)(2,1)S(1)} %bitcast.31, s16[768,640]{1,0:T(8,128)(2,1)S(1)} %collective-permute-done.38.theirs_ref, f32[3,512,512]{2,1,0:T(8,128)S(1)} %copy-done.1), custom_call_target="tpu_custom_call" | custom-call | flops 786 | bytes 9437 | tf_op jit(solution)/shard_map/finish/pallas_call | solution.py:345
  (76 shorter events, 43.6 us)
Async XLA Ops:
  3.5 12.0 %collective-permute-start.5 = (bf16[1,96,512]{2,1,0:T(8,128)(2,1)S(1)}, bf16[1,96,512]{2,1,0:T(8,128)(2,1)S(1)}, u32[]{:S(2)}, u32[]{:S(2)}) collective-permute-start(bf16[1,96,512]{2,1,0:T(8,128)(2,1)S(1)} %collective-permute-done.3), channel_id=1, source_target_pairs={{0,32},{1,0},{2,48},{3,16},{4,36},{5,4},{6,52},{7,20},{8,40},{9,8}... | collective-permute-start | bytes 294920 | tf_op jit(solution)/shard_map/ppermute | solution.py:43
  12.9 7.4 %collective-permute-start.4 = (bf16[1,96,512]{2,1,0:T(8,128)(2,1)S(1)}, bf16[1,96,512]{2,1,0:T(8,128)(2,1)S(1)}, u32[]{:S(2)}, u32[]{:S(2)}) collective-permute-start(bf16[1,96,512]{2,1,0:T(8,128)(2,1)S(1)} %collective-permute-done.3), channel_id=1, source_target_pairs={{0,0},{1,32},{2,16},{3,48},{4,4},{5,36},{6,20},{7,52},{8,8},{9,40}... | collective-permute-start | bytes 294920 | tf_op jit(solution)/shard_map/ppermute | solution.py:43
  20.4 16.3 %collective-permute-start.7 = (bf16[2,1,96,512]{3,2,0,1:T(8,128)(2,1)S(1)}, bf16[2,1,96,512]{3,2,0,1:T(8,128)(2,1)S(1)}, u32[]{:S(2)}, u32[]{:S(2)}) collective-permute-start(bf16[2,1,96,512]{3,2,0,1:T(8,128)(2,1)S(1)} %bitcast.35), channel_id=1, source_target_pairs={{0,128},{1,129},{2,130},{3,131},{4,132},{5,133},{6,134},{7,135},{8... | collective-permute-start | bytes 589832 | tf_op jit(solution)/shard_map/ppermute | solution.py:43
  31.4 8.1 %collective-permute-start.6 = (bf16[2,1,96,512]{3,2,0,1:T(8,128)(2,1)S(1)}, bf16[2,1,96,512]{3,2,0,1:T(8,128)(2,1)S(1)}, u32[]{:S(2)}, u32[]{:S(2)}) collective-permute-start(bf16[2,1,96,512]{3,2,0,1:T(8,128)(2,1)S(1)} %bitcast.36), channel_id=1, source_target_pairs={{0,64},{1,65},{2,66},{3,67},{4,68},{5,69},{6,70},{7,71},{8,72},{9,... | collective-permute-start | bytes 589832 | tf_op jit(solution)/shard_map/ppermute | solution.py:43
  32.4 7.3 %collective-permute-start.8 = (bf16[2,1,96,512]{3,2,1,0:T(8,128)(2,1)S(1)}, bf16[2,1,96,512]{3,2,1,0:T(8,128)(2,1)S(1)}, u32[]{:S(2)}, u32[]{:S(2)}) collective-permute-start(bf16[2,1,96,512]{3,2,1,0:T(8,128)(2,1)S(1)} %pad_maximum_fusion.3), channel_id=1, source_target_pairs={{0,192},{1,193},{2,194},{3,195},{4,196},{5,197},{6,198},{7,199},{8... | collective-permute-start | bytes 589832 | tf_op jit(solution)/shard_map/ppermute | solution.py:43
  32.4 7.4 %collective-permute-start.2 = (bf16[2,96,512]{2,1,0:T(8,128)(2,1)S(1)}, bf16[2,96,512]{2,1,0:T(8,128)(2,1)S(1)}, u32[]{:S(2)}, u32[]{:S(2)}) collective-permute-start(bf16[2,96,512]{2,1,0:T(8,128)(2,1)S(1)} %collective-permute-done), channel_id=1, source_target_pairs={{0,32},{1,0},{2,48},{3,16},{4,36},{5,4},{6,52},{7,20},{8,40},{9,8}... | collective-permute-start | bytes 589832 | tf_op jit(solution)/shard_map/ppermute | solution.py:43
  34.2 12.4 %collective-permute-start.1 = (bf16[2,96,512]{2,1,0:T(8,128)(2,1)S(1)}, bf16[2,96,512]{2,1,0:T(8,128)(2,1)S(1)}, u32[]{:S(2)}, u32[]{:S(2)}) collective-permute-start(bf16[2,96,512]{2,1,0:T(8,128)(2,1)S(1)} %collective-permute-done), channel_id=1, source_target_pairs={{0,0},{1,32},{2,16},{3,48},{4,4},{5,36},{6,20},{7,52},{8,8},{9,40}... | collective-permute-start | bytes 589832 | tf_op jit(solution)/shard_map/ppermute | solution.py:43
  46.6 10.4 %collective-permute-start.12 = (bf16[4,2,1,96,512]{4,3,1,2,0:T(8,128)(2,1)S(1)}, bf16[4,2,1,96,512]{4,3,1,2,0:T(8,128)(2,1)S(1)}, u32[]{:S(2)}, u32[]{:S(2)}) collective-permute-start(bf16[4,2,1,96,512]{4,3,1,2,0:T(8,128)(2,1)S(1)} %pad_maximum_fusion.1), channel_id=1, source_target_pairs={{0,16},{1,17},{2,18},{3,19},{4,20},{5,21},{6,22},{7,23},{8,24},{9,... | collective-permute-start | bytes 2359304 | tf_op jit(solution)/shard_map/ppermute | solution.py:43
  46.6 27.1 %collective-permute-start.11 = (bf16[2,2,96,512]{3,2,1,0:T(8,128)(2,1)S(1)}, bf16[2,2,96,512]{3,2,1,0:T(8,128)(2,1)S(1)}, u32[]{:S(2)}, u32[]{:S(2)}) collective-permute-start(bf16[2,2,96,512]{3,2,1,0:T(8,128)(2,1)S(1)} %pad_maximum_fusion.2), channel_id=1, source_target_pairs={{0,192},{1,193},{2,194},{3,195},{4,196},{5,197},{6,198},{7,199},{8... | collective-permute-start | bytes 1179656 | tf_op jit(solution)/shard_map/ppermute | solution.py:43
  56.3 17.5 %collective-permute-start.10 = (bf16[2,2,96,512]{3,2,1,0:T(8,128)(2,1)S(1)}, bf16[2,2,96,512]{3,2,1,0:T(8,128)(2,1)}, u32[]{:S(2)}, u32[]{:S(2)}) collective-permute-start(bf16[2,2,96,512]{3,2,1,0:T(8,128)(2,1)S(1)} %pad_maximum_fusion.2), channel_id=1, source_target_pairs={{0,128},{1,129},{2,130},{3,131},{4,132},{5,133},{6,134},{7,135},{8... | collective-permute-start | bytes 1179656 | tf_op jit(solution)/shard_map/ppermute | solution.py:43
  56.3 18.0 %collective-permute-start.9 = (bf16[2,2,96,512]{3,2,1,0:T(8,128)(2,1)S(1)}, bf16[2,2,96,512]{3,2,1,0:T(8,128)(2,1)}, u32[]{:S(2)}, u32[]{:S(2)}) collective-permute-start(bf16[2,2,96,512]{3,2,1,0:T(8,128)(2,1)S(1)} %pad_maximum_fusion.2), channel_id=1, source_target_pairs={{0,64},{1,65},{2,66},{3,67},{4,68},{5,69},{6,70},{7,71},{8,72},{9,... | collective-permute-start | bytes 1179656 | tf_op jit(solution)/shard_map/ppermute | solution.py:43
  64.4 11.2 %collective-permute-start.13 = (s16[400,512]{1,0:T(8,128)(2,1)S(1)}, s16[400,512]{1,0:T(8,128)(2,1)S(1)}, u32[]{:S(2)}, u32[]{:S(2)}) collective-permute-start(s16[400,512]{1,0:T(8,128)(2,1)S(1)} %get-tuple-element.55), channel_id=1, source_target_pairs={{0,1},{1,0},{2,3},{3,2},{4,5},{5,4},{6,7},{7,6},{8,9},{9,8},{10,11... | collective-permute-start | bytes 1228808 | tf_op jit(solution)/shard_map/ppermute | solution.py:43
  64.8 10.8 %collective-permute-start.14 = (s16[400,512]{1,0:T(8,128)(2,1)S(1)}, s16[400,512]{1,0:T(8,128)(2,1)S(1)}, u32[]{:S(2)}, u32[]{:S(2)}) collective-permute-start(s16[400,512]{1,0:T(8,128)(2,1)S(1)} %get-tuple-element.56), channel_id=1, source_target_pairs={{0,3},{1,2},{2,1},{3,0},{4,7},{5,6},{6,5},{7,4},{8,11},{9,10},{10,... | collective-permute-start | bytes 1228808 | tf_op jit(solution)/shard_map/ppermute | solution.py:43
  77.9 31.8 %collective-permute-start.23 = (s16[400,512]{1,0:T(8,128)(2,1)S(1)}, s16[400,512]{1,0:T(8,128)(2,1)S(1)}, u32[]{:S(2)}, u32[]{:S(2)}) collective-permute-start(s16[400,512]{1,0:T(8,128)(2,1)S(1)} %get-tuple-element.75), channel_id=1, source_target_pairs={{0,2},{1,3},{2,0},{3,1},{4,6},{5,7},{6,4},{7,5},{8,10},{9,11},{10,... | collective-permute-start | bytes 1228808 | tf_op jit(solution)/shard_map/ppermute | solution.py:43
  86.0 26.3 %collective-permute-start.17 = (s16[400,512]{1,0:T(8,128)(2,1)S(1)}, s16[400,512]{1,0:T(8,128)(2,1)S(1)}, u32[]{:S(2)}, u32[]{:S(2)}) collective-permute-start(s16[400,512]{1,0:T(8,128)(2,1)S(1)} %get-tuple-element.65), channel_id=1, source_target_pairs={{0,1},{1,0},{2,3},{3,2},{4,5},{5,4},{6,7},{7,6},{8,9},{9,8},{10,11... | collective-permute-start | bytes 1228808 | tf_op jit(solution)/shard_map/ppermute | solution.py:43
  86.1 17.2 %collective-permute-start.16 = (bf16[3,96,512]{2,1,0:T(8,128)(2,1)S(1)}, bf16[3,96,512]{2,1,0:T(8,128)(2,1)S(1)}, u32[]{:S(2)}, u32[]{:S(2)}) collective-permute-start(bf16[3,96,512]{2,1,0:T(8,128)(2,1)S(1)} %bitcast_multiply_fusion.refs_5_.refs_9_), channel_id=1, source_target_pairs={{0,8},{1,9},{2,10},{3,11},{4,12},{5,13},{6,14},{7,15},{8,0},{9,1},... | collective-permute-start | bytes 884744 | tf_op jit(solution)/shard_map/ppermute | solution.py:43
  90.1 22.3 %collective-permute-start.18 = (s16[400,512]{1,0:T(8,128)(2,1)S(1)}, s16[400,512]{1,0:T(8,128)(2,1)S(1)}, u32[]{:S(2)}, u32[]{:S(2)}) collective-permute-start(s16[400,512]{1,0:T(8,128)(2,1)S(1)} %get-tuple-element.66), channel_id=1, source_target_pairs={{0,2},{1,3},{2,0},{3,1},{4,6},{5,7},{6,4},{7,5},{8,10},{9,11},{10,... | collective-permute-start | bytes 1228808 | tf_op jit(solution)/shard_map/ppermute | solution.py:43
  93.6 20.4 %collective-permute-start.19 = (s16[400,512]{1,0:T(8,128)(2,1)S(1)}, s16[400,512]{1,0:T(8,128)(2,1)S(1)}, u32[]{:S(2)}, u32[]{:S(2)}) collective-permute-start(s16[400,512]{1,0:T(8,128)(2,1)S(1)} %get-tuple-element.67), channel_id=1, source_target_pairs={{0,3},{1,2},{2,1},{3,0},{4,7},{5,6},{6,5},{7,4},{8,11},{9,10},{10,... | collective-permute-start | bytes 1228808 | tf_op jit(solution)/shard_map/ppermute | solution.py:43
  108.3 22.6 %collective-permute-start.20 = (s16[400,512]{1,0:T(8,128)(2,1)S(1)}, s16[400,512]{1,0:T(8,128)(2,1)S(1)}, u32[]{:S(2)}, u32[]{:S(2)}) collective-permute-start(s16[400,512]{1,0:T(8,128)(2,1)S(1)} %get-tuple-element.71), channel_id=1, source_target_pairs={{0,1},{1,0},{2,3},{3,2},{4,5},{5,4},{6,7},{7,6},{8,9},{9,8},{10,11... | collective-permute-start | bytes 1228808 | tf_op jit(solution)/shard_map/ppermute | solution.py:43
  109.6 21.4 %collective-permute-start.21 = (s16[400,512]{1,0:T(8,128)(2,1)S(1)}, s16[400,512]{1,0:T(8,128)(2,1)S(1)}, u32[]{:S(2)}, u32[]{:S(2)}) collective-permute-start(s16[400,512]{1,0:T(8,128)(2,1)S(1)} %get-tuple-element.72), channel_id=1, source_target_pairs={{0,2},{1,3},{2,0},{3,1},{4,6},{5,7},{6,4},{7,5},{8,10},{9,11},{10,... | collective-permute-start | bytes 1228808 | tf_op jit(solution)/shard_map/ppermute | solution.py:43
  112.3 19.9 %collective-permute-start.22 = (s16[400,512]{1,0:T(8,128)(2,1)S(1)}, s16[400,512]{1,0:T(8,128)(2,1)S(1)}, u32[]{:S(2)}, u32[]{:S(2)}) collective-permute-start(s16[400,512]{1,0:T(8,128)(2,1)S(1)} %get-tuple-element.73), channel_id=1, source_target_pairs={{0,3},{1,2},{2,1},{3,0},{4,7},{5,6},{6,5},{7,4},{8,11},{9,10},{10,... | collective-permute-start | bytes 1228808 | tf_op jit(solution)/shard_map/ppermute | solution.py:43
  112.4 9.2 %collective-permute-start.25 = (bf16[3,96,512]{2,1,0:T(8,128)(2,1)S(1)}, bf16[3,96,512]{2,1,0:T(8,128)(2,1)S(1)}, u32[]{:S(2)}, u32[]{:S(2)}) collective-permute-start(bf16[3,96,512]{2,1,0:T(8,128)(2,1)S(1)} %bitcast_multiply_fusion.refs_5_.refs_9_), channel_id=1, source_target_pairs={{0,12},{1,13},{2,14},{3,15},{4,8},{5,9},{6,10},{7,11},{8,4},{9,5},... | collective-permute-start | bytes 884744 | tf_op jit(solution)/shard_map/ppermute | solution.py:43
  114.0 15.0 %collective-permute-start.24 = (bf16[3,96,512]{2,1,0:T(8,128)(2,1)S(1)}, bf16[3,96,512]{2,1,0:T(8,128)(2,1)S(1)}, u32[]{:S(2)}, u32[]{:S(2)}) collective-permute-start(bf16[3,96,512]{2,1,0:T(8,128)(2,1)S(1)} %bitcast_multiply_fusion.refs_5_.refs_9_), channel_id=1, source_target_pairs={{0,4},{1,5},{2,6},{3,7},{4,0},{5,1},{6,2},{7,3},{8,12},{9,13},{10,... | collective-permute-start | bytes 884744 | tf_op jit(solution)/shard_map/ppermute | solution.py:43
  141.8 19.3 %all-to-all-start = ((s16[16,48,640]{2,1,0:T(8,128)(2,1)}), s16[16,48,640]{2,1,0:T(8,128)(2,1)S(1)}, u32[]{:S(2)}, u32[]{:S(2)}) async-start(s16[16,48,640]{2,1,0:T(8,128)(2,1)} %bitcast.23), calls=%async_computation | async-start | bytes 1966080 | tf_op jit(solution)/shard_map/all_to_all | solution.py:407
  145.5 25.7 %collective-permute-start.26 = (s16[224,512]{1,0:T(8,128)(2,1)S(1)}, s16[224,512]{1,0:T(8,128)(2,1)S(1)}, u32[]{:S(2)}, u32[]{:S(2)}) collective-permute-start(s16[224,512]{1,0:T(8,128)(2,1)S(1)} %get-tuple-element.85), channel_id=1, source_target_pairs={{0,4},{1,5},{2,6},{3,7},{4,0},{5,1},{6,2},{7,3},{8,12},{9,13},{10,... | collective-permute-start | bytes 688136 | tf_op jit(solution)/shard_map/ppermute | solution.py:43
  145.6 27.5 %collective-permute-start.27 = (s16[224,512]{1,0:T(8,128)(2,1)S(1)}, s16[224,512]{1,0:T(8,128)(2,1)S(1)}, u32[]{:S(2)}, u32[]{:S(2)}) collective-permute-start(s16[224,512]{1,0:T(8,128)(2,1)S(1)} %get-tuple-element.86), channel_id=1, source_target_pairs={{0,8},{1,9},{2,10},{3,11},{4,12},{5,13},{6,14},{7,15},{8,0},{9,1},... | collective-permute-start | bytes 688136 | tf_op jit(solution)/shard_map/ppermute | solution.py:43
  147.4 25.6 %collective-permute-start.28 = (s16[224,512]{1,0:T(8,128)(2,1)S(1)}, s16[224,512]{1,0:T(8,128)(2,1)S(1)}, u32[]{:S(2)}, u32[]{:S(2)}) collective-permute-start(s16[224,512]{1,0:T(8,128)(2,1)S(1)} %get-tuple-element.87), channel_id=1, source_target_pairs={{0,12},{1,13},{2,14},{3,15},{4,8},{5,9},{6,10},{7,11},{8,4},{9,5},... | collective-permute-start | bytes 688136 | tf_op jit(solution)/shard_map/ppermute | solution.py:43
  161.4 8.0 %collective-permute-start.34 = (f32[48,512]{1,0:T(8,128)S(1)}, f32[48,512]{1,0:T(8,128)S(1)}, u32[]{:S(2)}, u32[]{:S(2)}) collective-permute-start(f32[48,512]{1,0:T(8,128)S(1)} %gathered.1), channel_id=1, source_target_pairs={{0,32},{1,33},{2,34},{3,35},{4,36},{5,37},{6,38},{7,39},{8,40},{9,... | collective-permute-start | bytes 294920 | tf_op jit(solution)/shard_map/ppermute | solution.py:43
  171.2 9.5 %collective-permute-start.36 = (f32[48,512]{1,0:T(8,128)S(1)}, f32[48,512]{1,0:T(8,128)S(1)}, u32[]{:S(2)}, u32[]{:S(2)}) collective-permute-start(f32[48,512]{1,0:T(8,128)S(1)} %add.45.own_ref), channel_id=1, source_target_pairs={{0,8},{1,9},{2,10},{3,11},{4,12},{5,13},{6,14},{7,15},{8,0},{9,1},... | collective-permute-start | bytes 294920 | tf_op jit(solution)/shard_map/ppermute | solution.py:43
  171.2 9.5 %collective-permute-start.35 = (f32[48,512]{1,0:T(8,128)S(1)}, f32[48,512]{1,0:T(8,128)S(1)}, u32[]{:S(2)}, u32[]{:S(2)}) collective-permute-start(f32[48,512]{1,0:T(8,128)S(1)} %add.45.own_ref), channel_id=1, source_target_pairs={{0,4},{1,5},{2,6},{3,7},{4,0},{5,1},{6,2},{7,3},{8,12},{9,13},{10,... | collective-permute-start | bytes 294920 | tf_op jit(solution)/shard_map/ppermute | solution.py:43
  181.8 20.2 %all-to-all-start.1 = ((s16[16,48,640]{2,1,0:T(8,128)(2,1)}), s16[16,48,640]{2,1,0:T(8,128)(2,1)S(1)}, u32[]{:S(2)}, u32[]{:S(2)}) async-start(s16[16,48,640]{2,1,0:T(8,128)(2,1)} %copies.1), calls=%async_computation.1 | async-start | bytes 1966080 | tf_op jit(solution)/shard_map/all_to_all | solution.py:412
  189.9 7.1 %collective-permute-start.33 = (s16[112,512]{1,0:T(8,128)(2,1)S(1)}, s16[112,512]{1,0:T(8,128)(2,1)S(1)}, u32[]{:S(2)}, u32[]{:S(2)}) collective-permute-start(s16[112,512]{1,0:T(8,128)(2,1)S(1)} %get-tuple-element.97), channel_id=1, source_target_pairs={{0,12},{1,13},{2,14},{3,15},{4,8},{5,9},{6,10},{7,11},{8,4},{9,5},... | collective-permute-start | bytes 344072 | tf_op jit(solution)/shard_map/ppermute | solution.py:43
  (11 other events, 44.8 us)

commit v7 on v6

--- a/solution.py
+++ b/solution.py
@@ -332,22 +332,27 @@
 
 
 def finish_kernel(at_ref, mine_ref, theirs_ref, diag_ref, out_ref):
-    half = diag_ref.shape[1] // 2
+    half = mine_ref.shape[0]
     core = at_ref[1]
-    for p in range(diag_ref.shape[0]):
-        for which, ref in ((core, mine_ref), (1 - core, theirs_ref)):
-            place = pl.ds(pl.multiple_of(which * half, 8), half)
-            part = decode_lanes(ref[p * half : (p + 1) * half, :])
-            out_ref[p, place, :] = diag_ref[p, place, :] + part
+    for which, ref in ((core, mine_ref), (1 - core, theirs_ref)):
+        place = pl.ds(pl.multiple_of(which * half, 8), half)
+        out_ref[0, place, :] = diag_ref[0, place, :] + decode_lanes(ref[...])
 
 
 def finish(at, mine, theirs, diag):
+    panels, rows, width = diag.shape
+    coded = pl.BlockSpec((rows // 2, width + LANES), lambda p, s: (p, 0))
+    whole = pl.BlockSpec((1, rows, width), lambda p, s: (p, 0, 0))
     return pl.pallas_call(
         finish_kernel,
-        in_specs=[SMEM] + [VMEM] * 3,
-        out_specs=VMEM,
+        grid_spec=pltpu.PrefetchScalarGridSpec(
+            num_scalar_prefetch=1,
+            grid=(panels,),
+            in_specs=[coded, coded, whole],
+            out_specs=whole,
+        ),
         out_shape=jax.ShapeDtypeStruct(diag.shape, F32),
-        compiler_params=params(),
+        compiler_params=params(54),
         cost_estimate=cost(diag.size, 12 * diag.size),
         name="finish",
     )(at, mine, theirs, diag)
@@ -384,11 +389,11 @@
     ((keep_a, *coded),) = product(at, a4, own_a, send(own_a, over_core))
     parts_a = [send(coded[k - 1], over_y(k)) for k in (1, 2, 3)]
     far = send(after(masked, own_a), over_l(2))
-    own_b = after(jnp.stack(own_b), parts_a[0], parts_a[2])
+    own_b = after(jnp.stack(own_b), parts_a[0], parts_a[2], far)
     other_b = send(own_b, over_core)
     ((keep_b, *coded),) = product(at, a4, own_b, other_b)
     parts_b = [send(q, over_y(k)) for k, q in zip((1, 2, 3), after(coded, parts_a[0], parts_a[2]))]
-    ((keep_c, *coded),) = product(after(at, far), a4, own_b, other_b, 1)
+    ((keep_c, *coded),) = product(at, a4, own_b, other_b, 1)
     parts_c = [send(q, over_y(k)) for k, q in zip((1, 2, 3), coded)]
     late = after(masked, keep_c)
     beside = [masked, send(late, over_l(1)), far, send(late, over_l(3))]

time: 213 us -> 223 us (1.047)
  waiting for transfers between devices: 91.9 us -> 101 us
  Pallas kernels: 26.9 us -> 29.8 us
    ppermute x39, waiting for transfers between devices: 74.8 us -> 84.7 us  [send(): return lax.ppermute(value, AXES, pairs)]
    pallas_call x1, Pallas kernels: 2.74 us -> 5.72 us  [finish(): pl.pallas_call(finish_kernel, grid_spec=pltpu.PrefetchScalarGridSpec(num_...]
  transfers between devices with their start and end apart: 41 -> 41, of which waited for: 22 -> 23; matrix products, arithmetic and copies ran while one was open for 1% -> 0% of each run, Pallas kernels for 9% -> 8%
where the time goes in v7:
time: 223 us
  waiting for transfers between devices  101 us (45%)
  starting transfers between devices  85.1 us (38%)
  Pallas kernels  29.8 us (13%)
  local copies, waits for them, and re-layouts  4.38 us (2%)
    ppermute x39, waiting for transfers between devices, send(): return lax.ppermute(value, AXES, pairs)  84.7 us
    ppermute x39, starting transfers between devices, send(): return lax.ppermute(value, AXES, pairs)  75.2 us
    pallas_call x3, Pallas kernels, product(): pl.pallas_call(functools.partial(product_kernel, panels), grid_spec=pltpu...  15.1 us
    all_to_all x1, waiting for transfers between devices, body(): total = gathered(lax.all_to_all(pieces, ('x', 'y'), 0, 0))  12 us
    all_to_all x1, starting transfers between devices, body(): lax.all_to_all(pieces, ('x', 'y'), 0, 0)  6.19 us
    pallas_call x1, Pallas kernels, finish(): pl.pallas_call(finish_kernel, grid_spec=pltpu.PrefetchScalarGridSpec(num_...  5.72 us
    pallas_call x2, Pallas kernels, middle(): pl.pallas_call(functools.partial(middle_kernel, panels, base), in_specs=[...  5.06 us
  transfers between devices with their start and end apart: 41, of which 23 were waited for; matrix products, arithmetic and copies ran while one was open for 0% of the time, Pallas kernels for 8%

profile of v7, /device:TPU:1, one launch (start us, length us, event | category | flops | bytes accessed | tf_op | source)
XLA Modules:
  0.0 222.8 jit_solution(4458987587527006422)
XLA Ops:
  3.5 9.4 %collective-permute-start.5 = (bf16[1,96,512]{2,1,0:T(8,128)(2,1)S(1)}, bf16[1,96,512]{2,1,0:T(8,128)(2,1)S(1)}, u32[]{:S(2)}, u32[]{:S(2)}) collective-permute-start(bf16[1,96,512]{2,1,0:T(8,128)(2,1)S(1)} %collective-permute-done.3), channel_id=1, source_target_pairs={{0,32},{1,0},{2,48},{3,16},{4,36},{5,4},{6,52},{7,20},{8,40},{9,8}... | collective-permute-start | bytes 294920 | tf_op jit(solution)/shard_map/ppermute | solution.py:43
  15.6 4.8 %collective-permute-done.4 = bf16[1,96,512]{2,1,0:T(8,128)(2,1)S(1)} collective-permute-done((bf16[1,96,512]{2,1,0:T(8,128)(2,1)S(1)}, bf16[1,96,512]{2,1,0:T(8,128)(2,1)S(1)}, u32[]{:S(2)}, u32[]{:S(2)}) %collective-permute-start.4) | collective-permute-done | bytes 98336 | tf_op jit(solution)/shard_map/ppermute | solution.py:43
  20.4 11.0 %collective-permute-start.7 = (bf16[2,1,96,512]{3,2,0,1:T(8,128)(2,1)S(1)}, bf16[2,1,96,512]{3,2,0,1:T(8,128)(2,1)S(1)}, u32[]{:S(2)}, u32[]{:S(2)}) collective-permute-start(bf16[2,1,96,512]{3,2,0,1:T(8,128)(2,1)S(1)} %bitcast.33), channel_id=1, source_target_pairs={{0,128},{1,129},{2,130},{3,131},{4,132},{5,133},{6,134},{7,135},{8... | collective-permute-start | bytes 589832 | tf_op jit(solution)/shard_map/ppermute | solution.py:43
  36.7 2.8 %collective-permute-done.6 = bf16[2,1,96,512]{3,2,0,1:T(8,128)(2,1)S(1)} collective-permute-done((bf16[2,1,96,512]{3,2,0,1:T(8,128)(2,1)S(1)}, bf16[2,1,96,512]{3,2,0,1:T(8,128)(2,1)S(1)}, u32[]{:S(2)}, u32[]{:S(2)}) %collective-permute-start.6) | collective-permute-done | bytes 196640 | tf_op jit(solution)/shard_map/ppermute | solution.py:43
  39.8 6.8 %collective-permute-done.1 = bf16[2,96,512]{2,1,0:T(8,128)(2,1)S(1)} collective-permute-done((bf16[2,96,512]{2,1,0:T(8,128)(2,1)S(1)}, bf16[2,96,512]{2,1,0:T(8,128)(2,1)S(1)}, u32[]{:S(2)}, u32[]{:S(2)}) %collective-permute-start.1) | collective-permute-done | bytes 196640 | tf_op jit(solution)/shard_map/ppermute | solution.py:43
  46.6 9.6 %collective-permute-start.11 = (bf16[2,2,96,512]{3,2,1,0:T(8,128)(2,1)S(1)}, bf16[2,2,96,512]{3,2,1,0:T(8,128)(2,1)S(1)}, u32[]{:S(2)}, u32[]{:S(2)}) collective-permute-start(bf16[2,2,96,512]{3,2,1,0:T(8,128)(2,1)S(1)} %pad_maximum_fusion.2), channel_id=1, source_target_pairs={{0,192},{1,193},{2,194},{3,195},{4,196},{5,197},{6,198},{7,199},{8... | collective-permute-start | bytes 1179656 | tf_op jit(solution)/shard_map/ppermute | solution.py:43
  59.4 5.0 %product.3 = (f32[384,512]{1,0:T(8,128)S(1)}, s16[400,512]{1,0:T(8,128)(2,1)S(1)}, s16[400,512]{1,0:T(8,128)(2,1)S(1)}, s16[400,512]{1,0:T(8,128)(2,1)S(1)}) custom-call(s32[6]{0:T(128)S(1)} %stack.75.at_ref.refs_0_, bf16[4,4,96,1536]{3,2,1,0:T(8,128)(2,1)S(1)} %bitcast.27, bf16[4,2,1,96,512]{4,3,2,1,0:T(8,128)(2,1)S(1)} %bitcast.30, ...), custom_call_target="tpu_custom_call" | custom-call | flops 2415919 | bytes 4718 | tf_op jit(solution)/shard_map/product/pallas_call | solution.py:152
  66.5 7.2 %collective-permute-done.11 = bf16[2,2,96,512]{3,2,1,0:T(8,128)(2,1)S(1)} collective-permute-done((bf16[2,2,96,512]{3,2,1,0:T(8,128)(2,1)S(1)}, bf16[2,2,96,512]{3,2,1,0:T(8,128)(2,1)S(1)}, u32[]{:S(2)}, u32[]{:S(2)}) %collective-permute-start.11) | collective-permute-done | bytes 393248 | tf_op jit(solution)/shard_map/ppermute | solution.py:43
  74.3 13.4 %collective-permute-done.15.refs_7_.refs_11_ = bf16[3,96,512]{2,1,0:T(8,128)(2,1)S(1)} collective-permute-done((bf16[3,96,512]{2,1,0:T(8,128)(2,1)S(1)}, bf16[3,96,512]{2,1,0:T(8,128)(2,1)S(1)}, u32[]{:S(2)}, u32[]{:S(2)}) %collective-permute-start.15) | collective-permute-done | bytes 294944 | tf_op jit(solution)/shard_map/ppermute | solution.py:43
  88.3 5.9 %collective-permute-start.23 = (s16[400,512]{1,0:T(8,128)(2,1)S(1)}, s16[400,512]{1,0:T(8,128)(2,1)S(1)}, u32[]{:S(2)}, u32[]{:S(2)}) collective-permute-start(s16[400,512]{1,0:T(8,128)(2,1)S(1)} %get-tuple-element.73), channel_id=1, source_target_pairs={{0,2},{1,3},{2,0},{3,1},{4,6},{5,7},{6,4},{7,5},{8,10},{9,11},{10,... | collective-permute-start | bytes 1228808 | tf_op jit(solution)/shard_map/ppermute | solution.py:43
  94.2 5.1 %product.4 = (f32[384,512]{1,0:T(8,128)S(1)}, s16[400,512]{1,0:T(8,128)(2,1)S(1)}, s16[400,512]{1,0:T(8,128)(2,1)S(1)}, s16[400,512]{1,0:T(8,128)(2,1)S(1)}) custom-call(s32[6]{0:T(128)S(1)} %stack.75.at_ref.refs_0_, bf16[4,4,96,1536]{3,2,1,0:T(8,128)(2,1)S(1)} %bitcast.28, bf16[4,2,2,96,512]{4,3,2,1,0:T(8,128)(2,1)S(1)} %pad_maximum_fusion.own_ref, ...), custom_call_target="tpu_custom_call" | custom-call | flops 2415919 | bytes 4718 | tf_op jit(solution)/shard_map/product/pallas_call | solution.py:152
  99.7 3.6 %collective-permute-start.18 = (s16[400,512]{1,0:T(8,128)(2,1)S(1)}, s16[400,512]{1,0:T(8,128)(2,1)S(1)}, u32[]{:S(2)}, u32[]{:S(2)}) collective-permute-start(s16[400,512]{1,0:T(8,128)(2,1)S(1)} %get-tuple-element.64), channel_id=1, source_target_pairs={{0,2},{1,3},{2,0},{3,1},{4,6},{5,7},{6,4},{7,5},{8,10},{9,11},{10,... | collective-permute-start | bytes 1228808 | tf_op jit(solution)/shard_map/ppermute | solution.py:43
  103.4 5.1 %product.5 = (f32[384,512]{1,0:T(8,128)S(1)}, s16[400,512]{1,0:T(8,128)(2,1)S(1)}, s16[400,512]{1,0:T(8,128)(2,1)S(1)}, s16[400,512]{1,0:T(8,128)(2,1)S(1)}) custom-call(s32[6]{0:T(128)S(1)} %stack.75.at_ref.refs_0_, bf16[4,4,96,1536]{3,2,1,0:T(8,128)(2,1)S(1)} %bitcast.29, bf16[4,2,2,96,512]{4,3,2,1,0:T(8,128)(2,1)S(1)} %pad_maximum_fusion.own_ref, ...), custom_call_target="tpu_custom_call" | custom-call | flops 2415919 | bytes 4718 | tf_op jit(solution)/shard_map/product/pallas_call | solution.py:152
  108.6 3.8 %collective-permute-start.21 = (s16[400,512]{1,0:T(8,128)(2,1)S(1)}, s16[400,512]{1,0:T(8,128)(2,1)S(1)}, u32[]{:S(2)}, u32[]{:S(2)}) collective-permute-start(s16[400,512]{1,0:T(8,128)(2,1)S(1)} %get-tuple-element.70), channel_id=1, source_target_pairs={{0,2},{1,3},{2,0},{3,1},{4,6},{5,7},{6,4},{7,5},{8,10},{9,11},{10,... | collective-permute-start | bytes 1228808 | tf_op jit(solution)/shard_map/ppermute | solution.py:43
  112.8 8.5 %collective-permute-done.18.refs_4_ = s16[400,512]{1,0:T(8,128)(2,1)S(1)} collective-permute-done((s16[400,512]{1,0:T(8,128)(2,1)S(1)}, s16[400,512]{1,0:T(8,128)(2,1)S(1)}, u32[]{:S(2)}, u32[]{:S(2)}) %collective-permute-start.18) | collective-permute-done | bytes 409632 | tf_op jit(solution)/shard_map/ppermute | solution.py:43
  123.7 6.1 %collective-permute-done.25.refs_8_.refs_12_ = bf16[3,96,512]{2,1,0:T(8,128)(2,1)S(1)} collective-permute-done((bf16[3,96,512]{2,1,0:T(8,128)(2,1)S(1)}, bf16[3,96,512]{2,1,0:T(8,128)(2,1)S(1)}, u32[]{:S(2)}, u32[]{:S(2)}) %collective-permute-start.25) | collective-permute-done | bytes 294944 | tf_op jit(solution)/shard_map/ppermute | solution.py:43
  129.8 8.7 %collective-permute-done.24.refs_6_.refs_10_ = bf16[3,96,512]{2,1,0:T(8,128)(2,1)S(1)} collective-permute-done((bf16[3,96,512]{2,1,0:T(8,128)(2,1)S(1)}, bf16[3,96,512]{2,1,0:T(8,128)(2,1)S(1)}, u32[]{:S(2)}, u32[]{:S(2)}) %collective-permute-start.24) | collective-permute-done | bytes 294944 | tf_op jit(solution)/shard_map/ppermute | solution.py:43
  140.9 3.1 %middle.3 = (f32[192,512]{1,0:T(8,128)S(1)}, s16[224,512]{1,0:T(8,128)(2,1)S(1)}, s16[224,512]{1,0:T(8,128)(2,1)S(1)}, s16[224,512]{1,0:T(8,128)(2,1)S(1)}, f32[...) custom-call(s32[6]{0:T(128)S(1)} %stack.75.at_ref.refs_0_, f32[384,512]{1,0:T(8,128)S(1)} %get-tuple-element.58.refs_1_, ...), custom_call_target="tpu_custom_call" | custom-call | flops 603979 | bytes 3145 | tf_op jit(solution)/shard_map/middle/pallas_call | solution.py:215
  146.1 2.9 %collective-permute-done.30.refs_3_ = f32[256,512]{1,0:T(8,128)S(1)} collective-permute-done((f32[256,512]{1,0:T(8,128)S(1)}, f32[256,512]{1,0:T(8,128)S(1)}, u32[]{:S(2)}, u32[]{:S(2)}) %collective-permute-start.30) | collective-permute-done | bytes 524320 | tf_op jit(solution)/shard_map/ppermute | solution.py:43
  150.4 3.6 %all-to-all-start = ((s16[16,48,640]{2,1,0:T(8,128)(2,1)}), s16[16,48,640]{2,1,0:T(8,128)(2,1)S(1)}, u32[]{:S(2)}, u32[]{:S(2)}) async-start(s16[16,48,640]{2,1,0:T(8,128)(2,1)} %bitcast.23), calls=%async_computation | async-start | bytes 1966080 | tf_op jit(solution)/shard_map/all_to_all | solution.py:412
  154.2 2.6 %collective-permute-start.27 = (s16[224,512]{1,0:T(8,128)(2,1)S(1)}, s16[224,512]{1,0:T(8,128)(2,1)S(1)}, u32[]{:S(2)}, u32[]{:S(2)}) collective-permute-start(s16[224,512]{1,0:T(8,128)(2,1)S(1)} %get-tuple-element.84), channel_id=1, source_target_pairs={{0,8},{1,9},{2,10},{3,11},{4,12},{5,13},{6,14},{7,15},{8,0},{9,1},... | collective-permute-start | bytes 688136 | tf_op jit(solution)/shard_map/ppermute | solution.py:43
  157.7 12.0 %all-to-all-done.in_ref = s16[16,48,640]{2,1,0:T(8,128)(2,1)S(1)} async-done(((s16[16,48,640]{2,1,0:T(8,128)(2,1)}), s16[16,48,640]{2,1,0:T(8,128)(2,1)S(1)}, u32[]{:S(2)}, u32[]{:S(2)}) %all-to-all-start) | async-done | bytes 983072 | tf_op jit(solution)/shard_map/all_to_all | solution.py:412
  171.1 7.0 %collective-permute-done.34 = f32[48,512]{1,0:T(8,128)S(1)} collective-permute-done((f32[48,512]{1,0:T(8,128)S(1)}, f32[48,512]{1,0:T(8,128)S(1)}, u32[]{:S(2)}, u32[]{:S(2)}) %collective-permute-start.34) | collective-permute-done | bytes 98336 | tf_op jit(solution)/shard_map/ppermute | solution.py:43
  178.1 2.4 %collective-permute-start.37 = (f32[48,512]{1,0:T(8,128)S(1)}, f32[48,512]{1,0:T(8,128)S(1)}, u32[]{:S(2)}, u32[]{:S(2)}) collective-permute-start(f32[48,512]{1,0:T(8,128)S(1)} %add.45.own_ref), channel_id=1, source_target_pairs={{0,12},{1,13},{2,14},{3,15},{4,8},{5,9},{6,10},{7,11},{8,4},{9,5},... | collective-permute-start | bytes 294920 | tf_op jit(solution)/shard_map/ppermute | solution.py:43
  183.6 5.4 %collective-permute-done.36.r2_ref = f32[48,512]{1,0:T(8,128)S(1)} collective-permute-done((f32[48,512]{1,0:T(8,128)S(1)}, f32[48,512]{1,0:T(8,128)S(1)}, u32[]{:S(2)}, u32[]{:S(2)}) %collective-permute-start.36) | collective-permute-done | bytes 98336 | tf_op jit(solution)/shard_map/ppermute | solution.py:43
  190.1 6.2 %all-to-all-start.1 = ((s16[16,48,640]{2,1,0:T(8,128)(2,1)}), s16[16,48,640]{2,1,0:T(8,128)(2,1)}, u32[]{:S(2)}, u32[]{:S(2)}) async-start(s16[16,48,640]{2,1,0:T(8,128)(2,1)} %copies.1), calls=%async_computation.1 | async-start | bytes 1966080 | tf_op jit(solution)/shard_map/all_to_all | solution.py:417
  196.5 2.8 %collective-permute-start.32 = (s16[112,512]{1,0:T(8,128)(2,1)S(1)}, s16[112,512]{1,0:T(8,128)(2,1)S(1)}, u32[]{:S(2)}, u32[]{:S(2)}) collective-permute-start(s16[112,512]{1,0:T(8,128)(2,1)S(1)} %get-tuple-element.94), channel_id=1, source_target_pairs={{0,8},{1,9},{2,10},{3,11},{4,12},{5,13},{6,14},{7,15},{8,0},{9,1},... | collective-permute-start | bytes 344072 | tf_op jit(solution)/shard_map/ppermute | solution.py:43
  200.0 2.8 %collective-permute-done.32.refs_6_ = s16[112,512]{1,0:T(8,128)(2,1)S(1)} collective-permute-done((s16[112,512]{1,0:T(8,128)(2,1)S(1)}, s16[112,512]{1,0:T(8,128)(2,1)S(1)}, u32[]{:S(2)}, u32[]{:S(2)}) %collective-permute-start.32) | collective-permute-done | bytes 114720 | tf_op jit(solution)/shard_map/ppermute | solution.py:43
  202.8 3.1 %collective-permute-done.33.refs_7_ = s16[112,512]{1,0:T(8,128)(2,1)S(1)} collective-permute-done((s16[112,512]{1,0:T(8,128)(2,1)S(1)}, s16[112,512]{1,0:T(8,128)(2,1)S(1)}, u32[]{:S(2)}, u32[]{:S(2)}) %collective-permute-start.33) | collective-permute-done | bytes 114720 | tf_op jit(solution)/shard_map/ppermute | solution.py:43
  205.9 4.4 %all-to-all-done.1 = s16[16,48,640]{2,1,0:T(8,128)(2,1)} async-done(((s16[16,48,640]{2,1,0:T(8,128)(2,1)}), s16[16,48,640]{2,1,0:T(8,128)(2,1)}, u32[]{:S(2)}, u32[]{:S(2)}) %all-to-all-start.1) | async-done | bytes 983072 | tf_op jit(solution)/shard_map/all_to_all | solution.py:417
  210.3 3.4 %collective-permute-start.38 = (s16[768,640]{1,0:T(8,128)(2,1)}, s16[768,640]{1,0:T(8,128)(2,1)S(1)}, u32[]{:S(2)}, u32[]{:S(2)}) collective-permute-start(s16[768,640]{1,0:T(8,128)(2,1)} %bitcast.25.mine_ref), channel_id=1, source_target_pairs={{0,16},{1,17},{2,18},{3,19},{4,20},{5,21},{6,22},{7,23},{8,24},{9,... | collective-permute-start | bytes 2949128 | tf_op jit(solution)/shard_map/ppermute | solution.py:43
  217.1 5.7 %finish.1 = f32[3,512,512]{2,1,0:T(8,128)} custom-call(s32[6]{0:T(128)} %copy-done.1, s16[768,640]{1,0:T(8,128)(2,1)} %bitcast.25.mine_ref, s16[768,640]{1,0:T(8,128)(2,1)} %copy-done.2, f32[3,512,512]{2,1,0:T(8,128)} %diag_ref.1), custom_call_target="tpu_custom_call" | custom-call | flops 786 | bytes 9437 | tf_op jit(solution)/shard_map/finish/pallas_call | solution.py:346
  (78 shorter events, 37.5 us)
Async XLA Ops:
  3.5 12.0 %collective-permute-start.5 = (bf16[1,96,512]{2,1,0:T(8,128)(2,1)S(1)}, bf16[1,96,512]{2,1,0:T(8,128)(2,1)S(1)}, u32[]{:S(2)}, u32[]{:S(2)}) collective-permute-start(bf16[1,96,512]{2,1,0:T(8,128)(2,1)S(1)} %collective-permute-done.3), channel_id=1, source_target_pairs={{0,32},{1,0},{2,48},{3,16},{4,36},{5,4},{6,52},{7,20},{8,40},{9,8}... | collective-permute-start | bytes 294920 | tf_op jit(solution)/shard_map/ppermute | solution.py:43
  12.9 7.4 %collective-permute-start.4 = (bf16[1,96,512]{2,1,0:T(8,128)(2,1)S(1)}, bf16[1,96,512]{2,1,0:T(8,128)(2,1)S(1)}, u32[]{:S(2)}, u32[]{:S(2)}) collective-permute-start(bf16[1,96,512]{2,1,0:T(8,128)(2,1)S(1)} %collective-permute-done.3), channel_id=1, source_target_pairs={{0,0},{1,32},{2,16},{3,48},{4,4},{5,36},{6,20},{7,52},{8,8},{9,40}... | collective-permute-start | bytes 294920 | tf_op jit(solution)/shard_map/ppermute | solution.py:43
  20.4 16.3 %collective-permute-start.7 = (bf16[2,1,96,512]{3,2,0,1:T(8,128)(2,1)S(1)}, bf16[2,1,96,512]{3,2,0,1:T(8,128)(2,1)S(1)}, u32[]{:S(2)}, u32[]{:S(2)}) collective-permute-start(bf16[2,1,96,512]{3,2,0,1:T(8,128)(2,1)S(1)} %bitcast.33), channel_id=1, source_target_pairs={{0,128},{1,129},{2,130},{3,131},{4,132},{5,133},{6,134},{7,135},{8... | collective-permute-start | bytes 589832 | tf_op jit(solution)/shard_map/ppermute | solution.py:43
  31.4 8.1 %collective-permute-start.6 = (bf16[2,1,96,512]{3,2,0,1:T(8,128)(2,1)S(1)}, bf16[2,1,96,512]{3,2,0,1:T(8,128)(2,1)S(1)}, u32[]{:S(2)}, u32[]{:S(2)}) collective-permute-start(bf16[2,1,96,512]{3,2,0,1:T(8,128)(2,1)S(1)} %bitcast.34), channel_id=1, source_target_pairs={{0,64},{1,65},{2,66},{3,67},{4,68},{5,69},{6,70},{7,71},{8,72},{9,... | collective-permute-start | bytes 589832 | tf_op jit(solution)/shard_map/ppermute | solution.py:43
  32.4 7.3 %collective-permute-start.8 = (bf16[2,1,96,512]{3,2,1,0:T(8,128)(2,1)S(1)}, bf16[2,1,96,512]{3,2,1,0:T(8,128)(2,1)S(1)}, u32[]{:S(2)}, u32[]{:S(2)}) collective-permute-start(bf16[2,1,96,512]{3,2,1,0:T(8,128)(2,1)S(1)} %pad_maximum_fusion.3), channel_id=1, source_target_pairs={{0,192},{1,193},{2,194},{3,195},{4,196},{5,197},{6,198},{7,199},{8... | collective-permute-start | bytes 589832 | tf_op jit(solution)/shard_map/ppermute | solution.py:43
  32.4 7.4 %collective-permute-start.2 = (bf16[2,96,512]{2,1,0:T(8,128)(2,1)S(1)}, bf16[2,96,512]{2,1,0:T(8,128)(2,1)S(1)}, u32[]{:S(2)}, u32[]{:S(2)}) collective-permute-start(bf16[2,96,512]{2,1,0:T(8,128)(2,1)S(1)} %collective-permute-done), channel_id=1, source_target_pairs={{0,32},{1,0},{2,48},{3,16},{4,36},{5,4},{6,52},{7,20},{8,40},{9,8}... | collective-permute-start | bytes 589832 | tf_op jit(solution)/shard_map/ppermute | solution.py:43
  34.2 12.4 %collective-permute-start.1 = (bf16[2,96,512]{2,1,0:T(8,128)(2,1)S(1)}, bf16[2,96,512]{2,1,0:T(8,128)(2,1)S(1)}, u32[]{:S(2)}, u32[]{:S(2)}) collective-permute-start(bf16[2,96,512]{2,1,0:T(8,128)(2,1)S(1)} %collective-permute-done), channel_id=1, source_target_pairs={{0,0},{1,32},{2,16},{3,48},{4,4},{5,36},{6,20},{7,52},{8,8},{9,40}... | collective-permute-start | bytes 589832 | tf_op jit(solution)/shard_map/ppermute | solution.py:43
  46.6 10.4 %collective-permute-start.12 = (bf16[4,2,1,96,512]{4,3,1,2,0:T(8,128)(2,1)S(1)}, bf16[4,2,1,96,512]{4,3,1,2,0:T(8,128)(2,1)S(1)}, u32[]{:S(2)}, u32[]{:S(2)}) collective-permute-start(bf16[4,2,1,96,512]{4,3,1,2,0:T(8,128)(2,1)S(1)} %pad_maximum_fusion.1), channel_id=1, source_target_pairs={{0,16},{1,17},{2,18},{3,19},{4,20},{5,21},{6,22},{7,23},{8,24},{9,... | collective-permute-start | bytes 2359304 | tf_op jit(solution)/shard_map/ppermute | solution.py:43
  46.6 27.1 %collective-permute-start.11 = (bf16[2,2,96,512]{3,2,1,0:T(8,128)(2,1)S(1)}, bf16[2,2,96,512]{3,2,1,0:T(8,128)(2,1)S(1)}, u32[]{:S(2)}, u32[]{:S(2)}) collective-permute-start(bf16[2,2,96,512]{3,2,1,0:T(8,128)(2,1)S(1)} %pad_maximum_fusion.2), channel_id=1, source_target_pairs={{0,192},{1,193},{2,194},{3,195},{4,196},{5,197},{6,198},{7,199},{8... | collective-permute-start | bytes 1179656 | tf_op jit(solution)/shard_map/ppermute | solution.py:43
  56.3 17.5 %collective-permute-start.10 = (bf16[2,2,96,512]{3,2,1,0:T(8,128)(2,1)S(1)}, bf16[2,2,96,512]{3,2,1,0:T(8,128)(2,1)S(1)}, u32[]{:S(2)}, u32[]{:S(2)}) collective-permute-start(bf16[2,2,96,512]{3,2,1,0:T(8,128)(2,1)S(1)} %pad_maximum_fusion.2), channel_id=1, source_target_pairs={{0,128},{1,129},{2,130},{3,131},{4,132},{5,133},{6,134},{7,135},{8... | collective-permute-start | bytes 1179656 | tf_op jit(solution)/shard_map/ppermute | solution.py:43
  56.3 17.9 %collective-permute-start.9 = (bf16[2,2,96,512]{3,2,1,0:T(8,128)(2,1)S(1)}, bf16[2,2,96,512]{3,2,1,0:T(8,128)(2,1)S(1)}, u32[]{:S(2)}, u32[]{:S(2)}) collective-permute-start(bf16[2,2,96,512]{3,2,1,0:T(8,128)(2,1)S(1)} %pad_maximum_fusion.2), channel_id=1, source_target_pairs={{0,64},{1,65},{2,66},{3,67},{4,68},{5,69},{6,70},{7,71},{8,72},{9,... | collective-permute-start | bytes 1179656 | tf_op jit(solution)/shard_map/ppermute | solution.py:43
  64.4 23.4 %collective-permute-start.13 = (s16[400,512]{1,0:T(8,128)(2,1)S(1)}, s16[400,512]{1,0:T(8,128)(2,1)S(1)}, u32[]{:S(2)}, u32[]{:S(2)}) collective-permute-start(s16[400,512]{1,0:T(8,128)(2,1)S(1)} %get-tuple-element.54), channel_id=1, source_target_pairs={{0,1},{1,0},{2,3},{3,2},{4,5},{5,4},{6,7},{7,6},{8,9},{9,8},{10,11... | collective-permute-start | bytes 1228808 | tf_op jit(solution)/shard_map/ppermute | solution.py:43
  64.8 23.0 %collective-permute-start.14 = (s16[400,512]{1,0:T(8,128)(2,1)S(1)}, s16[400,512]{1,0:T(8,128)(2,1)S(1)}, u32[]{:S(2)}, u32[]{:S(2)}) collective-permute-start(s16[400,512]{1,0:T(8,128)(2,1)S(1)} %get-tuple-element.55), channel_id=1, source_target_pairs={{0,3},{1,2},{2,1},{3,0},{4,7},{5,6},{6,5},{7,4},{8,11},{9,10},{10,... | collective-permute-start | bytes 1228808 | tf_op jit(solution)/shard_map/ppermute | solution.py:43
  73.7 14.0 %collective-permute-start.15 = (bf16[3,96,512]{2,1,0:T(8,128)(2,1)S(1)}, bf16[3,96,512]{2,1,0:T(8,128)(2,1)S(1)}, u32[]{:S(2)}, u32[]{:S(2)}) collective-permute-start(bf16[3,96,512]{2,1,0:T(8,128)(2,1)S(1)} %bitcast_multiply_fusion.refs_5_.refs_9_), channel_id=1, source_target_pairs={{0,8},{1,9},{2,10},{3,11},{4,12},{5,13},{6,14},{7,15},{8,0},{9,1},... | collective-permute-start | bytes 884744 | tf_op jit(solution)/shard_map/ppermute | solution.py:43
  88.3 20.3 %collective-permute-start.23 = (s16[400,512]{1,0:T(8,128)(2,1)S(1)}, s16[400,512]{1,0:T(8,128)(2,1)S(1)}, u32[]{:S(2)}, u32[]{:S(2)}) collective-permute-start(s16[400,512]{1,0:T(8,128)(2,1)S(1)} %get-tuple-element.73), channel_id=1, source_target_pairs={{0,2},{1,3},{2,0},{3,1},{4,6},{5,7},{6,4},{7,5},{8,10},{9,11},{10,... | collective-permute-start | bytes 1228808 | tf_op jit(solution)/shard_map/ppermute | solution.py:43
  99.3 13.4 %collective-permute-start.17 = (s16[400,512]{1,0:T(8,128)(2,1)S(1)}, s16[400,512]{1,0:T(8,128)(2,1)S(1)}, u32[]{:S(2)}, u32[]{:S(2)}) collective-permute-start(s16[400,512]{1,0:T(8,128)(2,1)S(1)} %get-tuple-element.63), channel_id=1, source_target_pairs={{0,1},{1,0},{2,3},{3,2},{4,5},{5,4},{6,7},{7,6},{8,9},{9,8},{10,11... | collective-permute-start | bytes 1228808 | tf_op jit(solution)/shard_map/ppermute | solution.py:43
  99.7 21.7 %collective-permute-start.18 = (s16[400,512]{1,0:T(8,128)(2,1)S(1)}, s16[400,512]{1,0:T(8,128)(2,1)S(1)}, u32[]{:S(2)}, u32[]{:S(2)}) collective-permute-start(s16[400,512]{1,0:T(8,128)(2,1)S(1)} %get-tuple-element.64), channel_id=1, source_target_pairs={{0,2},{1,3},{2,0},{3,1},{4,6},{5,7},{6,4},{7,5},{8,10},{9,11},{10,... | collective-permute-start | bytes 1228808 | tf_op jit(solution)/shard_map/ppermute | solution.py:43
  103.3 20.4 %collective-permute-start.19 = (s16[400,512]{1,0:T(8,128)(2,1)S(1)}, s16[400,512]{1,0:T(8,128)(2,1)S(1)}, u32[]{:S(2)}, u32[]{:S(2)}) collective-permute-start(s16[400,512]{1,0:T(8,128)(2,1)S(1)} %get-tuple-element.65), channel_id=1, source_target_pairs={{0,3},{1,2},{2,1},{3,0},{4,7},{5,6},{6,5},{7,4},{8,11},{9,10},{10,... | collective-permute-start | bytes 1228808 | tf_op jit(solution)/shard_map/ppermute | solution.py:43
  108.5 32.0 %collective-permute-start.20 = (s16[400,512]{1,0:T(8,128)(2,1)S(1)}, s16[400,512]{1,0:T(8,128)(2,1)S(1)}, u32[]{:S(2)}, u32[]{:S(2)}) collective-permute-start(s16[400,512]{1,0:T(8,128)(2,1)S(1)} %get-tuple-element.69), channel_id=1, source_target_pairs={{0,1},{1,0},{2,3},{3,2},{4,5},{5,4},{6,7},{7,6},{8,9},{9,8},{10,11... | collective-permute-start | bytes 1228808 | tf_op jit(solution)/shard_map/ppermute | solution.py:43
  108.6 31.9 %collective-permute-start.21 = (s16[400,512]{1,0:T(8,128)(2,1)S(1)}, s16[400,512]{1,0:T(8,128)(2,1)S(1)}, u32[]{:S(2)}, u32[]{:S(2)}) collective-permute-start(s16[400,512]{1,0:T(8,128)(2,1)S(1)} %get-tuple-element.70), channel_id=1, source_target_pairs={{0,2},{1,3},{2,0},{3,1},{4,6},{5,7},{6,4},{7,5},{8,10},{9,11},{10,... | collective-permute-start | bytes 1228808 | tf_op jit(solution)/shard_map/ppermute | solution.py:43
  112.7 28.2 %collective-permute-start.22 = (s16[400,512]{1,0:T(8,128)(2,1)S(1)}, s16[400,512]{1,0:T(8,128)(2,1)S(1)}, u32[]{:S(2)}, u32[]{:S(2)}) collective-permute-start(s16[400,512]{1,0:T(8,128)(2,1)S(1)} %get-tuple-element.71), channel_id=1, source_target_pairs={{0,3},{1,2},{2,1},{3,0},{4,7},{5,6},{6,5},{7,4},{8,11},{9,10},{10,... | collective-permute-start | bytes 1228808 | tf_op jit(solution)/shard_map/ppermute | solution.py:43
  121.4 8.4 %collective-permute-start.25 = (bf16[3,96,512]{2,1,0:T(8,128)(2,1)S(1)}, bf16[3,96,512]{2,1,0:T(8,128)(2,1)S(1)}, u32[]{:S(2)}, u32[]{:S(2)}) collective-permute-start(bf16[3,96,512]{2,1,0:T(8,128)(2,1)S(1)} %bitcast_multiply_fusion.refs_5_.refs_9_), channel_id=1, source_target_pairs={{0,12},{1,13},{2,14},{3,15},{4,8},{5,9},{6,10},{7,11},{8,4},{9,5},... | collective-permute-start | bytes 884744 | tf_op jit(solution)/shard_map/ppermute | solution.py:43
  123.7 14.8 %collective-permute-start.24 = (bf16[3,96,512]{2,1,0:T(8,128)(2,1)S(1)}, bf16[3,96,512]{2,1,0:T(8,128)(2,1)S(1)}, u32[]{:S(2)}, u32[]{:S(2)}) collective-permute-start(bf16[3,96,512]{2,1,0:T(8,128)(2,1)S(1)} %bitcast_multiply_fusion.refs_5_.refs_9_), channel_id=1, source_target_pairs={{0,4},{1,5},{2,6},{3,7},{4,0},{5,1},{6,2},{7,3},{8,12},{9,13},{10,... | collective-permute-start | bytes 884744 | tf_op jit(solution)/shard_map/ppermute | solution.py:43
  150.4 19.3 %all-to-all-start = ((s16[16,48,640]{2,1,0:T(8,128)(2,1)}), s16[16,48,640]{2,1,0:T(8,128)(2,1)S(1)}, u32[]{:S(2)}, u32[]{:S(2)}) async-start(s16[16,48,640]{2,1,0:T(8,128)(2,1)} %bitcast.23), calls=%async_computation | async-start | bytes 1966080 | tf_op jit(solution)/shard_map/all_to_all | solution.py:412
  154.1 26.4 %collective-permute-start.26 = (s16[224,512]{1,0:T(8,128)(2,1)S(1)}, s16[224,512]{1,0:T(8,128)(2,1)S(1)}, u32[]{:S(2)}, u32[]{:S(2)}) collective-permute-start(s16[224,512]{1,0:T(8,128)(2,1)S(1)} %get-tuple-element.83), channel_id=1, source_target_pairs={{0,4},{1,5},{2,6},{3,7},{4,0},{5,1},{6,2},{7,3},{8,12},{9,13},{10,... | collective-permute-start | bytes 688136 | tf_op jit(solution)/shard_map/ppermute | solution.py:43
  154.2 27.5 %collective-permute-start.27 = (s16[224,512]{1,0:T(8,128)(2,1)S(1)}, s16[224,512]{1,0:T(8,128)(2,1)S(1)}, u32[]{:S(2)}, u32[]{:S(2)}) collective-permute-start(s16[224,512]{1,0:T(8,128)(2,1)S(1)} %get-tuple-element.84), channel_id=1, source_target_pairs={{0,8},{1,9},{2,10},{3,11},{4,12},{5,13},{6,14},{7,15},{8,0},{9,1},... | collective-permute-start | bytes 688136 | tf_op jit(solution)/shard_map/ppermute | solution.py:43
  156.8 24.9 %collective-permute-start.28 = (s16[224,512]{1,0:T(8,128)(2,1)S(1)}, s16[224,512]{1,0:T(8,128)(2,1)S(1)}, u32[]{:S(2)}, u32[]{:S(2)}) collective-permute-start(s16[224,512]{1,0:T(8,128)(2,1)S(1)} %get-tuple-element.85), channel_id=1, source_target_pairs={{0,12},{1,13},{2,14},{3,15},{4,8},{5,9},{6,10},{7,11},{8,4},{9,5},... | collective-permute-start | bytes 688136 | tf_op jit(solution)/shard_map/ppermute | solution.py:43
  170.0 8.0 %collective-permute-start.34 = (f32[48,512]{1,0:T(8,128)S(1)}, f32[48,512]{1,0:T(8,128)S(1)}, u32[]{:S(2)}, u32[]{:S(2)}) collective-permute-start(f32[48,512]{1,0:T(8,128)S(1)} %gathered.1), channel_id=1, source_target_pairs={{0,32},{1,33},{2,34},{3,35},{4,36},{5,37},{6,38},{7,39},{8,40},{9,... | collective-permute-start | bytes 294920 | tf_op jit(solution)/shard_map/ppermute | solution.py:43
  180.5 8.5 %collective-permute-start.36 = (f32[48,512]{1,0:T(8,128)S(1)}, f32[48,512]{1,0:T(8,128)S(1)}, u32[]{:S(2)}, u32[]{:S(2)}) collective-permute-start(f32[48,512]{1,0:T(8,128)S(1)} %add.45.own_ref), channel_id=1, source_target_pairs={{0,8},{1,9},{2,10},{3,11},{4,12},{5,13},{6,14},{7,15},{8,0},{9,1},... | collective-permute-start | bytes 294920 | tf_op jit(solution)/shard_map/ppermute | solution.py:43
  180.5 8.5 %collective-permute-start.35 = (f32[48,512]{1,0:T(8,128)S(1)}, f32[48,512]{1,0:T(8,128)S(1)}, u32[]{:S(2)}, u32[]{:S(2)}) collective-permute-start(f32[48,512]{1,0:T(8,128)S(1)} %add.45.own_ref), channel_id=1, source_target_pairs={{0,4},{1,5},{2,6},{3,7},{4,0},{5,1},{6,2},{7,3},{8,12},{9,13},{10,... | collective-permute-start | bytes 294920 | tf_op jit(solution)/shard_map/ppermute | solution.py:43
  190.1 20.2 %all-to-all-start.1 = ((s16[16,48,640]{2,1,0:T(8,128)(2,1)}), s16[16,48,640]{2,1,0:T(8,128)(2,1)}, u32[]{:S(2)}, u32[]{:S(2)}) async-start(s16[16,48,640]{2,1,0:T(8,128)(2,1)} %copies.1), calls=%async_computation.1 | async-start | bytes 1966080 | tf_op jit(solution)/shard_map/all_to_all | solution.py:417
  199.3 6.6 %collective-permute-start.33 = (s16[112,512]{1,0:T(8,128)(2,1)S(1)}, s16[112,512]{1,0:T(8,128)(2,1)S(1)}, u32[]{:S(2)}, u32[]{:S(2)}) collective-permute-start(s16[112,512]{1,0:T(8,128)(2,1)S(1)} %get-tuple-element.95), channel_id=1, source_target_pairs={{0,12},{1,13},{2,14},{3,15},{4,8},{5,9},{6,10},{7,11},{8,4},{9,5},... | collective-permute-start | bytes 344072 | tf_op jit(solution)/shard_map/ppermute | solution.py:43
  (12 other events, 129.2 us)

commit v8 on v6

--- a/solution.py
+++ b/solution.py
@@ -311,9 +311,8 @@
     )(pieces)
 
 
-def copies_kernel(own_ref, r1_ref, r2_ref, r3_ref, out_ref):
-    total = (own_ref[...] + r1_ref[...]) + (r2_ref[...] + r3_ref[...])
-    encode_lanes(total, out_ref.at[0])
+def copies_kernel(own_ref, other_ref, out_ref):
+    encode_lanes(own_ref[...] + other_ref[...], out_ref.at[0])
     for k in range(1, out_ref.shape[0]):
         out_ref[k] = out_ref[0]
 
@@ -322,13 +321,13 @@
     rows, width = own.shape
     return pl.pallas_call(
         copies_kernel,
-        in_specs=[VMEM] * 4,
+        in_specs=[VMEM] * 2,
         out_specs=VMEM,
         out_shape=jax.ShapeDtypeStruct((16, rows, width + LANES), I16),
         compiler_params=params(),
         cost_estimate=cost(rows * width, 32 * rows * width),
         name="copies",
-    )(own, *found)
+    )(own, found)
 
 
 def finish_kernel(at_ref, mine_ref, theirs_ref, diag_ref, out_ref):
@@ -406,9 +405,9 @@
     pieces = halves.reshape(16, -1, width + LANES)
     total = gathered(lax.all_to_all(pieces, ("x", "y"), 0, 0))
     found_01 = after(found_01, total)
-    total = total + send(total, over_h)
-    beyond = [send(total, over_l(k)) for k in (1, 2, 3)]
-    pieces = copies(total, after(beyond, found_01))
+    near = [send(total, over_l(k)) for k in (1, 2, 3)]
+    total = (total + near[0]) + (near[1] + near[2])
+    pieces = copies(total, after(send(total, over_h), found_01))
     mine = after(lax.all_to_all(pieces, ("x", "y"), 0, 0), found_2).reshape(halves.shape)
     blocks = last([(own_01, found_01, (0, 1)), (own_2, found_2, (2,))], masked.shape)
     diagonal = finish(at, mine, send(mine, over_core), diag_inverse)

time: 213 us -> 222 us (1.042); the launches traced: 212 us -> 219 us
  blocking collectives: 0 us -> 17.9 us
  waiting for transfers between devices: 91.9 us -> 82 us
    all_to_all x0 -> x1, blocking collectives: none -> 17.9 us  [body(): total = gathered(lax.all_to_all(pieces, ('x', 'y'), 0, 0))]
    all_to_all x1 -> x0, waiting for transfers between devices: 12 us -> none  [body(): total = gathered(lax.all_to_all(pieces, ('x', 'y'), 0, 0))]
    ppermute x39, waiting for transfers between devices: 74.8 us -> 82 us  [send(): return lax.ppermute(value, AXES, pairs)]
    ppermute x39, starting transfers between devices: 74.7 us -> 79.9 us  [send(): return lax.ppermute(value, AXES, pairs)]
    all_to_all x1, waiting for transfers between devices: 5.04 us -> 0.01 us  [body(): lax.all_to_all(pieces, ('x', 'y'), 0, 0)]
    all_to_all x1 -> x0, starting transfers between devices: 3.64 us -> none  [body(): total = gathered(lax.all_to_all(pieces, ('x', 'y'), 0, 0))]
  transfers between devices with their start and end apart: 41 -> 40, of which waited for: 22 -> 20; matrix products, arithmetic and copies ran while one was open for 1% -> 1% of each run, Pallas kernels for 9% -> 8%
where the time goes in v8:
time: 222 us; the launch traced here: 219 us
  starting transfers between devices  83.8 us (38%)
  waiting for transfers between devices  82 us (37%)
  Pallas kernels  25.9 us (12%)
  blocking collectives  17.9 us (8%)
  local copies, waits for them, and re-layouts  5.31 us (2%)
  other arithmetic  2.65 us (1%)
    ppermute x39, waiting for transfers between devices, send(): return lax.ppermute(value, AXES, pairs)  82 us
    ppermute x39, starting transfers between devices, send(): return lax.ppermute(value, AXES, pairs)  79.9 us
    all_to_all x1, blocking collectives, body(): total = gathered(lax.all_to_all(pieces, ('x', 'y'), 0, 0))  17.9 us
    pallas_call x3, Pallas kernels, product(): pl.pallas_call(functools.partial(product_kernel, panels), grid_spec=pltpu...  15.1 us
    pallas_call x2, Pallas kernels, middle(): pl.pallas_call(functools.partial(middle_kernel, panels, base), in_specs=[...  5.06 us
  transfers between devices with their start and end apart: 40, of which 20 were waited for; matrix products, arithmetic and copies ran while one was open for 1% of the time, Pallas kernels for 8%

profile of v8, /device:TPU:1, one launch (start us, length us, event | category | flops | bytes accessed | tf_op | source)
XLA Modules:
  0.0 218.5 jit_solution(9840685161165198849)
XLA Ops:
  3.5 9.4 %collective-permute-start.5 = (bf16[1,96,512]{2,1,0:T(8,128)(2,1)S(1)}, bf16[1,96,512]{2,1,0:T(8,128)(2,1)S(1)}, u32[]{:S(2)}, u32[]{:S(2)}) collective-permute-start(bf16[1,96,512]{2,1,0:T(8,128)(2,1)S(1)} %collective-permute-done.3), channel_id=1, source_target_pairs={{0,32},{1,0},{2,48},{3,16},{4,36},{5,4},{6,52},{7,20},{8,40},{9,8}... | collective-permute-start | bytes 294920 | tf_op jit(solution)/shard_map/ppermute | solution.py:43
  15.6 4.8 %collective-permute-done.4 = bf16[1,96,512]{2,1,0:T(8,128)(2,1)S(1)} collective-permute-done((bf16[1,96,512]{2,1,0:T(8,128)(2,1)S(1)}, bf16[1,96,512]{2,1,0:T(8,128)(2,1)S(1)}, u32[]{:S(2)}, u32[]{:S(2)}) %collective-permute-start.4) | collective-permute-done | bytes 98336 | tf_op jit(solution)/shard_map/ppermute | solution.py:43
  20.4 11.0 %collective-permute-start.7 = (bf16[2,1,96,512]{3,2,0,1:T(8,128)(2,1)S(1)}, bf16[2,1,96,512]{3,2,0,1:T(8,128)(2,1)S(1)}, u32[]{:S(2)}, u32[]{:S(2)}) collective-permute-start(bf16[2,1,96,512]{3,2,0,1:T(8,128)(2,1)S(1)} %bitcast.36), channel_id=1, source_target_pairs={{0,128},{1,129},{2,130},{3,131},{4,132},{5,133},{6,134},{7,135},{8... | collective-permute-start | bytes 589832 | tf_op jit(solution)/shard_map/ppermute | solution.py:43
  36.7 2.8 %collective-permute-done.6 = bf16[2,1,96,512]{3,2,0,1:T(8,128)(2,1)S(1)} collective-permute-done((bf16[2,1,96,512]{3,2,0,1:T(8,128)(2,1)S(1)}, bf16[2,1,96,512]{3,2,0,1:T(8,128)(2,1)S(1)}, u32[]{:S(2)}, u32[]{:S(2)}) %collective-permute-start.6) | collective-permute-done | bytes 196640 | tf_op jit(solution)/shard_map/ppermute | solution.py:43
  39.8 6.8 %collective-permute-done.1 = bf16[2,96,512]{2,1,0:T(8,128)(2,1)S(1)} collective-permute-done((bf16[2,96,512]{2,1,0:T(8,128)(2,1)S(1)}, bf16[2,96,512]{2,1,0:T(8,128)(2,1)S(1)}, u32[]{:S(2)}, u32[]{:S(2)}) %collective-permute-start.1) | collective-permute-done | bytes 196640 | tf_op jit(solution)/shard_map/ppermute | solution.py:43
  46.6 9.6 %collective-permute-start.11 = (bf16[2,2,96,512]{3,2,1,0:T(8,128)(2,1)S(1)}, bf16[2,2,96,512]{3,2,1,0:T(8,128)(2,1)S(1)}, u32[]{:S(2)}, u32[]{:S(2)}) collective-permute-start(bf16[2,2,96,512]{3,2,1,0:T(8,128)(2,1)S(1)} %pad_maximum_fusion.2), channel_id=1, source_target_pairs={{0,192},{1,193},{2,194},{3,195},{4,196},{5,197},{6,198},{7,199},{8... | collective-permute-start | bytes 1179656 | tf_op jit(solution)/shard_map/ppermute | solution.py:43
  57.0 2.3 %copy-done = bf16[1536,1536]{1,0:T(8,128)(2,1)S(1)} copy-done((bf16[1536,1536]{1,0:T(8,128)(2,1)S(1)}, bf16[1536,1536]{1,0:T(8,128)(2,1)}, u32[]{:S(2)}) %copy-start) | copy-done | bytes 4718616
  59.4 5.0 %product.3 = (f32[384,512]{1,0:T(8,128)S(1)}, s16[400,512]{1,0:T(8,128)(2,1)S(1)}, s16[400,512]{1,0:T(8,128)(2,1)S(1)}, s16[400,512]{1,0:T(8,128)(2,1)S(1)}) custom-call(s32[6]{0:T(128)S(1)} %stack.75.at_ref.refs_0_, bf16[4,4,96,1536]{3,2,1,0:T(8,128)(2,1)S(1)} %bitcast.27, bf16[4,2,1,96,512]{4,3,2,1,0:T(8,128)(2,1)S(1)} %bitcast.33, ...), custom_call_target="tpu_custom_call" | custom-call | flops 2415919 | bytes 4718 | tf_op jit(solution)/shard_map/product/pallas_call | solution.py:152
  66.5 7.2 %collective-permute-done.11 = bf16[2,2,96,512]{3,2,1,0:T(8,128)(2,1)S(1)} collective-permute-done((bf16[2,2,96,512]{3,2,1,0:T(8,128)(2,1)S(1)}, bf16[2,2,96,512]{3,2,1,0:T(8,128)(2,1)S(1)}, u32[]{:S(2)}, u32[]{:S(2)}) %collective-permute-start.11) | collective-permute-done | bytes 393248 | tf_op jit(solution)/shard_map/ppermute | solution.py:43
  75.6 2.3 %collective-permute-start.15 = (bf16[4,2,2,96,512]{4,3,2,1,0:T(8,128)(2,1)S(1)}, bf16[4,2,2,96,512]{4,3,2,1,0:T(8,128)(2,1)S(1)}, u32[]{:S(2)}, u32[]{:S(2)}) collective-permute-start(bf16[4,2,2,96,512]{4,3,2,1,0:T(8,128)(2,1)S(1)} %pad_maximum_fusion.own_ref), channel_id=1, source_target_pairs={{0,16},{1,17},{2,18},{3,19},{4,20},{5,21},{6,22},{7,23},{8,24},{9,... | collective-permute-start | bytes 4718600 | tf_op jit(solution)/shard_map/ppermute | solution.py:43
  78.8 2.1 collective-permute-done.15.other_ref
  80.9 5.1 %product.4 = (f32[384,512]{1,0:T(8,128)S(1)}, s16[400,512]{1,0:T(8,128)(2,1)S(1)}, s16[400,512]{1,0:T(8,128)(2,1)S(1)}, s16[400,512]{1,0:T(8,128)(2,1)S(1)}) custom-call(s32[6]{0:T(128)S(1)} %stack.75.at_ref.refs_0_, bf16[4,4,96,1536]{3,2,1,0:T(8,128)(2,1)S(1)} %bitcast.28, bf16[4,2,2,96,512]{4,3,2,1,0:T(8,128)(2,1)S(1)} %pad_maximum_fusion.own_ref, ...), custom_call_target="tpu_custom_call" | custom-call | flops 2415919 | bytes 4718 | tf_op jit(solution)/shard_map/product/pallas_call | solution.py:152
  86.1 4.0 %collective-permute-start.16 = (bf16[3,96,512]{2,1,0:T(8,128)(2,1)S(1)}, bf16[3,96,512]{2,1,0:T(8,128)(2,1)S(1)}, u32[]{:S(2)}, u32[]{:S(2)}) collective-permute-start(bf16[3,96,512]{2,1,0:T(8,128)(2,1)S(1)} %bitcast_multiply_fusion.refs_5_.refs_9_), channel_id=1, source_target_pairs={{0,8},{1,9},{2,10},{3,11},{4,12},{5,13},{6,14},{7,15},{8,0},{9,1},... | collective-permute-start | bytes 884744 | tf_op jit(solution)/shard_map/ppermute | solution.py:43
  90.1 3.6 %collective-permute-start.18 = (s16[400,512]{1,0:T(8,128)(2,1)S(1)}, s16[400,512]{1,0:T(8,128)(2,1)S(1)}, u32[]{:S(2)}, u32[]{:S(2)}) collective-permute-start(s16[400,512]{1,0:T(8,128)(2,1)S(1)} %get-tuple-element.64), channel_id=1, source_target_pairs={{0,2},{1,3},{2,0},{3,1},{4,6},{5,7},{6,4},{7,5},{8,10},{9,11},{10,... | collective-permute-start | bytes 1228808 | tf_op jit(solution)/shard_map/ppermute | solution.py:43
  93.6 9.6 %collective-permute-done.16.refs_7_.refs_11_ = bf16[3,96,512]{2,1,0:T(8,128)(2,1)S(1)} collective-permute-done((bf16[3,96,512]{2,1,0:T(8,128)(2,1)S(1)}, bf16[3,96,512]{2,1,0:T(8,128)(2,1)S(1)}, u32[]{:S(2)}, u32[]{:S(2)}) %collective-permute-start.16) | collective-permute-done | bytes 294944 | tf_op jit(solution)/shard_map/ppermute | solution.py:43
  103.3 5.1 %product.5 = (f32[384,512]{1,0:T(8,128)S(1)}, s16[400,512]{1,0:T(8,128)(2,1)S(1)}, s16[400,512]{1,0:T(8,128)(2,1)S(1)}, s16[400,512]{1,0:T(8,128)(2,1)S(1)}) custom-call(s32[6]{0:T(128)S(1)} %stack.75.at_ref.refs_0_, bf16[4,4,96,1536]{3,2,1,0:T(8,128)(2,1)S(1)} %bitcast.29, bf16[4,2,2,96,512]{4,3,2,1,0:T(8,128)(2,1)S(1)} %pad_maximum_fusion.own_ref, ...), custom_call_target="tpu_custom_call" | custom-call | flops 2415919 | bytes 4718 | tf_op jit(solution)/shard_map/product/pallas_call | solution.py:152
  109.6 2.7 %collective-permute-start.21 = (s16[400,512]{1,0:T(8,128)(2,1)S(1)}, s16[400,512]{1,0:T(8,128)(2,1)S(1)}, u32[]{:S(2)}, u32[]{:S(2)}) collective-permute-start(s16[400,512]{1,0:T(8,128)(2,1)S(1)} %get-tuple-element.70), channel_id=1, source_target_pairs={{0,2},{1,3},{2,0},{3,1},{4,6},{5,7},{6,4},{7,5},{8,10},{9,11},{10,... | collective-permute-start | bytes 1228808 | tf_op jit(solution)/shard_map/ppermute | solution.py:43
  114.0 7.6 %collective-permute-done.25.refs_8_.refs_12_ = bf16[3,96,512]{2,1,0:T(8,128)(2,1)S(1)} collective-permute-done((bf16[3,96,512]{2,1,0:T(8,128)(2,1)S(1)}, bf16[3,96,512]{2,1,0:T(8,128)(2,1)S(1)}, u32[]{:S(2)}, u32[]{:S(2)}) %collective-permute-start.25) | collective-permute-done | bytes 294944 | tf_op jit(solution)/shard_map/ppermute | solution.py:43
  121.6 7.4 %collective-permute-done.24.refs_6_.refs_10_ = bf16[3,96,512]{2,1,0:T(8,128)(2,1)S(1)} collective-permute-done((bf16[3,96,512]{2,1,0:T(8,128)(2,1)S(1)}, bf16[3,96,512]{2,1,0:T(8,128)(2,1)S(1)}, u32[]{:S(2)}, u32[]{:S(2)}) %collective-permute-start.24) | collective-permute-done | bytes 294944 | tf_op jit(solution)/shard_map/ppermute | solution.py:43
  132.2 3.1 %middle.3 = (f32[192,512]{1,0:T(8,128)S(1)}, s16[224,512]{1,0:T(8,128)(2,1)S(1)}, s16[224,512]{1,0:T(8,128)(2,1)S(1)}, s16[224,512]{1,0:T(8,128)(2,1)S(1)}, f32[...) custom-call(s32[6]{0:T(128)S(1)} %stack.75.at_ref.refs_0_, f32[384,512]{1,0:T(8,128)S(1)} %get-tuple-element.56.refs_1_, ...), custom_call_target="tpu_custom_call" | custom-call | flops 603979 | bytes 3145 | tf_op jit(solution)/shard_map/middle/pallas_call | solution.py:215
  135.3 2.0 collective-permute-start.29
  137.5 2.9 %collective-permute-done.30.refs_3_ = f32[256,512]{1,0:T(8,128)S(1)} collective-permute-done((f32[256,512]{1,0:T(8,128)S(1)}, f32[256,512]{1,0:T(8,128)S(1)}, u32[]{:S(2)}, u32[]{:S(2)}) %collective-permute-start.30) | collective-permute-done | bytes 524320 | tf_op jit(solution)/shard_map/ppermute | solution.py:43
  140.9 17.9 %all_to_all.10.in_ref = s16[16,48,640]{2,1,0:T(8,128)(2,1)S(1)} all-to-all(s16[16,48,640]{2,1,0:T(8,128)(2,1)S(1)} %bitcast.30), channel_id=1, replica_groups=mesh['x'=4,'h'=2,'core'=2,'l'=4,'y'=4] {'x','y'}, dimensions={0} | all-to-all | bytes 1966080 | tf_op jit(solution)/shard_map/all_to_all | solution.py:406
  166.2 3.4 %collective-permute-done.35 = f32[48,512]{1,0:T(8,128)S(1)} collective-permute-done((f32[48,512]{1,0:T(8,128)S(1)}, f32[48,512]{1,0:T(8,128)S(1)}, u32[]{:S(2)}, u32[]{:S(2)}) %collective-permute-start.35) | collective-permute-done | bytes 98336 | tf_op jit(solution)/shard_map/ppermute | solution.py:43
  171.4 6.6 %collective-permute-done.26.refs_1_ = s16[224,512]{1,0:T(8,128)(2,1)S(1)} collective-permute-done((s16[224,512]{1,0:T(8,128)(2,1)S(1)}, s16[224,512]{1,0:T(8,128)(2,1)S(1)}, u32[]{:S(2)}, u32[]{:S(2)}) %collective-permute-start.26) | collective-permute-done | bytes 229408 | tf_op jit(solution)/shard_map/ppermute | solution.py:43
  178.0 4.1 %collective-permute-done.28.refs_3_ = s16[224,512]{1,0:T(8,128)(2,1)S(1)} collective-permute-done((s16[224,512]{1,0:T(8,128)(2,1)S(1)}, s16[224,512]{1,0:T(8,128)(2,1)S(1)}, u32[]{:S(2)}, u32[]{:S(2)}) %collective-permute-start.28) | collective-permute-done | bytes 229408 | tf_op jit(solution)/shard_map/ppermute | solution.py:43
  182.1 5.0 %collective-permute-done.37.other_ref = f32[48,512]{1,0:T(8,128)S(1)} collective-permute-done((f32[48,512]{1,0:T(8,128)S(1)}, f32[48,512]{1,0:T(8,128)S(1)}, u32[]{:S(2)}, u32[]{:S(2)}) %collective-permute-start.37) | collective-permute-done | bytes 98336 | tf_op jit(solution)/shard_map/ppermute | solution.py:43
  188.3 4.0 %all-to-all-start.1 = ((s16[16,48,640]{2,1,0:T(8,128)(2,1)}), s16[16,48,640]{2,1,0:T(8,128)(2,1)S(1)}, u32[]{:S(2)}, u32[]{:S(2)}) async-start(s16[16,48,640]{2,1,0:T(8,128)(2,1)} %copies.1), calls=%async_computation.1 | async-start | bytes 1966080 | tf_op jit(solution)/shard_map/all_to_all | solution.py:411
  192.2 7.2 %collective-permute-start.31 = (s16[112,512]{1,0:T(8,128)(2,1)S(1)}, s16[112,512]{1,0:T(8,128)(2,1)S(1)}, u32[]{:S(2)}, u32[]{:S(2)}) collective-permute-start(s16[112,512]{1,0:T(8,128)(2,1)S(1)} %get-tuple-element.93), channel_id=1, source_target_pairs={{0,4},{1,5},{2,6},{3,7},{4,0},{5,1},{6,2},{7,3},{8,12},{9,13},{10,... | collective-permute-start | bytes 344072 | tf_op jit(solution)/shard_map/ppermute | solution.py:43
  202.1 7.4 %collective-permute-done.32.refs_6_ = s16[112,512]{1,0:T(8,128)(2,1)S(1)} collective-permute-done((s16[112,512]{1,0:T(8,128)(2,1)S(1)}, s16[112,512]{1,0:T(8,128)(2,1)S(1)}, u32[]{:S(2)}, u32[]{:S(2)}) %collective-permute-start.32) | collective-permute-done | bytes 114720 | tf_op jit(solution)/shard_map/ppermute | solution.py:43
  209.5 2.2 collective-permute-start.38
  215.8 2.7 %finish.1 = f32[3,512,512]{2,1,0:T(8,128)} custom-call(s32[6]{0:T(128)S(1)} %stack.75.at_ref.refs_0_, s16[768,640]{1,0:T(8,128)(2,1)S(1)} %bitcast.32, s16[768,640]{1,0:T(8,128)(2,1)S(1)} %collective-permute-done.38.theirs_ref, f32[3,512,512]{2,1,0:T(8,128)S(1)} %copy-done.1), custom_call_target="tpu_custom_call" | custom-call | flops 786 | bytes 9437 | tf_op jit(solution)/shard_map/finish/pallas_call | solution.py:344
  (75 shorter events, 40.6 us)
Async XLA Ops:
  3.5 12.0 %collective-permute-start.5 = (bf16[1,96,512]{2,1,0:T(8,128)(2,1)S(1)}, bf16[1,96,512]{2,1,0:T(8,128)(2,1)S(1)}, u32[]{:S(2)}, u32[]{:S(2)}) collective-permute-start(bf16[1,96,512]{2,1,0:T(8,128)(2,1)S(1)} %collective-permute-done.3), channel_id=1, source_target_pairs={{0,32},{1,0},{2,48},{3,16},{4,36},{5,4},{6,52},{7,20},{8,40},{9,8}... | collective-permute-start | bytes 294920 | tf_op jit(solution)/shard_map/ppermute | solution.py:43
  12.9 7.4 %collective-permute-start.4 = (bf16[1,96,512]{2,1,0:T(8,128)(2,1)S(1)}, bf16[1,96,512]{2,1,0:T(8,128)(2,1)S(1)}, u32[]{:S(2)}, u32[]{:S(2)}) collective-permute-start(bf16[1,96,512]{2,1,0:T(8,128)(2,1)S(1)} %collective-permute-done.3), channel_id=1, source_target_pairs={{0,0},{1,32},{2,16},{3,48},{4,4},{5,36},{6,20},{7,52},{8,8},{9,40}... | collective-permute-start | bytes 294920 | tf_op jit(solution)/shard_map/ppermute | solution.py:43
  20.4 16.3 %collective-permute-start.7 = (bf16[2,1,96,512]{3,2,0,1:T(8,128)(2,1)S(1)}, bf16[2,1,96,512]{3,2,0,1:T(8,128)(2,1)S(1)}, u32[]{:S(2)}, u32[]{:S(2)}) collective-permute-start(bf16[2,1,96,512]{3,2,0,1:T(8,128)(2,1)S(1)} %bitcast.36), channel_id=1, source_target_pairs={{0,128},{1,129},{2,130},{3,131},{4,132},{5,133},{6,134},{7,135},{8... | collective-permute-start | bytes 589832 | tf_op jit(solution)/shard_map/ppermute | solution.py:43
  31.4 8.1 %collective-permute-start.6 = (bf16[2,1,96,512]{3,2,0,1:T(8,128)(2,1)S(1)}, bf16[2,1,96,512]{3,2,0,1:T(8,128)(2,1)S(1)}, u32[]{:S(2)}, u32[]{:S(2)}) collective-permute-start(bf16[2,1,96,512]{3,2,0,1:T(8,128)(2,1)S(1)} %bitcast.37), channel_id=1, source_target_pairs={{0,64},{1,65},{2,66},{3,67},{4,68},{5,69},{6,70},{7,71},{8,72},{9,... | collective-permute-start | bytes 589832 | tf_op jit(solution)/shard_map/ppermute | solution.py:43
  32.4 7.4 %collective-permute-start.2 = (bf16[2,96,512]{2,1,0:T(8,128)(2,1)S(1)}, bf16[2,96,512]{2,1,0:T(8,128)(2,1)S(1)}, u32[]{:S(2)}, u32[]{:S(2)}) collective-permute-start(bf16[2,96,512]{2,1,0:T(8,128)(2,1)S(1)} %collective-permute-done), channel_id=1, source_target_pairs={{0,32},{1,0},{2,48},{3,16},{4,36},{5,4},{6,52},{7,20},{8,40},{9,8}... | collective-permute-start | bytes 589832 | tf_op jit(solution)/shard_map/ppermute | solution.py:43
  34.2 12.4 %collective-permute-start.1 = (bf16[2,96,512]{2,1,0:T(8,128)(2,1)S(1)}, bf16[2,96,512]{2,1,0:T(8,128)(2,1)S(1)}, u32[]{:S(2)}, u32[]{:S(2)}) collective-permute-start(bf16[2,96,512]{2,1,0:T(8,128)(2,1)S(1)} %collective-permute-done), channel_id=1, source_target_pairs={{0,0},{1,32},{2,16},{3,48},{4,4},{5,36},{6,20},{7,52},{8,8},{9,40}... | collective-permute-start | bytes 589832 | tf_op jit(solution)/shard_map/ppermute | solution.py:43
  46.6 10.4 %collective-permute-start.12 = (bf16[4,2,1,96,512]{4,3,1,2,0:T(8,128)(2,1)S(1)}, bf16[4,2,1,96,512]{4,3,1,2,0:T(8,128)(2,1)S(1)}, u32[]{:S(2)}, u32[]{:S(2)}) collective-permute-start(bf16[4,2,1,96,512]{4,3,1,2,0:T(8,128)(2,1)S(1)} %pad_maximum_fusion.1), channel_id=1, source_target_pairs={{0,16},{1,17},{2,18},{3,19},{4,20},{5,21},{6,22},{7,23},{8,24},{9,... | collective-permute-start | bytes 2359304 | tf_op jit(solution)/shard_map/ppermute | solution.py:43
  46.6 27.1 %collective-permute-start.11 = (bf16[2,2,96,512]{3,2,1,0:T(8,128)(2,1)S(1)}, bf16[2,2,96,512]{3,2,1,0:T(8,128)(2,1)S(1)}, u32[]{:S(2)}, u32[]{:S(2)}) collective-permute-start(bf16[2,2,96,512]{3,2,1,0:T(8,128)(2,1)S(1)} %pad_maximum_fusion.2), channel_id=1, source_target_pairs={{0,192},{1,193},{2,194},{3,195},{4,196},{5,197},{6,198},{7,199},{8... | collective-permute-start | bytes 1179656 | tf_op jit(solution)/shard_map/ppermute | solution.py:43
  56.3 17.5 %collective-permute-start.10 = (bf16[2,2,96,512]{3,2,1,0:T(8,128)(2,1)S(1)}, bf16[2,2,96,512]{3,2,1,0:T(8,128)(2,1)}, u32[]{:S(2)}, u32[]{:S(2)}) collective-permute-start(bf16[2,2,96,512]{3,2,1,0:T(8,128)(2,1)S(1)} %pad_maximum_fusion.2), channel_id=1, source_target_pairs={{0,128},{1,129},{2,130},{3,131},{4,132},{5,133},{6,134},{7,135},{8... | collective-permute-start | bytes 1179656 | tf_op jit(solution)/shard_map/ppermute | solution.py:43
  56.3 18.0 %collective-permute-start.9 = (bf16[2,2,96,512]{3,2,1,0:T(8,128)(2,1)S(1)}, bf16[2,2,96,512]{3,2,1,0:T(8,128)(2,1)}, u32[]{:S(2)}, u32[]{:S(2)}) collective-permute-start(bf16[2,2,96,512]{3,2,1,0:T(8,128)(2,1)S(1)} %pad_maximum_fusion.2), channel_id=1, source_target_pairs={{0,64},{1,65},{2,66},{3,67},{4,68},{5,69},{6,70},{7,71},{8,72},{9,... | collective-permute-start | bytes 1179656 | tf_op jit(solution)/shard_map/ppermute | solution.py:43
  64.4 11.2 %collective-permute-start.13 = (s16[400,512]{1,0:T(8,128)(2,1)S(1)}, s16[400,512]{1,0:T(8,128)(2,1)S(1)}, u32[]{:S(2)}, u32[]{:S(2)}) collective-permute-start(s16[400,512]{1,0:T(8,128)(2,1)S(1)} %get-tuple-element.53), channel_id=1, source_target_pairs={{0,1},{1,0},{2,3},{3,2},{4,5},{5,4},{6,7},{7,6},{8,9},{9,8},{10,11... | collective-permute-start | bytes 1228808 | tf_op jit(solution)/shard_map/ppermute | solution.py:43
  64.8 10.8 %collective-permute-start.14 = (s16[400,512]{1,0:T(8,128)(2,1)S(1)}, s16[400,512]{1,0:T(8,128)(2,1)S(1)}, u32[]{:S(2)}, u32[]{:S(2)}) collective-permute-start(s16[400,512]{1,0:T(8,128)(2,1)S(1)} %get-tuple-element.54), channel_id=1, source_target_pairs={{0,3},{1,2},{2,1},{3,0},{4,7},{5,6},{6,5},{7,4},{8,11},{9,10},{10,... | collective-permute-start | bytes 1228808 | tf_op jit(solution)/shard_map/ppermute | solution.py:43
  77.9 31.8 %collective-permute-start.23 = (s16[400,512]{1,0:T(8,128)(2,1)S(1)}, s16[400,512]{1,0:T(8,128)(2,1)S(1)}, u32[]{:S(2)}, u32[]{:S(2)}) collective-permute-start(s16[400,512]{1,0:T(8,128)(2,1)S(1)} %get-tuple-element.73), channel_id=1, source_target_pairs={{0,2},{1,3},{2,0},{3,1},{4,6},{5,7},{6,4},{7,5},{8,10},{9,11},{10,... | collective-permute-start | bytes 1228808 | tf_op jit(solution)/shard_map/ppermute | solution.py:43
  86.0 26.3 %collective-permute-start.17 = (s16[400,512]{1,0:T(8,128)(2,1)S(1)}, s16[400,512]{1,0:T(8,128)(2,1)S(1)}, u32[]{:S(2)}, u32[]{:S(2)}) collective-permute-start(s16[400,512]{1,0:T(8,128)(2,1)S(1)} %get-tuple-element.63), channel_id=1, source_target_pairs={{0,1},{1,0},{2,3},{3,2},{4,5},{5,4},{6,7},{7,6},{8,9},{9,8},{10,11... | collective-permute-start | bytes 1228808 | tf_op jit(solution)/shard_map/ppermute | solution.py:43
  86.1 17.2 %collective-permute-start.16 = (bf16[3,96,512]{2,1,0:T(8,128)(2,1)S(1)}, bf16[3,96,512]{2,1,0:T(8,128)(2,1)S(1)}, u32[]{:S(2)}, u32[]{:S(2)}) collective-permute-start(bf16[3,96,512]{2,1,0:T(8,128)(2,1)S(1)} %bitcast_multiply_fusion.refs_5_.refs_9_), channel_id=1, source_target_pairs={{0,8},{1,9},{2,10},{3,11},{4,12},{5,13},{6,14},{7,15},{8,0},{9,1},... | collective-permute-start | bytes 884744 | tf_op jit(solution)/shard_map/ppermute | solution.py:43
  90.1 22.3 %collective-permute-start.18 = (s16[400,512]{1,0:T(8,128)(2,1)S(1)}, s16[400,512]{1,0:T(8,128)(2,1)S(1)}, u32[]{:S(2)}, u32[]{:S(2)}) collective-permute-start(s16[400,512]{1,0:T(8,128)(2,1)S(1)} %get-tuple-element.64), channel_id=1, source_target_pairs={{0,2},{1,3},{2,0},{3,1},{4,6},{5,7},{6,4},{7,5},{8,10},{9,11},{10,... | collective-permute-start | bytes 1228808 | tf_op jit(solution)/shard_map/ppermute | solution.py:43
  93.6 20.4 %collective-permute-start.19 = (s16[400,512]{1,0:T(8,128)(2,1)S(1)}, s16[400,512]{1,0:T(8,128)(2,1)S(1)}, u32[]{:S(2)}, u32[]{:S(2)}) collective-permute-start(s16[400,512]{1,0:T(8,128)(2,1)S(1)} %get-tuple-element.65), channel_id=1, source_target_pairs={{0,3},{1,2},{2,1},{3,0},{4,7},{5,6},{6,5},{7,4},{8,11},{9,10},{10,... | collective-permute-start | bytes 1228808 | tf_op jit(solution)/shard_map/ppermute | solution.py:43
  108.3 22.6 %collective-permute-start.20 = (s16[400,512]{1,0:T(8,128)(2,1)S(1)}, s16[400,512]{1,0:T(8,128)(2,1)S(1)}, u32[]{:S(2)}, u32[]{:S(2)}) collective-permute-start(s16[400,512]{1,0:T(8,128)(2,1)S(1)} %get-tuple-element.69), channel_id=1, source_target_pairs={{0,1},{1,0},{2,3},{3,2},{4,5},{5,4},{6,7},{7,6},{8,9},{9,8},{10,11... | collective-permute-start | bytes 1228808 | tf_op jit(solution)/shard_map/ppermute | solution.py:43
  109.6 21.4 %collective-permute-start.21 = (s16[400,512]{1,0:T(8,128)(2,1)S(1)}, s16[400,512]{1,0:T(8,128)(2,1)S(1)}, u32[]{:S(2)}, u32[]{:S(2)}) collective-permute-start(s16[400,512]{1,0:T(8,128)(2,1)S(1)} %get-tuple-element.70), channel_id=1, source_target_pairs={{0,2},{1,3},{2,0},{3,1},{4,6},{5,7},{6,4},{7,5},{8,10},{9,11},{10,... | collective-permute-start | bytes 1228808 | tf_op jit(solution)/shard_map/ppermute | solution.py:43
  112.3 19.9 %collective-permute-start.22 = (s16[400,512]{1,0:T(8,128)(2,1)S(1)}, s16[400,512]{1,0:T(8,128)(2,1)S(1)}, u32[]{:S(2)}, u32[]{:S(2)}) collective-permute-start(s16[400,512]{1,0:T(8,128)(2,1)S(1)} %get-tuple-element.71), channel_id=1, source_target_pairs={{0,3},{1,2},{2,1},{3,0},{4,7},{5,6},{6,5},{7,4},{8,11},{9,10},{10,... | collective-permute-start | bytes 1228808 | tf_op jit(solution)/shard_map/ppermute | solution.py:43
  112.4 9.2 %collective-permute-start.25 = (bf16[3,96,512]{2,1,0:T(8,128)(2,1)S(1)}, bf16[3,96,512]{2,1,0:T(8,128)(2,1)S(1)}, u32[]{:S(2)}, u32[]{:S(2)}) collective-permute-start(bf16[3,96,512]{2,1,0:T(8,128)(2,1)S(1)} %bitcast_multiply_fusion.refs_5_.refs_9_), channel_id=1, source_target_pairs={{0,12},{1,13},{2,14},{3,15},{4,8},{5,9},{6,10},{7,11},{8,4},{9,5},... | collective-permute-start | bytes 884744 | tf_op jit(solution)/shard_map/ppermute | solution.py:43
  114.0 15.0 %collective-permute-start.24 = (bf16[3,96,512]{2,1,0:T(8,128)(2,1)S(1)}, bf16[3,96,512]{2,1,0:T(8,128)(2,1)S(1)}, u32[]{:S(2)}, u32[]{:S(2)}) collective-permute-start(bf16[3,96,512]{2,1,0:T(8,128)(2,1)S(1)} %bitcast_multiply_fusion.refs_5_.refs_9_), channel_id=1, source_target_pairs={{0,4},{1,5},{2,6},{3,7},{4,0},{5,1},{6,2},{7,3},{8,12},{9,13},{10,... | collective-permute-start | bytes 884744 | tf_op jit(solution)/shard_map/ppermute | solution.py:43
  160.7 8.9 %collective-permute-start.35 = (f32[48,512]{1,0:T(8,128)S(1)}, f32[48,512]{1,0:T(8,128)S(1)}, u32[]{:S(2)}, u32[]{:S(2)}) collective-permute-start(f32[48,512]{1,0:T(8,128)S(1)} %gathered.1), channel_id=1, source_target_pairs={{0,8},{1,9},{2,10},{3,11},{4,12},{5,13},{6,14},{7,15},{8,0},{9,1},... | collective-permute-start | bytes 294920 | tf_op jit(solution)/shard_map/ppermute | solution.py:43
  160.7 8.9 %collective-permute-start.34 = (f32[48,512]{1,0:T(8,128)S(1)}, f32[48,512]{1,0:T(8,128)S(1)}, u32[]{:S(2)}, u32[]{:S(2)}) collective-permute-start(f32[48,512]{1,0:T(8,128)S(1)} %gathered.1), channel_id=1, source_target_pairs={{0,4},{1,5},{2,6},{3,7},{4,0},{5,1},{6,2},{7,3},{8,12},{9,13},{10,... | collective-permute-start | bytes 294920 | tf_op jit(solution)/shard_map/ppermute | solution.py:43
  162.7 15.3 %collective-permute-start.26 = (s16[224,512]{1,0:T(8,128)(2,1)S(1)}, s16[224,512]{1,0:T(8,128)(2,1)S(1)}, u32[]{:S(2)}, u32[]{:S(2)}) collective-permute-start(s16[224,512]{1,0:T(8,128)(2,1)S(1)} %get-tuple-element.83), channel_id=1, source_target_pairs={{0,4},{1,5},{2,6},{3,7},{4,0},{5,1},{6,2},{7,3},{8,12},{9,13},{10,... | collective-permute-start | bytes 688136 | tf_op jit(solution)/shard_map/ppermute | solution.py:43
  162.7 15.3 %collective-permute-start.27 = (s16[224,512]{1,0:T(8,128)(2,1)S(1)}, s16[224,512]{1,0:T(8,128)(2,1)S(1)}, u32[]{:S(2)}, u32[]{:S(2)}) collective-permute-start(s16[224,512]{1,0:T(8,128)(2,1)S(1)} %get-tuple-element.84), channel_id=1, source_target_pairs={{0,8},{1,9},{2,10},{3,11},{4,12},{5,13},{6,14},{7,15},{8,0},{9,1},... | collective-permute-start | bytes 688136 | tf_op jit(solution)/shard_map/ppermute | solution.py:43
  164.6 17.5 %collective-permute-start.28 = (s16[224,512]{1,0:T(8,128)(2,1)S(1)}, s16[224,512]{1,0:T(8,128)(2,1)S(1)}, u32[]{:S(2)}, u32[]{:S(2)}) collective-permute-start(s16[224,512]{1,0:T(8,128)(2,1)S(1)} %get-tuple-element.85), channel_id=1, source_target_pairs={{0,12},{1,13},{2,14},{3,15},{4,8},{5,9},{6,10},{7,11},{8,4},{9,5},... | collective-permute-start | bytes 688136 | tf_op jit(solution)/shard_map/ppermute | solution.py:43
  169.7 17.5 %collective-permute-start.37 = (f32[48,512]{1,0:T(8,128)S(1)}, f32[48,512]{1,0:T(8,128)S(1)}, u32[]{:S(2)}, u32[]{:S(2)}) collective-permute-start(f32[48,512]{1,0:T(8,128)S(1)} %add_add_fusion.own_ref), channel_id=1, source_target_pairs={{0,32},{1,33},{2,34},{3,35},{4,36},{5,37},{6,38},{7,39},{8,40},{9,... | collective-permute-start | bytes 294920 | tf_op jit(solution)/shard_map/ppermute | solution.py:43
  188.3 21.3 %all-to-all-start.1 = ((s16[16,48,640]{2,1,0:T(8,128)(2,1)}), s16[16,48,640]{2,1,0:T(8,128)(2,1)S(1)}, u32[]{:S(2)}, u32[]{:S(2)}) async-start(s16[16,48,640]{2,1,0:T(8,128)(2,1)} %copies.1), calls=%async_computation.1 | async-start | bytes 1966080 | tf_op jit(solution)/shard_map/all_to_all | solution.py:411
  192.2 9.9 %collective-permute-start.31 = (s16[112,512]{1,0:T(8,128)(2,1)S(1)}, s16[112,512]{1,0:T(8,128)(2,1)S(1)}, u32[]{:S(2)}, u32[]{:S(2)}) collective-permute-start(s16[112,512]{1,0:T(8,128)(2,1)S(1)} %get-tuple-element.93), channel_id=1, source_target_pairs={{0,4},{1,5},{2,6},{3,7},{4,0},{5,1},{6,2},{7,3},{8,12},{9,13},{10,... | collective-permute-start | bytes 344072 | tf_op jit(solution)/shard_map/ppermute | solution.py:43
  199.4 10.1 %collective-permute-start.32 = (s16[112,512]{1,0:T(8,128)(2,1)S(1)}, s16[112,512]{1,0:T(8,128)(2,1)S(1)}, u32[]{:S(2)}, u32[]{:S(2)}) collective-permute-start(s16[112,512]{1,0:T(8,128)(2,1)S(1)} %get-tuple-element.94), channel_id=1, source_target_pairs={{0,8},{1,9},{2,10},{3,11},{4,12},{5,13},{6,14},{7,15},{8,0},{9,1},... | collective-permute-start | bytes 344072 | tf_op jit(solution)/shard_map/ppermute | solution.py:43
  199.8 9.7 %collective-permute-start.33 = (s16[112,512]{1,0:T(8,128)(2,1)S(1)}, s16[112,512]{1,0:T(8,128)(2,1)S(1)}, u32[]{:S(2)}, u32[]{:S(2)}) collective-permute-start(s16[112,512]{1,0:T(8,128)(2,1)S(1)} %get-tuple-element.95), channel_id=1, source_target_pairs={{0,12},{1,13},{2,14},{3,15},{4,8},{5,9},{6,10},{7,11},{8,4},{9,5},... | collective-permute-start | bytes 344072 | tf_op jit(solution)/shard_map/ppermute | solution.py:43
  (10 other events, 41.0 us)
